TPU v7x, 32 devices: a whole 2x2x4 slice. The times are simulated.
32 devices in a mesh: fsdp: 8 (over y, x, core), expert: 4 (over z).
Axes of the slice: x: 2, y: 2, z: 4, core: 2. Of those that a mesh axis runs over, the one named last changes fastest.
Arguments:
- inputs: float32 [4096, 1536], P(('fsdp', 'expert')), may hold values from -6 to 6
- cotangent: float32 [4096, 1536], P(('fsdp', 'expert')), may hold values from -6 to 6
- norm1_gain: float32 [1536], P(('fsdp', 'expert')), may hold values from 0.5 to 1.5
- w_query: float32 [1536, 1536], P(('fsdp', 'expert')), may hold values from -0.15625 to 0.15625
- key_projection: float32 [1536, 512], P(('fsdp', 'expert')), may hold values from -0.15625 to 0.15625
- value_projection: float32 [1536, 512], P(('fsdp', 'expert')), may hold values from -0.15625 to 0.15625
- w_output: float32 [1536, 1536], P(('fsdp', 'expert')), may hold values from -2.5 to 2.5
- norm2_gain: float32 [1536], P(('fsdp', 'expert')), may hold values from 0.5 to 1.5
- w_router: float32 [1536, 20], P(('fsdp', 'expert')), may hold values from -0.078125 to 0.078125
- w_gate: float32 [20, 1536, 512], P('expert', 'fsdp'), may hold values from -0.15625 to 0.15625
- w_up: float32 [20, 1536, 512], P('expert', 'fsdp'), may hold values from -0.15625 to 0.15625
- w_down: float32 [20, 512, 1536], P('expert', 'fsdp'), may hold values from -1.5 to 1.5
- routes: int32 [4096, 8], P(('fsdp', 'expert')), may hold values from 0 to 19, all different within a row; in each aligned block of 128 rows (0 to 127, 128 to 255, ...) at most 80 rows name the same one
- piece_starts: int32 [8, 2], P('fsdp'), may hold values from 0 to 256, as said below
Outputs:
- output: float32 [4096, 1536], P(('fsdp', 'expert'))
- input_grad: float32 [4096, 1536], P(('fsdp', 'expert'))
- norm1_gain_grad: float32 [1536], P(('fsdp', 'expert'))
- w_query_grad: float32 [1536, 1536], P(('fsdp', 'expert'))
- w_key_grad: float32 [1536, 512], P(('fsdp', 'expert'))
- w_value_grad: float32 [1536, 512], P(('fsdp', 'expert'))
- w_output_grad: float32 [1536, 1536], P(('fsdp', 'expert'))
- norm2_gain_grad: float32 [1536], P(('fsdp', 'expert'))
- w_router_grad: float32 [1536, 20], P(('fsdp', 'expert'))
- w_gate_grad: float32 [20, 1536, 512], P('expert', 'fsdp')
- w_up_grad: float32 [20, 1536, 512], P('expert', 'fsdp')
- w_down_grad: float32 [20, 512, 1536], P('expert', 'fsdp')
Inputs may be any that keep to these rules, and one draw needn't show every extreme that they name: `routes`: each row names 8 different experts. In each aligned block of 128 rows (the rows of one device) no expert is named by more than 80 rows, a bound that some block reaches. `piece_starts`: the p-th image piece of a sequence lies inside positions p * (256) to (p + 1) * 256 - 1; pieces do not intersect.
All inputs are finite; a program needn't handle non-finite values.
Results may differ from a plain program's by a relative error of at most 0.02.
Values may be sent and summed in bfloat16 or wider, within the bound.
A program may use at most 192 MiB of HBM per device.

v0:
```python
import jax
import jax.numpy as jnp
from jax import lax
from jax.sharding import PartitionSpec as P

MODEL_WIDTH = 1536
QUERY_HEADS = 24
KEY_VALUE_HEADS = 8
HEAD_WIDTH = 64
TOPK = 8
EXP_DEV = 5
PIECE = 256
DEVICE_ROWS = 128


EPSILON = 1e-05
NEG_FILL = -1e30


def rms_scale(value_rows, gain_row):
    return (
        value_rows
        * lax.rsqrt(jnp.mean(value_rows * value_rows, axis=-1, keepdims=True) + EPSILON)
        * gain_row
    )


def apply_rotary(value_rows, position_index):
    half_width = value_rows.shape[-1] // 2
    inverse = 10000.0 ** (-(jnp.arange(half_width, dtype=jnp.float32) * 2.0 / value_rows.shape[-1]))
    angles = position_index.astype(jnp.float32)[:, None] * inverse[None, :]
    cosine = jnp.cos(angles)[:, None, :]
    sine_part = jnp.sin(angles)[:, None, :]
    first_half = value_rows[..., :half_width]
    second_half = value_rows[..., half_width:]
    return jnp.concatenate(
        [
            first_half * cosine - second_half * sine_part,
            second_half * cosine + first_half * sine_part,
        ],
        axis=-1,
    )


def piece_ids(position_index, starts):
    inside = (position_index[:, None] >= starts[None, :]) & (
        position_index[:, None] < starts[None, :] + PIECE
    )
    labels = jnp.arange(1, starts.shape[0] + 1, dtype=jnp.int32)[None, :]
    return jnp.sum(jnp.where(inside, labels, 0), axis=1, dtype=jnp.int32)


def visible_mask(query_places, key_places, starts):
    query_ids = piece_ids(query_places, starts)
    key_ids = piece_ids(key_places, starts)
    causal = key_places[None, :] <= query_places[:, None]
    shared = (query_ids[:, None] == key_ids[None, :]) & (query_ids[:, None] > 0)
    return causal | shared


def swiglu(gate_in, up_in):
    return jax.nn.silu(gate_in) * up_in


def on_device(
    inputs,
    cotangent,
    norm1_gain,
    w_query,
    key_projection,
    value_projection,
    w_output,
    norm2_gain,
    w_router,
    w_gate,
    w_up,
    w_down,
    routes,
    piece_starts,
):
    expert_ranks = lax.axis_size("expert")
    my_rank = lax.axis_index("expert")
    sequence_positions = DEVICE_ROWS * expert_ranks
    all_experts = EXP_DEV * expert_ranks
    capacity = 8 * (3 * DEVICE_ROWS * TOPK // (16 * all_experts) + 1)
    query_group_width = QUERY_HEADS // KEY_VALUE_HEADS
    key_value_width = KEY_VALUE_HEADS * HEAD_WIDTH
    q_width = QUERY_HEADS * HEAD_WIDTH
    score_scale = HEAD_WIDTH ** (-0.5)
    dense_local = (
        norm1_gain.astype(jnp.bfloat16),
        w_query.astype(jnp.bfloat16),
        key_projection.astype(jnp.bfloat16),
        value_projection.astype(jnp.bfloat16),
        w_output.astype(jnp.bfloat16),
        norm2_gain.astype(jnp.bfloat16),
        w_router.astype(jnp.bfloat16),
    )
    expert_local = (
        w_gate.astype(jnp.bfloat16),
        w_up.astype(jnp.bfloat16),
        w_down.astype(jnp.bfloat16),
    )
    gain_one, query_mat, key_mat, value_mat, output_mat, gain_two, router_mat = (
        lax.all_gather(dense_local[0], ("fsdp", "expert"), axis=0, tiled=True),
        lax.all_gather(dense_local[1], ("fsdp", "expert"), axis=0, tiled=True),
        lax.all_gather(dense_local[2], ("fsdp", "expert"), axis=0, tiled=True),
        lax.all_gather(dense_local[3], ("fsdp", "expert"), axis=0, tiled=True),
        lax.all_gather(dense_local[4], ("fsdp", "expert"), axis=0, tiled=True),
        lax.all_gather(dense_local[5], ("fsdp", "expert"), axis=0, tiled=True),
        lax.all_gather(dense_local[6], ("fsdp", "expert"), axis=0, tiled=True),
    )
    gate_mats, up_mats, down_mats = (
        lax.all_gather(expert_local[0], "fsdp", axis=1, tiled=True),
        lax.all_gather(expert_local[1], "fsdp", axis=1, tiled=True),
        lax.all_gather(expert_local[2], "fsdp", axis=1, tiled=True),
    )
    gain_one_f = gain_one.astype(jnp.float32)
    normed_one = rms_scale(inputs, gain_one_f)
    normed_low = normed_one.astype(jnp.bfloat16)
    query_linear = jnp.dot(normed_low, query_mat, preferred_element_type=jnp.float32)
    key_linear = jnp.dot(normed_low, key_mat, preferred_element_type=jnp.float32)
    value_lin = jnp.dot(normed_low, value_mat, preferred_element_type=jnp.float32)
    position_index = my_rank * DEVICE_ROWS + jnp.arange(DEVICE_ROWS, dtype=jnp.int32)
    query_rotated = apply_rotary(
        query_linear.reshape(DEVICE_ROWS, QUERY_HEADS, HEAD_WIDTH), position_index
    ).astype(jnp.bfloat16)
    key_rotated = (
        apply_rotary(key_linear.reshape(DEVICE_ROWS, KEY_VALUE_HEADS, HEAD_WIDTH), position_index)
        .astype(jnp.bfloat16)
        .reshape(DEVICE_ROWS, key_value_width)
    )
    value_reduced = value_lin.astype(jnp.bfloat16)
    gathered_keys, gathered_values = (
        lax.all_gather(key_rotated, "expert", axis=0, tiled=True),
        lax.all_gather(value_reduced, "expert", axis=0, tiled=True),
    )
    key_places = jnp.arange(sequence_positions, dtype=jnp.int32)
    visible = visible_mask(position_index, key_places, piece_starts[0])
    query_head_split = jnp.transpose(
        query_rotated.reshape(DEVICE_ROWS, KEY_VALUE_HEADS, query_group_width, HEAD_WIDTH),
        (1, 0, 2, 3),
    )
    key_head_split = jnp.transpose(
        gathered_keys.reshape(sequence_positions, KEY_VALUE_HEADS, HEAD_WIDTH), (1, 0, 2)
    )
    value_head_split = jnp.transpose(
        gathered_values.reshape(sequence_positions, KEY_VALUE_HEADS, HEAD_WIDTH), (1, 0, 2)
    )

    def head_scores(query_block, key_block):
        scores = score_scale * jnp.einsum(
            "rgd,jd->grj", query_block, key_block, preferred_element_type=jnp.float32
        )
        return jnp.where(visible[None, :, :], scores, NEG_FILL)

    def forward_head(operands):
        query_block, key_block, value_block = operands
        scores = head_scores(query_block, key_block)
        row_max = jnp.max(scores, axis=-1)
        weights_exp = jnp.exp(scores - row_max[..., None])
        row_total = jnp.sum(weights_exp, axis=-1)
        prob_low = (weights_exp / row_total[..., None]).astype(jnp.bfloat16)
        mixed_rows = jnp.einsum(
            "grj,jd->rgd", prob_low, value_block, preferred_element_type=jnp.float32
        )
        return (mixed_rows, row_max, row_total)

    head_out, row_maxes, row_totals = lax.map(
        forward_head, (query_head_split, key_head_split, value_head_split)
    )
    attended_low = (
        jnp.transpose(head_out, (1, 0, 2, 3)).reshape(DEVICE_ROWS, q_width).astype(jnp.bfloat16)
    )
    resid_mid = inputs + jnp.dot(attended_low, output_mat, preferred_element_type=jnp.float32)
    gain_two_f = gain_two.astype(jnp.float32)
    normed_two_low = rms_scale(resid_mid, gain_two_f).astype(jnp.bfloat16)
    router_logits = jnp.dot(normed_two_low, router_mat, preferred_element_type=jnp.float32)
    chosen = jnp.take_along_axis(router_logits, routes, axis=1)
    chosen_exp = jnp.exp(chosen - jnp.max(chosen, axis=1, keepdims=True))
    gate_probs = chosen_exp / jnp.sum(chosen_exp, axis=1, keepdims=True)
    flat_routes = routes.reshape(-1)
    expert_ids = jnp.arange(all_experts, dtype=jnp.int32)
    one_hot = (flat_routes[:, None] == expert_ids[None, :]).astype(jnp.int32)
    slot_rank = (
        jnp.sum(one_hot * jnp.cumsum(one_hot, axis=0, dtype=jnp.int32), axis=1, dtype=jnp.int32) - 1
    )
    slot_index = flat_routes * capacity + slot_rank

    def to_slots(slot_values):
        filled = (
            jnp.zeros((all_experts * capacity, MODEL_WIDTH), jnp.bfloat16)
            .at[slot_index]
            .set(slot_values)
        )
        return filled.reshape(expert_ranks, EXP_DEV, capacity, MODEL_WIDTH)

    def from_slots(slot_buffer):
        return (
            slot_buffer.reshape(all_experts * capacity, MODEL_WIDTH)[slot_index]
            .reshape(DEVICE_ROWS, TOPK, MODEL_WIDTH)
            .astype(jnp.float32)
        )

    sent_rows = to_slots(jnp.repeat(normed_two_low, TOPK, axis=0))
    expert_rows = lax.all_to_all(sent_rows, "expert", split_axis=0, concat_axis=0, tiled=True)
    gate_lin = jnp.einsum(
        "secd,edf->secf", expert_rows, gate_mats, preferred_element_type=jnp.float32
    )
    up_lin = jnp.einsum("secd,edf->secf", expert_rows, up_mats, preferred_element_type=jnp.float32)
    hidden_low = swiglu(gate_lin, up_lin).astype(jnp.bfloat16)
    expert_out = jnp.einsum(
        "secf,efd->secd", hidden_low, down_mats, preferred_element_type=jnp.float32
    ).astype(jnp.bfloat16)
    returned = lax.all_to_all(expert_out, "expert", split_axis=0, concat_axis=0, tiled=True)
    route_out = from_slots(returned)
    output = resid_mid + jnp.sum(gate_probs[:, :, None] * route_out, axis=1)
    gate_grad = jnp.sum(cotangent[:, None, :] * route_out, axis=-1)
    route_grad = (gate_probs[:, :, None] * cotangent[:, None, :]).astype(jnp.bfloat16)
    sent_grads = to_slots(route_grad.reshape(DEVICE_ROWS * TOPK, MODEL_WIDTH))
    gate_mats, up_mats, down_mats = (
        lax.all_gather(expert_local[0], "fsdp", axis=1, tiled=True),
        lax.all_gather(expert_local[1], "fsdp", axis=1, tiled=True),
        lax.all_gather(expert_local[2], "fsdp", axis=1, tiled=True),
    )
    out_grads = lax.all_to_all(sent_grads, "expert", split_axis=0, concat_axis=0, tiled=True)
    hidden_grad = jnp.einsum(
        "secd,efd->secf", out_grads, down_mats, preferred_element_type=jnp.float32
    )
    down_w_grad = jnp.einsum(
        "secf,secd->efd", hidden_low, out_grads, preferred_element_type=jnp.float32
    )
    unused, swiglu_back = jax.vjp(swiglu, gate_lin, up_lin)
    gate_lin_grad, up_lin_grad = swiglu_back(hidden_grad)
    gate_low_grad = gate_lin_grad.astype(jnp.bfloat16)
    up_low_grad = up_lin_grad.astype(jnp.bfloat16)
    gate_w_grad = jnp.einsum(
        "secd,secf->edf", expert_rows, gate_low_grad, preferred_element_type=jnp.float32
    )
    up_w_grad = jnp.einsum(
        "secd,secf->edf", expert_rows, up_low_grad, preferred_element_type=jnp.float32
    )
    rows_grad = (
        jnp.einsum("secf,edf->secd", gate_low_grad, gate_mats, preferred_element_type=jnp.float32)
        + jnp.einsum("secf,edf->secd", up_low_grad, up_mats, preferred_element_type=jnp.float32)
    ).astype(jnp.bfloat16)
    back_grads = lax.all_to_all(rows_grad, "expert", split_axis=0, concat_axis=0, tiled=True)
    gate_w_sum, up_w_sum, down_w_sum = (
        lax.psum_scatter(
            gate_w_grad.astype(jnp.bfloat16), "fsdp", scatter_dimension=1, tiled=True
        ).astype(jnp.float32),
        lax.psum_scatter(
            up_w_grad.astype(jnp.bfloat16), "fsdp", scatter_dimension=1, tiled=True
        ).astype(jnp.float32),
        lax.psum_scatter(
            down_w_grad.astype(jnp.bfloat16), "fsdp", scatter_dimension=1, tiled=True
        ).astype(jnp.float32),
    )
    chosen_grad = gate_probs * (gate_grad - jnp.sum(gate_probs * gate_grad, axis=1, keepdims=True))
    logit_grad = jnp.sum(
        jnp.where(routes[:, :, None] == expert_ids[None, None, :], chosen_grad[:, :, None], 0.0),
        axis=1,
    ).astype(jnp.bfloat16)
    gain_one, query_mat, key_mat, value_mat, output_mat, gain_two, router_mat = (
        lax.all_gather(dense_local[0], ("fsdp", "expert"), axis=0, tiled=True),
        lax.all_gather(dense_local[1], ("fsdp", "expert"), axis=0, tiled=True),
        lax.all_gather(dense_local[2], ("fsdp", "expert"), axis=0, tiled=True),
        lax.all_gather(dense_local[3], ("fsdp", "expert"), axis=0, tiled=True),
        lax.all_gather(dense_local[4], ("fsdp", "expert"), axis=0, tiled=True),
        lax.all_gather(dense_local[5], ("fsdp", "expert"), axis=0, tiled=True),
        lax.all_gather(dense_local[6], ("fsdp", "expert"), axis=0, tiled=True),
    )
    router_grad = jnp.dot(normed_two_low.T, logit_grad, preferred_element_type=jnp.float32)
    normed_two_grad = jnp.sum(from_slots(back_grads), axis=1) + jnp.dot(
        logit_grad, router_mat.T, preferred_element_type=jnp.float32
    )
    unused_two, norm_two_back = jax.vjp(rms_scale, resid_mid, gain_two_f)
    mid_from_norm, gain_two_grad = norm_two_back(normed_two_grad)
    mid_grad = cotangent + mid_from_norm
    branch_low = mid_grad.astype(jnp.bfloat16)
    output_w_grad = jnp.dot(attended_low.T, branch_low, preferred_element_type=jnp.float32)
    attention_out_grad = jnp.dot(
        branch_low, output_mat.T, preferred_element_type=jnp.float32
    ).astype(jnp.bfloat16)
    head_gradients = jnp.transpose(
        attention_out_grad.reshape(DEVICE_ROWS, KEY_VALUE_HEADS, query_group_width, HEAD_WIDTH),
        (1, 0, 2, 3),
    )

    def backward_head(operands):
        query_block, key_block, value_block, grad_block, row_max, row_total = operands
        scores = head_scores(query_block, key_block)
        prob_rows = jnp.exp(scores - row_max[..., None]) / row_total[..., None]
        prob_grad = jnp.einsum(
            "rgd,jd->grj", grad_block, value_block, preferred_element_type=jnp.float32
        )
        row_dot = jnp.sum(prob_rows * prob_grad, axis=-1)
        score_grad = (prob_rows * (prob_grad - row_dot[..., None])).astype(jnp.bfloat16)
        query_grad = score_scale * jnp.einsum(
            "grj,jd->rgd", score_grad, key_block, preferred_element_type=jnp.float32
        )
        key_grad = score_scale * jnp.einsum(
            "grj,rgd->jd", score_grad, query_block, preferred_element_type=jnp.float32
        )
        value_grad = jnp.einsum(
            "grj,rgd->jd",
            prob_rows.astype(jnp.bfloat16),
            grad_block,
            preferred_element_type=jnp.float32,
        )
        return (query_grad, key_grad, value_grad)

    query_grads, key_grads, value_grads = lax.map(
        backward_head,
        (query_head_split, key_head_split, value_head_split, head_gradients, row_maxes, row_totals),
    )
    key_full_grad = jnp.transpose(key_grads, (1, 0, 2)).reshape(sequence_positions, key_value_width)
    value_full_grad = jnp.transpose(value_grads, (1, 0, 2)).reshape(
        sequence_positions, key_value_width
    )
    local_keys, value_own = (
        lax.psum_scatter(
            key_full_grad.astype(jnp.bfloat16), "expert", scatter_dimension=0, tiled=True
        ).astype(jnp.float32),
        lax.psum_scatter(
            value_full_grad.astype(jnp.bfloat16), "expert", scatter_dimension=0, tiled=True
        ).astype(jnp.float32),
    )
    unused_q, query_rot_back = jax.vjp(
        lambda value_rows: apply_rotary(value_rows, position_index),
        query_linear.reshape(DEVICE_ROWS, QUERY_HEADS, HEAD_WIDTH),
    )
    unused_k, key_rotation_inverse = jax.vjp(
        lambda value_rows: apply_rotary(value_rows, position_index),
        key_linear.reshape(DEVICE_ROWS, KEY_VALUE_HEADS, HEAD_WIDTH),
    )
    query_rot_grad = jnp.transpose(query_grads, (1, 0, 2, 3)).reshape(
        DEVICE_ROWS, QUERY_HEADS, HEAD_WIDTH
    )
    query_low_grad = (
        query_rot_back(query_rot_grad)[0].reshape(DEVICE_ROWS, q_width).astype(jnp.bfloat16)
    )
    key_low_grad = (
        key_rotation_inverse(local_keys.reshape(DEVICE_ROWS, KEY_VALUE_HEADS, HEAD_WIDTH))[0]
        .reshape(DEVICE_ROWS, key_value_width)
        .astype(jnp.bfloat16)
    )
    value_low_grad = value_own.astype(jnp.bfloat16)
    query_w_grad = jnp.dot(normed_low.T, query_low_grad, preferred_element_type=jnp.float32)
    key_w_grad = jnp.dot(normed_low.T, key_low_grad, preferred_element_type=jnp.float32)
    value_w_grad = jnp.dot(normed_low.T, value_low_grad, preferred_element_type=jnp.float32)
    normed_one_grad = (
        jnp.dot(query_low_grad, query_mat.T, preferred_element_type=jnp.float32)
        + jnp.dot(key_low_grad, key_mat.T, preferred_element_type=jnp.float32)
        + jnp.dot(value_low_grad, value_mat.T, preferred_element_type=jnp.float32)
    )
    unused_one, norm_one_back = jax.vjp(rms_scale, inputs, gain_one_f)
    input_from_norm, gain_one_grad = norm_one_back(normed_one_grad)
    input_grad = mid_grad + input_from_norm
    dense_sums = (
        lax.psum_scatter(gain_one_grad, ("fsdp", "expert"), scatter_dimension=0, tiled=True),
        lax.psum_scatter(query_w_grad, ("fsdp", "expert"), scatter_dimension=0, tiled=True),
        lax.psum_scatter(key_w_grad, ("fsdp", "expert"), scatter_dimension=0, tiled=True),
        lax.psum_scatter(value_w_grad, ("fsdp", "expert"), scatter_dimension=0, tiled=True),
        lax.psum_scatter(output_w_grad, ("fsdp", "expert"), scatter_dimension=0, tiled=True),
        lax.psum_scatter(gain_two_grad, ("fsdp", "expert"), scatter_dimension=0, tiled=True),
        lax.psum_scatter(router_grad, ("fsdp", "expert"), scatter_dimension=0, tiled=True),
    )
    return (
        output,
        input_grad,
        dense_sums[0],
        dense_sums[1],
        dense_sums[2],
        dense_sums[3],
        dense_sums[4],
        dense_sums[5],
        dense_sums[6],
        gate_w_sum,
        up_w_sum,
        down_w_sum,
    )


def solution(mesh):
    in_specs = (
        P(("fsdp", "expert"), None),
        P(("fsdp", "expert"), None),
        P(("fsdp", "expert")),
        P(("fsdp", "expert"), None),
        P(("fsdp", "expert"), None),
        P(("fsdp", "expert"), None),
        P(("fsdp", "expert"), None),
        P(("fsdp", "expert")),
        P(("fsdp", "expert"), None),
        P("expert", "fsdp", None),
        P("expert", "fsdp", None),
        P("expert", "fsdp", None),
        P(("fsdp", "expert"), None),
        P("fsdp", None),
    )
    out_specs = (
        P(("fsdp", "expert"), None),
        P(("fsdp", "expert"), None),
        P(("fsdp", "expert")),
        P(("fsdp", "expert"), None),
        P(("fsdp", "expert"), None),
        P(("fsdp", "expert"), None),
        P(("fsdp", "expert"), None),
        P(("fsdp", "expert")),
        P(("fsdp", "expert"), None),
        P("expert", "fsdp", None),
        P("expert", "fsdp", None),
        P("expert", "fsdp", None),
    )
    return jax.shard_map(
        on_device, mesh=mesh, in_specs=in_specs, out_specs=out_specs, check_vma=False
    )
```

profile of v0, /device:TPU:27, one launch (start us, length us, event | category | flops | bytes accessed | tf_op | source)
XLA Modules:
  0.0 1705.5 jit_solution(7038965999893583246)
XLA Ops:
  18.9 38.3 %all-reduce.9 = (bf16[1536]{0:T(1024)(128)(2,1)S(1)}, bf16[1536]{0:T(1024)(128)(2,1)S(1)}) all-reduce(bf16[1536]{0:T(1024)(128)(2,1)S(1)} %dynamic-update-slice, bf16[1536]{0:T(1024)(128)(2,1)S(1)} %dynamic-update-slice.1), channel_id=1, replica_groups=mesh['fsdp'=8,'expert'=4] {'fsdp','expert'}, use_global_device_ids=true, to_apply=%add.4 | all-reduce | flops 3072 | bytes 12288
  58.1 65.6 %all-gather = bf16[32,48,20]{1,2,0:T(8,128)(2,1)S(1)} all-gather(bf16[1,48,20]{1,2,0:T(8,128)(2,1)S(1)} %convert_bitcast_fusion.1), channel_id=1, replica_groups=mesh['fsdp'=8,'expert'=4] {'fsdp','expert'}, dimensions={0}, use_global_device_ids=true | all-gather | bytes 63360 | tf_op jit(solution)/shard_map/all_gather | solution.py:111
  132.7 15.5 all_gather.46
  150.6 18.0 %all_gather.48 = bf16[512,512]{0,1:T(8,128)(2,1)S(1)} all-gather(bf16[128,512]{0,1:T(8,128)(2,1)S(1)} %bitcast.350), channel_id=1, replica_groups=mesh['fsdp'=8,'expert'=4] {'expert'}, dimensions={0}, use_global_device_ids=true | all-gather | bytes 655360 | tf_op jit(solution)/shard_map/all_gather | solution.py:135
  168.7 24.4 %all-gather.13.cloned.1.call-done = bf16[1536,1536]{1,0:T(8,128)(2,1)} async-done(((bf16[48,1536]{1,0:T(8,128)(2,1)}), bf16[1536,1536]{1,0:T(8,128)(2,1)}) %all-gather.13.cloned.1.call-update) | async-done | bytes 4718608 | tf_op jit(solution)/shard_map/all_gather | solution.py:106
  204.9 53.4 %all-gather.15.cloned.1.call-done = bf16[1536,1536]{1,0:T(8,128)(2,1)} async-done(((bf16[48,1536]{1,0:T(8,128)(2,1)}), bf16[1536,1536]{1,0:T(8,128)(2,1)}) %all-gather.15.cloned.1.call-update) | async-done | bytes 4718608 | tf_op jit(solution)/shard_map/all_gather | solution.py:109
  296.0 96.5 %all-to-all-done.2 = bf16[4,5,80,1536]{3,2,1,0:T(8,128)(2,1)} async-done(((bf16[4,5,80,1536]{3,2,1,0:T(8,128)(2,1)}), bf16[4,5,80,1536]{3,2,1,0:T(8,128)(2,1)}, u32[]{:S(2)}, u32[]{:S(2)}) %all-to-all-start.2) | async-done | bytes 4915232 | tf_op jit(solution)/shard_map/all_to_all | solution.py:226
  409.1 96.4 %all-to-all-done = bf16[4,5,80,1536]{3,2,1,0:T(8,128)(2,1)} async-done(((bf16[4,5,80,1536]{3,2,1,0:T(8,128)(2,1)}), bf16[4,5,80,1536]{3,2,1,0:T(8,128)(2,1)}, u32[]{:S(2)}, u32[]{:S(2)}) %all-to-all-start) | async-done | bytes 4915232 | tf_op jit(solution)/shard_map/all_to_all | solution.py:206
  514.6 11.7 fusion.79
  543.9 10.8 fusion.53
  566.5 82.7 %all-to-all-done.1 = bf16[4,5,80,1536]{3,2,1,0:T(8,128)(2,1)} async-done(((bf16[4,5,80,1536]{3,2,1,0:T(8,128)(2,1)}), bf16[4,5,80,1536]{3,2,1,0:T(8,128)(2,1)}, u32[]{:S(2)}, u32[]{:S(2)}) %all-to-all-start.1) | async-done | bytes 4915232 | tf_op jit(solution)/shard_map/all_to_all | solution.py:215
  657.4 9.7 gather_fusion
  671.6 90.8 %all-to-all-done.3 = bf16[4,5,80,1536]{3,2,1,0:T(8,128)(2,1)} async-done(((bf16[4,5,80,1536]{3,2,1,0:T(8,128)(2,1)}), bf16[4,5,80,1536]{3,2,1,0:T(8,128)(2,1)}, u32[]{:S(2)}, u32[]{:S(2)}) %all-to-all-start.3) | async-done | bytes 4915232 | tf_op jit(solution)/shard_map/all_to_all | solution.py:247
  762.5 10.4 gather_fusion.1
  782.8 55.0 %while.33 = (s32[]{:T(128)}, f32[8,128,3,64]{1,3,2,0:T(8,128)}, bf16[8,512,64]{1,2,0:T(8,128)(2,1)}, bf16[8,512,64]{1,2,0:T(8,128)(2,1)}, bf16[8,512,64]{1,2,0:T...) while((s32[]{:T(128)}, f32[8,128,3,64]{1,3,2,0:T(8,128)}, ...), condition=%wide.region_23.24_spmd.clone.clone, body=%wide.region_21.23_spmd.clone.sunk.clone | while | flops 128114304 | bytes 6803721 | solution.py:313
  902.8 80.0 %reduce-scatter.35.cloned.1.call-done = f32[48,20]{1,0:T(8,128)} async-done(((f32[1536,20]{1,0:T(8,128)}), f32[48,20]{1,0:T(8,128)}) %reduce-scatter.35.cloned.1.call-update) | async-done | bytes 3856
  989.1 40.8 %all-reduce.8 = (f32[1536]{0:T(1024)S(1)}, f32[1536]{0:T(1024)S(1)}) all-reduce(f32[1536]{0:T(1024)S(1)} %get-tuple-element.187, f32[1536]{0:T(1024)S(1)} %get-tuple-element.185), channel_id=4, replica_groups=mesh['fsdp'=8,'expert'=4] {'fsdp','expert'}, use_global_device_ids=true, to_apply=%region_28.29.clone | all-reduce | flops 3072 | bytes 24576
  1033.4 24.5 %reduce-scatter.29.cloned.1.call-done = bf16[5,64,1536]{2,1,0:T(8,128)(2,1)} async-done(((bf16[5,512,1536]{2,1,0:T(8,128)(2,1)}), bf16[5,64,1536]{2,1,0:T(8,128)(2,1)}) %reduce-scatter.29.cloned.1.call-update) | async-done | bytes 983056 | tf_op jit(solution)/shard_map/reduce_scatter | solution.py:255
  1060.6 69.9 %reduce-scatter.25.cloned.1.call-done = bf16[5,192,512]{2,1,0:T(8,128)(2,1)} async-done(((bf16[5,1536,512]{2,1,0:T(8,128)(2,1)}), bf16[5,192,512]{2,1,0:T(8,128)(2,1)}) %reduce-scatter.25.cloned.1.call-update) | async-done | bytes 983056 | tf_op jit(solution)/shard_map/reduce_scatter | solution.py:249
  1133.3 70.0 %reduce-scatter.27.cloned.1.call-done = bf16[5,192,512]{2,1,0:T(8,128)(2,1)} async-done(((bf16[5,1536,512]{2,1,0:T(8,128)(2,1)}), bf16[5,192,512]{2,1,0:T(8,128)(2,1)}) %reduce-scatter.27.cloned.1.call-update) | async-done | bytes 983056 | tf_op jit(solution)/shard_map/reduce_scatter | solution.py:252
  1206.0 102.7 %reduce-scatter.19.cloned.1.call-done = f32[48,512]{1,0:T(8,128)} async-done(((f32[1536,512]{1,0:T(8,128)}), f32[48,512]{1,0:T(8,128)}) %reduce-scatter.19.cloned.1.call-update) | async-done | bytes 98320 | tf_op jit(solution)/shard_map/reduce_scatter | solution.py:363
  1308.7 106.9 %reduce-scatter.21.cloned.1.call-done = f32[48,512]{1,0:T(8,128)} async-done(((f32[1536,512]{1,0:T(8,128)}), f32[48,512]{1,0:T(8,128)}) %reduce-scatter.21.cloned.1.call-update) | async-done | bytes 98320 | tf_op jit(solution)/shard_map/reduce_scatter | solution.py:364
  1415.6 141.5 %reduce-scatter.17.cloned.1.call-done = f32[48,1536]{1,0:T(8,128)} async-done(((f32[1536,1536]{1,0:T(8,128)}), f32[48,1536]{1,0:T(8,128)}) %reduce-scatter.17.cloned.1.call-update) | async-done | bytes 294928 | tf_op jit(solution)/shard_map/reduce_scatter | solution.py:362
  1557.1 141.7 %reduce-scatter.23.cloned.1.call-done = f32[48,1536]{1,0:T(8,128)} async-done(((f32[1536,1536]{1,0:T(8,128)}), f32[48,1536]{1,0:T(8,128)}) %reduce-scatter.23.cloned.1.call-update) | async-done | bytes 294928 | tf_op jit(solution)/shard_map/reduce_scatter | solution.py:365
  (355 shorter events, 294.8 us)
Async XLA Ops:
  7.2 123.7 %all-gather.9.cloned.1.call-start = ((), (), s32[]{:S(2)}) async-start(), calls=%async_computation.14 | async-start | bytes 1622016 | tf_op jit(solution)/shard_map/all_gather | solution.py:108
  8.9 139.3 %all-gather.11.cloned.1.call-start = ((), (), s32[]{:S(2)}) async-start(), calls=%async_computation.15 | async-start | bytes 1622016 | tf_op jit(solution)/shard_map/all_gather | solution.py:107
  10.5 182.6 %all-gather.13.cloned.1.call-start = ((), (), s32[]{:S(2)}) async-start(), calls=%async_computation.16 | async-start | bytes 4866048 | tf_op jit(solution)/shard_map/all_gather | solution.py:106
  12.2 246.0 %all-gather.15.cloned.1.call-start = ((), (), s32[]{:S(2)}) async-start(), calls=%async_computation.17 | async-start | bytes 4866048 | tf_op jit(solution)/shard_map/all_gather | solution.py:109
  14.0 385.9 %all-gather.21.cloned.1.call-start = ((), (), s32[]{:S(2)}) async-start(), calls=%async_computation.20 | async-start | bytes 8847360 | tf_op jit(solution)/shard_map/all_gather | solution.py:116
  16.7 392.4 %all-gather.19.cloned.1.call-start = ((), (), s32[]{:S(2)}) async-start(), calls=%async_computation.19 | async-start | bytes 8847360 | tf_op jit(solution)/shard_map/all_gather | solution.py:115
  57.2 93.2 %copy-start.30 = (f32[1536]{0:T(1024)}, f32[1536]{0:T(1024)S(1)}, u32[]{:S(2)}) copy-start(f32[1536]{0:T(1024)S(1)} %convert_element_type.187) | copy-start | bytes 18436
  279.1 113.4 %all-to-all-start.2 = ((bf16[4,5,80,1536]{3,2,1,0:T(8,128)(2,1)}), bf16[4,5,80,1536]{3,2,1,0:T(8,128)(2,1)}, u32[]{:S(2)}, u32[]{:S(2)}) async-start(bf16[4,5,80,1536]{3,2,1,0:T(8,128)(2,1)} %bitcast.335), calls=%async_computation.2 | async-start | bytes 9830400 | tf_op jit(solution)/shard_map/all_to_all | solution.py:226
  286.0 228.6 %all-gather.17.cloned.1.call-start = ((), (), s32[]{:S(2)}) async-start(), calls=%async_computation.18 | async-start | bytes 8847360 | tf_op jit(solution)/shard_map/all_gather | solution.py:114
  392.5 113.0 %all-to-all-start = ((bf16[4,5,80,1536]{3,2,1,0:T(8,128)(2,1)}), bf16[4,5,80,1536]{3,2,1,0:T(8,128)(2,1)}, u32[]{:S(2)}, u32[]{:S(2)}) async-start(bf16[4,5,80,1536]{3,2,1,0:T(8,128)(2,1)} %bitcast.336), calls=%async_computation | async-start | bytes 9830400 | tf_op jit(solution)/shard_map/all_to_all | solution.py:206
  536.2 113.0 %all-to-all-start.1 = ((bf16[4,5,80,1536]{3,2,1,0:T(8,128)(2,1)}), bf16[4,5,80,1536]{3,2,1,0:T(8,128)(2,1)}, u32[]{:S(2)}, u32[]{:S(2)}) async-start(bf16[4,5,80,1536]{3,2,1,0:T(8,128)(2,1)} %copy.165), calls=%async_computation.1 | async-start | bytes 9830400 | tf_op jit(solution)/shard_map/all_to_all | solution.py:215
  649.2 113.2 %all-to-all-start.3 = ((bf16[4,5,80,1536]{3,2,1,0:T(8,128)(2,1)}), bf16[4,5,80,1536]{3,2,1,0:T(8,128)(2,1)}, u32[]{:S(2)}, u32[]{:S(2)}) async-start(bf16[4,5,80,1536]{3,2,1,0:T(8,128)(2,1)} %copy.168), calls=%async_computation.3 | async-start | bytes 9830400 | tf_op jit(solution)/shard_map/all_to_all | solution.py:247
  657.1 216.7 %reduce-scatter.31.cloned.1.call-start = ((), (), s32[]{:S(2)}) async-start(), calls=%async_computation.28 | async-start | bytes 655360
  840.0 42.0 %reduce-scatter.33.cloned.1.call-start = ((), (), s32[]{:S(2)}) async-start(), calls=%async_computation.29 | async-start | bytes 655360
  842.2 140.7 %reduce-scatter.35.cloned.1.call-start = ((), (), s32[]{:S(2)}) async-start(), calls=%async_computation.30 | async-start | bytes 811008
  843.4 214.5 %reduce-scatter.29.cloned.1.call-start = ((), (), s32[]{:S(2)}) async-start(), calls=%async_computation.27 | async-start | bytes 8847360 | tf_op jit(solution)/shard_map/reduce_scatter | solution.py:255
  852.4 278.2 %reduce-scatter.25.cloned.1.call-start = ((), (), s32[]{:S(2)}) async-start(), calls=%async_computation.25 | async-start | bytes 8847360 | tf_op jit(solution)/shard_map/reduce_scatter | solution.py:249
  863.1 340.2 %reduce-scatter.27.cloned.1.call-start = ((), (), s32[]{:S(2)}) async-start(), calls=%async_computation.26 | async-start | bytes 8847360 | tf_op jit(solution)/shard_map/reduce_scatter | solution.py:252
  873.8 434.9 %reduce-scatter.19.cloned.1.call-start = ((), (), s32[]{:S(2)}) async-start(), calls=%async_computation.22 | async-start | bytes 3244032 | tf_op jit(solution)/shard_map/reduce_scatter | solution.py:363
  877.3 538.3 %reduce-scatter.21.cloned.1.call-start = ((), (), s32[]{:S(2)}) async-start(), calls=%async_computation.23 | async-start | bytes 3244032 | tf_op jit(solution)/shard_map/reduce_scatter | solution.py:364
  885.2 671.9 %reduce-scatter.17.cloned.1.call-start = ((), (), s32[]{:S(2)}) async-start(), calls=%async_computation.21 | async-start | bytes 9732096 | tf_op jit(solution)/shard_map/reduce_scatter | solution.py:362
  891.7 807.1 %reduce-scatter.23.cloned.1.call-start = ((), (), s32[]{:S(2)}) async-start(), calls=%async_computation.24 | async-start | bytes 9732096 | tf_op jit(solution)/shard_map/reduce_scatter | solution.py:365
  902.8 128.3 %copy-start.37 = (f32[128]{0:T(128)S(1)}, f32[128]{0:T(128)}, u32[]{:S(2)}) copy-start(f32[128]{0:T(128)} %copy-done.36) | copy-start | bytes 1540
  902.8 128.3 %copy-start.34 = (f32[128]{0:T(128)S(1)}, f32[128]{0:T(128)}, u32[]{:S(2)}) copy-start(f32[128]{0:T(128)} %copy-done.33) | copy-start | bytes 1540
  (37 other events, 1126.2 us)
Sparse Core Ops, SparseCore 0:
  11.4 55.4 all-gather.8
  70.4 54.0 all-gather.10
  127.9 65.1 all-gather.12
  196.3 61.9 all-gather.14
  260.6 52.0 all-gather.20
  315.1 52.0 all-gather.18
  369.6 52.0 all-gather.16
  840.1 19.3 reduce-scatter.30
  861.8 20.1 reduce-scatter.32
  886.9 95.9 reduce-scatter.34
  986.3 71.5 reduce-scatter.28
  1061.2 69.2 reduce-scatter.24
  1134.0 69.2 reduce-scatter.26
  1209.1 99.5 reduce-scatter.18
  1314.6 101.0 reduce-scatter.20
  1422.0 135.0 reduce-scatter.16
  1563.4 135.3 reduce-scatter.22
where the time goes:
time: 1720 us; the launch traced here: 1710 us
  waiting for transfers between devices  1190 us (69%)
  matrix products  185 us (11%)
  blocking collectives  178 us (10%)
  local copies, waits for them, and re-layouts  56.1 us (3%)
  other arithmetic  52.5 us (3%)
  starting transfers between devices  31.4 us (2%)
    reduce_scatter x1, waiting for transfers between devices, on_device(): lax.psum_scatter(output_w_grad, ('fsdp', 'expert'), scatter_dimension=0,...  142 us
    reduce_scatter x1, waiting for transfers between devices, on_device(): lax.psum_scatter(query_w_grad, ('fsdp', 'expert'), scatter_dimension=0, t...  141 us
    reduce_scatter x1, waiting for transfers between devices, on_device(): lax.psum_scatter(value_w_grad, ('fsdp', 'expert'), scatter_dimension=0, t...  107 us
    reduce_scatter x1, waiting for transfers between devices, on_device(): lax.psum_scatter(key_w_grad, ('fsdp', 'expert'), scatter_dimension=0, til...  103 us
    all_to_all x1, waiting for transfers between devices, on_device(): lax.all_to_all(sent_grads, 'expert', split_axis=0, concat_axis=0, tiled=T...  96.5 us
    all_to_all x1, waiting for transfers between devices, on_device(): lax.all_to_all(sent_rows, 'expert', split_axis=0, concat_axis=0, tiled=True)  96.4 us
    all_to_all x1, waiting for transfers between devices, on_device(): lax.all_to_all(rows_grad, 'expert', split_axis=0, concat_axis=0, tiled=True)  90.8 us
    unnamed x20, waiting for transfers between devices  84.9 us
  transfers between devices with their start and end apart: 21, of which 15 were waited for; matrix products, arithmetic and copies ran while one was open for 11% of the time, Pallas kernels for 0%

commit v1 on v0

v1 whole, which is shorter than its diff:
```python
import functools

import jax
import jax.numpy as jnp
from jax import lax
from jax.experimental import pallas as pl
from jax.experimental.pallas import tpu as pltpu
from jax.sharding import PartitionSpec as P

QUERY_HEADS = 24
KEY_VALUE_HEADS = 8
GROUP = QUERY_HEADS // KEY_VALUE_HEADS
HEAD_WIDTH = 64
PIECE = 256
LANES = 128
EPSILON = 1e-05
NEG_FILL = -1e30
SCORE_SCALE = HEAD_WIDTH ** (-0.5)
F32 = jnp.float32
BF16 = jnp.bfloat16

VMEM = pl.BlockSpec(memory_space=pltpu.VMEM)
SMEM = pl.BlockSpec(memory_space=pltpu.SMEM)
ANY = pl.BlockSpec(memory_space=pl.ANY)


def dot(a, b):
    return lax.dot_general(a, b, (((1,), (0,)), ((), ())), preferred_element_type=F32)


def dot_nt(a, b):
    return lax.dot_general(a, b, (((1,), (1,)), ((), ())), preferred_element_type=F32)


def dot_tn(a, b):
    return lax.dot_general(a, b, (((0,), (0,)), ((), ())), preferred_element_type=F32)


def shape_of(dims, dtype):
    return jax.ShapeDtypeStruct(tuple(dims), dtype)


def params(**kw):
    return pltpu.CompilerParams(vmem_limit_bytes=60 * 1024 * 1024, **kw)


class Plane:
    def __init__(self):
        self.size = lax.axis_size("fsdp")
        self.rows = self.size // 4
        index = lax.axis_index("fsdp")
        self.index = index
        self.core = index % 2
        self.mid = (index // 2) % 2
        self.row = index // 4

    def other_core(self, x):
        return lax.ppermute(x, "fsdp", [(i, i ^ 1) for i in range(self.size)])

    def other_mid(self, x):
        return lax.ppermute(x, "fsdp", [(i, i ^ 2) for i in range(self.size)])

    def next_row(self, x, step):
        return lax.ppermute(
            x, "fsdp", [(i, (i // 4 + step) % self.rows * 4 + i % 4) for i in range(self.size)]
        )


def natural_pair(own, got, bit, axis=0):
    first = jnp.where(bit == 0, own, got)
    second = jnp.where(bit == 0, got, own)
    return jnp.stack([first, second], axis=axis)


def natural_ring(by_step, me):
    count = len(by_step)
    if count == 2:
        return natural_pair(by_step[0], by_step[1], me)
    out = []
    for place in range(count):
        value = by_step[0]
        for step in range(1, count):
            value = jnp.where((me - place) % count == step, by_step[step], value)
        out.append(value)
    return jnp.stack(out)


def plane_gather(plane, x):
    half = x.shape[1] // 2
    a, b = x[:, :half], x[:, half:]
    a_pair = natural_pair(a, plane.other_mid(a), plane.mid)
    b_rows = natural_ring([b] + [plane.next_row(b, s) for s in range(1, plane.rows)], plane.row)
    a_all = natural_ring(
        [a_pair] + [plane.next_row(a_pair, s) for s in range(1, plane.rows)], plane.row
    )
    b_all = natural_pair(b_rows, plane.other_mid(b_rows), plane.mid, axis=1)
    own = jnp.concatenate([a_all, b_all], axis=-1)
    both = natural_pair(own, plane.other_core(own), plane.core, axis=2)
    return both.reshape((plane.size,) + x.shape)


def plane_scatter(plane, x):
    n, width = x.shape[1:]
    half = width // 2
    x = x.reshape(plane.size // 2, 2, n, width)
    got = plane.other_core(lax.dynamic_index_in_dim(x, 1 - plane.core, 1, keepdims=False))
    kept = lax.dynamic_index_in_dim(x, plane.core, 1, keepdims=False)
    part = (kept.astype(F32) + got.astype(F32)).astype(BF16)
    part = part.reshape(plane.rows, 2, n, width)
    a, b = part[..., :half], part[..., half:]

    def row_of(v, step):
        return lax.dynamic_index_in_dim(v, (plane.row + step) % plane.rows, 0, keepdims=False)

    a_got = [plane.next_row(row_of(a, s), s) for s in range(1, plane.rows)]
    b_got = plane.other_mid(lax.dynamic_index_in_dim(b, 1 - plane.mid, 1, keepdims=False))
    a_sum = row_of(a, 0).astype(F32)
    for v in a_got:
        a_sum = a_sum + v.astype(F32)
    b_sum = lax.dynamic_index_in_dim(b, plane.mid, 1, keepdims=False).astype(F32)
    b_sum = b_sum + b_got.astype(F32)
    a_last = plane.other_mid(
        lax.dynamic_index_in_dim(a_sum, 1 - plane.mid, 0, keepdims=False).astype(BF16)
    )
    b_low = b_sum.astype(BF16)
    b_last = [plane.next_row(row_of(b_low, s), s) for s in range(1, plane.rows)]
    a_out = lax.dynamic_index_in_dim(a_sum, plane.mid, 0, keepdims=False) + a_last.astype(F32)
    b_out = row_of(b_sum, 0)
    for v in b_last:
        b_out = b_out + v.astype(F32)
    return jnp.concatenate([a_out, b_out], axis=-1)


def expert_shift(x, step):
    count = lax.axis_size("expert")
    return lax.ppermute(x, "expert", [(i, (i + step) % count) for i in range(count)])


def expert_gather(x):
    count = lax.axis_size("expert")
    return [x] + [expert_shift(x, s) for s in range(1, count)]


def expert_scatter(blocks):
    count = lax.axis_size("expert")
    return [expert_shift(blocks[s], count - s) for s in range(1, count)]


def pack_kernel(gate, up, down, out_a, out_b):
    width = gate.shape[2]
    half = width // 2
    for place, ref in ((0, gate), (1, up)):
        value = ref[0].astype(BF16)
        out_a[place, 0] = value[:, :half]
        out_b[place, 0] = value[:, half:]
    value = down[0].astype(BF16)
    rows = value.shape[0]
    for j in range(value.shape[1] // width):
        out_a[2, 0, j * rows : (j + 1) * rows] = value[:, j * width : j * width + half]
        out_b[2, 0, j * rows : (j + 1) * rows] = value[:, j * width + half : (j + 1) * width]


def pack_experts(w_gate, w_up, w_down):
    experts, depth, width = w_gate.shape
    out = shape_of((3, experts, depth, width // 2), BF16)
    block = pl.BlockSpec((3, 1, depth, width // 2), lambda e: (0, e, 0, 0))
    return pl.pallas_call(
        pack_kernel,
        grid=(experts,),
        in_specs=[
            pl.BlockSpec((1,) + w.shape[1:], lambda e: (e, 0, 0)) for w in (w_gate, w_up, w_down)
        ],
        out_specs=[block, block],
        out_shape=[out, out],
        name="pack_experts",
    )(w_gate, w_up, w_down)


def swap_halves(x):
    lane = lax.broadcasted_iota(jnp.int32, x.shape, 1)
    return jnp.where(
        lane % HEAD_WIDTH < HEAD_WIDTH // 2, pltpu.roll(x, LANES - 32, 1), pltpu.roll(x, 32, 1)
    )


def head_slice(ref, start):
    return ref[:, start : start + HEAD_WIDTH]


def attend_kernel(
    blocks,
    kv_heads,
    *refs,
):
    x_refs = refs[:blocks]
    gain, weights, out_weights, bias, cosine, sine = refs[blocks : blocks + 6]
    (a1, qk, val, mixed, maxes, inverse) = refs[blocks + 6 : blocks + 12]
    sums = refs[blocks + 12 : blocks + 12 + blocks]
    mixed_t = refs[blocks + 12 + blocks]
    rows = x_refs[0].shape[0]
    rope_width = qk.shape[1]
    q_width = kv_heads * GROUP * HEAD_WIDTH
    for b in range(blocks):
        a1[b * rows : (b + 1) * rows, :] = (x_refs[b][...].astype(F32) * gain[...]).astype(BF16)
    linear = dot(a1[...], weights[:, : rope_width + val.shape[1]])
    for c in range(rope_width // LANES):
        x = linear[:, c * LANES : (c + 1) * LANES]
        qk[:, c * LANES : (c + 1) * LANES] = (
            x * cosine[...] + swap_halves(x) * sine[...]
        ).astype(BF16)
    val[...] = linear[:, rope_width:].astype(BF16)
    for g in range(kv_heads):
        key = head_slice(qk, q_width + g * HEAD_WIDTH)
        value_t = head_slice(val, g * HEAD_WIDTH).T
        for j in range(GROUP):
            h = g * GROUP + j
            scores = dot_nt(key, head_slice(qk, h * HEAD_WIDTH)) * SCORE_SCALE + bias[...]
            top = jnp.max(scores, axis=0, keepdims=True)
            weight = jnp.exp(scores - top)
            inv = 1.0 / jnp.sum(weight, axis=0, keepdims=True)
            maxes[h : h + 1, :] = top
            inverse[h : h + 1, :] = inv
            mixed_t[h * HEAD_WIDTH : (h + 1) * HEAD_WIDTH, :] = dot(
                value_t, (weight * inv).astype(BF16)
            )
    mixed[...] = mixed_t[...].T.astype(BF16)
    total = dot(mixed[...], out_weights[...])
    for b in range(blocks):
        sums[b][...] = total[b * rows : (b + 1) * rows, :].astype(sums[b].dtype)


def attend(x_blocks, gain, weights, out_weights, bias, cosine, sine, kv_heads, rope_width):
    blocks = len(x_blocks)
    rows, model = x_blocks[0].shape
    seq = rows * blocks
    q_width = kv_heads * GROUP * HEAD_WIDTH
    value_width = weights.shape[1] - LANES - rope_width
    heads = kv_heads * GROUP
    outs = [
        shape_of((seq, model), BF16),
        shape_of((seq, rope_width), BF16),
        shape_of((seq, value_width), BF16),
        shape_of((seq, q_width), BF16),
        shape_of((heads, seq), F32),
        shape_of((heads, seq), F32),
    ] + [shape_of((rows, model), F32 if b == 0 else BF16) for b in range(blocks)]
    out = pl.pallas_call(
        functools.partial(attend_kernel, blocks, kv_heads),
        in_specs=[VMEM] * (blocks + 6),
        out_specs=[VMEM] * len(outs),
        out_shape=outs,
        scratch_shapes=[pltpu.VMEM((q_width, seq), F32)],
        compiler_params=params(),
        name="attend",
    )(*x_blocks, gain, weights, out_weights, bias, cosine, sine)
    return out[:6], out[6:]


def middle_kernel(parts, x, gain, *refs):
    h, a2 = refs[parts:]
    total = x[...] + refs[0][...]
    for i in range(1, parts):
        total = total + refs[i][...].astype(F32)
    h[...] = total
    scale = lax.rsqrt(jnp.mean(total * total, axis=-1, keepdims=True) + EPSILON)
    a2[...] = (total * scale * gain[...]).astype(BF16)


def middle(x, gain, parts):
    return pl.pallas_call(
        functools.partial(middle_kernel, len(parts)),
        in_specs=[VMEM] * (2 + len(parts)),
        out_specs=[VMEM] * 2,
        out_shape=[shape_of(x.shape, F32), shape_of(x.shape, BF16)],
        name="middle",
    )(x, gain, *parts)


def experts_kernel(blocks, pieces, place, row_block, *refs):
    a2_in = refs[:blocks]
    grads_in, router_t, where_ref = refs[blocks : blocks + 3]
    piece_refs = refs[blocks + 3 : blocks + 3 + pieces]
    rest = refs[blocks + 3 + pieces :]
    outs = rest[:blocks]
    dxs = rest[blocks : 2 * blocks]
    gates_out, a2_t, hidden_t, d_gate, d_up = rest[2 * blocks : 2 * blocks + 5]
    (a2, gate_w, up_w, down_w, out_sum, dx_sum, gates, dgates, in_sem, w_sem) = rest[
        2 * blocks + 5 :
    ]
    step, steps = pl.program_id(0), pl.num_programs(0)
    rows = a2_in[0].shape[0]
    seq, model = a2.shape
    depth, width = piece_refs[0].shape[2], gate_w.shape[2]
    half = width // 2
    down_rows = depth * width // model
    slot = lax.rem(step, 2)

    def fetch(e, to):
        for i, (row_step, mid, core, part) in enumerate(place):
            source = where_ref[1 + (row_step * 2 + mid) * 2 + core]
            col = part * half
            at = pl.multiple_of(source * depth, 32)
            for which, buf in ((0, gate_w), (1, up_w)):
                pltpu.make_async_copy(
                    piece_refs[i].at[which, e],
                    buf.at[to, pl.ds(at, depth), pl.ds(col, half)],
                    w_sem.at[which, to],
                ).start()
            at = pl.multiple_of(source * down_rows, 32)
            for j in range(model // width):
                pltpu.make_async_copy(
                    piece_refs[i].at[2, e, pl.ds(j * down_rows, down_rows)],
                    down_w.at[to, pl.ds(at, down_rows), pl.ds(j * width + col, half)],
                    w_sem.at[2, to],
                ).start()

    @pl.when(step == 0)
    def _():
        for b in range(blocks):
            pltpu.make_async_copy(
                a2_in[b], a2.at[pl.ds(b * rows, rows)], in_sem.at[0]
            ).start()
        fetch(0, 0)
        pltpu.make_async_copy(a2, a2, in_sem.at[0]).wait()
        logits = dot_nt(a2[...], router_t[...])
        routed = grads_in[:, model:].astype(F32) > 0.5
        top = jnp.max(jnp.where(routed, logits, NEG_FILL), axis=1, keepdims=True)
        weight = jnp.where(routed, jnp.exp(jnp.where(routed, logits, top) - top), 0.0)
        gates[...] = weight / jnp.sum(weight, axis=1, keepdims=True)
        gates_out[...] = gates[:rows, :]
        dgates[...] = jnp.zeros_like(dgates)
        a2_t[...] = a2[...].T

    @pl.when(step + 1 < steps)
    def _():
        fetch(step + 1, 1 - slot)

    for which, buf in ((0, gate_w), (1, up_w), (2, down_w)):
        pltpu.make_async_copy(buf.at[slot], buf.at[slot], w_sem.at[which, slot]).wait()

    mine = where_ref[0] * steps + step

    def block(i, carry):
        at = pl.ds(pl.multiple_of(i * row_block, row_block), row_block)
        left = a2[at, :]
        gate_lin = dot(left, gate_w[slot])
        up_lin = dot(left, up_w[slot])
        back = dot_nt(grads_in[at, :model], down_w[slot])
        lane = lax.broadcasted_iota(jnp.int32, (row_block, LANES), 1)
        here = lane == mine
        gate = jnp.sum(jnp.where(here, gates[at, :], 0.0), axis=1, keepdims=True)
        sig = 1.0 / (1.0 + jnp.exp(-gate_lin))
        silu = gate_lin * sig
        hidden = silu * up_lin
        dgates[at, :] += jnp.where(here, jnp.sum(hidden * back, axis=1, keepdims=True), 0.0)
        hidden_low = (hidden * gate).astype(BF16)
        d_hidden = back * gate
        d_gate_low = (d_hidden * up_lin * (sig + silu * (1.0 - sig))).astype(BF16)
        d_up_low = (d_hidden * silu).astype(BF16)
        d_gate[at, :] = d_gate_low
        d_up[at, :] = d_up_low
        hidden_t[0, :, at] = hidden_low.T
        out_new = dot(hidden_low, down_w[slot])
        dx_new = dot_nt(d_gate_low, gate_w[slot]) + dot_nt(d_up_low, up_w[slot])

        @pl.when(step == 0)
        def _():
            out_sum[at, :] = out_new
            dx_sum[at, :] = dx_new

        @pl.when(step > 0)
        def _():
            out_sum[at, :] += out_new
            dx_sum[at, :] += dx_new

        return carry

    lax.fori_loop(0, seq // row_block, block, 0)

    @pl.when(step == steps - 1)
    def _():
        high = dgates[...].astype(BF16).astype(F32)
        low = dgates[...] - high
        lane = lax.broadcasted_iota(jnp.int32, high.shape, 1)
        tail = jnp.where(lane < LANES // 2, high, pltpu.roll(low, LANES // 2, 1))
        for b in range(blocks):
            at = slice(b * rows, (b + 1) * rows)
            outs[b][...] = out_sum[at, :].astype(outs[b].dtype)
            dxs[b][:, :model] = dx_sum[at, :].astype(dxs[b].dtype)
            dxs[b][:, model:] = tail[at, :].astype(dxs[b].dtype)


def experts(a2_blocks, grads, router_t, where, pieces, place, width):
    blocks = len(a2_blocks)
    rows, model = a2_blocks[0].shape
    seq = rows * blocks
    local, depth = pieces[0].shape[1:3]
    outs = (
        [shape_of((rows, model), F32 if b == 0 else BF16) for b in range(blocks)]
        + [shape_of((rows, model + LANES), F32 if b == 0 else BF16) for b in range(blocks)]
        + [
            shape_of((rows, LANES), F32),
            shape_of((model, seq), BF16),
            shape_of((local, width, seq), BF16),
            shape_of((seq, local * width), BF16),
            shape_of((seq, local * width), BF16),
        ]
    )
    whole = lambda dims: pl.BlockSpec(dims, lambda e: (0,) * len(dims))
    once = lambda dims: pl.BlockSpec(
        dims, lambda e: (0,) * len(dims), pipeline_mode=pl.Buffered(1)
    )
    out_specs = (
        [whole(o.shape) for o in outs[: 2 * blocks + 2]]
        + [pl.BlockSpec((1, width, seq), lambda e: (e, 0, 0))]
        + [pl.BlockSpec((seq, width), lambda e: (0, e))] * 2
    )
    out = pl.pallas_call(
        functools.partial(experts_kernel, blocks, len(pieces), place, 256),
        grid=(local,),
        in_specs=[ANY] * blocks
        + [once(grads.shape), once(router_t.shape), SMEM]
        + [ANY] * len(pieces),
        out_specs=out_specs,
        out_shape=outs,
        scratch_shapes=[
            pltpu.VMEM((seq, model), BF16),
            pltpu.VMEM((2, model, width), BF16),
            pltpu.VMEM((2, model, width), BF16),
            pltpu.VMEM((2, width, model), BF16),
            pltpu.VMEM((seq, model), F32),
            pltpu.VMEM((seq, model), F32),
            pltpu.VMEM((seq, LANES), F32),
            pltpu.VMEM((seq, LANES), F32),
            pltpu.SemaphoreType.DMA((1,)),
            pltpu.SemaphoreType.DMA((3, 2)),
        ],
        compiler_params=params(dimension_semantics=("arbitrary",)),
        name="experts",
    )(*a2_blocks, grads, router_t, where, *pieces)
    return out[:blocks], out[blocks : 2 * blocks], out[2 * blocks :]


def expert_grads_kernel(depth, down_rows, where_ref, a2_t, hidden_t, grads, d_gate, d_up, *outs):
    model, width = a2_t.shape[0], d_gate.shape[1]
    for place, out in enumerate(outs):
        source = where_ref[place]
        at = pl.ds(pl.multiple_of(source * depth, 32), depth)
        out[0, 0] = dot(a2_t[at, :], d_gate[...]).astype(BF16)
        out[1, 0] = dot(a2_t[at, :], d_up[...]).astype(BF16)
        at = pl.ds(pl.multiple_of(source * down_rows, 32), down_rows)
        down = dot(hidden_t[0, at, :], grads[...]).astype(BF16)
        for j in range(model // width):
            out[2, 0, j * down_rows : (j + 1) * down_rows, :] = down[
                :, j * width : (j + 1) * width
            ]


def expert_grads(a2_t, hidden_t, grads, d_gate, d_up, where, plane_size):
    model, seq = a2_t.shape
    local, width = hidden_t.shape[:2]
    depth, down_rows = model // plane_size, width // plane_size
    out = shape_of((3, local, depth, width), BF16)
    block = pl.BlockSpec((3, 1, depth, width), lambda e: (0, e, 0, 0))
    return pl.pallas_call(
        functools.partial(expert_grads_kernel, depth, down_rows),
        grid=(local,),
        in_specs=[
            SMEM,
            pl.BlockSpec((model, seq), lambda e: (0, 0), pipeline_mode=pl.Buffered(1)),
            pl.BlockSpec((1, width, seq), lambda e: (e, 0, 0)),
            pl.BlockSpec((seq, model), lambda e: (0, 0), pipeline_mode=pl.Buffered(1)),
            pl.BlockSpec((seq, width), lambda e: (0, e)),
            pl.BlockSpec((seq, width), lambda e: (0, e)),
        ],
        out_specs=[block, block],
        out_shape=[out, out],
        name="expert_grads",
    )(where, a2_t, hidden_t, grads, d_gate, d_up)


def finish_kernel(kept_a, got_a, kept_b, got_b, gate, up, down):
    half = kept_a.shape[3]
    for part, kept, got in ((0, kept_a, got_a), (1, kept_b, got_b)):
        at = slice(part * half, (part + 1) * half)
        gate[0, :, at] = kept[0, 0].astype(F32) + got[0, 0].astype(F32)
        up[0, :, at] = kept[1, 0].astype(F32) + got[1, 0].astype(F32)
        value = kept[2, 0].astype(F32) + got[2, 0].astype(F32)
        rows = down.shape[1]
        for j in range(value.shape[0] // rows):
            start = j * 2 * half + part * half
            down[0, :, start : start + half] = value[j * rows : (j + 1) * rows]


def finish(kept_a, got_a, kept_b, got_b, down_rows, model):
    local, depth, half = kept_a.shape[1:]
    block = pl.BlockSpec((3, 1, depth, half), lambda e: (0, e, 0, 0))
    outs = [
        shape_of((local, depth, 2 * half), F32),
        shape_of((local, depth, 2 * half), F32),
        shape_of((local, down_rows, model), F32),
    ]
    return pl.pallas_call(
        finish_kernel,
        grid=(local,),
        in_specs=[block] * 4,
        out_specs=[pl.BlockSpec((1,) + o.shape[1:], lambda e: (e, 0, 0)) for o in outs],
        out_shape=outs,
        name="finish",
    )(kept_a, got_a, kept_b, got_b)


def rejoin_kernel(parts, gain_row, gates, h, dz, router_t, a2, *refs):
    dh, dh_low, extra = refs[parts:]
    model = h.shape[1]
    total = refs[0][...]
    for i in range(1, parts):
        total = total + refs[i][...].astype(F32)
    tail = total[:, model:]
    dgates = tail + pltpu.roll(tail, LANES // 2, 1)
    gate = gates[...]
    mean = jnp.sum(gate * dgates, axis=1, keepdims=True)
    d_logits = (gate * (dgates - mean)).astype(BF16)
    da2 = total[:, :model] + dot(d_logits, router_t[...])
    value = h[...]
    scale = lax.rsqrt(jnp.mean(value * value, axis=-1, keepdims=True) + EPSILON)
    normed = value * scale
    gain = router_t[gain_row : gain_row + 1, :].astype(F32)
    weighted = da2 * gain
    grad = dz[...] + scale * (
        weighted - normed * jnp.mean(weighted * normed, axis=-1, keepdims=True)
    )
    dh[...] = grad
    dh_low[...] = grad.astype(BF16)
    gain_grad = jnp.sum(da2 * normed, axis=0, keepdims=True)
    line = lax.broadcasted_iota(jnp.int32, (LANES, model), 0)
    extra[...] = jnp.where(line == gain_row, gain_grad, dot_tn(d_logits, a2[...]))


def rejoin(parts, gates, h, dz, router_t, a2, gain_row):
    return pl.pallas_call(
        functools.partial(rejoin_kernel, len(parts), gain_row),
        in_specs=[VMEM] * (5 + len(parts)),
        out_specs=[VMEM] * 3,
        out_shape=[
            shape_of(h.shape, F32),
            shape_of(h.shape, BF16),
            shape_of((LANES, h.shape[1]), F32),
        ],
        name="rejoin",
    )(gates, h, dz, router_t, a2, *parts)


def attend_back_kernel(blocks, kv_heads, gain_row, *refs):
    dh_refs, x_refs = refs[:blocks], refs[blocks : 2 * blocks]
    (weights, out_weights, a1, qk, val, mixed, maxes, inverse, bias, cosine, sine, extra) = refs[
        2 * blocks : 2 * blocks + 12
    ]
    d_weights, d_out_weights = refs[2 * blocks + 12 : 2 * blocks + 14]
    sums = refs[2 * blocks + 14 : 3 * blocks + 14]
    grads, d_mixed, dq_t, d_qk, d_lin = refs[3 * blocks + 14 :]
    rows = x_refs[0].shape[0]
    rope_width, value_width = qk.shape[1], val.shape[1]
    q_width = kv_heads * GROUP * HEAD_WIDTH
    for b in range(blocks):
        grads[b * rows : (b + 1) * rows, :] = dh_refs[b][...]
    d_mixed[...] = dot_nt(grads[...], out_weights[...]).astype(BF16)
    d_out_weights[...] = dot_tn(mixed[...], grads[...]).astype(BF16)
    if value_width > kv_heads * HEAD_WIDTH:
        d_lin[:, rope_width:] = jnp.zeros((d_lin.shape[0], value_width), BF16)
    for g in range(kv_heads):
        key = head_slice(qk, q_width + g * HEAD_WIDTH)
        key_t = key.T
        value = head_slice(val, g * HEAD_WIDTH)
        d_key, d_value = None, None
        for j in range(GROUP):
            h = g * GROUP + j
            query = head_slice(qk, h * HEAD_WIDTH)
            grad = head_slice(d_mixed, h * HEAD_WIDTH)
            scores = dot_nt(key, query) * SCORE_SCALE + bias[...]
            prob = jnp.exp(scores - maxes[h : h + 1, :]) * inverse[h : h + 1, :]
            d_prob = dot_nt(value, grad)
            inner = jnp.sum(prob * d_prob, axis=0, keepdims=True)
            d_scores = (prob * (d_prob - inner)).astype(BF16)
            dk = dot(d_scores, query)
            dv = dot(prob.astype(BF16), grad)
            d_key = dk if d_key is None else d_key + dk
            d_value = dv if d_value is None else d_value + dv
            dq_t[h * HEAD_WIDTH : (h + 1) * HEAD_WIDTH, :] = dot(key_t, d_scores)
        start = q_width + g * HEAD_WIDTH
        d_qk[:, start : start + HEAD_WIDTH] = d_key * SCORE_SCALE
        start = rope_width + g * HEAD_WIDTH
        d_lin[:, start : start + HEAD_WIDTH] = d_value.astype(BF16)
    d_qk[:, :q_width] = dq_t[...].T * SCORE_SCALE
    for c in range(rope_width // LANES):
        at = slice(c * LANES, (c + 1) * LANES)
        x = d_qk[:, at]
        d_lin[:, at] = (x * cosine[...] - swap_halves(x) * sine[...]).astype(BF16)
    total = dot_nt(d_lin[...], weights[:, : rope_width + value_width])
    gain_grad = None
    for b in range(blocks):
        part = total[b * rows : (b + 1) * rows, :]
        sums[b][...] = part.astype(sums[b].dtype)
        new = jnp.sum(part * x_refs[b][...].astype(F32), axis=0, keepdims=True)
        gain_grad = new if gain_grad is None else gain_grad + new
    d_weights[:, : rope_width + value_width] = dot_tn(a1[...], d_lin[...]).astype(BF16)
    line = lax.broadcasted_iota(jnp.int32, extra.shape, 0)
    tail = jnp.where(line == gain_row, gain_grad, extra[...])
    d_weights[:, rope_width + value_width :] = tail.T.astype(BF16)


def attend_back(dh_blocks, x_blocks, weights, out_weights, kept, bias, cosine, sine, extra, kv_heads, gain_row):
    blocks = len(dh_blocks)
    rows, model = dh_blocks[0].shape
    seq = rows * blocks
    q_width = out_weights.shape[0]
    rope_width, value_width = kept[1].shape[1], kept[2].shape[1]
    outs = [shape_of(weights.shape, BF16), shape_of(out_weights.shape, BF16)] + [
        shape_of((rows, model), F32 if b == 0 else BF16) for b in range(blocks)
    ]
    out = pl.pallas_call(
        functools.partial(attend_back_kernel, blocks, kv_heads, gain_row),
        in_specs=[VMEM] * (2 * blocks + 12),
        out_specs=[VMEM] * len(outs),
        out_shape=outs,
        scratch_shapes=[
            pltpu.VMEM((seq, model), BF16),
            pltpu.VMEM((seq, q_width), BF16),
            pltpu.VMEM((q_width, seq), F32),
            pltpu.VMEM((seq, rope_width), F32),
            pltpu.VMEM((seq, rope_width + value_width), BF16),
        ],
        compiler_params=params(),
        name="attend_back",
    )(*dh_blocks, *x_blocks, weights, out_weights, *kept, bias, cosine, sine, extra)
    return out[0], out[1], out[2:]


def last_kernel(parts, x, dh, gain, *refs):
    out = refs[parts]
    total = refs[0][...]
    for i in range(1, parts):
        total = total + refs[i][...].astype(F32)
    value = x[...]
    scale = lax.rsqrt(jnp.mean(value * value, axis=-1, keepdims=True) + EPSILON)
    normed = value * scale
    weighted = total * gain[...]
    out[...] = dh[...] + scale * (
        weighted - normed * jnp.mean(weighted * normed, axis=-1, keepdims=True)
    )


def last(x, dh, gain, parts):
    return pl.pallas_call(
        functools.partial(last_kernel, len(parts)),
        in_specs=[VMEM] * (3 + len(parts)),
        out_specs=VMEM,
        out_shape=shape_of(x.shape, F32),
        name="last",
    )(x, dh, gain, *parts)


def piece_ids(position_index, starts):
    inside = (position_index[:, None] >= starts[None, :]) & (
        position_index[:, None] < starts[None, :] + PIECE
    )
    labels = jnp.arange(1, starts.shape[0] + 1, dtype=jnp.int32)[None, :]
    return jnp.sum(jnp.where(inside, labels, 0), axis=1, dtype=jnp.int32)


def on_device(
    inputs,
    cotangent,
    norm1_gain,
    w_query,
    key_projection,
    value_projection,
    w_output,
    norm2_gain,
    w_router,
    w_gate,
    w_up,
    w_down,
    routes,
    piece_starts,
):
    plane = Plane()
    ranks = lax.axis_size("expert")
    me = lax.axis_index("expert")
    rows, model = inputs.shape
    seq = rows * ranks
    weight_rows = w_query.shape[0]
    n_experts = w_router.shape[1]
    ff = w_gate.shape[2]
    kv_heads = KEY_VALUE_HEADS // ranks
    q_cols, kv_cols = kv_heads * GROUP * HEAD_WIDTH, kv_heads * HEAD_WIDTH
    rope_width = q_cols + kv_cols
    value_width = -(-kv_cols // LANES) * LANES
    columns = rope_width + value_width + LANES
    gain_one_row, gain_two_row = n_experts, n_experts + 1

    scale_one = lax.rsqrt(jnp.mean(inputs * inputs, axis=-1, keepdims=True) + EPSILON)
    x_blocks = expert_gather((inputs * scale_one).astype(BF16))

    extra_cols = jnp.concatenate(
        [
            w_router,
            norm1_gain[:, None],
            norm2_gain[:, None],
            jnp.zeros((weight_rows, LANES - n_experts - 2), F32),
        ],
        axis=1,
    )
    by_rank = jnp.concatenate(
        [
            w_query.reshape(weight_rows, ranks, q_cols),
            key_projection.reshape(weight_rows, ranks, kv_cols),
            jnp.pad(
                value_projection.reshape(weight_rows, ranks, kv_cols),
                ((0, 0), (0, 0), (0, value_width - kv_cols)),
            ),
            jnp.broadcast_to(extra_cols[:, None, :], (weight_rows, ranks, LANES)),
        ],
        axis=2,
    ).astype(BF16)
    by_rank = jnp.transpose(by_rank, (1, 0, 2))
    from_ranks = [
        expert_shift(
            lax.dynamic_index_in_dim(by_rank, (me + s) % ranks, 0, keepdims=False), s
        )
        if s
        else lax.dynamic_index_in_dim(by_rank, me, 0, keepdims=False)
        for s in range(ranks)
    ]
    column_shard = natural_ring(from_ranks, me).reshape(ranks * weight_rows, columns)
    weights = plane_gather(plane, column_shard).reshape(model, columns)

    axes = ("fsdp", "expert")
    total = plane.size * ranks
    move = [
        (j, (j % plane.size) * ranks + j // plane.size) for j in range(total)
    ]
    out_shard = lax.ppermute(w_output.astype(BF16), axes, move)
    out_weights = plane_gather(plane, out_shard).reshape(q_cols, model)

    lane_ids = jnp.arange(LANES, dtype=jnp.int32)
    routed = jnp.sum((routes[:, :, None] == lane_ids[None, None, :]).astype(F32), axis=1)
    grads = jnp.concatenate(
        expert_gather(jnp.concatenate([cotangent, routed], axis=1).astype(BF16)), axis=0
    )

    part_a, part_b = pack_experts(w_gate, w_up, w_down)
    found = {(0, 0, 0): part_a, (0, 1, 0): plane.other_mid(part_a)}
    found[0, 0, 1] = part_b
    for s in range(1, plane.rows):
        found[s, 0, 1] = plane.next_row(part_b, s)
        for mid in range(2):
            found[s, mid, 0] = plane.next_row(found[0, mid, 0], s)
    for s in range(plane.rows):
        found[s, 1, 1] = plane.other_mid(found[s, 0, 1])
    place, pieces = [], []
    for (s, mid, part), value in found.items():
        place += [(s, mid, 0, part), (s, mid, 1, part)]
        pieces += [value, plane.other_core(value)]
    sources = [
        (((plane.row - s) % plane.rows) * 2 + (plane.mid + mid) % 2) * 2 + (plane.core + core) % 2
        for s in range(plane.rows)
        for mid in range(2)
        for core in range(2)
    ]
    where = jnp.stack([me] + sources).astype(jnp.int32)

    block_ids = jnp.arange(seq, dtype=jnp.int32) // rows
    places = ((me - block_ids) % ranks) * rows + jnp.arange(seq, dtype=jnp.int32) % rows
    ids = piece_ids(places, piece_starts[0])
    visible = (places[:, None] <= places[None, :]) | (
        (ids[:, None] == ids[None, :]) & (ids[None, :] > 0)
    )
    bias = jnp.where(visible, 0.0, NEG_FILL).astype(F32)
    half = HEAD_WIDTH // 2
    inverse = 10000.0 ** (-(jnp.arange(half, dtype=F32) * 2.0 / HEAD_WIDTH))
    angles = places.astype(F32)[:, None] * inverse[None, :]
    cosine = jnp.tile(jnp.cos(angles), (1, LANES // half))
    sine = jnp.tile(jnp.sin(angles), (1, LANES // half)) * jnp.where(
        lane_ids % HEAD_WIDTH < half, -1.0, 1.0
    )
    extra_t = weights[:, columns - LANES :].T
    gain_one = extra_t[gain_one_row : gain_one_row + 1].astype(F32)
    gain_two = extra_t[gain_two_row : gain_two_row + 1].astype(F32)
    kept, sums = attend(
        x_blocks, gain_one, weights, out_weights, bias, cosine, sine, kv_heads, rope_width
    )
    mid_rows, a2 = middle(inputs, gain_two, [sums[0]] + expert_scatter(sums))

    a2_blocks = expert_gather(a2)
    outs, dxs, (gates, a2_t, hidden_t, d_gate, d_up) = experts(
        a2_blocks, grads, extra_t, where, pieces, tuple(place), ff
    )
    dx_got = expert_scatter(dxs)
    grad_rows = grads[:, :model]
    summed = {}
    for s in reversed(range(plane.rows)):
        for mid in (1, 0):
            chip = ((plane.row + s) % plane.rows) * 2 + (plane.mid + mid) % 2
            target = jnp.stack([chip * 2 + plane.core, chip * 2 + 1 - plane.core])
            mine, theirs = expert_grads(
                a2_t, hidden_t, grad_rows, d_gate, d_up, target.astype(jnp.int32), plane.size
            )
            got = plane.other_core(theirs)
            for part in range(2):
                at = slice(part * ff // 2, (part + 1) * ff // 2)
                summed[s, mid, part] = (
                    mine[..., at].astype(F32) + got[..., at].astype(F32)
                ).astype(BF16)

    def add(first, *others):
        value = first.astype(F32)
        for v in others:
            value = value + v.astype(F32)
        return value.astype(BF16)

    steps = range(1, plane.rows)
    a_sums = [
        add(summed[0, mid, 0], *[plane.next_row(summed[s, mid, 0], s) for s in steps])
        for mid in range(2)
    ]
    b_sums = [
        add(summed[s, 0, 1], plane.other_mid(summed[s, 1, 1])) for s in range(plane.rows)
    ]
    a_got = plane.other_mid(a_sums[1])
    b_got = [plane.next_row(b_sums[s], s) for s in steps]
    b_kept = b_sums[0]
    if len(b_got) > 1:
        b_kept = add(b_kept, *b_got[:-1])
    gate_grad, up_grad, down_grad = finish(
        a_sums[0], a_got, b_kept, b_got[-1], w_down.shape[1], model
    )

    dh, dh_low, extra = rejoin(
        [dxs[0]] + dx_got, gates, mid_rows, cotangent, extra_t, a2, gain_two_row
    )

    d_weights, d_out_weights, da1 = attend_back(
        expert_gather(dh_low),
        x_blocks,
        weights,
        out_weights,
        kept,
        bias,
        cosine,
        sine,
        extra,
        kv_heads,
        gain_one_row,
    )
    input_grad = last(inputs, dh, gain_one, [da1[0]] + expert_scatter(da1))
    output = mid_rows + outs[0]
    for v in expert_scatter(outs):
        output = output + v.astype(F32)

    out_part = plane_scatter(
        plane, d_out_weights.reshape(plane.size, q_cols // plane.size, model)
    )
    w_output_grad = lax.ppermute(
        out_part.astype(BF16), axes, [(b, a) for a, b in move]
    ).astype(F32)
    d_shard = plane_scatter(
        plane, d_weights.reshape(plane.size, model // plane.size, columns)
    ).astype(BF16)
    d_shard = d_shard.reshape(ranks, weight_rows, columns)
    own = lax.dynamic_index_in_dim(d_shard, me, 0, keepdims=False)
    arrived = [own] + [
        expert_shift(
            lax.dynamic_index_in_dim(d_shard, (me + s) % ranks, 0, keepdims=False), s
        )
        for s in range(1, ranks)
    ]
    by_rank = natural_ring(arrived, me).astype(F32)

    def columns_of(start, width):
        piece = by_rank[:, :, start : start + width]
        return jnp.transpose(piece, (1, 0, 2)).reshape(weight_rows, ranks * width)

    extra_grad = jnp.sum(by_rank[:, :, columns - LANES :], axis=0)
    return (
        output,
        input_grad,
        extra_grad[:, gain_one_row],
        columns_of(0, q_cols),
        columns_of(q_cols, kv_cols),
        columns_of(rope_width, kv_cols),
        w_output_grad,
        extra_grad[:, gain_two_row],
        extra_grad[:, :n_experts],
        gate_grad,
        up_grad,
        down_grad,
    )


def solution(mesh):
    both = ("fsdp", "expert")
    rows, flat, stack = P(both, None), P(both), P("expert", "fsdp", None)
    weights = (flat, rows, rows, rows, rows, flat, rows, stack, stack, stack)
    return jax.shard_map(
        on_device,
        mesh=mesh,
        in_specs=(rows, rows) + weights + (rows, P("fsdp", None)),
        out_specs=(rows, rows) + weights,
        check_vma=False,
    )
```

time: 1720 us -> 629 us (0.37)
  waiting for transfers between devices: 1190 us -> 329 us
  matrix products: 185 us -> 0 us
  blocking collectives: 178 us -> 0 us
  Pallas kernels: 0 us -> 131 us
  starting transfers between devices: 31.4 us -> 111 us
  local copies, waits for them, and re-layouts: 56.1 us -> 15.8 us
  other arithmetic: 52.5 us -> 32 us
    reduce_scatter x7 -> x0, waiting for transfers between devices: 657 us -> none  [the longest x1 142 us: on_device(): lax.psum_scatter(output_w_grad, ('fsdp', 'expert'), scatter_dimension=0,...]
    all_to_all x4 -> x0, waiting for transfers between devices: 366 us -> none  [the longest x1 96.5 us: on_device(): lax.all_to_all(sent_grads, 'expert', split_axis=0, concat_axis=0, tiled=T...]
    ppermute x0 -> x76, waiting for transfers between devices: none -> 329 us  [the longest x30 180 us: expert_shift(): lax.ppermute(x, 'expert', [(i, (i + step) % count) for i in range(count)])]
    dot_general x79 -> x0, matrix products: 184 us -> none  [the longest x8 13.5 us: backward_head(): jnp.einsum('grj,jd->rgd', score_grad, key_block, preferred_element_type=j...]
    pallas_call x0 -> x12, Pallas kernels: none -> 131 us  [the longest x4 42.2 us: expert_grads(): pl.pallas_call(functools.partial(expert_grads_kernel, depth, down_rows),...]
    ppermute x0 -> x76, starting transfers between devices: none -> 111 us  [the longest x30 64.7 us: expert_shift(): lax.ppermute(x, 'expert', [(i, (i + step) % count) for i in range(count)])]
    all_gather x3 -> x0, blocking collectives: 99.2 us -> none  [the longest x1 65.6 us: on_device(): lax.all_gather(dense_local[6], ('fsdp', 'expert'), axis=0, tiled=True)]
    unnamed x20 -> x0, waiting for transfers between devices: 84.9 us -> none
  transfers between devices with their start and end apart: 21 -> 76, of which waited for: 15 -> 39; matrix products, arithmetic and copies ran while one was open for 11% -> 6% of each run, Pallas kernels for 0% -> 10%
where the time goes in v1:
time: 629 us; the launch traced here: 621 us
  waiting for transfers between devices  329 us (52%)
  Pallas kernels  131 us (21%)
  starting transfers between devices  111 us (18%)
  other arithmetic  32 us (5%)
  local copies, waits for them, and re-layouts  15.8 us (3%)
    ppermute x30, waiting for transfers between devices, expert_shift(): lax.ppermute(x, 'expert', [(i, (i + step) % count) for i in range(count)])  180 us
    ppermute x14, waiting for transfers between devices, other_mid(): return lax.ppermute(x, 'fsdp', [(i, i ^ 2) for i in range(self.size)])  95.4 us
    ppermute x30, starting transfers between devices, expert_shift(): lax.ppermute(x, 'expert', [(i, (i + step) % count) for i in range(count)])  64.7 us
    pallas_call x4, Pallas kernels, expert_grads(): pl.pallas_call(functools.partial(expert_grads_kernel, depth, down_rows),...  42.2 us
    pallas_call x1, Pallas kernels, experts(): pl.pallas_call(functools.partial(experts_kernel, blocks, len(pieces), pla...  40.2 us
    ppermute x14, waiting for transfers between devices, next_row(): lax.ppermute(x, 'fsdp', [(i, (i // 4 + step) % self.rows * 4 + i % 4) for...  33.8 us
    ppermute x16, starting transfers between devices, other_core(): return lax.ppermute(x, 'fsdp', [(i, i ^ 1) for i in range(self.size)])  26.6 us
    pallas_call x1, Pallas kernels, attend_back(): pl.pallas_call(functools.partial(attend_back_kernel, blocks, kv_heads, ga...  15.4 us
  transfers between devices with their start and end apart: 76, of which 39 were waited for; matrix products, arithmetic and copies ran while one was open for 6% of the time, Pallas kernels for 10%

profile of v1, /device:TPU:27, one launch (start us, length us, event | category | flops | bytes accessed | tf_op | source)
XLA Modules:
  0.0 620.8 jit_solution(7947123937321313677)
XLA Ops:
  23.0 12.2 %collective-permute-start.10 = (bf16[128,1536]{1,0:T(8,128)(2,1)S(1)}, bf16[128,1536]{1,0:T(8,128)(2,1)S(1)}, u32[]{:S(2)}, u32[]{:S(2)}) collective-permute-start(bf16[128,1536]{1,0:T(8,128)(2,1)S(1)} %multiply_convert_fusion.refs_0_.refs_4_), channel_id=1, source_target_pairs={{0,3},{1,0},{2,1},{3,2},{4,7},{5,4},{6,5},{7,6},{8,11},{9,8},{10,9... | collective-permute-start | bytes 1179656 | tf_op jit(solution)/shard_map/ppermute | solution.py:136
  35.1 8.1 %collective-permute-done.1 = bf16[48,768]{1,0:T(8,128)(2,1)S(1)} collective-permute-done((bf16[48,768]{1,0:T(8,128)(2,1)}, bf16[48,768]{1,0:T(8,128)(2,1)S(1)}, u32[]{:S(2)}, u32[]{:S(2)}) %collective-permute-start.1) | collective-permute-done | bytes 73760 | tf_op jit(solution)/shard_map/ppermute | solution.py:136
  78.7 8.3 %collective-permute-start.16 = (bf16[2,2,48,1536]{3,2,0,1:T(8,128)(2,1)S(1)}, bf16[2,2,48,1536]{3,2,0,1:T(8,128)(2,1)S(1)}, u32[]{:S(2)}, u32[]{:S(2)}) collective-permute-start(bf16[2,2,48,1536]{3,2,0,1:T(8,128)(2,1)S(1)} %maximum_maximum_fusion.1), channel_id=1, source_target_pairs={{0,4},{4,0},{8,12},{12,8},{16,20},{20,16},{24,28},{28,24},{1,5},{5... | collective-permute-start | bytes 1769480 | tf_op jit(solution)/shard_map/ppermute | solution.py:58
  89.2 19.6 %collective-permute-done.24 = bf16[128,1664]{1,0:T(8,128)(2,1)S(1)} collective-permute-done((bf16[128,1664]{1,0:T(8,128)(2,1)}, bf16[128,1664]{1,0:T(8,128)(2,1)S(1)}, u32[]{:S(2)}, u32[]{:S(2)}) %collective-permute-start.24) | collective-permute-done | bytes 426016 | tf_op jit(solution)/shard_map/ppermute | solution.py:136
  114.1 9.9 %collective-permute-done.23 = bf16[128,1664]{1,0:T(8,128)(2,1)} collective-permute-done((bf16[128,1664]{1,0:T(8,128)(2,1)}, bf16[128,1664]{1,0:T(8,128)(2,1)}, u32[]{:S(2)}, u32[]{:S(2)}) %collective-permute-start.23) | collective-permute-done | bytes 426016 | tf_op jit(solution)/shard_map/ppermute | solution.py:136
  125.2 10.2 %attend.1 = (bf16[512,1536]{1,0:T(8,128)(2,1)}, bf16[512,512]{1,0:T(8,128)(2,1)}, bf16[512,128]{1,0:T(8,128)(2,1)}, bf16[512,384]{1,0:T(8,128)(2,1)}, f32[6,512]...) custom-call(bf16[128,1536]{1,0:T(8,128)(2,1)} %copy-done.3, ...), custom_call_target="tpu_custom_call" | custom-call | tf_op jit(solution)/shard_map/attend/pallas_call | solution.py:247
  151.2 14.4 %collective-permute-done.18.refs_2_ = bf16[128,1536]{1,0:T(8,128)(2,1)} collective-permute-done((bf16[128,1536]{1,0:T(8,128)(2,1)}, bf16[128,1536]{1,0:T(8,128)(2,1)}, u32[]{:S(2)}, u32[]{:S(2)}) %collective-permute-start.18) | collective-permute-done | bytes 393248 | tf_op jit(solution)/shard_map/ppermute | solution.py:136
  190.1 23.7 %collective-permute-done.21.refs_2_ = bf16[128,1536]{1,0:T(8,128)(2,1)S(1)} collective-permute-done((bf16[128,1536]{1,0:T(8,128)(2,1)}, bf16[128,1536]{1,0:T(8,128)(2,1)S(1)}, u32[]{:S(2)}, u32[]{:S(2)}) %collective-permute-start.21) | collective-permute-done | bytes 393248 | tf_op jit(solution)/shard_map/ppermute | solution.py:136
  227.1 40.2 %experts.1 = (f32[128,1536]{1,0:T(8,128)}, bf16[128,1536]{1,0:T(8,128)(2,1)}, bf16[128,1536]{1,0:T(8,128)(2,1)}, bf16[128,1536]{1,0:T(8,128)(2,1)}, f32[128,1664...) custom-call(bf16[128,1536]{1,0:T(8,128)(2,1)} %get-tuple-element.64., ...), custom_call_target="tpu_custom_call" | custom-call | tf_op jit(solution)/shard_map/experts/pallas_call | solution.py:418
  270.6 9.8 %collective-permute-done.43.refs_1_ = bf16[128,1664]{1,0:T(8,128)(2,1)S(1)} collective-permute-done((bf16[128,1664]{1,0:T(8,128)(2,1)}, bf16[128,1664]{1,0:T(8,128)(2,1)S(1)}, u32[]{:S(2)}, u32[]{:S(2)}) %collective-permute-start.43) | collective-permute-done | bytes 426016 | tf_op jit(solution)/shard_map/ppermute | solution.py:136
  280.4 17.4 %collective-permute-done.44.refs_2_ = bf16[128,1664]{1,0:T(8,128)(2,1)S(1)} collective-permute-done((bf16[128,1664]{1,0:T(8,128)(2,1)}, bf16[128,1664]{1,0:T(8,128)(2,1)S(1)}, u32[]{:S(2)}, u32[]{:S(2)}) %collective-permute-start.44) | collective-permute-done | bytes 426016 | tf_op jit(solution)/shard_map/ppermute | solution.py:136
  303.1 8.4 %collective-permute-start.46 = (bf16[128,1536]{1,0:T(8,128)(2,1)}, bf16[128,1536]{1,0:T(8,128)(2,1)S(1)}, u32[]{:S(2)}, u32[]{:S(2)}) collective-permute-start(bf16[128,1536]{1,0:T(8,128)(2,1)} %get-tuple-element.77.refs_0_), channel_id=1, source_target_pairs={{0,1},{1,2},{2,3},{3,0},{4,5},{5,6},{6,7},{7,4},{8,9},{9,10},{10,1... | collective-permute-start | bytes 1179656 | tf_op jit(solution)/shard_map/ppermute | solution.py:136
  320.8 26.2 %collective-permute-done.47.refs_2_ = bf16[128,1536]{1,0:T(8,128)(2,1)S(1)} collective-permute-done((bf16[128,1536]{1,0:T(8,128)(2,1)}, bf16[128,1536]{1,0:T(8,128)(2,1)S(1)}, u32[]{:S(2)}, u32[]{:S(2)}) %collective-permute-start.47) | collective-permute-done | bytes 393248 | tf_op jit(solution)/shard_map/ppermute | solution.py:136
  347.9 15.4 %attend_back.1 = (bf16[1536,768]{1,0:T(8,128)(2,1)}, bf16[384,1536]{1,0:T(8,128)(2,1)}, f32[128,1536]{1,0:T(8,128)}, bf16[128,1536]{1,0:T(8,128)(2,1)}, bf16[128...) custom-call(bf16[128,1536]{1,0:T(8,128)(2,1)} %get-tuple-element.77.refs_0_, bf16[128,1536]{1,0:T(8,128)(2,1)} %copy-done.22, ...), custom_call_target="tpu_custom_call" | custom-call | tf_op jit(solution)/shard_map/attend_back/pallas_call | solution.py:621
  368.4 10.6 %expert_grads.7 = (bf16[3,5,192,512]{3,2,1,0:T(8,128)(2,1)}, bf16[3,5,192,512]{3,2,1,0:T(8,128)(2,1)}) custom-call(s32[2]{0:T(128)} %get-tuple-element.210.where_ref, bf16[1536,512]{1,0:T(8,128)(2,1)} %get-tuple-element.91.a2_t, bf16[5,512,512]{2,1,0:T(8,128)(2,1)} %get-tuple-element.92.hidden_t, bf16[512,1536]{1,0:T(8,128)(2,1)} %slice.155.grads, ...), custom_call_target="tpu_custom_call" | custom-call | tf_op jit(solution)/shard_map/expert_grads/pallas_call | solution.py:465
  379.9 10.6 %expert_grads.6 = (bf16[3,5,192,512]{3,2,1,0:T(8,128)(2,1)}, bf16[3,5,192,512]{3,2,1,0:T(8,128)(2,1)}) custom-call(s32[2]{0:T(128)} %get-tuple-element.209.where_ref, bf16[1536,512]{1,0:T(8,128)(2,1)} %get-tuple-element.91.a2_t, bf16[5,512,512]{2,1,0:T(8,128)(2,1)} %get-tuple-element.92.hidden_t, bf16[512,1536]{1,0:T(8,128)(2,1)} %slice.155.grads, ...), custom_call_target="tpu_custom_call" | custom-call | tf_op jit(solution)/shard_map/expert_grads/pallas_call | solution.py:465
  390.9 10.5 %expert_grads.4 = (bf16[3,5,192,512]{3,2,1,0:T(8,128)(2,1)}, bf16[3,5,192,512]{3,2,1,0:T(8,128)(2,1)}) custom-call(s32[2]{0:T(128)} %get-tuple-element.207.where_ref, bf16[1536,512]{1,0:T(8,128)(2,1)} %get-tuple-element.91.a2_t, bf16[5,512,512]{2,1,0:T(8,128)(2,1)} %get-tuple-element.92.hidden_t, bf16[512,1536]{1,0:T(8,128)(2,1)} %slice.155.grads, ...), custom_call_target="tpu_custom_call" | custom-call | tf_op jit(solution)/shard_map/expert_grads/pallas_call | solution.py:465
  401.4 10.5 %expert_grads.5 = (bf16[3,5,192,512]{3,2,1,0:T(8,128)(2,1)}, bf16[3,5,192,512]{3,2,1,0:T(8,128)(2,1)}) custom-call(s32[2]{0:T(128)} %get-tuple-element.208.where_ref, bf16[1536,512]{1,0:T(8,128)(2,1)} %get-tuple-element.91.a2_t, bf16[5,512,512]{2,1,0:T(8,128)(2,1)} %get-tuple-element.92.hidden_t, bf16[512,1536]{1,0:T(8,128)(2,1)} %slice.155.grads, ...), custom_call_target="tpu_custom_call" | custom-call | tf_op jit(solution)/shard_map/expert_grads/pallas_call | solution.py:465
  451.0 35.2 %collective-permute-done.54 = bf16[192,384]{1,0:T(8,128)(2,1)S(1)} collective-permute-done((bf16[192,384]{1,0:T(8,128)(2,1)S(1)}, bf16[192,384]{1,0:T(8,128)(2,1)S(1)}, u32[]{:S(2)}, u32[]{:S(2)}) %collective-permute-start.54) | collective-permute-done | bytes 147488 | tf_op jit(solution)/shard_map/ppermute | solution.py:61
  506.3 8.5 %collective-permute-done.49.refs_1_ = bf16[128,1536]{1,0:T(8,128)(2,1)S(1)} collective-permute-done((bf16[128,1536]{1,0:T(8,128)(2,1)S(1)}, bf16[128,1536]{1,0:T(8,128)(2,1)S(1)}, u32[]{:S(2)}, u32[]{:S(2)}) %collective-permute-start.49) | collective-permute-done | bytes 393248 | tf_op jit(solution)/shard_map/ppermute | solution.py:136
  523.0 8.8 %collective-permute-done.50.refs_2_ = bf16[128,1536]{1,0:T(8,128)(2,1)S(1)} collective-permute-done((bf16[128,1536]{1,0:T(8,128)(2,1)S(1)}, bf16[128,1536]{1,0:T(8,128)(2,1)S(1)}, u32[]{:S(2)}, u32[]{:S(2)}) %collective-permute-start.50) | collective-permute-done | bytes 393248 | tf_op jit(solution)/shard_map/ppermute | solution.py:136
  534.2 8.2 %collective-permute-start.59 = (bf16[48,768]{1,0:T(8,128)(2,1)S(1)}, bf16[48,768]{1,0:T(8,128)(2,1)S(1)}, u32[]{:S(2)}, u32[]{:S(2)}) collective-permute-start(bf16[48,768]{1,0:T(8,128)(2,1)S(1)} %get-tuple-element.179), channel_id=1, source_target_pairs={{0,1},{1,2},{2,3},{3,0},{4,5},{5,6},{6,7},{7,4},{8,9},{9,10},{10,1... | collective-permute-start | bytes 221192 | tf_op jit(solution)/shard_map/ppermute | solution.py:136
  561.3 20.9 %collective-permute-done.73 = bf16[3,5,192,256]{3,2,1,0:T(8,128)(2,1)} collective-permute-done((bf16[3,5,192,256]{3,2,1,0:T(8,128)(2,1)}, bf16[3,5,192,256]{3,2,1,0:T(8,128)(2,1)}, u32[]{:S(2)}, u32[]{:S(2)}) %collective-permute-start.73) | collective-permute-done | bytes 1474592 | tf_op jit(solution)/shard_map/ppermute | solution.py:61
  587.8 26.0 %collective-permute-done.72.got_a = bf16[3,5,192,256]{3,2,1,0:T(8,128)(2,1)} collective-permute-done((bf16[3,5,192,256]{3,2,1,0:T(8,128)(2,1)}, bf16[3,5,192,256]{3,2,1,0:T(8,128)(2,1)}, u32[]{:S(2)}, u32[]{:S(2)}) %collective-permute-start.72) | collective-permute-done | bytes 1474592 | tf_op jit(solution)/shard_map/ppermute | solution.py:61
  (350 shorter events, 245.3 us)
Async XLA Ops:
  3.3 83.9 %collective-permute-start.8 = (bf16[128,1536]{1,0:T(8,128)(2,1)S(1)}, bf16[128,1536]{1,0:T(8,128)(2,1)S(1)}, u32[]{:S(2)}, u32[]{:S(2)}) collective-permute-start(bf16[128,1536]{1,0:T(8,128)(2,1)S(1)} %multiply_convert_fusion.refs_0_.refs_4_), channel_id=1, source_target_pairs={{0,1},{1,2},{2,3},{3,0},{4,5},{5,6},{6,7},{7,4},{8,9},{9,10},{10,1... | collective-permute-start | bytes 1179656 | tf_op jit(solution)/shard_map/ppermute | solution.py:136
  3.4 83.9 %collective-permute-start.9 = (bf16[128,1536]{1,0:T(8,128)(2,1)S(1)}, bf16[128,1536]{1,0:T(8,128)(2,1)S(1)}, u32[]{:S(2)}, u32[]{:S(2)}) collective-permute-start(bf16[128,1536]{1,0:T(8,128)(2,1)S(1)} %multiply_convert_fusion.refs_0_.refs_4_), channel_id=1, source_target_pairs={{0,2},{1,3},{2,0},{3,1},{4,6},{5,7},{6,4},{7,5},{8,10},{9,11},{10,... | collective-permute-start | bytes 1179656 | tf_op jit(solution)/shard_map/ppermute | solution.py:136
  7.7 35.6 %collective-permute-start.1 = (bf16[48,768]{1,0:T(8,128)(2,1)}, bf16[48,768]{1,0:T(8,128)(2,1)S(1)}, u32[]{:S(2)}, u32[]{:S(2)}) collective-permute-start(bf16[48,768]{1,0:T(8,128)(2,1)} %bitcast.207), channel_id=1, source_target_pairs={{0,2},{1,3},{2,0},{3,1},{4,6},{5,7},{6,4},{7,5},{8,10},{9,11},{10,... | collective-permute-start | bytes 221192 | tf_op jit(solution)/shard_map/ppermute | solution.py:136
  23.0 65.8 %collective-permute-start.10 = (bf16[128,1536]{1,0:T(8,128)(2,1)S(1)}, bf16[128,1536]{1,0:T(8,128)(2,1)S(1)}, u32[]{:S(2)}, u32[]{:S(2)}) collective-permute-start(bf16[128,1536]{1,0:T(8,128)(2,1)S(1)} %multiply_convert_fusion.refs_0_.refs_4_), channel_id=1, source_target_pairs={{0,3},{1,0},{2,1},{3,2},{4,7},{5,4},{6,5},{7,6},{8,11},{9,8},{10,9... | collective-permute-start | bytes 1179656 | tf_op jit(solution)/shard_map/ppermute | solution.py:136
  88.7 46.7 %collective-permute-start.26 = (bf16[3,5,192,256]{3,2,1,0:T(8,128)(2,1)}, bf16[3,5,192,256]{3,2,1,0:T(8,128)(2,1)}, u32[]{:S(2)}, u32[]{:S(2)}) collective-permute-start(bf16[3,5,192,256]{3,2,1,0:T(8,128)(2,1)} %get-tuple-element.65.refs_7_), channel_id=1, source_target_pairs={{0,4},{4,0},{8,12},{12,8},{16,20},{20,16},{24,28},{28,24},{1,5},{5... | collective-permute-start | bytes 4423688 | tf_op jit(solution)/shard_map/ppermute | solution.py:58
  89.2 46.3 %collective-permute-start.27 = (bf16[3,5,192,256]{3,2,1,0:T(8,128)(2,1)}, bf16[3,5,192,256]{3,2,1,0:T(8,128)(2,1)}, u32[]{:S(2)}, u32[]{:S(2)}) collective-permute-start(bf16[3,5,192,256]{3,2,1,0:T(8,128)(2,1)} %get-tuple-element.65.refs_7_), channel_id=1, source_target_pairs={{0,8},{4,12},{8,0},{12,4},{16,24},{20,28},{24,16},{28,20},{1,9},{5... | collective-permute-start | bytes 4423688 | tf_op jit(solution)/shard_map/ppermute | solution.py:61
  124.0 51.4 %collective-permute-start.32 = (bf16[3,5,192,256]{3,2,1,0:T(8,128)(2,1)}, bf16[3,5,192,256]{3,2,1,0:T(8,128)(2,1)}, u32[]{:S(2)}, u32[]{:S(2)}) collective-permute-start(bf16[3,5,192,256]{3,2,1,0:T(8,128)(2,1)} %get-tuple-element.65.refs_7_), channel_id=1, source_target_pairs={{0,16},{4,20},{8,24},{12,28},{16,0},{20,4},{24,8},{28,12},{1,17},{... | collective-permute-start | bytes 4423688 | tf_op jit(solution)/shard_map/ppermute | solution.py:64
  135.4 41.2 %collective-permute-start.36 = (bf16[3,5,192,256]{3,2,1,0:T(8,128)(2,1)}, bf16[3,5,192,256]{3,2,1,0:T(8,128)(2,1)S(1)}, u32[]{:S(2)}, u32[]{:S(2)}) collective-permute-start(bf16[3,5,192,256]{3,2,1,0:T(8,128)(2,1)} %get-tuple-element.66.refs_11_), channel_id=1, source_target_pairs={{0,8},{4,12},{8,0},{12,4},{16,24},{20,28},{24,16},{28,20},{1,9},{5... | collective-permute-start | bytes 4423688 | tf_op jit(solution)/shard_map/ppermute | solution.py:61
  147.0 68.5 %collective-permute-start.28 = (bf16[3,5,192,256]{3,2,1,0:T(8,128)(2,1)}, bf16[3,5,192,256]{3,2,1,0:T(8,128)(2,1)S(1)}, u32[]{:S(2)}, u32[]{:S(2)}) collective-permute-start(bf16[3,5,192,256]{3,2,1,0:T(8,128)(2,1)} %collective-permute-done.27.refs_9_), channel_id=1, source_target_pairs={{0,4},{4,0},{8,12},{12,8},{16,20},{20,16},{24,28},{28,24},{1,5},{5... | collective-permute-start | bytes 4423688 | tf_op jit(solution)/shard_map/ppermute | solution.py:58
  165.6 50.4 %collective-permute-start.34 = (bf16[3,5,192,256]{3,2,1,0:T(8,128)(2,1)}, bf16[3,5,192,256]{3,2,1,0:T(8,128)(2,1)}, u32[]{:S(2)}, u32[]{:S(2)}) collective-permute-start(bf16[3,5,192,256]{3,2,1,0:T(8,128)(2,1)} %collective-permute-done.27.refs_9_), channel_id=1, source_target_pairs={{0,16},{4,20},{8,24},{12,28},{16,0},{20,4},{24,8},{28,12},{1,17},{... | collective-permute-start | bytes 4423688 | tf_op jit(solution)/shard_map/ppermute | solution.py:64
  165.6 50.7 %collective-permute-start.38 = (bf16[3,5,192,256]{3,2,1,0:T(8,128)(2,1)}, bf16[3,5,192,256]{3,2,1,0:T(8,128)(2,1)}, u32[]{:S(2)}, u32[]{:S(2)}) collective-permute-start(bf16[3,5,192,256]{3,2,1,0:T(8,128)(2,1)} %collective-permute-done.30.refs_13_), channel_id=1, source_target_pairs={{0,8},{4,12},{8,0},{12,4},{16,24},{20,28},{24,16},{28,20},{1,9},{5... | collective-permute-start | bytes 4423688 | tf_op jit(solution)/shard_map/ppermute | solution.py:61
  176.6 37.2 %collective-permute-start.21 = (bf16[128,1536]{1,0:T(8,128)(2,1)}, bf16[128,1536]{1,0:T(8,128)(2,1)S(1)}, u32[]{:S(2)}, u32[]{:S(2)}) collective-permute-start(bf16[128,1536]{1,0:T(8,128)(2,1)} %get-tuple-element.64.refs_0_.a2), channel_id=1, source_target_pairs={{0,2},{1,3},{2,0},{3,1},{4,6},{5,7},{6,4},{7,5},{8,10},{9,11},{10,... | collective-permute-start | bytes 1179656 | tf_op jit(solution)/shard_map/ppermute | solution.py:136
  311.4 35.6 %collective-permute-start.47 = (bf16[128,1536]{1,0:T(8,128)(2,1)}, bf16[128,1536]{1,0:T(8,128)(2,1)S(1)}, u32[]{:S(2)}, u32[]{:S(2)}) collective-permute-start(bf16[128,1536]{1,0:T(8,128)(2,1)} %get-tuple-element.77.refs_0_), channel_id=1, source_target_pairs={{0,2},{1,3},{2,0},{3,1},{4,6},{5,7},{6,4},{7,5},{8,10},{9,11},{10,... | collective-permute-start | bytes 1179656 | tf_op jit(solution)/shard_map/ppermute | solution.py:136
  364.4 47.6 %collective-permute-start.60 = (bf16[4,48,1536]{2,1,0:T(8,128)(2,1)S(1)}, bf16[4,48,1536]{2,1,0:T(8,128)(2,1)}, u32[]{:S(2)}, u32[]{:S(2)}) collective-permute-start(bf16[4,48,1536]{2,1,0:T(8,128)(2,1)S(1)} %dynamic-slice_bitcast_fusion.1), channel_id=1, source_target_pairs={{0,4},{4,0},{8,12},{12,8},{16,20},{20,16},{24,28},{28,24},{1,5},{5... | collective-permute-start | bytes 1769480 | tf_op jit(solution)/shard_map/ppermute | solution.py:58
  378.9 56.1 %collective-permute-start.70 = (bf16[3,5,192,512]{3,2,1,0:T(8,128)(2,1)}, bf16[3,5,192,512]{3,2,1,0:T(8,128)(2,1)}, u32[]{:S(2)}, u32[]{:S(2)}) collective-permute-start(bf16[3,5,192,512]{3,2,1,0:T(8,128)(2,1)} %get-tuple-element.102), channel_id=1, source_target_pairs={{0,4},{4,0},{8,12},{12,8},{16,20},{20,16},{24,28},{28,24},{1,5},{5... | collective-permute-start | bytes 8847368 | tf_op jit(solution)/shard_map/ppermute | solution.py:58
  379.6 59.9 %collective-permute-start.42 = (bf16[128,1536]{1,0:T(8,128)(2,1)}, bf16[128,1536]{1,0:T(8,128)(2,1)}, u32[]{:S(2)}, u32[]{:S(2)}) collective-permute-start(bf16[128,1536]{1,0:T(8,128)(2,1)} %get-tuple-element.70), channel_id=1, source_target_pairs={{0,1},{1,2},{2,3},{3,0},{4,5},{5,6},{6,7},{7,4},{8,9},{9,10},{10,1... | collective-permute-start | bytes 1179656 | tf_op jit(solution)/shard_map/ppermute | solution.py:136
  390.5 102.6 %collective-permute-start.69 = (bf16[3,5,192,512]{3,2,1,0:T(8,128)(2,1)}, bf16[3,5,192,512]{3,2,1,0:T(8,128)(2,1)S(1)}, u32[]{:S(2)}, u32[]{:S(2)}) collective-permute-start(bf16[3,5,192,512]{3,2,1,0:T(8,128)(2,1)} %get-tuple-element.100), channel_id=1, source_target_pairs={{0,4},{4,0},{8,12},{12,8},{16,20},{20,16},{24,28},{28,24},{1,5},{5... | collective-permute-start | bytes 8847368 | tf_op jit(solution)/shard_map/ppermute | solution.py:58
  430.2 86.0 %collective-permute-start.67 = (bf16[3,5,192,512]{3,2,1,0:T(8,128)(2,1)S(1)}, bf16[3,5,192,512]{3,2,1,0:T(8,128)(2,1)S(1)}, u32[]{:S(2)}, u32[]{:S(2)}) collective-permute-start(bf16[3,5,192,512]{3,2,1,0:T(8,128)(2,1)S(1)} %copy-done.43), channel_id=1, source_target_pairs={{0,4},{4,0},{8,12},{12,8},{16,20},{20,16},{24,28},{28,24},{1,5},{5... | collective-permute-start | bytes 8847368 | tf_op jit(solution)/shard_map/ppermute | solution.py:58
  439.5 55.4 %collective-permute-start.71 = (bf16[3,5,192,256]{3,2,1,0:T(8,128)(2,1)S(1)}, bf16[3,5,192,256]{3,2,1,0:T(8,128)(2,1)S(1)}, u32[]{:S(2)}, u32[]{:S(2)}) collective-permute-start(bf16[3,5,192,256]{3,2,1,0:T(8,128)(2,1)S(1)} %get-tuple-element.151), channel_id=1, source_target_pairs={{0,16},{4,20},{8,24},{12,28},{16,0},{20,4},{24,8},{28,12},{1,17},{... | collective-permute-start | bytes 4423688 | tf_op jit(solution)/shard_map/ppermute | solution.py:64
  448.8 70.5 %collective-permute-start.74 = (bf16[3,5,192,256]{3,2,1,0:T(8,128)(2,1)S(1)}, bf16[3,5,192,256]{3,2,1,0:T(8,128)(2,1)S(1)}, u32[]{:S(2)}, u32[]{:S(2)}) collective-permute-start(bf16[3,5,192,256]{3,2,1,0:T(8,128)(2,1)S(1)} %get-tuple-element.150), channel_id=1, source_target_pairs={{0,8},{4,12},{8,0},{12,4},{16,24},{20,28},{24,16},{28,20},{1,9},{5... | collective-permute-start | bytes 4423688 | tf_op jit(solution)/shard_map/ppermute | solution.py:61
  450.9 35.4 %collective-permute-start.54 = (bf16[192,384]{1,0:T(8,128)(2,1)S(1)}, bf16[192,384]{1,0:T(8,128)(2,1)S(1)}, u32[]{:S(2)}, u32[]{:S(2)}) collective-permute-start(bf16[192,384]{1,0:T(8,128)(2,1)S(1)} %fusion.4), channel_id=1, source_target_pairs={{0,8},{4,12},{8,0},{12,4},{16,24},{20,28},{24,16},{28,20},{1,9},{5... | collective-permute-start | bytes 442376 | tf_op jit(solution)/shard_map/ppermute | solution.py:61
  490.3 71.0 %collective-permute-start.66 = (bf16[3,5,192,512]{3,2,1,0:T(8,128)(2,1)}, bf16[3,5,192,512]{3,2,1,0:T(8,128)(2,1)}, u32[]{:S(2)}, u32[]{:S(2)}) collective-permute-start(bf16[3,5,192,512]{3,2,1,0:T(8,128)(2,1)} %get-tuple-element.96), channel_id=1, source_target_pairs={{0,4},{4,0},{8,12},{12,8},{16,20},{20,16},{24,28},{28,24},{1,5},{5... | collective-permute-start | bytes 8847368 | tf_op jit(solution)/shard_map/ppermute | solution.py:58
  555.3 58.5 %collective-permute-start.72 = (bf16[3,5,192,256]{3,2,1,0:T(8,128)(2,1)}, bf16[3,5,192,256]{3,2,1,0:T(8,128)(2,1)}, u32[]{:S(2)}, u32[]{:S(2)}) collective-permute-start(bf16[3,5,192,256]{3,2,1,0:T(8,128)(2,1)} %get-tuple-element.155), channel_id=1, source_target_pairs={{0,8},{4,12},{8,0},{12,4},{16,24},{20,28},{24,16},{28,20},{1,9},{5... | collective-permute-start | bytes 4423688 | tf_op jit(solution)/shard_map/ppermute | solution.py:61
  556.9 57.0 %collective-permute-start.75 = (bf16[3,5,192,256]{3,2,1,0:T(8,128)(2,1)}, bf16[3,5,192,256]{3,2,1,0:T(8,128)(2,1)}, u32[]{:S(2)}, u32[]{:S(2)}) collective-permute-start(bf16[3,5,192,256]{3,2,1,0:T(8,128)(2,1)} %get-tuple-element.148), channel_id=1, source_target_pairs={{0,16},{4,20},{8,24},{12,28},{16,0},{20,4},{24,8},{28,12},{1,17},{... | collective-permute-start | bytes 4423688 | tf_op jit(solution)/shard_map/ppermute | solution.py:64
  (101 other events, 1655.3 us)

commit v2 on v1

v2 whole, which is shorter than its diff:
```python
import functools

import jax
import jax.numpy as jnp
from jax import lax
from jax.experimental import pallas as pl
from jax.experimental.pallas import tpu as pltpu
from jax.sharding import PartitionSpec as P

QUERY_HEADS = 24
KEY_VALUE_HEADS = 8
GROUP = QUERY_HEADS // KEY_VALUE_HEADS
HEAD_WIDTH = 64
PIECE = 256
LANES = 128
DEVICE_ROWS = 128
EPSILON = 1e-05
NEG_FILL = -1e30
SCORE_SCALE = HEAD_WIDTH ** (-0.5)
F32 = jnp.float32
BF16 = jnp.bfloat16

VMEM = pl.BlockSpec(memory_space=pltpu.VMEM)
SMEM = pl.BlockSpec(memory_space=pltpu.SMEM)
ANY = pl.BlockSpec(memory_space=pl.ANY)
MESH = pl.DeviceIdType.MESH


def dot(a, b):
    return lax.dot_general(a, b, (((1,), (0,)), ((), ())), preferred_element_type=F32)


def dot_nt(a, b):
    return lax.dot_general(a, b, (((1,), (1,)), ((), ())), preferred_element_type=F32)


def dot_tn(a, b):
    return lax.dot_general(a, b, (((0,), (0,)), ((), ())), preferred_element_type=F32)


def shape_of(dims, dtype):
    return jax.ShapeDtypeStruct(tuple(dims), dtype)


def params(**kw):
    return pltpu.CompilerParams(vmem_limit_bytes=60 * 1024 * 1024, **kw)


class Plane:
    def __init__(self):
        self.size = lax.axis_size("fsdp")
        self.rows = self.size // 4
        index = lax.axis_index("fsdp")
        self.index = index
        self.core = index % 2
        self.mid = (index // 2) % 2
        self.row = index // 4

    def other_core(self, x):
        return lax.ppermute(x, "fsdp", [(i, i ^ 1) for i in range(self.size)])

    def other_mid(self, x):
        return lax.ppermute(x, "fsdp", [(i, i ^ 2) for i in range(self.size)])

    def next_row(self, x, step):
        return lax.ppermute(
            x, "fsdp", [(i, (i // 4 + step) % self.rows * 4 + i % 4) for i in range(self.size)]
        )


def expert_shift(x, step):
    count = lax.axis_size("expert")
    return lax.ppermute(x, "expert", [(i, (i + step) % count) for i in range(count)])


def expert_gather(x):
    count = lax.axis_size("expert")
    return [x] + [expert_shift(x, s) for s in range(1, count)]


def expert_scatter(blocks):
    count = lax.axis_size("expert")
    return [expert_shift(blocks[s], count - s) for s in range(1, count)]


def chooser(width, blocks, part, dtype=BF16):
    n = width // blocks
    line = lax.broadcasted_iota(jnp.int32, (width // 2, width), 0)
    column = lax.broadcasted_iota(jnp.int32, (width // 2, width), 1)
    want = (2 * (line // n) + part) * n + line % n
    return jnp.where(column == want, 1.0, 0.0).astype(dtype)


def pack_kernel(blocks, core, gate, up, down, keep, send, halves):
    width = gate.shape[2]
    mine = chooser(width, blocks, core[0])
    theirs = chooser(width, blocks, 1 - core[0])
    for place, ref in ((0, gate), (1, up)):
        value = ref[0].astype(BF16)
        keep[place, 0] = dot_nt(value, mine).astype(BF16)
        send[place, 0] = dot_nt(value, theirs).astype(BF16)
    value = down[0].astype(BF16)
    rows, wide = value.shape[0] // 2, width // 2
    for part in range(2):
        for j in range(value.shape[1] // wide):
            halves[part, 0, j * rows : (j + 1) * rows] = value[
                part * rows : (part + 1) * rows, j * wide : (j + 1) * wide
            ]


def pack_experts(core, w_gate, w_up, w_down, blocks):
    local, depth, width = w_gate.shape
    out = shape_of((2, local, depth, width // 2), BF16)
    block = pl.BlockSpec((2, 1, depth, width // 2), lambda e: (0, e, 0, 0))
    return pl.pallas_call(
        functools.partial(pack_kernel, blocks),
        grid=(local,),
        in_specs=[SMEM]
        + [pl.BlockSpec((1,) + w.shape[1:], lambda e: (e, 0, 0)) for w in (w_gate, w_up, w_down)],
        out_specs=[block] * 3,
        out_shape=[out] * 3,
        name="pack_experts",
    )(core, w_gate, w_up, w_down)


def swap_halves(x):
    lane = lax.broadcasted_iota(jnp.int32, x.shape, 1)
    return jnp.where(
        lane % HEAD_WIDTH < HEAD_WIDTH // 2, pltpu.roll(x, LANES - 32, 1), pltpu.roll(x, 32, 1)
    )


def head_slice(ref, start):
    return ref[:, start : start + HEAD_WIDTH]


def attend_kernel(
    blocks,
    kv_heads,
    *refs,
):
    x_refs = refs[:blocks]
    gain, weights, out_weights, bias, cosine, sine = refs[blocks : blocks + 6]
    (a1, qk, val, mixed, maxes, inverse) = refs[blocks + 6 : blocks + 12]
    sums = refs[blocks + 12 : blocks + 12 + blocks]
    mixed_t = refs[blocks + 12 + blocks]
    rows = x_refs[0].shape[0]
    rope_width = qk.shape[1]
    q_width = kv_heads * GROUP * HEAD_WIDTH
    for b in range(blocks):
        a1[b * rows : (b + 1) * rows, :] = (x_refs[b][...].astype(F32) * gain[...]).astype(BF16)
    linear = dot(a1[...], weights[:, : rope_width + val.shape[1]])
    for c in range(rope_width // LANES):
        x = linear[:, c * LANES : (c + 1) * LANES]
        qk[:, c * LANES : (c + 1) * LANES] = (
            x * cosine[...] + swap_halves(x) * sine[...]
        ).astype(BF16)
    val[...] = linear[:, rope_width:].astype(BF16)
    for g in range(kv_heads):
        key = head_slice(qk, q_width + g * HEAD_WIDTH)
        value_t = head_slice(val, g * HEAD_WIDTH).T
        for j in range(GROUP):
            h = g * GROUP + j
            scores = dot_nt(key, head_slice(qk, h * HEAD_WIDTH)) * SCORE_SCALE + bias[...]
            top = jnp.max(scores, axis=0, keepdims=True)
            weight = jnp.exp(scores - top)
            inv = 1.0 / jnp.sum(weight, axis=0, keepdims=True)
            maxes[h : h + 1, :] = top
            inverse[h : h + 1, :] = inv
            mixed_t[h * HEAD_WIDTH : (h + 1) * HEAD_WIDTH, :] = dot(
                value_t, (weight * inv).astype(BF16)
            )
    mixed[...] = mixed_t[...].T.astype(BF16)
    total = dot(mixed[...], out_weights[...])
    for b in range(blocks):
        sums[b][...] = total[b * rows : (b + 1) * rows, :].astype(sums[b].dtype)


def attend(x_blocks, gain, weights, out_weights, bias, cosine, sine, kv_heads, rope_width):
    blocks = len(x_blocks)
    rows, model = x_blocks[0].shape
    seq = rows * blocks
    q_width = kv_heads * GROUP * HEAD_WIDTH
    value_width = weights.shape[1] - LANES - rope_width
    heads = kv_heads * GROUP
    outs = [
        shape_of((seq, model), BF16),
        shape_of((seq, rope_width), BF16),
        shape_of((seq, value_width), BF16),
        shape_of((seq, q_width), BF16),
        shape_of((heads, seq), F32),
        shape_of((heads, seq), F32),
    ] + [shape_of((rows, model), F32 if b == 0 else BF16) for b in range(blocks)]
    out = pl.pallas_call(
        functools.partial(attend_kernel, blocks, kv_heads),
        in_specs=[VMEM] * (blocks + 6),
        out_specs=[VMEM] * len(outs),
        out_shape=outs,
        scratch_shapes=[pltpu.VMEM((q_width, seq), F32)],
        compiler_params=params(),
        name="attend",
    )(*x_blocks, gain, weights, out_weights, bias, cosine, sine)
    return out[:6], out[6:]


def experts_kernel(blocks, pieces, place, row_block, *refs):
    a2_in = refs[:blocks]
    grads_in, router_t, where_ref = refs[blocks : blocks + 3]
    piece_refs = refs[blocks + 3 : blocks + 3 + pieces]
    (out_all, dx_all, gates_out, a2_t, hidden_t, d_gate, d_up) = refs[
        blocks + 3 + pieces : blocks + 10 + pieces
    ]
    (a2, gate_w, up_w, down_w, out_sum, dx_sum, gates, dgates, in_sem, w_sem) = refs[
        blocks + 10 + pieces :
    ]
    step, steps = pl.program_id(0), pl.num_programs(0)
    rows = a2_in[0].shape[0]
    seq, model = a2.shape
    depth, width = piece_refs[0].shape[2], gate_w.shape[2]
    down_rows = depth * width // model
    slot = lax.rem(step, 2)

    def fetch(e, to):
        for i, (row_step, mid, part) in enumerate(place):
            source = where_ref[1 + row_step * 2 + mid] * 2 + part
            at = pl.multiple_of(source * depth, 32)
            for which, buf in ((0, gate_w), (1, up_w)):
                pltpu.make_async_copy(
                    piece_refs[i].at[which, e], buf.at[to, pl.ds(at, depth)], w_sem.at[which, to]
                ).start()
            at = pl.multiple_of(source * down_rows, 16)
            for j in range(model // width):
                pltpu.make_async_copy(
                    piece_refs[i].at[2, e, pl.ds(j * down_rows, down_rows)],
                    down_w.at[to, pl.ds(at, down_rows), pl.ds(j * width, width)],
                    w_sem.at[2, to],
                ).start()

    @pl.when(step == 0)
    def _():
        for b in range(blocks):
            pltpu.make_async_copy(
                a2_in[b], a2.at[pl.ds(b * rows, rows)], in_sem.at[0]
            ).start()
        fetch(0, 0)
        pltpu.make_async_copy(a2, a2, in_sem.at[0]).wait()
        logits = dot_nt(a2[...], router_t[...])
        routed = grads_in[:, model:].astype(F32) > 0.5
        top = jnp.max(jnp.where(routed, logits, NEG_FILL), axis=1, keepdims=True)
        weight = jnp.where(routed, jnp.exp(jnp.where(routed, logits, top) - top), 0.0)
        gates[...] = weight / jnp.sum(weight, axis=1, keepdims=True)
        gates_out[...] = gates[: gates_out.shape[0], :]
        dgates[...] = jnp.zeros_like(dgates)
        a2_t[...] = a2[...].T

    @pl.when(step + 1 < steps)
    def _():
        fetch(step + 1, 1 - slot)

    for which, buf in ((0, gate_w), (1, up_w), (2, down_w)):
        pltpu.make_async_copy(buf.at[slot], buf.at[slot], w_sem.at[which, slot]).wait()

    mine = where_ref[0] * steps + step

    def block(i, carry):
        at = pl.ds(pl.multiple_of(i * row_block, row_block), row_block)
        left = a2[at, :]
        gate_lin = dot(left, gate_w[slot])
        up_lin = dot(left, up_w[slot])
        back = dot_nt(grads_in[at, :model], down_w[slot])
        lane = lax.broadcasted_iota(jnp.int32, (row_block, LANES), 1)
        here = lane == mine
        gate = jnp.sum(jnp.where(here, gates[at, :], 0.0), axis=1, keepdims=True)
        sig = 1.0 / (1.0 + jnp.exp(-gate_lin))
        silu = gate_lin * sig
        hidden = silu * up_lin
        dgates[at, :] += jnp.where(here, jnp.sum(hidden * back, axis=1, keepdims=True), 0.0)
        hidden_low = (hidden * gate).astype(BF16)
        d_hidden = back * gate
        d_gate_low = (d_hidden * up_lin * (sig + silu * (1.0 - sig))).astype(BF16)
        d_up_low = (d_hidden * silu).astype(BF16)
        d_gate[at, :] = d_gate_low
        d_up[at, :] = d_up_low
        hidden_t[0, :, at] = hidden_low.T
        out_new = dot(hidden_low, down_w[slot])
        dx_new = dot_nt(d_gate_low, gate_w[slot]) + dot_nt(d_up_low, up_w[slot])

        @pl.when(step == 0)
        def _():
            out_sum[at, :] = out_new
            dx_sum[at, :] = dx_new

        @pl.when(step > 0)
        def _():
            out_sum[at, :] += out_new
            dx_sum[at, :] += dx_new

        return carry

    lax.fori_loop(0, seq // row_block, block, 0)

    @pl.when(step == steps - 1)
    def _():
        high = dgates[...].astype(BF16).astype(F32)
        low = dgates[...] - high
        lane = lax.broadcasted_iota(jnp.int32, high.shape, 1)
        tail = jnp.where(lane < LANES // 2, high, pltpu.roll(low, LANES // 2, 1))
        out_all[...] = out_sum[...].astype(out_all.dtype)
        dx_all[:, :model] = dx_sum[...].astype(dx_all.dtype)
        dx_all[:, model:] = tail.astype(dx_all.dtype)


def experts(a2_blocks, grads, router_t, where, pieces, place, dtype):
    blocks = len(a2_blocks)
    rows, model = a2_blocks[0].shape
    seq = rows * blocks
    local, depth, width = pieces[0].shape[1:]
    outs = [
        shape_of((seq, model), dtype),
        shape_of((seq, model + LANES), dtype),
        shape_of((DEVICE_ROWS, LANES), F32),
        shape_of((model, seq), BF16),
        shape_of((local, width, seq), BF16),
        shape_of((seq, local * width), BF16),
        shape_of((seq, local * width), BF16),
    ]
    whole = lambda dims: pl.BlockSpec(
        dims, lambda e: (0,) * len(dims), pipeline_mode=pl.Buffered(1)
    )
    out_specs = (
        [whole(o.shape) for o in outs[:4]]
        + [pl.BlockSpec((1, width, seq), lambda e: (e, 0, 0))]
        + [pl.BlockSpec((seq, width), lambda e: (0, e))] * 2
    )
    return pl.pallas_call(
        functools.partial(experts_kernel, blocks, len(pieces), place, 256),
        grid=(local,),
        in_specs=[ANY] * blocks
        + [whole(grads.shape), whole(router_t.shape), SMEM]
        + [ANY] * len(pieces),
        out_specs=out_specs,
        out_shape=outs,
        scratch_shapes=[
            pltpu.VMEM((seq, model), BF16),
            pltpu.VMEM((2, model, width), BF16),
            pltpu.VMEM((2, model, width), BF16),
            pltpu.VMEM((2, width, model), BF16),
            pltpu.VMEM((seq, model), F32),
            pltpu.VMEM((seq, model), F32),
            pltpu.VMEM((seq, LANES), F32),
            pltpu.VMEM((seq, LANES), F32),
            pltpu.SemaphoreType.DMA((1,)),
            pltpu.SemaphoreType.DMA((3, 2)),
        ],
        compiler_params=params(dimension_semantics=("arbitrary",)),
        name="experts",
    )(*a2_blocks, grads, router_t, where, *pieces)


def expert_grads_kernel(chips, depth, down_rows, where_ref, *refs):
    (a2_t0, a2_t1, hid0, hid1, grads0, grads1, dg0, dg1, du0, du1) = refs[:10]
    outs, down_sum = refs[10 : 10 + 2 * chips], refs[10 + 2 * chips]
    model, width = a2_t0.shape[0], dg0.shape[1]
    down_sum[...] = (dot(hid0[0], grads0[...]) + dot(hid1[0], grads1[...])).astype(BF16)
    for place in range(chips):
        source = where_ref[place]
        at = pl.ds(pl.multiple_of(source * 2 * depth, 32), 2 * depth)
        left0, left1 = a2_t0[at, :], a2_t1[at, :]
        gate = (dot(left0, dg0[...]) + dot(left1, dg1[...])).astype(BF16)
        up = (dot(left0, du0[...]) + dot(left1, du1[...])).astype(BF16)
        for part in range(2):
            out = outs[2 * place + part]
            out[0, 0] = gate[part * depth : (part + 1) * depth]
            out[1, 0] = up[part * depth : (part + 1) * depth]
            at = pl.ds(pl.multiple_of((source * 2 + part) * down_rows, 16), down_rows)
            down = down_sum[at, :]
            for j in range(model // width):
                out[2, 0, j * down_rows : (j + 1) * down_rows, :] = down[
                    :, j * width : (j + 1) * width
                ]


def expert_grads(where, first, second, plane_size):
    model, seq = first[0].shape
    local, width = first[1].shape[:2]
    chips = plane_size // 2
    depth, down_rows = model // plane_size, width // plane_size
    out = shape_of((3, local, depth, width), BF16)
    block = pl.BlockSpec((3, 1, depth, width), lambda e: (0, e, 0, 0))
    once = lambda dims: pl.BlockSpec(dims, lambda e: (0, 0), pipeline_mode=pl.Buffered(1))
    specs = [
        once((model, seq)),
        pl.BlockSpec((1, width, seq), lambda e: (e, 0, 0)),
        once((seq, model)),
        pl.BlockSpec((seq, width), lambda e: (0, e)),
        pl.BlockSpec((seq, width), lambda e: (0, e)),
    ]
    operands = [v for pair in zip(first, second) for v in pair]
    return pl.pallas_call(
        functools.partial(expert_grads_kernel, chips, depth, down_rows),
        grid=(local,),
        in_specs=[SMEM] + [spec for spec in specs for _ in range(2)],
        out_specs=[block] * (2 * chips),
        out_shape=[out] * (2 * chips),
        scratch_shapes=[pltpu.VMEM((width, model), BF16)],
        compiler_params=params(),
        name="expert_grads",
    )(where, *operands)


def finish_kernel(blocks, core, kept_a, got_a, kept_b, got_b, other, gate, up, down):
    width, wide = gate.shape[2], kept_a.shape[3]
    mine = chooser(width, blocks, core[0])
    theirs = chooser(width, blocks, 1 - core[0])
    first = core[0] == 0
    for place, out in ((0, gate), (1, up)):
        kept = jnp.where(first, kept_a[place, 0].astype(F32), kept_b[place, 0].astype(F32))
        got = jnp.where(first, got_a[place, 0].astype(F32), got_b[place, 0].astype(F32))
        out[0] = (
            dot(kept.astype(BF16), mine)
            + dot(got.astype(BF16), mine)
            + dot(other[place, 0], theirs)
        )
    rows = down.shape[1] // 2
    for part, kept, got in ((0, kept_a, got_a), (1, kept_b, got_b)):
        value = kept[2, 0].astype(F32) + got[2, 0].astype(F32)
        for j in range(value.shape[0] // rows):
            down[0, part * rows : (part + 1) * rows, j * wide : (j + 1) * wide] = value[
                j * rows : (j + 1) * rows
            ]


def finish(core, kept_a, got_a, kept_b, got_b, other, down_rows, model, blocks):
    local, depth, wide = kept_a.shape[1:]
    block = pl.BlockSpec((3, 1, depth, wide), lambda e: (0, e, 0, 0))
    outs = [
        shape_of((local, depth, 2 * wide), F32),
        shape_of((local, depth, 2 * wide), F32),
        shape_of((local, down_rows, model), F32),
    ]
    return pl.pallas_call(
        functools.partial(finish_kernel, blocks),
        grid=(local,),
        in_specs=[SMEM]
        + [block] * 4
        + [pl.BlockSpec((2, 1, depth, wide), lambda e: (0, e, 0, 0))],
        out_specs=[pl.BlockSpec((1,) + o.shape[1:], lambda e: (e, 0, 0)) for o in outs],
        out_shape=outs,
        name="finish",
    )(core, kept_a, got_a, kept_b, got_b, other)


def attend_back_kernel(blocks, kv_heads, gain_row, *refs):
    dh_ref, x_refs = refs[0], refs[1 : blocks + 1]
    (weights, out_weights, a1, qk, val, mixed, maxes, inverse, bias, cosine, sine, extra) = refs[
        blocks + 1 : blocks + 13
    ]
    d_weights, d_out_weights = refs[blocks + 13 : blocks + 15]
    sums = refs[blocks + 15 : 2 * blocks + 15]
    grads, d_mixed, dq_t, d_qk, d_lin = refs[2 * blocks + 15 :]
    rows = x_refs[0].shape[0]
    rope_width, value_width = qk.shape[1], val.shape[1]
    q_width = kv_heads * GROUP * HEAD_WIDTH
    for b in range(blocks):
        grads[b * rows : (b + 1) * rows, :] = dh_ref[b]
    d_mixed[...] = dot_nt(grads[...], out_weights[...]).astype(BF16)
    d_out_weights[...] = dot_tn(mixed[...], grads[...]).astype(BF16)
    if value_width > kv_heads * HEAD_WIDTH:
        d_lin[:, rope_width:] = jnp.zeros((d_lin.shape[0], value_width), BF16)
    for g in range(kv_heads):
        key = head_slice(qk, q_width + g * HEAD_WIDTH)
        key_t = key.T
        value = head_slice(val, g * HEAD_WIDTH)
        d_key, d_value = None, None
        for j in range(GROUP):
            h = g * GROUP + j
            query = head_slice(qk, h * HEAD_WIDTH)
            grad = head_slice(d_mixed, h * HEAD_WIDTH)
            scores = dot_nt(key, query) * SCORE_SCALE + bias[...]
            prob = jnp.exp(scores - maxes[h : h + 1, :]) * inverse[h : h + 1, :]
            d_prob = dot_nt(value, grad)
            inner = jnp.sum(prob * d_prob, axis=0, keepdims=True)
            d_scores = (prob * (d_prob - inner)).astype(BF16)
            dk = dot(d_scores, query)
            dv = dot(prob.astype(BF16), grad)
            d_key = dk if d_key is None else d_key + dk
            d_value = dv if d_value is None else d_value + dv
            dq_t[h * HEAD_WIDTH : (h + 1) * HEAD_WIDTH, :] = dot(key_t, d_scores)
        start = q_width + g * HEAD_WIDTH
        d_qk[:, start : start + HEAD_WIDTH] = d_key * SCORE_SCALE
        start = rope_width + g * HEAD_WIDTH
        d_lin[:, start : start + HEAD_WIDTH] = d_value.astype(BF16)
    d_qk[:, :q_width] = dq_t[...].T * SCORE_SCALE
    for c in range(rope_width // LANES):
        at = slice(c * LANES, (c + 1) * LANES)
        x = d_qk[:, at]
        d_lin[:, at] = (x * cosine[...] - swap_halves(x) * sine[...]).astype(BF16)
    total = dot_nt(d_lin[...], weights[:, : rope_width + value_width])
    gain_grad = None
    for b in range(blocks):
        part = total[b * rows : (b + 1) * rows, :]
        sums[b][...] = part.astype(sums[b].dtype)
        new = jnp.sum(part * x_refs[b][...].astype(F32), axis=0, keepdims=True)
        gain_grad = new if gain_grad is None else gain_grad + new
    d_weights[:, : rope_width + value_width] = dot_tn(a1[...], d_lin[...]).astype(BF16)
    line = lax.broadcasted_iota(jnp.int32, extra.shape, 0)
    tail = jnp.where(line == gain_row, gain_grad, extra[...])
    d_weights[:, rope_width + value_width :] = tail.T.astype(BF16)


def attend_back(
    dh_stack, x_blocks, weights, out_weights, kept, bias, cosine, sine, extra, kv_heads, gain_row
):
    blocks, rows, model = dh_stack.shape
    seq = rows * blocks
    q_width = out_weights.shape[0]
    rope_width, value_width = kept[1].shape[1], kept[2].shape[1]
    outs = [shape_of(weights.shape, BF16), shape_of(out_weights.shape, BF16)] + [
        shape_of((rows, model), F32 if b == 0 else BF16) for b in range(blocks)
    ]
    out = pl.pallas_call(
        functools.partial(attend_back_kernel, blocks, kv_heads, gain_row),
        in_specs=[VMEM] * (blocks + 13),
        out_specs=[VMEM] * len(outs),
        out_shape=outs,
        scratch_shapes=[
            pltpu.VMEM((seq, model), BF16),
            pltpu.VMEM((seq, q_width), BF16),
            pltpu.VMEM((q_width, seq), F32),
            pltpu.VMEM((seq, rope_width), F32),
            pltpu.VMEM((seq, rope_width + value_width), BF16),
        ],
        compiler_params=params(),
        name="attend_back",
    )(dh_stack, *x_blocks, weights, out_weights, *kept, bias, cosine, sine, extra)
    return out[0], out[1], out[2:]


class Spot:
    def __init__(self, ranks, plane_size):
        self.ranks, self.chips = ranks, plane_size // 2
        self.rank = lax.axis_index("expert")
        self.index = lax.axis_index("fsdp")
        self.chip = self.index // 2
        self.core = self.index % 2

    def behind(self, s):
        return {"expert": lax.rem(self.rank - s + self.ranks, self.ranks)}

    def ahead(self, s):
        return {"expert": lax.rem(self.rank + s, self.ranks)}

    def partner(self):
        return {"fsdp": self.chip * 2 + (1 - self.core)}

    def chip_ahead(self, k):
        return lax.rem(self.chip + k, self.chips)

    def chip_behind(self, k):
        return lax.rem(self.chip - k + self.chips, self.chips)

    def on_chip(self, chip):
        return {"fsdp": chip * 2 + self.core}


def meet(peers):
    barrier = pltpu.get_barrier_semaphore()
    for peer in peers:
        pl.semaphore_signal(barrier, inc=1, device_id=peer, device_id_type=MESH)
    pl.semaphore_wait(barrier, len(peers))


def send(src, dst, send_sem, recv_sem, peer):
    copy = pltpu.make_async_remote_copy(
        src_ref=src,
        dst_ref=dst,
        send_sem=send_sem,
        recv_sem=recv_sem,
        device_id=peer,
        device_id_type=MESH,
    )
    copy.start()
    return copy


def remote(collective_id):
    return params(collective_id=collective_id, has_side_effects=True)


def gather_weights_kernel(ranks, plane_size, by_rank, rows_in, weights, out_rows, *sems):
    z_send, z_recv, p_send, p_recv, c_send, c_recv, local = sems
    spot = Spot(ranks, plane_size)
    f, me, chips = spot.index, spot.rank, spot.chips
    others = range(1, ranks)
    meet(
        [spot.ahead(s) for s in others]
        + [spot.on_chip(spot.chip_ahead(k)) for k in range(1, chips)]
        + [spot.partner()]
    )
    waits = []
    z_copies = [
        send(
            by_rank.at[lax.rem(me + s, ranks)],
            weights.at[f, me],
            z_send.at[s - 1],
            z_recv.at[s - 1],
            spot.ahead(s),
        )
        for s in others
    ]
    kept = [
        pltpu.make_async_copy(by_rank.at[me], weights.at[f, me], local.at[0]),
        pltpu.make_async_copy(rows_in, out_rows.at[f], local.at[1]),
    ]
    for copy in kept:
        copy.start()

    def spread(which, src, buf):
        return [
            send(
                src,
                buf.at[f],
                p_send.at[which, k - 1],
                p_recv.at[which, k - 1],
                spot.on_chip(spot.chip_ahead(k)),
            )
            for k in range(1, chips)
        ] + [send(src, buf.at[f], c_send.at[which, 0], c_recv.at[which, 0], spot.partner())]

    row_copies = spread(1, rows_in, out_rows)
    for copy in kept + z_copies:
        copy.wait()
    weight_copies = spread(0, weights.at[f], weights)
    for k in range(1, chips):
        source = spot.chip_behind(k) * 2 + spot.core
        for which, copies, buf in ((1, row_copies, out_rows), (0, weight_copies, weights)):
            copies[k - 1].wait()
            waits.append(
                send(
                    buf.at[source],
                    buf.at[source],
                    c_send.at[which, k],
                    c_recv.at[which, k],
                    spot.partner(),
                )
            )
    row_copies[-1].wait()
    weight_copies[-1].wait()
    for copy in waits:
        copy.wait()


def gather_weights(by_rank, rows_in, plane_size):
    ranks, rows, columns = by_rank.shape
    chips = plane_size // 2
    dma = pltpu.SemaphoreType.DMA
    return pl.pallas_call(
        functools.partial(gather_weights_kernel, ranks, plane_size),
        in_specs=[VMEM] * 2,
        out_specs=[VMEM] * 2,
        out_shape=[
            shape_of((plane_size, ranks, rows, columns), BF16),
            shape_of((plane_size,) + rows_in.shape, BF16),
        ],
        scratch_shapes=[
            dma((ranks - 1,)),
            dma((ranks - 1,)),
            dma((2, chips - 1)),
            dma((2, chips - 1)),
            dma((2, chips)),
            dma((2, chips)),
            dma((2,)),
        ],
        compiler_params=remote(0),
        name="gather_weights",
    )(by_rank, rows_in)


def scatter_start(spot, refs, buf, send_sem, recv_sem):
    return [
        send(refs[s], buf.at[s - 1], send_sem.at[s - 1], recv_sem.at[s - 1], spot.behind(s))
        for s in range(1, spot.ranks)
    ]


def middle_kernel(ranks, plane_size, x, gain, *refs):
    sums = refs[:ranks]
    h, a2, gathered, other = refs[ranks : ranks + 4]
    got, r_send, r_recv, g_send, g_recv, c_send, c_recv = refs[ranks + 4 :]
    spot = Spot(ranks, plane_size)
    meet([spot.ahead(s) for s in range(1, ranks)] + [spot.partner()])
    copies = scatter_start(spot, sums, got, r_send, r_recv)
    total = x[...] + sums[0][...]
    for s in range(1, ranks):
        copies[s - 1].wait()
        total = total + got[s - 1].astype(F32)
    scale = lax.rsqrt(jnp.mean(total * total, axis=-1, keepdims=True) + EPSILON)
    low = (total * scale * gain[...]).astype(BF16)
    gathered[0] = low
    a2[...] = low
    h[...] = total
    copies = [
        send(
            gathered.at[0], gathered.at[s], g_send.at[s - 1], g_recv.at[s - 1], spot.ahead(s)
        )
        for s in range(1, ranks)
    ]
    across = [
        send(gathered.at[0], other.at[0], c_send.at[0], c_recv.at[0], spot.partner())
    ]
    for s in range(1, ranks):
        copies[s - 1].wait()
        across.append(
            send(gathered.at[s], other.at[s], c_send.at[s], c_recv.at[s], spot.partner())
        )
    for copy in across:
        copy.wait()


def middle(x, gain, sums, plane_size):
    ranks = len(sums)
    dma = pltpu.SemaphoreType.DMA
    stack = shape_of((ranks,) + x.shape, BF16)
    return pl.pallas_call(
        functools.partial(middle_kernel, ranks, plane_size),
        in_specs=[VMEM] * (2 + ranks),
        out_specs=[VMEM] * 4,
        out_shape=[shape_of(x.shape, F32), shape_of(x.shape, BF16), stack, stack],
        scratch_shapes=[
            pltpu.VMEM((ranks - 1,) + x.shape, BF16),
            dma((ranks - 1,)),
            dma((ranks - 1,)),
            dma((ranks - 1,)),
            dma((ranks - 1,)),
            dma((ranks,)),
            dma((ranks,)),
        ],
        compiler_params=remote(1),
        name="middle",
    )(x, gain, *sums)


def rejoin_kernel(ranks, plane_size, gain_row, gates, h, dz, router_t, a2, *refs):
    parts = refs[:ranks]
    dh, gathered, extra, g_send, g_recv = refs[ranks:]
    model = h.shape[1]
    spot = Spot(ranks, plane_size)
    meet([spot.ahead(s) for s in range(1, ranks)])
    total = parts[0][...]
    for i in range(1, ranks):
        total = total + parts[i][...].astype(F32)
    tail = total[:, model:]
    dgates = tail + pltpu.roll(tail, LANES // 2, 1)
    gate = gates[...]
    mean = jnp.sum(gate * dgates, axis=1, keepdims=True)
    d_logits = (gate * (dgates - mean)).astype(BF16)
    da2 = total[:, :model] + dot(d_logits, router_t[...])
    value = h[...]
    scale = lax.rsqrt(jnp.mean(value * value, axis=-1, keepdims=True) + EPSILON)
    normed = value * scale
    gain = router_t[gain_row : gain_row + 1, :].astype(F32)
    weighted = da2 * gain
    grad = dz[...] + scale * (
        weighted - normed * jnp.mean(weighted * normed, axis=-1, keepdims=True)
    )
    gathered[0] = grad.astype(BF16)
    dh[...] = grad
    copies = [
        send(
            gathered.at[0], gathered.at[s], g_send.at[s - 1], g_recv.at[s - 1], spot.ahead(s)
        )
        for s in range(1, ranks)
    ]
    gain_grad = jnp.sum(da2 * normed, axis=0, keepdims=True)
    line = lax.broadcasted_iota(jnp.int32, (LANES, model), 0)
    extra[...] = jnp.where(line == gain_row, gain_grad, dot_tn(d_logits, a2[...]))
    for copy in copies:
        copy.wait()


def rejoin(parts, gates, h, dz, router_t, a2, gain_row, plane_size):
    ranks = len(parts)
    dma = pltpu.SemaphoreType.DMA
    return pl.pallas_call(
        functools.partial(rejoin_kernel, ranks, plane_size, gain_row),
        in_specs=[VMEM] * (5 + ranks),
        out_specs=[VMEM] * 3,
        out_shape=[
            shape_of(h.shape, F32),
            shape_of((ranks,) + h.shape, BF16),
            shape_of((LANES, h.shape[1]), F32),
        ],
        scratch_shapes=[dma((ranks - 1,)), dma((ranks - 1,))],
        compiler_params=remote(2),
        name="rejoin",
    )(gates, h, dz, router_t, a2, *parts)


def last_kernel(ranks, plane_size, x, dh, gain, d_weights, d_rows, *refs):
    sums = refs[:ranks]
    out, columns_out, rows_out = refs[ranks : ranks + 3]
    (got, core_w, core_r, sum_w, sum_r, chip_w, chip_r, final) = refs[ranks + 3 : ranks + 11]
    r_send, r_recv, c_send, c_recv, p_send, p_recv, z_send, z_recv, local = refs[ranks + 11 :]
    spot = Spot(ranks, plane_size)
    chips, core, me = spot.chips, spot.core, spot.rank
    meet(
        [spot.ahead(s) for s in range(1, ranks)]
        + [spot.on_chip(spot.chip_ahead(k)) for k in range(1, chips)]
        + [spot.partner()]
    )
    z_copies = scatter_start(spot, sums, got, r_send, r_recv)
    pairs = ((0, d_weights, core_w, sum_w, chip_w), (1, d_rows, core_r, sum_r, chip_r))
    across = {}
    for k in range(chips):
        at = spot.chip_ahead(k)
        for which, src, buf, _, _ in pairs:
            across[k, which] = send(
                src.at[at, 1 - core],
                buf.at[k],
                c_send.at[which, k],
                c_recv.at[which, k],
                spot.partner(),
            )
    for k in list(range(1, chips)) + [0]:
        at = spot.chip_ahead(k)
        for which, src, buf, total, _ in pairs:
            across[k, which].wait()
            total[k] = (src[at, core].astype(F32) + buf[k].astype(F32)).astype(BF16)
    hops = {}
    for k in range(1, chips):
        for which, _, _, total, buf in pairs:
            hops[k, which] = send(
                total.at[k],
                buf.at[k - 1],
                p_send.at[which, k - 1],
                p_recv.at[which, k - 1],
                spot.on_chip(spot.chip_ahead(k)),
            )
    value = x[...]
    scale = lax.rsqrt(jnp.mean(value * value, axis=-1, keepdims=True) + EPSILON)
    normed = value * scale
    total = sums[0][...]
    for s in range(1, ranks):
        z_copies[s - 1].wait()
        total = total + got[s - 1].astype(F32)
    weighted = total * gain[...]
    grad = scale * (weighted - normed * jnp.mean(weighted * normed, axis=-1, keepdims=True))
    for k in range(1, chips):
        for which in range(2):
            hops[k, which].wait()
    value = sum_w[0].astype(F32)
    for k in range(1, chips):
        value = value + chip_w[k - 1].astype(F32)
    final[...] = value.astype(BF16)
    out[...] = dh[...] + grad
    value = sum_r[0].astype(F32)
    for k in range(1, chips):
        value = value + chip_r[k - 1].astype(F32)
    rows_out[...] = value
    kept = pltpu.make_async_copy(final.at[me], columns_out.at[me], local.at[0])
    kept.start()
    copies = [
        send(
            final.at[lax.rem(me + s, ranks)],
            columns_out.at[me],
            z_send.at[s - 1],
            z_recv.at[s - 1],
            spot.ahead(s),
        )
        for s in range(1, ranks)
    ]
    for copy in copies:
        copy.wait()
    kept.wait()


def last(x, dh, gain, d_weights, d_rows, sums):
    ranks = len(sums)
    chips, _, _, rows, columns = d_weights.shape
    dma = pltpu.SemaphoreType.DMA
    w_shape, r_shape = d_weights.shape[2:], d_rows.shape[2:]
    return pl.pallas_call(
        functools.partial(last_kernel, ranks, 2 * chips),
        in_specs=[VMEM] * (5 + ranks),
        out_specs=[VMEM] * 3,
        out_shape=[shape_of(x.shape, F32), shape_of(w_shape, BF16), shape_of(r_shape, F32)],
        scratch_shapes=[
            pltpu.VMEM((ranks - 1,) + x.shape, BF16),
            pltpu.VMEM((chips,) + w_shape, BF16),
            pltpu.VMEM((chips,) + r_shape, BF16),
            pltpu.VMEM((chips,) + w_shape, BF16),
            pltpu.VMEM((chips,) + r_shape, BF16),
            pltpu.VMEM((chips - 1,) + w_shape, BF16),
            pltpu.VMEM((chips - 1,) + r_shape, BF16),
            pltpu.VMEM(w_shape, BF16),
            dma((ranks - 1,)),
            dma((ranks - 1,)),
            dma((2, chips)),
            dma((2, chips)),
            dma((2, chips - 1)),
            dma((2, chips - 1)),
            dma((ranks - 1,)),
            dma((ranks - 1,)),
            dma((1,)),
        ],
        compiler_params=remote(3),
        name="last",
    )(x, dh, gain, d_weights, d_rows, *sums)


def piece_ids(position_index, starts):
    inside = (position_index[:, None] >= starts[None, :]) & (
        position_index[:, None] < starts[None, :] + PIECE
    )
    labels = jnp.arange(1, starts.shape[0] + 1, dtype=jnp.int32)[None, :]
    return jnp.sum(jnp.where(inside, labels, 0), axis=1, dtype=jnp.int32)


def on_device(
    inputs,
    cotangent,
    norm1_gain,
    w_query,
    key_projection,
    value_projection,
    w_output,
    norm2_gain,
    w_router,
    w_gate,
    w_up,
    w_down,
    routes,
    piece_starts,
):
    plane = Plane()
    ranks = lax.axis_size("expert")
    me = lax.axis_index("expert")
    rows, model = inputs.shape
    seq = rows * ranks
    weight_rows = w_query.shape[0]
    n_experts = w_router.shape[1]
    ff = w_gate.shape[2]
    kv_heads = KEY_VALUE_HEADS // ranks
    q_cols, kv_cols = kv_heads * GROUP * HEAD_WIDTH, kv_heads * HEAD_WIDTH
    rope_width = q_cols + kv_cols
    value_width = -(-kv_cols // LANES) * LANES
    columns = rope_width + value_width + LANES
    gain_one_row, gain_two_row = n_experts, n_experts + 1

    scale_one = lax.rsqrt(jnp.mean(inputs * inputs, axis=-1, keepdims=True) + EPSILON)
    x_blocks = expert_gather((inputs * scale_one).astype(BF16))

    extra_cols = jnp.concatenate(
        [
            w_router,
            norm1_gain[:, None],
            norm2_gain[:, None],
            jnp.zeros((weight_rows, LANES - n_experts - 2), F32),
        ],
        axis=1,
    )
    by_rank = jnp.concatenate(
        [
            w_query.reshape(weight_rows, ranks, q_cols),
            key_projection.reshape(weight_rows, ranks, kv_cols),
            jnp.pad(
                value_projection.reshape(weight_rows, ranks, kv_cols),
                ((0, 0), (0, 0), (0, value_width - kv_cols)),
            ),
            jnp.broadcast_to(extra_cols[:, None, :], (weight_rows, ranks, LANES)),
        ],
        axis=2,
    ).astype(BF16)
    by_rank = jnp.transpose(by_rank, (1, 0, 2))

    axes = ("fsdp", "expert")
    total = plane.size * ranks
    move = [
        (j, (j % plane.size) * ranks + j // plane.size) for j in range(total)
    ]
    out_shard = lax.ppermute(w_output.astype(BF16), axes, move)

    lane_ids = jnp.arange(LANES, dtype=jnp.int32)
    routed = jnp.sum((routes[:, :, None] == lane_ids[None, None, :]).astype(F32), axis=1)
    grads = jnp.concatenate(
        expert_gather(jnp.concatenate([cotangent, routed], axis=1).astype(BF16)), axis=0
    )

    core = plane.core.astype(jnp.int32)[None]
    keep, send, halves = pack_experts(core, w_gate, w_up, w_down, plane.size)
    got = plane.other_core(send)
    parts = [
        jnp.concatenate([jnp.where(plane.core == part, keep, got), halves[part][None]], axis=0)
        for part in range(2)
    ]
    found = {(0, 0, 0): parts[0], (0, 0, 1): parts[1]}
    found[0, 1, 0] = plane.other_mid(parts[0])
    for s in range(1, plane.rows):
        found[s, 0, 1] = plane.next_row(parts[1], s)
        for mid in range(2):
            found[s, mid, 0] = plane.next_row(found[0, mid, 0], s)
    for s in range(plane.rows):
        found[s, 1, 1] = plane.other_mid(found[s, 0, 1])
    place, pieces = tuple(found.keys()), list(found.values())
    sources = [
        ((plane.row - s) % plane.rows) * 2 + (plane.mid + mid) % 2
        for s in range(plane.rows)
        for mid in range(2)
    ]
    where = jnp.stack([me] + sources).astype(jnp.int32)

    by_rank, parts, out_shard = lax.optimization_barrier((by_rank, parts, out_shard))
    weights, out_weights = gather_weights(by_rank, out_shard, plane.size)
    weights = weights.reshape(model, columns)
    out_weights = out_weights.reshape(q_cols, model)

    block_ids = jnp.arange(seq, dtype=jnp.int32) // rows
    places = ((me - block_ids) % ranks) * rows + jnp.arange(seq, dtype=jnp.int32) % rows
    ids = piece_ids(places, piece_starts[0])
    visible = (places[:, None] <= places[None, :]) | (
        (ids[:, None] == ids[None, :]) & (ids[None, :] > 0)
    )
    bias = jnp.where(visible, 0.0, NEG_FILL).astype(F32)
    half = HEAD_WIDTH // 2
    inverse = 10000.0 ** (-(jnp.arange(half, dtype=F32) * 2.0 / HEAD_WIDTH))
    angles = places.astype(F32)[:, None] * inverse[None, :]
    cosine = jnp.tile(jnp.cos(angles), (1, LANES // half))
    sine = jnp.tile(jnp.sin(angles), (1, LANES // half)) * jnp.where(
        lane_ids % HEAD_WIDTH < half, -1.0, 1.0
    )
    extra_t = weights[:, columns - LANES :].T
    gain_one = extra_t[gain_one_row : gain_one_row + 1].astype(F32)
    gain_two = extra_t[gain_two_row : gain_two_row + 1].astype(F32)
    kept, sums = attend(
        x_blocks, gain_one, weights, out_weights, bias, cosine, sine, kv_heads, rope_width
    )
    grads, sums = lax.optimization_barrier((grads, sums))
    mid_rows, a2, own_a2, other_a2 = middle(inputs, gain_two, sums, plane.size)

    other_grads = plane.other_core(grads)
    other_out, other_dx, _, *other_kept = experts(
        [other_a2.reshape(seq, model)], other_grads, extra_t, where, pieces, place, BF16
    )
    out_all, dx_all, gates, *own_kept = experts(
        [own_a2.reshape(seq, model)], grads, extra_t, where, pieces, place, F32
    )
    dx_all = dx_all + plane.other_core(other_dx).astype(F32)
    dxs = [
        dx_all[b * rows : (b + 1) * rows].astype(F32 if b == 0 else BF16) for b in range(ranks)
    ]
    dx_got = expert_scatter(dxs)
    order = [(s, mid) for s in reversed(range(plane.rows)) for mid in (1, 0)]
    chips = [
        ((plane.row + s) % plane.rows) * 2 + (plane.mid + mid) % 2 for s, mid in order
    ]
    own_kept.insert(2, grads[:, :model])
    other_kept.insert(2, other_grads[:, :model])
    flat = expert_grads(
        jnp.stack(chips).astype(jnp.int32), own_kept, other_kept, plane.size
    )
    dx_got, flat = lax.optimization_barrier((dx_got, flat))
    summed = {
        (s, mid, part): flat[2 * i + part]
        for i, (s, mid) in enumerate(order)
        for part in range(2)
    }

    def add(first, *others):
        value = first.astype(F32)
        for v in others:
            value = value + v.astype(F32)
        return value.astype(BF16)

    steps = range(1, plane.rows)
    a_sums = [
        add(summed[0, mid, 0], *[plane.next_row(summed[s, mid, 0], s) for s in steps])
        for mid in range(2)
    ]
    b_sums = [
        add(summed[s, 0, 1], plane.other_mid(summed[s, 1, 1])) for s in range(plane.rows)
    ]
    a_got = plane.other_mid(a_sums[1])
    b_got = [plane.next_row(b_sums[s], s) for s in steps]
    b_kept = b_sums[0]
    if len(b_got) > 1:
        b_kept = add(b_kept, *b_got[:-1])
    b_got = b_got[-1]
    other = plane.other_core(
        jnp.where(
            plane.core == 0,
            b_kept[:2].astype(F32) + b_got[:2].astype(F32),
            a_sums[0][:2].astype(F32) + a_got[:2].astype(F32),
        ).astype(BF16)
    )
    gate_grad, up_grad, down_grad = finish(
        core, a_sums[0], a_got, b_kept, b_got, other, w_down.shape[1], model, plane.size
    )

    dh, dh_stack, extra = rejoin(
        [dxs[0]] + dx_got, gates, mid_rows, cotangent, extra_t, a2, gain_two_row, plane.size
    )

    d_weights, d_out_weights, da1 = attend_back(
        dh_stack,
        x_blocks,
        weights,
        out_weights,
        kept,
        bias,
        cosine,
        sine,
        extra,
        kv_heads,
        gain_one_row,
    )
    chip_count = plane.size // 2
    input_grad, by_rank, out_part = last(
        inputs,
        dh,
        gain_one,
        d_weights.reshape(chip_count, 2, ranks, weight_rows, columns),
        d_out_weights.reshape(chip_count, 2, weight_rows, model),
        da1,
    )
    out_all = out_all + plane.other_core(other_out).astype(F32)
    outs = [out_all[b * rows : (b + 1) * rows] for b in range(ranks)]
    output = mid_rows + outs[0]
    for v in expert_scatter([v.astype(BF16) for v in outs]):
        output = output + v.astype(F32)

    w_output_grad = lax.ppermute(
        out_part.astype(BF16), axes, [(b, a) for a, b in move]
    ).astype(F32)
    by_rank = by_rank.astype(F32)

    def columns_of(start, width):
        piece = by_rank[:, :, start : start + width]
        return jnp.transpose(piece, (1, 0, 2)).reshape(weight_rows, ranks * width)

    extra_grad = jnp.sum(by_rank[:, :, columns - LANES :], axis=0)
    return (
        output,
        input_grad,
        extra_grad[:, gain_one_row],
        columns_of(0, q_cols),
        columns_of(q_cols, kv_cols),
        columns_of(rope_width, kv_cols),
        w_output_grad,
        extra_grad[:, gain_two_row],
        extra_grad[:, :n_experts],
        gate_grad,
        up_grad,
        down_grad,
    )


def solution(mesh):
    both = ("fsdp", "expert")
    rows, flat, stack = P(both, None), P(both), P("expert", "fsdp", None)
    weights = (flat, rows, rows, rows, rows, flat, rows, stack, stack, stack)
    return jax.shard_map(
        on_device,
        mesh=mesh,
        in_specs=(rows, rows) + weights + (rows, P("fsdp", None)),
        out_specs=(rows, rows) + weights,
        check_vma=False,
    )
```

time: 629 us -> 555 us (0.88)
  waiting for transfers between devices: 329 us -> 85.6 us
  Pallas kernels: 131 us -> 336 us
  starting transfers between devices: 111 us -> 78.7 us
  other arithmetic: 32 us -> 24 us
    pallas_call x9 -> x7, Pallas kernels: 65.3 us -> 257 us  [the longest x1 86.4 us: middle(): pl.pallas_call(functools.partial(middle_kernel, ranks, plane_size), in_sp...]
    ppermute x30 -> x12, waiting for transfers between devices: 180 us -> 22.1 us  [expert_shift(): lax.ppermute(x, 'expert', [(i, (i + step) % count) for i in range(count)])]
    ppermute x14 -> x6, waiting for transfers between devices: 95.4 us -> 41 us  [other_mid(): return lax.ppermute(x, 'fsdp', [(i, i ^ 2) for i in range(self.size)])]
    ppermute x30 -> x12, starting transfers between devices: 64.7 us -> 41.6 us  [expert_shift(): lax.ppermute(x, 'expert', [(i, (i + step) % count) for i in range(count)])]
    ppermute x16 -> x5, starting transfers between devices: 26.6 us -> 7.8 us  [other_core(): return lax.ppermute(x, 'fsdp', [(i, i ^ 1) for i in range(self.size)])]
    ppermute x14 -> x6, waiting for transfers between devices: 33.8 us -> 18.1 us  [next_row(): lax.ppermute(x, 'fsdp', [(i, (i // 4 + step) % self.rows * 4 + i % 4) for...]
    pallas_call x1 -> x2, Pallas kernels: 40.2 us -> 53.5 us  [experts(): pl.pallas_call(functools.partial(experts_kernel, blocks, len(pieces), pla...]
    ppermute x1, starting transfers between devices: 2.22 us -> 14.3 us  [on_device(): out_shard = lax.ppermute(w_output.astype(BF16), axes, move)]
  transfers between devices with their start and end apart: 76 -> 31, of which waited for: 39 -> 7; matrix products, arithmetic and copies ran while one was open for 6% -> 6% of each run, Pallas kernels for 10% -> 55%
where the time goes in v2:
time: 555 us; the launch traced here: 547 us
  Pallas kernels  336 us (61%)
  waiting for transfers between devices  85.6 us (15%)
  starting transfers between devices  78.7 us (14%)
  other arithmetic  24 us (4%)
  local copies, waits for them, and re-layouts  21.4 us (4%)
    pallas_call x1, Pallas kernels, middle(): pl.pallas_call(functools.partial(middle_kernel, ranks, plane_size), in_sp...  86.4 us
    pallas_call x2, Pallas kernels, experts(): pl.pallas_call(functools.partial(experts_kernel, blocks, len(pieces), pla...  53.5 us
    pallas_call x1, Pallas kernels, rejoin(): pl.pallas_call(functools.partial(rejoin_kernel, ranks, plane_size, gain_r...  49.7 us
    pallas_call x1, Pallas kernels, last(): pl.pallas_call(functools.partial(last_kernel, ranks, 2 * chips), in_specs...  49.3 us
    ppermute x12, starting transfers between devices, expert_shift(): lax.ppermute(x, 'expert', [(i, (i + step) % count) for i in range(count)])  41.6 us
    ppermute x6, waiting for transfers between devices, other_mid(): return lax.ppermute(x, 'fsdp', [(i, i ^ 2) for i in range(self.size)])  41 us
    pallas_call x1, Pallas kernels, gather_weights(): pl.pallas_call(functools.partial(gather_weights_kernel, ranks, plane_size...  38.3 us
    ppermute x12, waiting for transfers between devices, expert_shift(): lax.ppermute(x, 'expert', [(i, (i + step) % count) for i in range(count)])  22.1 us
  transfers between devices with their start and end apart: 31, of which 7 were waited for; matrix products, arithmetic and copies ran while one was open for 6% of the time, Pallas kernels for 55%

profile of v2, /device:TPU:27, one launch (start us, length us, event | category | flops | bytes accessed | tf_op | source)
XLA Modules:
  0.0 547.5 jit_solution(788754712746710945)
XLA Ops:
  5.2 6.9 %pack_experts.1 = (bf16[2,5,192,256]{3,2,1,0:T(8,128)(2,1)}, bf16[2,5,192,256]{3,2,1,0:T(8,128)(2,1)}, bf16[2,5,192,256]{3,2,1,0:T(8,128)(2,1)}) custom-call(s32[1]{0:T(128)} %bitcast.3.core, f32[5,192,512]{2,1,0:T(8,128)} %gate.1, f32[5,192,512]{2,1,0:T(8,128)} %up.1, f32[5,64,1536]{2,1,0:T(8,128)} %down.1), custom_call_target="tpu_custom_call" | custom-call | tf_op jit(solution)/shard_map/pack_experts/pallas_call | solution.py:115
  27.1 18.1 %collective-permute-done.3 = bf16[128,1664]{1,0:T(8,128)(2,1)} collective-permute-done((bf16[128,1664]{1,0:T(8,128)(2,1)}, bf16[128,1664]{1,0:T(8,128)(2,1)}, u32[]{:S(2)}, u32[]{:S(2)}) %collective-permute-start.3) | collective-permute-done | bytes 426016 | tf_op jit(solution)/shard_map/ppermute | solution.py:73
  45.3 14.3 %collective-permute-start.1 = (bf16[48,1536]{1,0:T(8,128)(2,1)S(1)}, bf16[48,1536]{1,0:T(8,128)(2,1)S(1)}, u32[]{:S(2)}, u32[]{:S(2)}) collective-permute-start(bf16[48,1536]{1,0:T(8,128)(2,1)S(1)} %convert_element_type.105), channel_id=1, source_target_pairs={{0,0},{1,4},{2,8},{3,12},{4,16},{5,20},{6,24},{7,28},{8,1},{9,5},{... | collective-permute-start | bytes 442376 | tf_op jit(solution)/shard_map/ppermute | solution.py:981
  62.9 11.0 %collective-permute-start.7 = (bf16[128,1536]{1,0:T(8,128)(2,1)}, bf16[128,1536]{1,0:T(8,128)(2,1)}, u32[]{:S(2)}, u32[]{:S(2)}) collective-permute-start(bf16[128,1536]{1,0:T(8,128)(2,1)} %multiply_convert_fusion.refs_0_.refs_1_), channel_id=1, source_target_pairs={{0,3},{1,0},{2,1},{3,2},{4,7},{5,4},{6,5},{7,6},{8,11},{9,8},{10,9... | collective-permute-start | bytes 1179656 | tf_op jit(solution)/shard_map/ppermute | solution.py:73
  73.8 38.3 %gather_weights.1 = (bf16[8,4,48,768]{3,2,1,0:T(8,128)(2,1)}, bf16[8,48,1536]{2,1,0:T(8,128)(2,1)}) custom-call(bf16[4,48,768]{2,1,0:T(8,128)(2,1)} %maximum_bitcast_fusion.by_rank, bf16[48,1536]{1,0:T(8,128)(2,1)} %copy-done.22), custom_call_target="tpu_custom_call" | custom-call | tf_op jit(solution)/shard_map/gather_weights/pallas_call | solution.py:657
  117.3 10.2 %attend.1 = (bf16[512,1536]{1,0:T(8,128)(2,1)}, bf16[512,512]{1,0:T(8,128)(2,1)}, bf16[512,128]{1,0:T(8,128)(2,1)}, bf16[512,384]{1,0:T(8,128)(2,1)}, f32[6,512]...) custom-call(bf16[128,1536]{1,0:T(8,128)(2,1)} %multiply_convert_fusi, ...), custom_call_target="tpu_custom_call" | custom-call | tf_op jit(solution)/shard_map/attend/pallas_call | solution.py:194
  131.3 86.4 %middle.1 = (f32[128,1536]{1,0:T(8,128)}, bf16[128,1536]{1,0:T(8,128)(2,1)}, bf16[4,128,1536]{2,1,0:T(8,128)(2,1)}, bf16[4,128,1536]{2,1,0:T(8,128)(2,1)}) custom-call(f32[128,1536]{1,0:T(8,128)} %x.3, f32[1,1536]{1,0:T(1,128)} %get-tuple-element.214.gain, f32[128,1536]{1,0:T(8,128)} %get-tuple-element.96.refs_0_, ...), custom_call_target="tpu_custom_call" | custom-call | tf_op jit(solution)/shard_map/middle/pallas_call | solution.py:724
  217.7 26.1 %experts.3 = (bf16[512,1536]{1,0:T(8,128)(2,1)}, bf16[512,1664]{1,0:T(8,128)(2,1)}, f32[128,128]{1,0:T(8,128)}, bf16[1536,512]{1,0:T(8,128)(2,1)}, bf16[5,256,51...) custom-call(bf16[512,1536]{1,0:T(8,128)(2,1)} %bitcast.66, ...), custom_call_target="tpu_custom_call" | custom-call | tf_op jit(solution)/shard_map/experts/pallas_call | solution.py:335
  244.1 27.4 %experts.2 = (f32[512,1536]{1,0:T(8,128)}, f32[512,1664]{1,0:T(8,128)}, f32[128,128]{1,0:T(8,128)}, bf16[1536,512]{1,0:T(8,128)(2,1)}, bf16[5,256,512]{2,1,0:T(8...) custom-call(bf16[512,1536]{1,0:T(8,128)(2,1)} %bitcast.65, bf16[512,1664]{1,0:T(8,128)(2,1)} %copy-done, ...), custom_call_target="tpu_custom_call" | custom-call | tf_op jit(solution)/shard_map/experts/pallas_call | solution.py:335
  271.5 4.1 fusion.16
  276.7 3.3 collective-permute-start.22
  284.5 18.6 %expert_grads.1 = (bf16[3,5,192,256]{3,2,1,0:T(8,128)(2,1)}, bf16[3,5,192,256]{3,2,1,0:T(8,128)(2,1)}, bf16[3,5,192,256]{3,2,1,0:T(8,128)(2,1)}, bf16[3,5,192,25...) custom-call(s32[4]{0:T(128)} %pad_add_fusion.where_ref, ...), custom_call_target="tpu_custom_call" | custom-call | tf_op jit(solution)/shard_map/expert_grads/pallas_call | solution.py:399
  303.2 4.0 collective-permute-done.21.refs_2_
  312.8 26.4 %collective-permute-done.28 = bf16[3,5,192,256]{3,2,1,0:T(8,128)(2,1)S(1)} collective-permute-done((bf16[3,5,192,256]{3,2,1,0:T(8,128)(2,1)}, bf16[3,5,192,256]{3,2,1,0:T(8,128)(2,1)S(1)}, u32[]{:S(2)}, u32[]{:S(2)}) %collective-permute-start.28) | collective-permute-done | bytes 1474592 | tf_op jit(solution)/shard_map/ppermute | solution.py:63
  343.9 10.2 %collective-permute-start.16 = (bf16[128,1536]{1,0:T(8,128)(2,1)S(1)}, bf16[128,1536]{1,0:T(8,128)(2,1)S(1)}, u32[]{:S(2)}, u32[]{:S(2)}) collective-permute-start(bf16[128,1536]{1,0:T(8,128)(2,1)S(1)} %get-tuple-element.205), channel_id=1, source_target_pairs={{0,3},{1,0},{2,1},{3,2},{4,7},{5,4},{6,5},{7,6},{8,11},{9,8},{10,9... | collective-permute-start | bytes 1179656 | tf_op jit(solution)/shard_map/ppermute | solution.py:73
  356.2 14.6 %collective-permute-done.27 = bf16[3,5,192,256]{3,2,1,0:T(8,128)(2,1)S(1)} collective-permute-done((bf16[3,5,192,256]{3,2,1,0:T(8,128)(2,1)}, bf16[3,5,192,256]{3,2,1,0:T(8,128)(2,1)S(1)}, u32[]{:S(2)}, u32[]{:S(2)}) %collective-permute-start.27) | collective-permute-done | bytes 1474592 | tf_op jit(solution)/shard_map/ppermute | solution.py:63
  370.8 9.3 %collective-permute-start.17 = (bf16[128,1536]{1,0:T(8,128)(2,1)S(1)}, bf16[128,1536]{1,0:T(8,128)(2,1)S(1)}, u32[]{:S(2)}, u32[]{:S(2)}) collective-permute-start(bf16[128,1536]{1,0:T(8,128)(2,1)S(1)} %get-tuple-element.207), channel_id=1, source_target_pairs={{0,2},{1,3},{2,0},{3,1},{4,6},{5,7},{6,4},{7,5},{8,10},{9,11},{10,... | collective-permute-start | bytes 1179656 | tf_op jit(solution)/shard_map/ppermute | solution.py:73
  380.6 3.3 collective-permute-start.18
  384.3 18.1 %collective-permute-done.29.got_b = bf16[3,5,192,256]{3,2,1,0:T(8,128)(2,1)S(1)} collective-permute-done((bf16[3,5,192,256]{3,2,1,0:T(8,128)(2,1)S(1)}, bf16[3,5,192,256]{3,2,1,0:T(8,128)(2,1)S(1)}, u32[]{:S(2)}, u32[]{:S(2)}) %collective-permute-start.29) | collective-permute-done | bytes 1474592 | tf_op jit(solution)/shard_map/ppermute | solution.py:66
  408.4 49.7 %rejoin.1 = (f32[128,1536]{1,0:T(8,128)}, bf16[4,128,1536]{2,1,0:T(8,128)(2,1)}, f32[128,1536]{1,0:T(8,128)}) custom-call(f32[128,128]{1,0:T(8,128)} %get-tuple-element.106.gates, f32[128,1536]{1,0:T(8,128)} %get-tuple-element.100.h, f32[128,1536]{1,0:T(8,128)} %dz.1, bf16[128,1536]{1,0:T(8,128)(2,1)} %bitcast.61, bf16[128,1536]{1,0:T(8,128)(2,1)} %get-tuple-element.107.a2, ...), custom_call_target="tpu_custom_call" | custom-call | tf_op jit(solution)/shard_map/rejoin/pallas_call | solution.py:784
  458.1 15.3 %attend_back.1 = (bf16[1536,768]{1,0:T(8,128)(2,1)}, bf16[384,1536]{1,0:T(8,128)(2,1)}, f32[128,1536]{1,0:T(8,128)}, bf16[128,1536]{1,0:T(8,128)(2,1)}, bf16[128...) custom-call(bf16[4,128,1536]{2,1,0:T(8,128)(2,1)} %get-tuple-element.130.refs_0_, ...), custom_call_target="tpu_custom_call" | custom-call | tf_op jit(solution)/shard_map/attend_back/pallas_call | solution.py:521
  473.4 49.3 %last.1 = (f32[128,1536]{1,0:T(8,128)}, bf16[4,48,768]{2,1,0:T(8,128)(2,1)}, f32[48,1536]{1,0:T(8,128)}) custom-call(f32[128,1536]{1,0:T(8,128)} %x.3, f32[128,1536]{1,0:T(8,128)} %get-tuple-element.129.dh, f32[1,1536]{1,0:T(1,128)} %get-tuple-element.213.refs_4_.gain, bf16[4,2,4,48,768]{4,3,2,1,0:T(8,128)(2,1)} %bitcast.64, ...), custom_call_target="tpu_custom_call" | custom-call | tf_op jit(solution)/shard_map/last/pallas_call | solution.py:882
  524.7 5.8 %collective-permute-start.23 = (bf16[48,1536]{1,0:T(8,128)(2,1)S(1)}, bf16[48,1536]{1,0:T(8,128)(2,1)S(1)}, u32[]{:S(2)}, u32[]{:S(2)}) collective-permute-start(bf16[48,1536]{1,0:T(8,128)(2,1)S(1)} %convert_element_type.117), channel_id=1, source_target_pairs={{0,0},{4,1},{8,2},{12,3},{16,4},{20,5},{24,6},{28,7},{1,8},{5,9},{... | collective-permute-start | bytes 442376 | tf_op jit(solution)/shard_map/ppermute | solution.py:1131
  538.2 7.9 %finish.1 = (f32[5,192,512]{2,1,0:T(8,128)}, f32[5,192,512]{2,1,0:T(8,128)}, f32[5,64,1536]{2,1,0:T(8,128)}) custom-call(s32[1]{0:T(128)} %bitcast.3.core, bf16[3,5,192,256]{3,2,1,0:T(8,128)(2,1)} %copy-done.5, bf16[3,5,192,256]{3,2,1,0:T(8,128)(2,1)} %copy-done.7, bf16[3,5,192,256]{3,2,1,0:T(8,128)(2,1)} %copy-done.4, bf16[3,5,192,256]{3,2,1,0:T(8,128)(2,1)} %copy-done.6, ...), custom_call_target="tpu_custom_call" | custom-call | tf_op jit(solution)/shard_map/finish/pallas_call | solution.py:441
  (177 shorter events, 67.3 us)
Async XLA Ops:
  3.7 41.6 %collective-permute-start.3 = (bf16[128,1664]{1,0:T(8,128)(2,1)}, bf16[128,1664]{1,0:T(8,128)(2,1)}, u32[]{:S(2)}, u32[]{:S(2)}) collective-permute-start(bf16[128,1664]{1,0:T(8,128)(2,1)} %pad_maximum_fusion.3), channel_id=1, source_target_pairs={{0,2},{1,3},{2,0},{3,1},{4,6},{5,7},{6,4},{7,5},{8,10},{9,11},{10,... | collective-permute-start | bytes 1277960 | tf_op jit(solution)/shard_map/ppermute | solution.py:73
  5.0 40.2 %collective-permute-start.4 = (bf16[128,1664]{1,0:T(8,128)(2,1)}, bf16[128,1664]{1,0:T(8,128)(2,1)}, u32[]{:S(2)}, u32[]{:S(2)}) collective-permute-start(bf16[128,1664]{1,0:T(8,128)(2,1)} %pad_maximum_fusion.3), channel_id=1, source_target_pairs={{0,3},{1,0},{2,1},{3,2},{4,7},{5,4},{6,5},{7,6},{8,11},{9,8},{10,9... | collective-permute-start | bytes 1277960 | tf_op jit(solution)/shard_map/ppermute | solution.py:73
  18.7 110.1 %collective-permute-start.9 = (bf16[3,5,192,256]{3,2,1,0:T(8,128)(2,1)S(1)}, bf16[3,5,192,256]{3,2,1,0:T(8,128)(2,1)}, u32[]{:S(2)}, u32[]{:S(2)}) collective-permute-start(bf16[3,5,192,256]{3,2,1,0:T(8,128)(2,1)S(1)} %pad_maximum_fusion.2.refs_5_), channel_id=1, source_target_pairs={{0,16},{4,20},{8,24},{12,28},{16,0},{20,4},{24,8},{28,12},{1,17},{... | collective-permute-start | bytes 4423688 | tf_op jit(solution)/shard_map/ppermute | solution.py:66
  21.3 109.0 %collective-permute-start.8 = (bf16[3,5,192,256]{3,2,1,0:T(8,128)(2,1)}, bf16[3,5,192,256]{3,2,1,0:T(8,128)(2,1)}, u32[]{:S(2)}, u32[]{:S(2)}) collective-permute-start(bf16[3,5,192,256]{3,2,1,0:T(8,128)(2,1)} %pad_maximum_fusion.1.refs_4_), channel_id=1, source_target_pairs={{0,8},{4,12},{8,0},{12,4},{16,24},{20,28},{24,16},{28,20},{1,9},{5... | collective-permute-start | bytes 4423688 | tf_op jit(solution)/shard_map/ppermute | solution.py:63
  24.0 93.3 %collective-permute-start.5 = (bf16[128,1536]{1,0:T(8,128)(2,1)}, bf16[128,1536]{1,0:T(8,128)(2,1)}, u32[]{:S(2)}, u32[]{:S(2)}) collective-permute-start(bf16[128,1536]{1,0:T(8,128)(2,1)} %multiply_convert_fusion.refs_0_.refs_1_), channel_id=1, source_target_pairs={{0,1},{1,2},{2,3},{3,0},{4,5},{5,6},{6,7},{7,4},{8,9},{9,10},{10,1... | collective-permute-start | bytes 1179656 | tf_op jit(solution)/shard_map/ppermute | solution.py:73
  45.3 72.0 %collective-permute-start.6 = (bf16[128,1536]{1,0:T(8,128)(2,1)}, bf16[128,1536]{1,0:T(8,128)(2,1)}, u32[]{:S(2)}, u32[]{:S(2)}) collective-permute-start(bf16[128,1536]{1,0:T(8,128)(2,1)} %multiply_convert_fusion.refs_0_.refs_1_), channel_id=1, source_target_pairs={{0,2},{1,3},{2,0},{3,1},{4,6},{5,7},{6,4},{7,5},{8,10},{9,11},{10,... | collective-permute-start | bytes 1179656 | tf_op jit(solution)/shard_map/ppermute | solution.py:73
  62.9 54.4 %collective-permute-start.7 = (bf16[128,1536]{1,0:T(8,128)(2,1)}, bf16[128,1536]{1,0:T(8,128)(2,1)}, u32[]{:S(2)}, u32[]{:S(2)}) collective-permute-start(bf16[128,1536]{1,0:T(8,128)(2,1)} %multiply_convert_fusion.refs_0_.refs_1_), channel_id=1, source_target_pairs={{0,3},{1,0},{2,1},{3,2},{4,7},{5,4},{6,5},{7,6},{8,11},{9,8},{10,9... | collective-permute-start | bytes 1179656 | tf_op jit(solution)/shard_map/ppermute | solution.py:73
  127.5 90.2 %collective-permute-start.14 = (bf16[512,1664]{1,0:T(8,128)(2,1)S(1)}, bf16[512,1664]{1,0:T(8,128)(2,1)}, u32[]{:S(2)}, u32[]{:S(2)}) collective-permute-start(bf16[512,1664]{1,0:T(8,128)(2,1)S(1)} %pad_maximum_fusion.refs_1_), channel_id=1, source_target_pairs={{0,4},{4,0},{8,12},{12,8},{16,20},{20,16},{24,28},{28,24},{1,5},{5... | collective-permute-start | bytes 5111816 | tf_op jit(solution)/shard_map/ppermute | solution.py:60
  127.7 90.0 %collective-permute-start.12 = (bf16[3,5,192,256]{3,2,1,0:T(8,128)(2,1)S(1)}, bf16[3,5,192,256]{3,2,1,0:T(8,128)(2,1)}, u32[]{:S(2)}, u32[]{:S(2)}) collective-permute-start(bf16[3,5,192,256]{3,2,1,0:T(8,128)(2,1)S(1)} %pad_maximum_fusion.2.refs_5_), channel_id=1, source_target_pairs={{0,8},{4,12},{8,0},{12,4},{16,24},{20,28},{24,16},{28,20},{1,9},{5... | collective-permute-start | bytes 4423688 | tf_op jit(solution)/shard_map/ppermute | solution.py:63
  127.7 90.0 %collective-permute-start.10 = (bf16[3,5,192,256]{3,2,1,0:T(8,128)(2,1)}, bf16[3,5,192,256]{3,2,1,0:T(8,128)(2,1)}, u32[]{:S(2)}, u32[]{:S(2)}) collective-permute-start(bf16[3,5,192,256]{3,2,1,0:T(8,128)(2,1)} %pad_maximum_fusion.1.refs_4_), channel_id=1, source_target_pairs={{0,16},{4,20},{8,24},{12,28},{16,0},{20,4},{24,8},{28,12},{1,17},{... | collective-permute-start | bytes 4423688 | tf_op jit(solution)/shard_map/ppermute | solution.py:66
  128.8 88.9 %collective-permute-start.13 = (bf16[3,5,192,256]{3,2,1,0:T(8,128)(2,1)}, bf16[3,5,192,256]{3,2,1,0:T(8,128)(2,1)}, u32[]{:S(2)}, u32[]{:S(2)}) collective-permute-start(bf16[3,5,192,256]{3,2,1,0:T(8,128)(2,1)} %collective-permute-done.9.refs_7_), channel_id=1, source_target_pairs={{0,8},{4,12},{8,0},{12,4},{16,24},{20,28},{24,16},{28,20},{1,9},{5... | collective-permute-start | bytes 4423688 | tf_op jit(solution)/shard_map/ppermute | solution.py:63
  130.3 87.4 %collective-permute-start.11 = (bf16[3,5,192,256]{3,2,1,0:T(8,128)(2,1)}, bf16[3,5,192,256]{3,2,1,0:T(8,128)(2,1)}, u32[]{:S(2)}, u32[]{:S(2)}) collective-permute-start(bf16[3,5,192,256]{3,2,1,0:T(8,128)(2,1)} %collective-permute-done.8.refs_6_), channel_id=1, source_target_pairs={{0,16},{4,20},{8,24},{12,28},{16,0},{20,4},{24,8},{28,12},{1,17},{... | collective-permute-start | bytes 4423688 | tf_op jit(solution)/shard_map/ppermute | solution.py:66
  276.7 30.4 %collective-permute-start.21 = (bf16[128,1664]{1,0:T(8,128)(2,1)}, bf16[128,1664]{1,0:T(8,128)(2,1)S(1)}, u32[]{:S(2)}, u32[]{:S(2)}) collective-permute-start(bf16[128,1664]{1,0:T(8,128)(2,1)} %get-tuple-element.203), channel_id=1, source_target_pairs={{0,2},{1,3},{2,0},{3,1},{4,6},{5,7},{6,4},{7,5},{8,10},{9,11},{10,... | collective-permute-start | bytes 1277960 | tf_op jit(solution)/shard_map/ppermute | solution.py:73
  276.7 30.4 %collective-permute-start.22 = (bf16[128,1664]{1,0:T(8,128)(2,1)}, bf16[128,1664]{1,0:T(8,128)(2,1)S(1)}, u32[]{:S(2)}, u32[]{:S(2)}) collective-permute-start(bf16[128,1664]{1,0:T(8,128)(2,1)} %get-tuple-element.202), channel_id=1, source_target_pairs={{0,1},{1,2},{2,3},{3,0},{4,5},{5,6},{6,7},{7,4},{8,9},{9,10},{10,1... | collective-permute-start | bytes 1277960 | tf_op jit(solution)/shard_map/ppermute | solution.py:73
  307.1 32.1 %collective-permute-start.28 = (bf16[3,5,192,256]{3,2,1,0:T(8,128)(2,1)}, bf16[3,5,192,256]{3,2,1,0:T(8,128)(2,1)S(1)}, u32[]{:S(2)}, u32[]{:S(2)}) collective-permute-start(bf16[3,5,192,256]{3,2,1,0:T(8,128)(2,1)} %get-tuple-element.154), channel_id=1, source_target_pairs={{0,8},{4,12},{8,0},{12,4},{16,24},{20,28},{24,16},{28,20},{1,9},{5... | collective-permute-start | bytes 4423688 | tf_op jit(solution)/shard_map/ppermute | solution.py:63
  307.5 34.8 %collective-permute-start.25 = (bf16[3,5,192,256]{3,2,1,0:T(8,128)(2,1)}, bf16[3,5,192,256]{3,2,1,0:T(8,128)(2,1)S(1)}, u32[]{:S(2)}, u32[]{:S(2)}) collective-permute-start(bf16[3,5,192,256]{3,2,1,0:T(8,128)(2,1)} %get-tuple-element.150), channel_id=1, source_target_pairs={{0,16},{4,20},{8,24},{12,28},{16,0},{20,4},{24,8},{28,12},{1,17},{... | collective-permute-start | bytes 4423688 | tf_op jit(solution)/shard_map/ppermute | solution.py:66
  308.8 34.4 %collective-permute-start.15 = (bf16[512,1536]{1,0:T(8,128)(2,1)S(1)}, bf16[512,1536]{1,0:T(8,128)(2,1)S(1)}, u32[]{:S(2)}, u32[]{:S(2)}) collective-permute-start(bf16[512,1536]{1,0:T(8,128)(2,1)S(1)} %copy-done.29), channel_id=1, source_target_pairs={{0,4},{4,0},{8,12},{12,8},{16,20},{20,16},{24,28},{28,24},{1,5},{5... | collective-permute-start | bytes 4718600 | tf_op jit(solution)/shard_map/ppermute | solution.py:60
  311.4 59.4 %collective-permute-start.27 = (bf16[3,5,192,256]{3,2,1,0:T(8,128)(2,1)}, bf16[3,5,192,256]{3,2,1,0:T(8,128)(2,1)S(1)}, u32[]{:S(2)}, u32[]{:S(2)}) collective-permute-start(bf16[3,5,192,256]{3,2,1,0:T(8,128)(2,1)} %get-tuple-element.152), channel_id=1, source_target_pairs={{0,8},{4,12},{8,0},{12,4},{16,24},{20,28},{24,16},{28,20},{1,9},{5... | collective-permute-start | bytes 4423688 | tf_op jit(solution)/shard_map/ppermute | solution.py:63
  312.5 68.0 %collective-permute-start.24 = (bf16[3,5,192,256]{3,2,1,0:T(8,128)(2,1)}, bf16[3,5,192,256]{3,2,1,0:T(8,128)(2,1)S(1)}, u32[]{:S(2)}, u32[]{:S(2)}) collective-permute-start(bf16[3,5,192,256]{3,2,1,0:T(8,128)(2,1)} %get-tuple-element.148), channel_id=1, source_target_pairs={{0,16},{4,20},{8,24},{12,28},{16,0},{20,4},{24,8},{28,12},{1,17},{... | collective-permute-start | bytes 4423688 | tf_op jit(solution)/shard_map/ppermute | solution.py:66
  341.0 61.4 %collective-permute-start.29 = (bf16[3,5,192,256]{3,2,1,0:T(8,128)(2,1)S(1)}, bf16[3,5,192,256]{3,2,1,0:T(8,128)(2,1)S(1)}, u32[]{:S(2)}, u32[]{:S(2)}) collective-permute-start(bf16[3,5,192,256]{3,2,1,0:T(8,128)(2,1)S(1)} %add_convert_fusion), channel_id=1, source_target_pairs={{0,16},{4,20},{8,24},{12,28},{16,0},{20,4},{24,8},{28,12},{1,17},{... | collective-permute-start | bytes 4423688 | tf_op jit(solution)/shard_map/ppermute | solution.py:66
  342.8 59.7 %collective-permute-start.26 = (bf16[3,5,192,256]{3,2,1,0:T(8,128)(2,1)S(1)}, bf16[3,5,192,256]{3,2,1,0:T(8,128)(2,1)S(1)}, u32[]{:S(2)}, u32[]{:S(2)}) collective-permute-start(bf16[3,5,192,256]{3,2,1,0:T(8,128)(2,1)S(1)} %add_convert_fusion.2), channel_id=1, source_target_pairs={{0,8},{4,12},{8,0},{12,4},{16,24},{20,28},{24,16},{28,20},{1,9},{5... | collective-permute-start | bytes 4423688 | tf_op jit(solution)/shard_map/ppermute | solution.py:63
  343.9 63.4 %collective-permute-start.16 = (bf16[128,1536]{1,0:T(8,128)(2,1)S(1)}, bf16[128,1536]{1,0:T(8,128)(2,1)S(1)}, u32[]{:S(2)}, u32[]{:S(2)}) collective-permute-start(bf16[128,1536]{1,0:T(8,128)(2,1)S(1)} %get-tuple-element.205), channel_id=1, source_target_pairs={{0,3},{1,0},{2,1},{3,2},{4,7},{5,4},{6,5},{7,6},{8,11},{9,8},{10,9... | collective-permute-start | bytes 1179656 | tf_op jit(solution)/shard_map/ppermute | solution.py:73
  370.8 36.5 %collective-permute-start.17 = (bf16[128,1536]{1,0:T(8,128)(2,1)S(1)}, bf16[128,1536]{1,0:T(8,128)(2,1)S(1)}, u32[]{:S(2)}, u32[]{:S(2)}) collective-permute-start(bf16[128,1536]{1,0:T(8,128)(2,1)S(1)} %get-tuple-element.207), channel_id=1, source_target_pairs={{0,2},{1,3},{2,0},{3,1},{4,6},{5,7},{6,4},{7,5},{8,10},{9,11},{10,... | collective-permute-start | bytes 1179656 | tf_op jit(solution)/shard_map/ppermute | solution.py:73
  404.1 133.1 %collective-permute-start.30 = (bf16[2,5,192,256]{3,2,1,0:T(8,128)(2,1)S(1)}, bf16[2,5,192,256]{3,2,1,0:T(8,128)(2,1)S(1)}, u32[]{:S(2)}, u32[]{:S(2)}) collective-permute-start(bf16[2,5,192,256]{3,2,1,0:T(8,128)(2,1)S(1)} %select_convert_fusion), channel_id=1, source_target_pairs={{0,4},{4,0},{8,12},{12,8},{16,20},{20,16},{24,28},{28,24},{1,5},{5... | collective-permute-start | bytes 2949128 | tf_op jit(solution)/shard_map/ppermute | solution.py:60
  (37 other events, 693.8 us)

commit v3 on v2

--- a/solution.py
+++ b/solution.py
@@ -71,11 +71,6 @@
 def expert_shift(x, step):
     count = lax.axis_size("expert")
     return lax.ppermute(x, "expert", [(i, (i + step) % count) for i in range(count)])
-
-
-def expert_gather(x):
-    count = lax.axis_size("expert")
-    return [x] + [expert_shift(x, s) for s in range(1, count)]
 
 
 def expert_scatter(blocks):
@@ -132,75 +127,6 @@
 
 def head_slice(ref, start):
     return ref[:, start : start + HEAD_WIDTH]
-
-
-def attend_kernel(
-    blocks,
-    kv_heads,
-    *refs,
-):
-    x_refs = refs[:blocks]
-    gain, weights, out_weights, bias, cosine, sine = refs[blocks : blocks + 6]
-    (a1, qk, val, mixed, maxes, inverse) = refs[blocks + 6 : blocks + 12]
-    sums = refs[blocks + 12 : blocks + 12 + blocks]
-    mixed_t = refs[blocks + 12 + blocks]
-    rows = x_refs[0].shape[0]
-    rope_width = qk.shape[1]
-    q_width = kv_heads * GROUP * HEAD_WIDTH
-    for b in range(blocks):
-        a1[b * rows : (b + 1) * rows, :] = (x_refs[b][...].astype(F32) * gain[...]).astype(BF16)
-    linear = dot(a1[...], weights[:, : rope_width + val.shape[1]])
-    for c in range(rope_width // LANES):
-        x = linear[:, c * LANES : (c + 1) * LANES]
-        qk[:, c * LANES : (c + 1) * LANES] = (
-            x * cosine[...] + swap_halves(x) * sine[...]
-        ).astype(BF16)
-    val[...] = linear[:, rope_width:].astype(BF16)
-    for g in range(kv_heads):
-        key = head_slice(qk, q_width + g * HEAD_WIDTH)
-        value_t = head_slice(val, g * HEAD_WIDTH).T
-        for j in range(GROUP):
-            h = g * GROUP + j
-            scores = dot_nt(key, head_slice(qk, h * HEAD_WIDTH)) * SCORE_SCALE + bias[...]
-            top = jnp.max(scores, axis=0, keepdims=True)
-            weight = jnp.exp(scores - top)
-            inv = 1.0 / jnp.sum(weight, axis=0, keepdims=True)
-            maxes[h : h + 1, :] = top
-            inverse[h : h + 1, :] = inv
-            mixed_t[h * HEAD_WIDTH : (h + 1) * HEAD_WIDTH, :] = dot(
-                value_t, (weight * inv).astype(BF16)
-            )
-    mixed[...] = mixed_t[...].T.astype(BF16)
-    total = dot(mixed[...], out_weights[...])
-    for b in range(blocks):
-        sums[b][...] = total[b * rows : (b + 1) * rows, :].astype(sums[b].dtype)
-
-
-def attend(x_blocks, gain, weights, out_weights, bias, cosine, sine, kv_heads, rope_width):
-    blocks = len(x_blocks)
-    rows, model = x_blocks[0].shape
-    seq = rows * blocks
-    q_width = kv_heads * GROUP * HEAD_WIDTH
-    value_width = weights.shape[1] - LANES - rope_width
-    heads = kv_heads * GROUP
-    outs = [
-        shape_of((seq, model), BF16),
-        shape_of((seq, rope_width), BF16),
-        shape_of((seq, value_width), BF16),
-        shape_of((seq, q_width), BF16),
-        shape_of((heads, seq), F32),
-        shape_of((heads, seq), F32),
-    ] + [shape_of((rows, model), F32 if b == 0 else BF16) for b in range(blocks)]
-    out = pl.pallas_call(
-        functools.partial(attend_kernel, blocks, kv_heads),
-        in_specs=[VMEM] * (blocks + 6),
-        out_specs=[VMEM] * len(outs),
-        out_shape=outs,
-        scratch_shapes=[pltpu.VMEM((q_width, seq), F32)],
-        compiler_params=params(),
-        name="attend",
-    )(*x_blocks, gain, weights, out_weights, bias, cosine, sine)
-    return out[:6], out[6:]
 
 
 def experts_kernel(blocks, pieces, place, row_block, *refs):
@@ -451,14 +377,12 @@
 
 
 def attend_back_kernel(blocks, kv_heads, gain_row, *refs):
-    dh_ref, x_refs = refs[0], refs[1 : blocks + 1]
-    (weights, out_weights, a1, qk, val, mixed, maxes, inverse, bias, cosine, sine, extra) = refs[
-        blocks + 1 : blocks + 13
-    ]
-    d_weights, d_out_weights = refs[blocks + 13 : blocks + 15]
-    sums = refs[blocks + 15 : 2 * blocks + 15]
-    grads, d_mixed, dq_t, d_qk, d_lin = refs[2 * blocks + 15 :]
-    rows = x_refs[0].shape[0]
+    dh_ref, x_all = refs[:2]
+    (weights, out_weights, a1, qk, val, mixed, maxes, inverse, bias, cosine, sine, extra) = refs[2:14]
+    d_weights, d_out_weights = refs[14:16]
+    sums = refs[16 : blocks + 16]
+    grads, d_mixed, dq_t, d_qk, d_lin = refs[blocks + 16 :]
+    rows = x_all.shape[1]
     rope_width, value_width = qk.shape[1], val.shape[1]
     q_width = kv_heads * GROUP * HEAD_WIDTH
     for b in range(blocks):
@@ -500,7 +424,7 @@
     for b in range(blocks):
         part = total[b * rows : (b + 1) * rows, :]
         sums[b][...] = part.astype(sums[b].dtype)
-        new = jnp.sum(part * x_refs[b][...].astype(F32), axis=0, keepdims=True)
+        new = jnp.sum(part * x_all[b].astype(F32), axis=0, keepdims=True)
         gain_grad = new if gain_grad is None else gain_grad + new
     d_weights[:, : rope_width + value_width] = dot_tn(a1[...], d_lin[...]).astype(BF16)
     line = lax.broadcasted_iota(jnp.int32, extra.shape, 0)
@@ -509,7 +433,7 @@
 
 
 def attend_back(
-    dh_stack, x_blocks, weights, out_weights, kept, bias, cosine, sine, extra, kv_heads, gain_row
+    dh_stack, x_all, weights, out_weights, kept, bias, cosine, sine, extra, kv_heads, gain_row
 ):
     blocks, rows, model = dh_stack.shape
     seq = rows * blocks
@@ -520,7 +444,7 @@
     ]
     out = pl.pallas_call(
         functools.partial(attend_back_kernel, blocks, kv_heads, gain_row),
-        in_specs=[VMEM] * (blocks + 13),
+        in_specs=[VMEM] * 14,
         out_specs=[VMEM] * len(outs),
         out_shape=outs,
         scratch_shapes=[
@@ -532,7 +456,7 @@
         ],
         compiler_params=params(),
         name="attend_back",
-    )(dh_stack, *x_blocks, weights, out_weights, *kept, bias, cosine, sine, extra)
+    )(dh_stack, x_all, weights, out_weights, *kept, bias, cosine, sine, extra)
     return out[0], out[1], out[2:]
 
 
@@ -563,11 +487,19 @@
         return {"fsdp": chip * 2 + self.core}
 
 
-def meet(peers):
+def greet(peers):
     barrier = pltpu.get_barrier_semaphore()
     for peer in peers:
         pl.semaphore_signal(barrier, inc=1, device_id=peer, device_id_type=MESH)
-    pl.semaphore_wait(barrier, len(peers))
+
+
+def await_peers(peers):
+    pl.semaphore_wait(pltpu.get_barrier_semaphore(), len(peers))
+
+
+def meet(peers):
+    greet(peers)
+    await_peers(peers)
 
 
 def send(src, dst, send_sem, recv_sem, peer):
@@ -587,8 +519,10 @@
     return params(collective_id=collective_id, has_side_effects=True)
 
 
-def gather_weights_kernel(ranks, plane_size, by_rank, rows_in, weights, out_rows, *sems):
-    z_send, z_recv, p_send, p_recv, c_send, c_recv, local = sems
+def gather_weights_kernel(
+    ranks, plane_size, by_rank, rows_in, x_in, grads_in, weights, out_rows, x_all, grads_all, *sems
+):
+    z_send, z_recv, p_send, p_recv, c_send, c_recv, local = sems[:7]
     spot = Spot(ranks, plane_size)
     f, me, chips = spot.index, spot.rank, spot.chips
     others = range(1, ranks)
@@ -611,9 +545,15 @@
     kept = [
         pltpu.make_async_copy(by_rank.at[me], weights.at[f, me], local.at[0]),
         pltpu.make_async_copy(rows_in, out_rows.at[f], local.at[1]),
+        pltpu.make_async_copy(x_in, x_all.at[0], local.at[2]),
+        pltpu.make_async_copy(grads_in, grads_all.at[0], local.at[3]),
     ]
     for copy in kept:
         copy.start()
+    lines = [
+        LineGather(spot, x_all, sems[7], sems[8]),
+        LineGather(spot, grads_all, sems[9], sems[10]),
+    ]
 
     def spread(which, src, buf):
         return [
@@ -628,9 +568,18 @@
         ] + [send(src, buf.at[f], c_send.at[which, 0], c_recv.at[which, 0], spot.partner())]
 
     row_copies = spread(1, rows_in, out_rows)
-    for copy in kept + z_copies:
+    for copy in kept:
+        copy.wait()
+    lines[0].start(0)
+    for copy in z_copies:
         copy.wait()
     weight_copies = spread(0, weights.at[f], weights)
+    for hop in range(ranks - 1):
+        lines[0].arrive(hop)
+        if hop + 1 < ranks - 1:
+            lines[0].start(hop + 1)
+        else:
+            lines[1].start(0)
     for k in range(1, chips):
         source = spot.chip_behind(k) * 2 + spot.core
         for which, copies, buf in ((1, row_copies, out_rows), (0, weight_copies, weights)):
@@ -644,23 +593,31 @@
                     spot.partner(),
                 )
             )
+    for hop in range(ranks - 1):
+        lines[1].arrive(hop)
+        if hop + 1 < ranks - 1:
+            lines[1].start(hop + 1)
     row_copies[-1].wait()
     weight_copies[-1].wait()
     for copy in waits:
         copy.wait()
-
-
-def gather_weights(by_rank, rows_in, plane_size):
+    for line in lines:
+        line.drain()
+
+
+def gather_weights(by_rank, rows_in, x_in, grads_in, plane_size):
     ranks, rows, columns = by_rank.shape
     chips = plane_size // 2
     dma = pltpu.SemaphoreType.DMA
     return pl.pallas_call(
         functools.partial(gather_weights_kernel, ranks, plane_size),
-        in_specs=[VMEM] * 2,
-        out_specs=[VMEM] * 2,
+        in_specs=[VMEM] * 4,
+        out_specs=[VMEM] * 4,
         out_shape=[
             shape_of((plane_size, ranks, rows, columns), BF16),
             shape_of((plane_size,) + rows_in.shape, BF16),
+            shape_of((ranks,) + x_in.shape, BF16),
+            shape_of((ranks,) + grads_in.shape, BF16),
         ],
         scratch_shapes=[
             dma((ranks - 1,)),
@@ -669,11 +626,12 @@
             dma((2, chips - 1)),
             dma((2, chips)),
             dma((2, chips)),
-            dma((2,)),
-        ],
+            dma((4,)),
+        ]
+        + [dma((2, ranks - 1))] * 4,
         compiler_params=remote(0),
         name="gather_weights",
-    )(by_rank, rows_in)
+    )(by_rank, rows_in, x_in, grads_in)
 
 
 def scatter_start(spot, refs, buf, send_sem, recv_sem):
@@ -683,61 +641,180 @@
     ]
 
 
-def middle_kernel(ranks, plane_size, x, gain, *refs):
-    sums = refs[:ranks]
-    h, a2, gathered, other = refs[ranks : ranks + 4]
-    got, r_send, r_recv, g_send, g_recv, c_send, c_recv = refs[ranks + 4 :]
+class LineGather:
+    def __init__(self, spot, buf, send_sem, recv_sem):
+        self.spot, self.buf, self.sems = spot, buf, (send_sem, recv_sem)
+        me, n = spot.rank, spot.ranks
+        self.hops = n - 1
+        self.sends = [(me - h >= 0) & (me + 1 < n) for h in range(n - 1)], [
+            (me + h < n) & (me >= 1) for h in range(n - 1)
+        ]
+        self.gets = [me - 1 - h >= 0 for h in range(n - 1)], [
+            me + 1 + h < n for h in range(n - 1)
+        ]
+
+    def slots(self, way, h):
+        n = self.spot.ranks
+        return (h, h + 1) if way == 0 else ((n - h) % n, n - h - 1)
+
+    def copy(self, way, h):
+        source, target = self.slots(way, h)
+        return pltpu.make_async_remote_copy(
+            src_ref=self.buf.at[source],
+            dst_ref=self.buf.at[target],
+            send_sem=self.sems[0].at[way, h],
+            recv_sem=self.sems[1].at[way, h],
+            device_id=self.spot.ahead(1) if way == 0 else self.spot.behind(1),
+            device_id_type=MESH,
+        )
+
+    def start(self, h):
+        for way in range(2):
+
+            @pl.when(self.sends[way][h])
+            def _():
+                self.copy(way, h).start()
+
+    def arrive(self, h):
+        for way in range(2):
+
+            @pl.when(self.gets[way][h])
+            def _():
+                self.copy(way, h).wait_recv()
+
+    def passed(self, h, then):
+        for way in range(2):
+
+            @pl.when(self.gets[way][h])
+            def _():
+                then(self.slots(way, h)[1])
+
+    def drain(self):
+        for h in range(self.hops):
+            for way in range(2):
+
+                @pl.when(self.sends[way][h])
+                def _():
+                    self.copy(way, h).wait_send()
+
+
+def attend_kernel(ranks, plane_size, kv_heads, *refs):
+    x_all, gain, weights, out_weights, bias, cosine, sine, x, gain_two = refs[:9]
+    (a1, qk, val, mixed, maxes, inverse, h_out, a2, gathered, other) = refs[9:19]
+    mixed_t, sums, got, r_send, r_recv, g_send, g_recv, c_send, c_recv = refs[19:]
     spot = Spot(ranks, plane_size)
-    meet([spot.ahead(s) for s in range(1, ranks)] + [spot.partner()])
-    copies = scatter_start(spot, sums, got, r_send, r_recv)
-    total = x[...] + sums[0][...]
+    peers = [spot.ahead(s) for s in range(1, ranks)] + [spot.partner()]
+    greet(peers)
+    rows = x_all.shape[1]
+    rope_width = qk.shape[1]
+    q_width = kv_heads * GROUP * HEAD_WIDTH
+    for b in range(ranks):
+        a1[b * rows : (b + 1) * rows, :] = (x_all[b].astype(F32) * gain[...]).astype(BF16)
+    linear = dot(a1[...], weights[:, : rope_width + val.shape[1]])
+    for c in range(rope_width // LANES):
+        part = linear[:, c * LANES : (c + 1) * LANES]
+        qk[:, c * LANES : (c + 1) * LANES] = (
+            part * cosine[...] + swap_halves(part) * sine[...]
+        ).astype(BF16)
+    val[...] = linear[:, rope_width:].astype(BF16)
+    for g in range(kv_heads):
+        key = head_slice(qk, q_width + g * HEAD_WIDTH)
+        value_t = head_slice(val, g * HEAD_WIDTH).T
+        for j in range(GROUP):
+            h = g * GROUP + j
+            scores = dot_nt(key, head_slice(qk, h * HEAD_WIDTH)) * SCORE_SCALE + bias[...]
+            top = jnp.max(scores, axis=0, keepdims=True)
+            weight = jnp.exp(scores - top)
+            inv = 1.0 / jnp.sum(weight, axis=0, keepdims=True)
+            maxes[h : h + 1, :] = top
+            inverse[h : h + 1, :] = inv
+            mixed_t[h * HEAD_WIDTH : (h + 1) * HEAD_WIDTH, :] = dot(
+                value_t, (weight * inv).astype(BF16)
+            )
+    mixed[...] = mixed_t[...].T.astype(BF16)
+    await_peers(peers)
+    total = dot(mixed[...], out_weights[...])
+    for b in range(1, ranks):
+        sums[b - 1] = total[b * rows : (b + 1) * rows, :].astype(BF16)
+    copies = scatter_start(
+        spot, [None] + [sums.at[s - 1] for s in range(1, ranks)], got, r_send, r_recv
+    )
+    total = x[...] + total[:rows, :]
     for s in range(1, ranks):
         copies[s - 1].wait()
         total = total + got[s - 1].astype(F32)
     scale = lax.rsqrt(jnp.mean(total * total, axis=-1, keepdims=True) + EPSILON)
-    low = (total * scale * gain[...]).astype(BF16)
+    low = (total * scale * gain_two[...]).astype(BF16)
     gathered[0] = low
+    line = LineGather(spot, gathered, g_send, g_recv)
+    line.start(0)
+
+    def across(s):
+        return pltpu.make_async_remote_copy(
+            src_ref=gathered.at[s],
+            dst_ref=other.at[s],
+            send_sem=c_send.at[s],
+            recv_sem=c_recv.at[s],
+            device_id=spot.partner(),
+            device_id_type=MESH,
+        )
+
+    across(0).start()
     a2[...] = low
-    h[...] = total
-    copies = [
-        send(
-            gathered.at[0], gathered.at[s], g_send.at[s - 1], g_recv.at[s - 1], spot.ahead(s)
-        )
-        for s in range(1, ranks)
-    ]
-    across = [
-        send(gathered.at[0], other.at[0], c_send.at[0], c_recv.at[0], spot.partner())
-    ]
-    for s in range(1, ranks):
-        copies[s - 1].wait()
-        across.append(
-            send(gathered.at[s], other.at[s], c_send.at[s], c_recv.at[s], spot.partner())
-        )
-    for copy in across:
-        copy.wait()
-
-
-def middle(x, gain, sums, plane_size):
-    ranks = len(sums)
+    h_out[...] = total
+    for hop in range(line.hops):
+        line.arrive(hop)
+        if hop + 1 < line.hops:
+            line.start(hop + 1)
+        line.passed(hop, lambda s: across(s).start())
+    line.drain()
+    for s in range(ranks):
+        across(s).wait()
+
+
+def attend(
+    x_all, gain, weights, out_weights, bias, cosine, sine, x, gain_two, kv_heads, rope_width,
+    plane_size,
+):
+    ranks, rows, model = x_all.shape
+    seq = rows * ranks
+    q_width = kv_heads * GROUP * HEAD_WIDTH
+    value_width = weights.shape[1] - LANES - rope_width
+    heads = kv_heads * GROUP
+    stack = shape_of((ranks, rows, model), BF16)
+    outs = [
+        shape_of((seq, model), BF16),
+        shape_of((seq, rope_width), BF16),
+        shape_of((seq, value_width), BF16),
+        shape_of((seq, q_width), BF16),
+        shape_of((heads, seq), F32),
+        shape_of((heads, seq), F32),
+        shape_of((rows, model), F32),
+        shape_of((rows, model), BF16),
+        stack,
+        stack,
+    ]
     dma = pltpu.SemaphoreType.DMA
-    stack = shape_of((ranks,) + x.shape, BF16)
-    return pl.pallas_call(
-        functools.partial(middle_kernel, ranks, plane_size),
-        in_specs=[VMEM] * (2 + ranks),
-        out_specs=[VMEM] * 4,
-        out_shape=[shape_of(x.shape, F32), shape_of(x.shape, BF16), stack, stack],
+    out = pl.pallas_call(
+        functools.partial(attend_kernel, ranks, plane_size, kv_heads),
+        in_specs=[VMEM] * 9,
+        out_specs=[VMEM] * len(outs),
+        out_shape=outs,
         scratch_shapes=[
-            pltpu.VMEM((ranks - 1,) + x.shape, BF16),
+            pltpu.VMEM((q_width, seq), F32),
+            pltpu.VMEM((ranks - 1, rows, model), BF16),
+            pltpu.VMEM((ranks - 1, rows, model), BF16),
             dma((ranks - 1,)),
             dma((ranks - 1,)),
-            dma((ranks - 1,)),
-            dma((ranks - 1,)),
+            dma((2, ranks - 1)),
+            dma((2, ranks - 1)),
             dma((ranks,)),
             dma((ranks,)),
         ],
         compiler_params=remote(1),
-        name="middle",
-    )(x, gain, *sums)
+        name="attend",
+    )(x_all, gain, weights, out_weights, bias, cosine, sine, x, gain_two)
+    return out[:6], out[6:]
 
 
 def rejoin_kernel(ranks, plane_size, gain_row, gates, h, dz, router_t, a2, *refs):
@@ -765,17 +842,16 @@
     )
     gathered[0] = grad.astype(BF16)
     dh[...] = grad
-    copies = [
-        send(
-            gathered.at[0], gathered.at[s], g_send.at[s - 1], g_recv.at[s - 1], spot.ahead(s)
-        )
-        for s in range(1, ranks)
-    ]
+    line_out = LineGather(spot, gathered, g_send, g_recv)
+    line_out.start(0)
     gain_grad = jnp.sum(da2 * normed, axis=0, keepdims=True)
     line = lax.broadcasted_iota(jnp.int32, (LANES, model), 0)
     extra[...] = jnp.where(line == gain_row, gain_grad, dot_tn(d_logits, a2[...]))
-    for copy in copies:
-        copy.wait()
+    for hop in range(line_out.hops):
+        line_out.arrive(hop)
+        if hop + 1 < line_out.hops:
+            line_out.start(hop + 1)
+    line_out.drain()
 
 
 def rejoin(parts, gates, h, dz, router_t, a2, gain_row, plane_size):
@@ -790,7 +866,7 @@
             shape_of((ranks,) + h.shape, BF16),
             shape_of((LANES, h.shape[1]), F32),
         ],
-        scratch_shapes=[dma((ranks - 1,)), dma((ranks - 1,))],
+        scratch_shapes=[dma((2, ranks - 1)), dma((2, ranks - 1))],
         compiler_params=remote(2),
         name="rejoin",
     )(gates, h, dz, router_t, a2, *parts)
@@ -948,7 +1024,7 @@
     gain_one_row, gain_two_row = n_experts, n_experts + 1
 
     scale_one = lax.rsqrt(jnp.mean(inputs * inputs, axis=-1, keepdims=True) + EPSILON)
-    x_blocks = expert_gather((inputs * scale_one).astype(BF16))
+    x_own = (inputs * scale_one).astype(BF16)
 
     extra_cols = jnp.concatenate(
         [
@@ -982,9 +1058,7 @@
 
     lane_ids = jnp.arange(LANES, dtype=jnp.int32)
     routed = jnp.sum((routes[:, :, None] == lane_ids[None, None, :]).astype(F32), axis=1)
-    grads = jnp.concatenate(
-        expert_gather(jnp.concatenate([cotangent, routed], axis=1).astype(BF16)), axis=0
-    )
+    grads_own = jnp.concatenate([cotangent, routed], axis=1).astype(BF16)
 
     core = plane.core.astype(jnp.int32)[None]
     keep, send, halves = pack_experts(core, w_gate, w_up, w_down, plane.size)
@@ -993,10 +1067,20 @@
         jnp.concatenate([jnp.where(plane.core == part, keep, got), halves[part][None]], axis=0)
         for part in range(2)
     ]
-    found = {(0, 0, 0): parts[0], (0, 0, 1): parts[1]}
-    found[0, 1, 0] = plane.other_mid(parts[0])
+    by_rank, parts, out_shard, x_own, grads_own = lax.optimization_barrier(
+        (by_rank, parts, out_shard, x_own, grads_own)
+    )
+    first = [plane.other_mid(parts[0])] + [
+        plane.next_row(parts[1], s) for s in range(1, plane.rows)
+    ]
+    weights, out_weights, x_all, grads = gather_weights(
+        by_rank, out_shard, x_own, grads_own, plane.size
+    )
+    first, weights = lax.optimization_barrier((first, weights))
+    grads = grads.reshape(seq, grads.shape[2])
+    found = {(0, 0, 0): parts[0], (0, 0, 1): parts[1], (0, 1, 0): first[0]}
     for s in range(1, plane.rows):
-        found[s, 0, 1] = plane.next_row(parts[1], s)
+        found[s, 0, 1] = first[s]
         for mid in range(2):
             found[s, mid, 0] = plane.next_row(found[0, mid, 0], s)
     for s in range(plane.rows):
@@ -1009,8 +1093,6 @@
     ]
     where = jnp.stack([me] + sources).astype(jnp.int32)
 
-    by_rank, parts, out_shard = lax.optimization_barrier((by_rank, parts, out_shard))
-    weights, out_weights = gather_weights(by_rank, out_shard, plane.size)
     weights = weights.reshape(model, columns)
     out_weights = out_weights.reshape(q_cols, model)
 
@@ -1031,11 +1113,20 @@
     extra_t = weights[:, columns - LANES :].T
     gain_one = extra_t[gain_one_row : gain_one_row + 1].astype(F32)
     gain_two = extra_t[gain_two_row : gain_two_row + 1].astype(F32)
-    kept, sums = attend(
-        x_blocks, gain_one, weights, out_weights, bias, cosine, sine, kv_heads, rope_width
-    )
-    grads, sums = lax.optimization_barrier((grads, sums))
-    mid_rows, a2, own_a2, other_a2 = middle(inputs, gain_two, sums, plane.size)
+    kept, (mid_rows, a2, own_a2, other_a2) = attend(
+        x_all,
+        gain_one,
+        weights,
+        out_weights,
+        bias,
+        cosine,
+        sine,
+        inputs,
+        gain_two,
+        kv_heads,
+        rope_width,
+        plane.size,
+    )
 
     other_grads = plane.other_core(grads)
     other_out, other_dx, _, *other_kept = experts(
@@ -1072,15 +1163,42 @@
         return value.astype(BF16)
 
     steps = range(1, plane.rows)
-    a_sums = [
-        add(summed[0, mid, 0], *[plane.next_row(summed[s, mid, 0], s) for s in steps])
-        for mid in range(2)
-    ]
-    b_sums = [
-        add(summed[s, 0, 1], plane.other_mid(summed[s, 1, 1])) for s in range(plane.rows)
-    ]
+    a_first = [[plane.next_row(summed[s, mid, 0], s) for s in steps] for mid in range(2)]
+    b_first = [plane.other_mid(summed[s, 1, 1]) for s in range(plane.rows)]
+
+    dh, dh_stack, extra = rejoin(
+        [dxs[0]] + dx_got, gates, mid_rows, cotangent, extra_t, a2, gain_two_row, plane.size
+    )
+
+    d_weights, d_out_weights, da1 = attend_back(
+        dh_stack,
+        x_all,
+        weights,
+        out_weights,
+        kept,
+        bias,
+        cosine,
+        sine,
+        extra,
+        kv_heads,
+        gain_one_row,
+    )
+    a_first, b_first, d_weights = lax.optimization_barrier((a_first, b_first, d_weights))
+    a_sums = [add(summed[0, mid, 0], *a_first[mid]) for mid in range(2)]
+    b_sums = [add(summed[s, 0, 1], b_first[s]) for s in range(plane.rows)]
+    a_sums, b_sums, d_weights = lax.optimization_barrier((a_sums, b_sums, d_weights))
     a_got = plane.other_mid(a_sums[1])
     b_got = [plane.next_row(b_sums[s], s) for s in steps]
+    chip_count = plane.size // 2
+    input_grad, by_rank, out_part = last(
+        inputs,
+        dh,
+        gain_one,
+        d_weights.reshape(chip_count, 2, ranks, weight_rows, columns),
+        d_out_weights.reshape(chip_count, 2, weight_rows, model),
+        da1,
+    )
+    a_got, b_got, out_part = lax.optimization_barrier((a_got, b_got, out_part))
     b_kept = b_sums[0]
     if len(b_got) > 1:
         b_kept = add(b_kept, *b_got[:-1])
@@ -1094,33 +1212,6 @@
     )
     gate_grad, up_grad, down_grad = finish(
         core, a_sums[0], a_got, b_kept, b_got, other, w_down.shape[1], model, plane.size
-    )
-
-    dh, dh_stack, extra = rejoin(
-        [dxs[0]] + dx_got, gates, mid_rows, cotangent, extra_t, a2, gain_two_row, plane.size
-    )
-
-    d_weights, d_out_weights, da1 = attend_back(
-        dh_stack,
-        x_blocks,
-        weights,
-        out_weights,
-        kept,
-        bias,
-        cosine,
-        sine,
-        extra,
-        kv_heads,
-        gain_one_row,
-    )
-    chip_count = plane.size // 2
-    input_grad, by_rank, out_part = last(
-        inputs,
-        dh,
-        gain_one,
-        d_weights.reshape(chip_count, 2, ranks, weight_rows, columns),
-        d_out_weights.reshape(chip_count, 2, weight_rows, model),
-        da1,
     )
     out_all = out_all + plane.other_core(other_out).astype(F32)
     outs = [out_all[b * rows : (b + 1) * rows] for b in range(ranks)]

time: 555 us -> 483 us (0.87)
  waiting for transfers between devices: 85.6 us -> 9.71 us
  starting transfers between devices: 78.7 us -> 42.8 us
  Pallas kernels: 336 us -> 366 us
  other arithmetic: 24 us -> 31 us
    ppermute x6, waiting for transfers between devices: 41 us -> 0.02 us  [other_mid(): return lax.ppermute(x, 'fsdp', [(i, i ^ 2) for i in range(self.size)])]
    pallas_call x1, Pallas kernels: 38.3 us -> 72.3 us  [gather_weights(): pl.pallas_call(functools.partial(gather_weights_kernel, ranks, plane_size...]
    ppermute x12 -> x6, starting transfers between devices: 41.6 us -> 13.7 us  [expert_shift(): lax.ppermute(x, 'expert', [(i, (i + step) % count) for i in range(count)])]
    pallas_call x1, Pallas kernels: 49.3 us -> 74.7 us  [last(): pl.pallas_call(functools.partial(last_kernel, ranks, 2 * chips), in_specs...]
    pallas_call x2 -> x1, Pallas kernels: 96.6 us -> 74.6 us  [attend(): pl.pallas_call(functools.partial(attend_kernel, ranks, plane_size, kv_hea...]
    ppermute x6, waiting for transfers between devices: 18.1 us -> 0.02 us  [next_row(): lax.ppermute(x, 'fsdp', [(i, (i // 4 + step) % self.rows * 4 + i % 4) for...]
    ppermute x12 -> x6, waiting for transfers between devices: 22.1 us -> 4.22 us  [expert_shift(): lax.ppermute(x, 'expert', [(i, (i + step) % count) for i in range(count)])]
    ppermute x1, starting transfers between devices: 14.3 us -> 2.92 us  [on_device(): out_shard = lax.ppermute(w_output.astype(BF16), axes, move)]
  transfers between devices with their start and end apart: 31 -> 25, of which waited for: 7 -> 2; matrix products, arithmetic and copies ran while one was open for 6% -> 9% of each run, Pallas kernels for 55% -> 69%
where the time goes in v3:
time: 483 us; the launch traced here: 473 us
  Pallas kernels  366 us (76%)
  starting transfers between devices  42.8 us (9%)
  other arithmetic  31 us (6%)
  local copies, waits for them, and re-layouts  21.6 us (4%)
  waiting for transfers between devices  9.71 us (2%)
    pallas_call x1, Pallas kernels, last(): pl.pallas_call(functools.partial(last_kernel, ranks, 2 * chips), in_specs...  74.7 us
    pallas_call x1, Pallas kernels, attend(): pl.pallas_call(functools.partial(attend_kernel, ranks, plane_size, kv_hea...  74.6 us
    pallas_call x1, Pallas kernels, gather_weights(): pl.pallas_call(functools.partial(gather_weights_kernel, ranks, plane_size...  72.3 us
    pallas_call x2, Pallas kernels, experts(): pl.pallas_call(functools.partial(experts_kernel, blocks, len(pieces), pla...  53.5 us
    pallas_call x1, Pallas kernels, rejoin(): pl.pallas_call(functools.partial(rejoin_kernel, ranks, plane_size, gain_r...  42.4 us
    pallas_call x1, Pallas kernels, expert_grads(): pl.pallas_call(functools.partial(expert_grads_kernel, chips, depth, down_...  18.5 us
    pallas_call x1, Pallas kernels, attend_back(): pl.pallas_call(functools.partial(attend_back_kernel, blocks, kv_heads, ga...  15.4 us
    ppermute x6, starting transfers between devices, expert_shift(): lax.ppermute(x, 'expert', [(i, (i + step) % count) for i in range(count)])  13.7 us
  transfers between devices with their start and end apart: 25, of which 2 were waited for; matrix products, arithmetic and copies ran while one was open for 9% of the time, Pallas kernels for 69%

profile of v3, /device:TPU:27, one launch (start us, length us, event | category | flops | bytes accessed | tf_op | source)
XLA Modules:
  0.0 473.1 jit_solution(6549179998794684462)
XLA Ops:
  0.7 6.9 %pack_experts.1 = (bf16[2,5,192,256]{3,2,1,0:T(8,128)(2,1)}, bf16[2,5,192,256]{3,2,1,0:T(8,128)(2,1)}, bf16[2,5,192,256]{3,2,1,0:T(8,128)(2,1)}) custom-call(s32[1]{0:T(128)} %bitcast.3.core, f32[5,192,512]{2,1,0:T(8,128)} %gate.1, f32[5,192,512]{2,1,0:T(8,128)} %up.1, f32[5,64,1536]{2,1,0:T(8,128)} %down.1), custom_call_target="tpu_custom_call" | custom-call | tf_op jit(solution)/shard_map/pack_experts/pallas_call | solution.py:110
  8.3 2.9 collective-permute-start.1
  16.7 5.4 %collective-permute-start.2 = (bf16[3,5,192,256]{3,2,1,0:T(8,128)(2,1)S(1)}, bf16[3,5,192,256]{3,2,1,0:T(8,128)(2,1)}, u32[]{:S(2)}, u32[]{:S(2)}) collective-permute-start(bf16[3,5,192,256]{3,2,1,0:T(8,128)(2,1)S(1)} %get-tuple-element.106.refs_4_), channel_id=1, source_target_pairs={{0,8},{4,12},{8,0},{12,4},{16,24},{20,28},{24,16},{28,20},{1,9},{5... | collective-permute-start | bytes 4423688 | tf_op jit(solution)/shard_map/ppermute | solution.py:63
  24.1 72.3 %gather_weights.1 = (bf16[8,4,48,768]{3,2,1,0:T(8,128)(2,1)}, bf16[8,48,1536]{2,1,0:T(8,128)(2,1)}, bf16[4,128,1536]{2,1,0:T(8,128)(2,1)}, bf16[4,128,1664]{2,1,0:T(8,128)(2,1)}) custom-call(bf16[4,48,768]{2,1,0:T(8,128)(2,1)} %maximum_bitcast_fusion.by_rank, bf16[48,1536]{1,0:T(8,128)(2,1)} %copy-done.27, bf16[128,1536]{1,0:T(8,128)(2,1)} %multiply_convert_fusion.x_in, ...), custom_call_target="tpu_custom_call" | custom-call | tf_op jit(solution)/shard_map/gather_weights/pallas_call | solution.py:612
  106.7 74.6 %attend.1 = (bf16[512,1536]{1,0:T(8,128)(2,1)}, bf16[512,512]{1,0:T(8,128)(2,1)}, bf16[512,128]{1,0:T(8,128)(2,1)}, bf16[512,384]{1,0:T(8,128)(2,1)}, f32[6,512]...) custom-call(bf16[4,128,1536]{2,1,0:T(8,128)(2,1)} %get-tuple-element, ...), custom_call_target="tpu_custom_call" | custom-call | tf_op jit(solution)/shard_map/attend/pallas_call | solution.py:798
  181.4 26.1 %experts.3 = (bf16[512,1536]{1,0:T(8,128)(2,1)}, bf16[512,1664]{1,0:T(8,128)(2,1)}, f32[128,128]{1,0:T(8,128)}, bf16[1536,512]{1,0:T(8,128)(2,1)}, bf16[5,256,51...) custom-call(bf16[512,1536]{1,0:T(8,128)(2,1)} %bitcast.70, ...), custom_call_target="tpu_custom_call" | custom-call | tf_op jit(solution)/shard_map/experts/pallas_call | solution.py:261
  207.7 27.4 %experts.2 = (f32[512,1536]{1,0:T(8,128)}, f32[512,1664]{1,0:T(8,128)}, f32[128,128]{1,0:T(8,128)}, bf16[1536,512]{1,0:T(8,128)(2,1)}, bf16[5,256,512]{2,1,0:T(8...) custom-call(bf16[512,1536]{1,0:T(8,128)(2,1)} %bitcast.69, bf16[512,1664]{1,0:T(8,128)(2,1)} %bitcast.64, ...), custom_call_target="tpu_custom_call" | custom-call | tf_op jit(solution)/shard_map/experts/pallas_call | solution.py:261
  235.1 4.1 fusion.16
  240.3 2.4 collective-permute-start.15
  245.5 2.7 slice.122.refs_5_
  248.1 18.5 %expert_grads.1 = (bf16[3,5,192,256]{3,2,1,0:T(8,128)(2,1)}, bf16[3,5,192,256]{3,2,1,0:T(8,128)(2,1)}, bf16[3,5,192,256]{3,2,1,0:T(8,128)(2,1)}, bf16[3,5,192,25...) custom-call(s32[4]{0:T(128)} %pad_add_fusion.where_ref, ...), custom_call_target="tpu_custom_call" | custom-call | tf_op jit(solution)/shard_map/expert_grads/pallas_call | solution.py:325
  266.7 4.2 collective-permute-done.15.refs_2_
  274.6 3.1 collective-permute-start.9
  279.8 42.4 %rejoin.1 = (f32[128,1536]{1,0:T(8,128)}, bf16[4,128,1536]{2,1,0:T(8,128)(2,1)}, f32[128,1536]{1,0:T(8,128)}) custom-call(f32[128,128]{1,0:T(8,128)} %get-tuple-element.119.gates, f32[128,1536]{1,0:T(8,128)} %get-tuple-element.111.h, f32[128,1536]{1,0:T(8,128)} %dz.1, bf16[128,1536]{1,0:T(8,128)(2,1)} %bitcast.62, bf16[128,1536]{1,0:T(8,128)(2,1)} %get-tuple-element.120.a2, ...), custom_call_target="tpu_custom_call" | custom-call | tf_op jit(solution)/shard_map/rejoin/pallas_call | solution.py:860
  322.3 15.4 %attend_back.1 = (bf16[1536,768]{1,0:T(8,128)(2,1)}, bf16[384,1536]{1,0:T(8,128)(2,1)}, f32[128,1536]{1,0:T(8,128)}, bf16[128,1536]{1,0:T(8,128)(2,1)}, bf16[128...) custom-call(bf16[4,128,1536]{2,1,0:T(8,128)(2,1)} %get-tuple-element.148.refs_0_, ...), custom_call_target="tpu_custom_call" | custom-call | tf_op jit(solution)/shard_map/attend_back/pallas_call | solution.py:445
  337.7 3.5 add_convert_fusion
  343.2 3.5 add_convert_fusion.2
  349.1 3.8 fusion.17
  354.0 8.3 %collective-permute-start.10 = (bf16[128,1536]{1,0:T(8,128)(2,1)}, bf16[128,1536]{1,0:T(8,128)(2,1)}, u32[]{:S(2)}, u32[]{:S(2)}) collective-permute-start(bf16[128,1536]{1,0:T(8,128)(2,1)} %get-tuple-element.231), channel_id=1, source_target_pairs={{0,3},{1,0},{2,1},{3,2},{4,7},{5,4},{6,5},{7,6},{8,11},{9,8},{10,9... | collective-permute-start | bytes 1179656 | tf_op jit(solution)/shard_map/ppermute | solution.py:73
  364.4 74.7 %last.1 = (f32[128,1536]{1,0:T(8,128)}, bf16[4,48,768]{2,1,0:T(8,128)(2,1)}, f32[48,1536]{1,0:T(8,128)}) custom-call(f32[128,1536]{1,0:T(8,128)} %x.1, f32[128,1536]{1,0:T(8,128)} %get-tuple-element.142.dh, f32[1,1536]{1,0:T(1,128)} %get-tuple-element.240.refs_1_.gain, bf16[4,2,4,48,768]{4,3,2,1,0:T(8,128)(2,1)} %bitcast.68, ...), custom_call_target="tpu_custom_call" | custom-call | tf_op jit(solution)/shard_map/last/pallas_call | solution.py:958
  441.4 5.7 %collective-permute-start.24 = (bf16[2,5,192,256]{3,2,1,0:T(8,128)(2,1)S(1)}, bf16[2,5,192,256]{3,2,1,0:T(8,128)(2,1)S(1)}, u32[]{:S(2)}, u32[]{:S(2)}) collective-permute-start(bf16[2,5,192,256]{3,2,1,0:T(8,128)(2,1)S(1)} %select_convert_fusion), channel_id=1, source_target_pairs={{0,4},{4,0},{8,12},{12,8},{16,20},{20,16},{24,28},{28,24},{1,5},{5... | collective-permute-start | bytes 2949128 | tf_op jit(solution)/shard_map/ppermute | solution.py:60
  447.1 2.6 fusion.2
  456.6 5.4 %collective-permute-done.23 = bf16[48,1536]{1,0:T(8,128)(2,1)S(1)} collective-permute-done((bf16[48,1536]{1,0:T(8,128)(2,1)S(1)}, bf16[48,1536]{1,0:T(8,128)(2,1)S(1)}, u32[]{:S(2)}, u32[]{:S(2)}) %collective-permute-start.23) | collective-permute-done | bytes 147488 | tf_op jit(solution)/shard_map/ppermute | solution.py:1222
  463.8 7.9 %finish.1 = (f32[5,192,512]{2,1,0:T(8,128)}, f32[5,192,512]{2,1,0:T(8,128)}, f32[5,64,1536]{2,1,0:T(8,128)}) custom-call(s32[1]{0:T(128)} %bitcast.3.core, bf16[3,5,192,256]{3,2,1,0:T(8,128)(2,1)} %copy-done.4, bf16[3,5,192,256]{3,2,1,0:T(8,128)(2,1)} %collective-permute-done.21.got_a, bf16[3,5,192,256]{3,2,1,0:T(8,128)(2,1)} %copy-done.3, ...), custom_call_target="tpu_custom_call" | custom-call | tf_op jit(solution)/shard_map/finish/pallas_call | solution.py:367
  (167 shorter events, 47.2 us)
Async XLA Ops:
  8.3 8.3 %collective-permute-start.1 = (bf16[48,1536]{1,0:T(8,128)(2,1)S(1)}, bf16[48,1536]{1,0:T(8,128)(2,1)S(1)}, u32[]{:S(2)}, u32[]{:S(2)}) collective-permute-start(bf16[48,1536]{1,0:T(8,128)(2,1)S(1)} %convert_element_type.105), channel_id=1, source_target_pairs={{0,0},{1,4},{2,8},{3,12},{4,16},{5,20},{6,24},{7,28},{8,1},{9,5},{... | collective-permute-start | bytes 442376 | tf_op jit(solution)/shard_map/ppermute | solution.py:1057
  16.7 82.3 %collective-permute-start.2 = (bf16[3,5,192,256]{3,2,1,0:T(8,128)(2,1)S(1)}, bf16[3,5,192,256]{3,2,1,0:T(8,128)(2,1)}, u32[]{:S(2)}, u32[]{:S(2)}) collective-permute-start(bf16[3,5,192,256]{3,2,1,0:T(8,128)(2,1)S(1)} %get-tuple-element.106.refs_4_), channel_id=1, source_target_pairs={{0,8},{4,12},{8,0},{12,4},{16,24},{20,28},{24,16},{28,20},{1,9},{5... | collective-permute-start | bytes 4423688 | tf_op jit(solution)/shard_map/ppermute | solution.py:63
  22.1 76.9 %collective-permute-start.3 = (bf16[3,5,192,256]{3,2,1,0:T(8,128)(2,1)S(1)}, bf16[3,5,192,256]{3,2,1,0:T(8,128)(2,1)}, u32[]{:S(2)}, u32[]{:S(2)}) collective-permute-start(bf16[3,5,192,256]{3,2,1,0:T(8,128)(2,1)S(1)} %get-tuple-element.107.refs_5_), channel_id=1, source_target_pairs={{0,16},{4,20},{8,24},{12,28},{16,0},{20,4},{24,8},{28,12},{1,17},{... | collective-permute-start | bytes 4423688 | tf_op jit(solution)/shard_map/ppermute | solution.py:66
  96.4 84.9 %collective-permute-start.8 = (bf16[512,1664]{1,0:T(8,128)(2,1)}, bf16[512,1664]{1,0:T(8,128)(2,1)}, u32[]{:S(2)}, u32[]{:S(2)}) collective-permute-start(bf16[512,1664]{1,0:T(8,128)(2,1)} %bitcast.63), channel_id=1, source_target_pairs={{0,4},{4,0},{8,12},{12,8},{16,20},{20,16},{24,28},{28,24},{1,5},{5... | collective-permute-start | bytes 5111816 | tf_op jit(solution)/shard_map/ppermute | solution.py:60
  97.9 83.4 %collective-permute-start.4 = (bf16[3,5,192,256]{3,2,1,0:T(8,128)(2,1)S(1)}, bf16[3,5,192,256]{3,2,1,0:T(8,128)(2,1)}, u32[]{:S(2)}, u32[]{:S(2)}) collective-permute-start(bf16[3,5,192,256]{3,2,1,0:T(8,128)(2,1)S(1)} %get-tuple-element.106.refs_4_), channel_id=1, source_target_pairs={{0,16},{4,20},{8,24},{12,28},{16,0},{20,4},{24,8},{28,12},{1,17},{... | collective-permute-start | bytes 4423688 | tf_op jit(solution)/shard_map/ppermute | solution.py:66
  98.0 83.4 %collective-permute-start.6 = (bf16[3,5,192,256]{3,2,1,0:T(8,128)(2,1)S(1)}, bf16[3,5,192,256]{3,2,1,0:T(8,128)(2,1)}, u32[]{:S(2)}, u32[]{:S(2)}) collective-permute-start(bf16[3,5,192,256]{3,2,1,0:T(8,128)(2,1)S(1)} %get-tuple-element.107.refs_5_), channel_id=1, source_target_pairs={{0,8},{4,12},{8,0},{12,4},{16,24},{20,28},{24,16},{28,20},{1,9},{5... | collective-permute-start | bytes 4423688 | tf_op jit(solution)/shard_map/ppermute | solution.py:63
  99.0 82.3 %collective-permute-start.5 = (bf16[3,5,192,256]{3,2,1,0:T(8,128)(2,1)}, bf16[3,5,192,256]{3,2,1,0:T(8,128)(2,1)}, u32[]{:S(2)}, u32[]{:S(2)}) collective-permute-start(bf16[3,5,192,256]{3,2,1,0:T(8,128)(2,1)} %collective-permute-done.2.refs_6_), channel_id=1, source_target_pairs={{0,16},{4,20},{8,24},{12,28},{16,0},{20,4},{24,8},{28,12},{1,17},{... | collective-permute-start | bytes 4423688 | tf_op jit(solution)/shard_map/ppermute | solution.py:66
  99.5 81.9 %collective-permute-start.7 = (bf16[3,5,192,256]{3,2,1,0:T(8,128)(2,1)}, bf16[3,5,192,256]{3,2,1,0:T(8,128)(2,1)}, u32[]{:S(2)}, u32[]{:S(2)}) collective-permute-start(bf16[3,5,192,256]{3,2,1,0:T(8,128)(2,1)} %collective-permute-done.3.refs_7_), channel_id=1, source_target_pairs={{0,8},{4,12},{8,0},{12,4},{16,24},{20,28},{24,16},{28,20},{1,9},{5... | collective-permute-start | bytes 4423688 | tf_op jit(solution)/shard_map/ppermute | solution.py:63
  207.5 27.6 %collective-permute-start.13 = (bf16[512,1664]{1,0:T(8,128)(2,1)}, bf16[512,1664]{1,0:T(8,128)(2,1)S(1)}, u32[]{:S(2)}, u32[]{:S(2)}) collective-permute-start(bf16[512,1664]{1,0:T(8,128)(2,1)} %get-tuple-element.122), channel_id=1, source_target_pairs={{0,4},{4,0},{8,12},{12,8},{16,20},{20,16},{24,28},{28,24},{1,5},{5... | collective-permute-start | bytes 5111816 | tf_op jit(solution)/shard_map/ppermute | solution.py:60
  240.3 26.3 %collective-permute-start.14 = (bf16[128,1664]{1,0:T(8,128)(2,1)}, bf16[128,1664]{1,0:T(8,128)(2,1)S(1)}, u32[]{:S(2)}, u32[]{:S(2)}) collective-permute-start(bf16[128,1664]{1,0:T(8,128)(2,1)} %get-tuple-element.230), channel_id=1, source_target_pairs={{0,3},{1,0},{2,1},{3,2},{4,7},{5,4},{6,5},{7,6},{8,11},{9,8},{10,9... | collective-permute-start | bytes 1277960 | tf_op jit(solution)/shard_map/ppermute | solution.py:73
  240.3 30.5 %collective-permute-start.15 = (bf16[128,1664]{1,0:T(8,128)(2,1)}, bf16[128,1664]{1,0:T(8,128)(2,1)S(1)}, u32[]{:S(2)}, u32[]{:S(2)}) collective-permute-start(bf16[128,1664]{1,0:T(8,128)(2,1)} %get-tuple-element.229), channel_id=1, source_target_pairs={{0,2},{1,3},{2,0},{3,1},{4,6},{5,7},{6,4},{7,5},{8,10},{9,11},{10,... | collective-permute-start | bytes 1277960 | tf_op jit(solution)/shard_map/ppermute | solution.py:73
  242.8 28.1 %collective-permute-start.16 = (bf16[128,1664]{1,0:T(8,128)(2,1)}, bf16[128,1664]{1,0:T(8,128)(2,1)S(1)}, u32[]{:S(2)}, u32[]{:S(2)}) collective-permute-start(bf16[128,1664]{1,0:T(8,128)(2,1)} %get-tuple-element.228), channel_id=1, source_target_pairs={{0,1},{1,2},{2,3},{3,0},{4,5},{5,6},{6,7},{7,4},{8,9},{9,10},{10,1... | collective-permute-start | bytes 1277960 | tf_op jit(solution)/shard_map/ppermute | solution.py:73
  271.6 66.0 %collective-permute-start.17 = (bf16[3,5,192,256]{3,2,1,0:T(8,128)(2,1)}, bf16[3,5,192,256]{3,2,1,0:T(8,128)(2,1)S(1)}, u32[]{:S(2)}, u32[]{:S(2)}) collective-permute-start(bf16[3,5,192,256]{3,2,1,0:T(8,128)(2,1)} %get-tuple-element.144), channel_id=1, source_target_pairs={{0,16},{4,20},{8,24},{12,28},{16,0},{20,4},{24,8},{28,12},{1,17},{... | collective-permute-start | bytes 4423688 | tf_op jit(solution)/shard_map/ppermute | solution.py:66
  272.3 65.4 %collective-permute-start.18 = (bf16[3,5,192,256]{3,2,1,0:T(8,128)(2,1)}, bf16[3,5,192,256]{3,2,1,0:T(8,128)(2,1)}, u32[]{:S(2)}, u32[]{:S(2)}) collective-permute-start(bf16[3,5,192,256]{3,2,1,0:T(8,128)(2,1)} %get-tuple-element.145), channel_id=1, source_target_pairs={{0,16},{4,20},{8,24},{12,28},{16,0},{20,4},{24,8},{28,12},{1,17},{... | collective-permute-start | bytes 4423688 | tf_op jit(solution)/shard_map/ppermute | solution.py:66
  273.1 64.6 %collective-permute-start.19 = (bf16[3,5,192,256]{3,2,1,0:T(8,128)(2,1)}, bf16[3,5,192,256]{3,2,1,0:T(8,128)(2,1)}, u32[]{:S(2)}, u32[]{:S(2)}) collective-permute-start(bf16[3,5,192,256]{3,2,1,0:T(8,128)(2,1)} %get-tuple-element.146), channel_id=1, source_target_pairs={{0,8},{4,12},{8,0},{12,4},{16,24},{20,28},{24,16},{28,20},{1,9},{5... | collective-permute-start | bytes 4423688 | tf_op jit(solution)/shard_map/ppermute | solution.py:63
  273.7 64.0 %collective-permute-start.20 = (bf16[3,5,192,256]{3,2,1,0:T(8,128)(2,1)}, bf16[3,5,192,256]{3,2,1,0:T(8,128)(2,1)}, u32[]{:S(2)}, u32[]{:S(2)}) collective-permute-start(bf16[3,5,192,256]{3,2,1,0:T(8,128)(2,1)} %get-tuple-element.147), channel_id=1, source_target_pairs={{0,8},{4,12},{8,0},{12,4},{16,24},{20,28},{24,16},{28,20},{1,9},{5... | collective-permute-start | bytes 4423688 | tf_op jit(solution)/shard_map/ppermute | solution.py:63
  274.6 73.8 %collective-permute-start.9 = (bf16[512,1536]{1,0:T(8,128)(2,1)}, bf16[512,1536]{1,0:T(8,128)(2,1)}, u32[]{:S(2)}, u32[]{:S(2)}) collective-permute-start(bf16[512,1536]{1,0:T(8,128)(2,1)} %get-tuple-element.118), channel_id=1, source_target_pairs={{0,4},{4,0},{8,12},{12,8},{16,20},{20,16},{24,28},{28,24},{1,5},{5... | collective-permute-start | bytes 4718600 | tf_op jit(solution)/shard_map/ppermute | solution.py:60
  347.2 92.0 %collective-permute-start.21 = (bf16[3,5,192,256]{3,2,1,0:T(8,128)(2,1)}, bf16[3,5,192,256]{3,2,1,0:T(8,128)(2,1)}, u32[]{:S(2)}, u32[]{:S(2)}) collective-permute-start(bf16[3,5,192,256]{3,2,1,0:T(8,128)(2,1)} %add_convert_fusion.2), channel_id=1, source_target_pairs={{0,8},{4,12},{8,0},{12,4},{16,24},{20,28},{24,16},{28,20},{1,9},{5... | collective-permute-start | bytes 4423688 | tf_op jit(solution)/shard_map/ppermute | solution.py:63
  347.9 91.3 %collective-permute-start.22 = (bf16[3,5,192,256]{3,2,1,0:T(8,128)(2,1)}, bf16[3,5,192,256]{3,2,1,0:T(8,128)(2,1)}, u32[]{:S(2)}, u32[]{:S(2)}) collective-permute-start(bf16[3,5,192,256]{3,2,1,0:T(8,128)(2,1)} %add_convert_fusion), channel_id=1, source_target_pairs={{0,16},{4,20},{8,24},{12,28},{16,0},{20,4},{24,8},{28,12},{1,17},{... | collective-permute-start | bytes 4423688 | tf_op jit(solution)/shard_map/ppermute | solution.py:66
  354.0 93.1 %collective-permute-start.10 = (bf16[128,1536]{1,0:T(8,128)(2,1)}, bf16[128,1536]{1,0:T(8,128)(2,1)}, u32[]{:S(2)}, u32[]{:S(2)}) collective-permute-start(bf16[128,1536]{1,0:T(8,128)(2,1)} %get-tuple-element.231), channel_id=1, source_target_pairs={{0,3},{1,0},{2,1},{3,2},{4,7},{5,4},{6,5},{7,6},{8,11},{9,8},{10,9... | collective-permute-start | bytes 1179656 | tf_op jit(solution)/shard_map/ppermute | solution.py:73
  362.4 84.8 %collective-permute-start.11 = (bf16[128,1536]{1,0:T(8,128)(2,1)}, bf16[128,1536]{1,0:T(8,128)(2,1)}, u32[]{:S(2)}, u32[]{:S(2)}) collective-permute-start(bf16[128,1536]{1,0:T(8,128)(2,1)} %get-tuple-element.233), channel_id=1, source_target_pairs={{0,2},{1,3},{2,0},{3,1},{4,6},{5,7},{6,4},{7,5},{8,10},{9,11},{10,... | collective-permute-start | bytes 1179656 | tf_op jit(solution)/shard_map/ppermute | solution.py:73
  362.4 84.8 %collective-permute-start.12 = (bf16[128,1536]{1,0:T(8,128)(2,1)}, bf16[128,1536]{1,0:T(8,128)(2,1)}, u32[]{:S(2)}, u32[]{:S(2)}) collective-permute-start(bf16[128,1536]{1,0:T(8,128)(2,1)} %get-tuple-element.232), channel_id=1, source_target_pairs={{0,1},{1,2},{2,3},{3,0},{4,5},{5,6},{6,7},{7,4},{8,9},{9,10},{10,1... | collective-permute-start | bytes 1179656 | tf_op jit(solution)/shard_map/ppermute | solution.py:73
  441.4 21.4 %collective-permute-start.24 = (bf16[2,5,192,256]{3,2,1,0:T(8,128)(2,1)S(1)}, bf16[2,5,192,256]{3,2,1,0:T(8,128)(2,1)S(1)}, u32[]{:S(2)}, u32[]{:S(2)}) collective-permute-start(bf16[2,5,192,256]{3,2,1,0:T(8,128)(2,1)S(1)} %select_convert_fusion), channel_id=1, source_target_pairs={{0,4},{4,0},{8,12},{12,8},{16,20},{20,16},{24,28},{28,24},{1,5},{5... | collective-permute-start | bytes 2949128 | tf_op jit(solution)/shard_map/ppermute | solution.py:60
  450.8 11.3 %collective-permute-start.23 = (bf16[48,1536]{1,0:T(8,128)(2,1)S(1)}, bf16[48,1536]{1,0:T(8,128)(2,1)S(1)}, u32[]{:S(2)}, u32[]{:S(2)}) collective-permute-start(bf16[48,1536]{1,0:T(8,128)(2,1)S(1)} %convert_element_type.129), channel_id=1, source_target_pairs={{0,0},{4,1},{8,2},{12,3},{16,4},{20,5},{24,6},{28,7},{1,8},{5,9},{... | collective-permute-start | bytes 442376 | tf_op jit(solution)/shard_map/ppermute | solution.py:1222
  (34 other events, 676.5 us)

commit v4 on v3

--- a/solution.py
+++ b/solution.py
@@ -283,36 +283,35 @@
     )(*a2_blocks, grads, router_t, where, *pieces)
 
 
-def expert_grads_kernel(chips, depth, down_rows, where_ref, *refs):
+def expert_grads_kernel(plane_rows, depth, down_rows, where_ref, *refs):
     (a2_t0, a2_t1, hid0, hid1, grads0, grads1, dg0, dg1, du0, du1) = refs[:10]
-    outs, down_sum = refs[10 : 10 + 2 * chips], refs[10 + 2 * chips]
+    row_outs, mid_outs = refs[10 : 10 + plane_rows], refs[10 + plane_rows : 12 + plane_rows]
+    down_sum = refs[12 + plane_rows]
     model, width = a2_t0.shape[0], dg0.shape[1]
     down_sum[...] = (dot(hid0[0], grads0[...]) + dot(hid1[0], grads1[...])).astype(BF16)
-    for place in range(chips):
-        source = where_ref[place]
-        at = pl.ds(pl.multiple_of(source * 2 * depth, 32), 2 * depth)
-        left0, left1 = a2_t0[at, :], a2_t1[at, :]
-        gate = (dot(left0, dg0[...]) + dot(left1, dg1[...])).astype(BF16)
-        up = (dot(left0, du0[...]) + dot(left1, du1[...])).astype(BF16)
-        for part in range(2):
-            out = outs[2 * place + part]
-            out[0, 0] = gate[part * depth : (part + 1) * depth]
-            out[1, 0] = up[part * depth : (part + 1) * depth]
-            at = pl.ds(pl.multiple_of((source * 2 + part) * down_rows, 16), down_rows)
-            down = down_sum[at, :]
-            for j in range(model // width):
-                out[2, 0, j * down_rows : (j + 1) * down_rows, :] = down[
-                    :, j * width : (j + 1) * width
-                ]
-
-
-def expert_grads(where, first, second, plane_size):
+    for s in range(plane_rows):
+        for mid in range(2):
+            source = where_ref[2 * s + mid]
+            at = pl.ds(pl.multiple_of(source * 2 * depth, 32), 2 * depth)
+            left0, left1 = a2_t0[at, :], a2_t1[at, :]
+            gate = (dot(left0, dg0[...]) + dot(left1, dg1[...])).astype(BF16)
+            up = (dot(left0, du0[...]) + dot(left1, du1[...])).astype(BF16)
+            for part, out in ((0, row_outs[s].at[mid]), (1, mid_outs[mid].at[s])):
+                out[0, 0] = gate[part * depth : (part + 1) * depth]
+                out[1, 0] = up[part * depth : (part + 1) * depth]
+                at = pl.ds(pl.multiple_of((source * 2 + part) * down_rows, 16), down_rows)
+                down = down_sum[at, :]
+                for j in range(model // width):
+                    out[2, 0, j * down_rows : (j + 1) * down_rows, :] = down[
+                        :, j * width : (j + 1) * width
+                    ]
+
+
+def expert_grads(where, first, second, plane_size, plane_rows):
     model, seq = first[0].shape
     local, width = first[1].shape[:2]
-    chips = plane_size // 2
     depth, down_rows = model // plane_size, width // plane_size
-    out = shape_of((3, local, depth, width), BF16)
-    block = pl.BlockSpec((3, 1, depth, width), lambda e: (0, e, 0, 0))
+    counts = [2] * plane_rows + [plane_rows] * 2
     once = lambda dims: pl.BlockSpec(dims, lambda e: (0, 0), pipeline_mode=pl.Buffered(1))
     specs = [
         once((model, seq)),
@@ -323,11 +322,13 @@
     ]
     operands = [v for pair in zip(first, second) for v in pair]
     return pl.pallas_call(
-        functools.partial(expert_grads_kernel, chips, depth, down_rows),
+        functools.partial(expert_grads_kernel, plane_rows, depth, down_rows),
         grid=(local,),
         in_specs=[SMEM] + [spec for spec in specs for _ in range(2)],
-        out_specs=[block] * (2 * chips),
-        out_shape=[out] * (2 * chips),
+        out_specs=[
+            pl.BlockSpec((n, 3, 1, depth, width), lambda e: (0, 0, e, 0, 0)) for n in counts
+        ],
+        out_shape=[shape_of((n, 3, local, depth, width), BF16) for n in counts],
         scratch_shapes=[pltpu.VMEM((width, model), BF16)],
         compiler_params=params(),
         name="expert_grads",
@@ -1140,21 +1141,18 @@
         dx_all[b * rows : (b + 1) * rows].astype(F32 if b == 0 else BF16) for b in range(ranks)
     ]
     dx_got = expert_scatter(dxs)
-    order = [(s, mid) for s in reversed(range(plane.rows)) for mid in (1, 0)]
     chips = [
-        ((plane.row + s) % plane.rows) * 2 + (plane.mid + mid) % 2 for s, mid in order
+        ((plane.row + s) % plane.rows) * 2 + (plane.mid + mid) % 2
+        for s in range(plane.rows)
+        for mid in range(2)
     ]
     own_kept.insert(2, grads[:, :model])
     other_kept.insert(2, other_grads[:, :model])
     flat = expert_grads(
-        jnp.stack(chips).astype(jnp.int32), own_kept, other_kept, plane.size
+        jnp.stack(chips).astype(jnp.int32), own_kept, other_kept, plane.size, plane.rows
     )
     dx_got, flat = lax.optimization_barrier((dx_got, flat))
-    summed = {
-        (s, mid, part): flat[2 * i + part]
-        for i, (s, mid) in enumerate(order)
-        for part in range(2)
-    }
+    by_row, by_mid = flat[: plane.rows], flat[plane.rows :]
 
     def add(first, *others):
         value = first.astype(F32)
@@ -1163,12 +1161,19 @@
         return value.astype(BF16)
 
     steps = range(1, plane.rows)
-    a_first = [[plane.next_row(summed[s, mid, 0], s) for s in steps] for mid in range(2)]
-    b_first = [plane.other_mid(summed[s, 1, 1]) for s in range(plane.rows)]
+    a_first = [plane.next_row(by_row[s], s) for s in steps]
+    b_first = plane.other_mid(by_mid[1])
 
     dh, dh_stack, extra = rejoin(
         [dxs[0]] + dx_got, gates, mid_rows, cotangent, extra_t, a2, gain_two_row, plane.size
     )
+    other_out = plane.other_core(other_out)
+    dh_stack, other_out, out_all = lax.optimization_barrier((dh_stack, other_out, out_all))
+    out_all = out_all + other_out.astype(F32)
+    outs = [out_all[b * rows : (b + 1) * rows] for b in range(ranks)]
+    outs = [outs[0]] + [v.astype(BF16) for v in outs[1:]]
+    dh_stack, outs = lax.optimization_barrier((dh_stack, outs))
+    out_got = expert_scatter(outs)
 
     d_weights, d_out_weights, da1 = attend_back(
         dh_stack,
@@ -1183,9 +1188,11 @@
         kv_heads,
         gain_one_row,
     )
-    a_first, b_first, d_weights = lax.optimization_barrier((a_first, b_first, d_weights))
-    a_sums = [add(summed[0, mid, 0], *a_first[mid]) for mid in range(2)]
-    b_sums = [add(summed[s, 0, 1], b_first[s]) for s in range(plane.rows)]
+    a_first, b_first, d_weights, out_got = lax.optimization_barrier(
+        (a_first, b_first, d_weights, out_got)
+    )
+    a_sums = [add(by_row[0][mid], *[v[mid] for v in a_first]) for mid in range(2)]
+    b_sums = [add(by_mid[0][s], b_first[s]) for s in range(plane.rows)]
     a_sums, b_sums, d_weights = lax.optimization_barrier((a_sums, b_sums, d_weights))
     a_got = plane.other_mid(a_sums[1])
     b_got = [plane.next_row(b_sums[s], s) for s in steps]
@@ -1213,10 +1220,8 @@
     gate_grad, up_grad, down_grad = finish(
         core, a_sums[0], a_got, b_kept, b_got, other, w_down.shape[1], model, plane.size
     )
-    out_all = out_all + plane.other_core(other_out).astype(F32)
-    outs = [out_all[b * rows : (b + 1) * rows] for b in range(ranks)]
     output = mid_rows + outs[0]
-    for v in expert_scatter([v.astype(BF16) for v in outs]):
+    for v in out_got:
         output = output + v.astype(F32)
 
     w_output_grad = lax.ppermute(

time: 483 us -> 457 us (0.946)
  starting transfers between devices: 42.8 us -> 29 us
  Pallas kernels: 366 us -> 353 us
  waiting for transfers between devices: 9.71 us -> 19.1 us
    ppermute x6, waiting for transfers between devices: 4.22 us -> 14.1 us  [expert_shift(): lax.ppermute(x, 'expert', [(i, (i + step) % count) for i in range(count)])]
    pallas_call x1, Pallas kernels: 74.7 us -> 65.1 us  [last(): pl.pallas_call(functools.partial(last_kernel, ranks, 2 * chips), in_specs...]
    ppermute x6, starting transfers between devices: 13.7 us -> 6.81 us  [expert_shift(): lax.ppermute(x, 'expert', [(i, (i + step) % count) for i in range(count)])]
    ppermute x5, starting transfers between devices: 11.3 us -> 5.36 us  [other_core(): return lax.ppermute(x, 'fsdp', [(i, i ^ 1) for i in range(self.size)])]
    ppermute x6 -> x5, starting transfers between devices: 9.93 us -> 9.15 us  [other_mid(): return lax.ppermute(x, 'fsdp', [(i, i ^ 2) for i in range(self.size)])]
    convert_element_type x4 -> x2, other arithmetic: 9.41 us -> 9.76 us  [add(): return value.astype(BF16)]
  transfers between devices with their start and end apart: 25 -> 23, of which waited for: 2 -> 3; matrix products, arithmetic and copies ran while one was open for 9% -> 6% of each run, Pallas kernels for 69% -> 69%
where the time goes in v4:
time: 457 us; the launch traced here: 451 us
  Pallas kernels  353 us (77%)
  other arithmetic  29.9 us (7%)
  starting transfers between devices  29 us (6%)
  waiting for transfers between devices  19.1 us (4%)
  local copies, waits for them, and re-layouts  19 us (4%)
    pallas_call x1, Pallas kernels, attend(): pl.pallas_call(functools.partial(attend_kernel, ranks, plane_size, kv_hea...  74.6 us
    pallas_call x1, Pallas kernels, gather_weights(): pl.pallas_call(functools.partial(gather_weights_kernel, ranks, plane_size...  72.2 us
    pallas_call x1, Pallas kernels, last(): pl.pallas_call(functools.partial(last_kernel, ranks, 2 * chips), in_specs...  65.1 us
    pallas_call x2, Pallas kernels, experts(): pl.pallas_call(functools.partial(experts_kernel, blocks, len(pieces), pla...  53.5 us
    pallas_call x1, Pallas kernels, rejoin(): pl.pallas_call(functools.partial(rejoin_kernel, ranks, plane_size, gain_r...  38.5 us
    pallas_call x1, Pallas kernels, expert_grads(): pl.pallas_call(functools.partial(expert_grads_kernel, plane_rows, depth,...  18.5 us
    pallas_call x1, Pallas kernels, attend_back(): pl.pallas_call(functools.partial(attend_back_kernel, blocks, kv_heads, ga...  15.4 us
    ppermute x6, waiting for transfers between devices, expert_shift(): lax.ppermute(x, 'expert', [(i, (i + step) % count) for i in range(count)])  14.1 us
  transfers between devices with their start and end apart: 23, of which 3 were waited for; matrix products, arithmetic and copies ran while one was open for 6% of the time, Pallas kernels for 69%

profile of v4, /device:TPU:27, one launch (start us, length us, event | category | flops | bytes accessed | tf_op | source)
XLA Modules:
  0.0 451.3 jit_solution(5540969074703332011)
XLA Ops:
  0.7 6.9 %pack_experts.1 = (bf16[2,5,192,256]{3,2,1,0:T(8,128)(2,1)}, bf16[2,5,192,256]{3,2,1,0:T(8,128)(2,1)}, bf16[2,5,192,256]{3,2,1,0:T(8,128)(2,1)}) custom-call(s32[1]{0:T(128)} %bitcast.3.core, f32[5,192,512]{2,1,0:T(8,128)} %gate.1, f32[5,192,512]{2,1,0:T(8,128)} %up.1, f32[5,64,1536]{2,1,0:T(8,128)} %down.1), custom_call_target="tpu_custom_call" | custom-call | tf_op jit(solution)/shard_map/pack_experts/pallas_call | solution.py:110
  8.3 2.9 collective-permute-start.1
  16.7 5.4 %collective-permute-start.2 = (bf16[3,5,192,256]{3,2,1,0:T(8,128)(2,1)S(1)}, bf16[3,5,192,256]{3,2,1,0:T(8,128)(2,1)}, u32[]{:S(2)}, u32[]{:S(2)}) collective-permute-start(bf16[3,5,192,256]{3,2,1,0:T(8,128)(2,1)S(1)} %get-tuple-element.107.refs_4_), channel_id=1, source_target_pairs={{0,8},{4,12},{8,0},{12,4},{16,24},{20,28},{24,16},{28,20},{1,9},{5... | collective-permute-start | bytes 4423688 | tf_op jit(solution)/shard_map/ppermute | solution.py:63
  24.2 72.2 %gather_weights.1 = (bf16[8,4,48,768]{3,2,1,0:T(8,128)(2,1)}, bf16[8,48,1536]{2,1,0:T(8,128)(2,1)}, bf16[4,128,1536]{2,1,0:T(8,128)(2,1)}, bf16[4,128,1664]{2,1,0:T(8,128)(2,1)}) custom-call(bf16[4,48,768]{2,1,0:T(8,128)(2,1)} %maximum_bitcast_fusion.by_rank, bf16[48,1536]{1,0:T(8,128)(2,1)} %copy-done.25, bf16[128,1536]{1,0:T(8,128)(2,1)} %multiply_convert_fusion.x_in, ...), custom_call_target="tpu_custom_call" | custom-call | tf_op jit(solution)/shard_map/gather_weights/pallas_call | solution.py:613
  106.6 74.6 %attend.1 = (bf16[512,1536]{1,0:T(8,128)(2,1)}, bf16[512,512]{1,0:T(8,128)(2,1)}, bf16[512,128]{1,0:T(8,128)(2,1)}, bf16[512,384]{1,0:T(8,128)(2,1)}, f32[6,512]...) custom-call(bf16[4,128,1536]{2,1,0:T(8,128)(2,1)} %get-tuple-element, ...), custom_call_target="tpu_custom_call" | custom-call | tf_op jit(solution)/shard_map/attend/pallas_call | solution.py:799
  181.2 26.1 %experts.3 = (bf16[512,1536]{1,0:T(8,128)(2,1)}, bf16[512,1664]{1,0:T(8,128)(2,1)}, f32[128,128]{1,0:T(8,128)}, bf16[1536,512]{1,0:T(8,128)(2,1)}, bf16[5,256,51...) custom-call(bf16[512,1536]{1,0:T(8,128)(2,1)} %bitcast.78, ...), custom_call_target="tpu_custom_call" | custom-call | tf_op jit(solution)/shard_map/experts/pallas_call | solution.py:261
  207.6 27.4 %experts.2 = (f32[512,1536]{1,0:T(8,128)}, f32[512,1664]{1,0:T(8,128)}, f32[128,128]{1,0:T(8,128)}, bf16[1536,512]{1,0:T(8,128)(2,1)}, bf16[5,256,512]{2,1,0:T(8...) custom-call(bf16[512,1536]{1,0:T(8,128)(2,1)} %bitcast.77, bf16[512,1664]{1,0:T(8,128)(2,1)} %bitcast.72, ...), custom_call_target="tpu_custom_call" | custom-call | tf_op jit(solution)/shard_map/experts/pallas_call | solution.py:261
  235.0 4.1 fusion.18
  240.1 2.4 collective-permute-start.11
  246.1 2.6 slice.150.refs_5_
  248.7 18.5 %expert_grads.1 = (bf16[2,3,5,192,256]{4,3,2,1,0:T(8,128)(2,1)}, bf16[2,3,5,192,256]{4,3,2,1,0:T(8,128)(2,1)}, bf16[2,3,5,192,256]{4,3,2,1,0:T(8,128)(2,1)}, bf16[2,3,5,192,256]{4,3,2,1,0:T(8,128)(2,1)}) custom-call(s32[4]{0:T(128)} %pad_add_fusion.where_ref, bf16[1536,512]{1,0:T(8,128)(2,1)} %get-tuple-element.122.refs_0_, ...), custom_call_target="tpu_custom_call" | custom-call | tf_op jit(solution)/shard_map/expert_grads/pallas_call | solution.py:324
  267.2 3.3 collective-permute-done.11.refs_2_
  271.8 2.1 slice.145.refs_0_
  273.9 38.5 %rejoin.1 = (f32[128,1536]{1,0:T(8,128)}, bf16[4,128,1536]{2,1,0:T(8,128)(2,1)}, f32[128,1536]{1,0:T(8,128)}) custom-call(f32[128,128]{1,0:T(8,128)} %get-tuple-element.117.gates, f32[128,1536]{1,0:T(8,128)} %get-tuple-element.112.h, f32[128,1536]{1,0:T(8,128)} %dz.1, bf16[128,1536]{1,0:T(8,128)(2,1)} %bitcast.70, bf16[128,1536]{1,0:T(8,128)(2,1)} %get-tuple-element.118.a2, ...), custom_call_target="tpu_custom_call" | custom-call | tf_op jit(solution)/shard_map/rejoin/pallas_call | solution.py:861
  314.6 3.2 collective-permute-start.17
  318.1 15.4 %attend_back.1 = (bf16[1536,768]{1,0:T(8,128)(2,1)}, bf16[384,1536]{1,0:T(8,128)(2,1)}, f32[128,1536]{1,0:T(8,128)}, bf16[128,1536]{1,0:T(8,128)(2,1)}, bf16[128...) custom-call(bf16[4,128,1536]{2,1,0:T(8,128)(2,1)} %get-tuple-element.146.refs_0_, ...), custom_call_target="tpu_custom_call" | custom-call | tf_op jit(solution)/shard_map/attend_back/pallas_call | solution.py:446
  333.5 10.7 %collective-permute-done.17 = bf16[128,1536]{1,0:T(8,128)(2,1)S(1)} collective-permute-done((bf16[128,1536]{1,0:T(8,128)(2,1)S(1)}, bf16[128,1536]{1,0:T(8,128)(2,1)S(1)}, u32[]{:S(2)}, u32[]{:S(2)}) %collective-permute-start.17) | collective-permute-done | bytes 393248 | tf_op jit(solution)/shard_map/ppermute | solution.py:73
  345.1 5.1 %fusion.3 = (bf16[3,5,192,256]{3,2,1,0:T(8,128)(2,1)}, bf16[3,5,192,256]{3,2,1,0:T(8,128)(2,1)S(1)}) fusion(bf16[2,3,5,192,256]{4,3,2,1,0:T(8,128)(2,1)} %collective-permute-done.15, bf16[2,3,5,192,256]{4,3,2,1,0:T(8,128)(2,1)} %get-tuple-element.164), kind=kLoop, calls=%fused_computation.10 | loop fusion | flops 5898240 | bytes 8847360 | tf_op jit(solution)/shard_map/convert_element_type | solution.py:1161
  350.3 4.6 %fusion.1 = (bf16[3,5,192,256]{3,2,1,0:T(8,128)(2,1)}, bf16[3,5,192,256]{3,2,1,0:T(8,128)(2,1)S(1)}) fusion(bf16[2,3,5,192,256]{4,3,2,1,0:T(8,128)(2,1)} %collective-permute-done.14, bf16[2,3,5,192,256]{4,3,2,1,0:T(8,128)(2,1)S(1)} %copy-done.10), kind=kLoop, calls=%fused_computation.8 | loop fusion | flops 5898240 | bytes 8847360 | tf_op jit(solution)/shard_map/convert_element_type | solution.py:1161
  356.6 65.1 %last.1 = (f32[128,1536]{1,0:T(8,128)}, bf16[4,48,768]{2,1,0:T(8,128)(2,1)}, f32[48,1536]{1,0:T(8,128)}) custom-call(f32[128,1536]{1,0:T(8,128)} %x.1, f32[128,1536]{1,0:T(8,128)} %get-tuple-element.161.dh, f32[1,1536]{1,0:T(1,128)} %get-tuple-element.246.refs_1_.gain, bf16[4,2,4,48,768]{4,3,2,1,0:T(8,128)(2,1)} %bitcast.76, ...), custom_call_target="tpu_custom_call" | custom-call | tf_op jit(solution)/shard_map/last/pallas_call | solution.py:959
  422.9 3.1 select_convert_fusion
  429.2 2.7 collective-permute-start.21
  435.3 5.0 %collective-permute-done.21 = bf16[48,1536]{1,0:T(8,128)(2,1)S(1)} collective-permute-done((bf16[48,1536]{1,0:T(8,128)(2,1)S(1)}, bf16[48,1536]{1,0:T(8,128)(2,1)S(1)}, u32[]{:S(2)}, u32[]{:S(2)}) %collective-permute-start.21) | collective-permute-done | bytes 147488 | tf_op jit(solution)/shard_map/ppermute | solution.py:1227
  442.1 7.9 %finish.1 = (f32[5,192,512]{2,1,0:T(8,128)}, f32[5,192,512]{2,1,0:T(8,128)}, f32[5,64,1536]{2,1,0:T(8,128)}) custom-call(s32[1]{0:T(128)} %bitcast.3.core, bf16[3,5,192,256]{3,2,1,0:T(8,128)(2,1)} %copy-done.4, bf16[3,5,192,256]{3,2,1,0:T(8,128)(2,1)} %collective-permute-done.19.got_a, bf16[3,5,192,256]{3,2,1,0:T(8,128)(2,1)} %copy-done.3, ...), custom_call_target="tpu_custom_call" | custom-call | tf_op jit(solution)/shard_map/finish/pallas_call | solution.py:368
  (158 shorter events, 39.6 us)
Async XLA Ops:
  7.6 8.3 %collective-permute-start = (bf16[2,5,192,256]{3,2,1,0:T(8,128)(2,1)}, bf16[2,5,192,256]{3,2,1,0:T(8,128)(2,1)S(1)}, u32[]{:S(2)}, u32[]{:S(2)}) collective-permute-start(bf16[2,5,192,256]{3,2,1,0:T(8,128)(2,1)} %get-tuple-element.100), channel_id=1, source_target_pairs={{0,4},{4,0},{8,12},{12,8},{16,20},{20,16},{24,28},{28,24},{1,5},{5... | collective-permute-start | bytes 2949128 | tf_op jit(solution)/shard_map/ppermute | solution.py:60
  8.3 8.3 %collective-permute-start.1 = (bf16[48,1536]{1,0:T(8,128)(2,1)S(1)}, bf16[48,1536]{1,0:T(8,128)(2,1)S(1)}, u32[]{:S(2)}, u32[]{:S(2)}) collective-permute-start(bf16[48,1536]{1,0:T(8,128)(2,1)S(1)} %convert_element_type.125), channel_id=1, source_target_pairs={{0,0},{1,4},{2,8},{3,12},{4,16},{5,20},{6,24},{7,28},{8,1},{9,5},{... | collective-permute-start | bytes 442376 | tf_op jit(solution)/shard_map/ppermute | solution.py:1058
  16.7 81.2 %copy-start.1 = (bf16[3,5,192,256]{3,2,1,0:T(8,128)(2,1)}, bf16[3,5,192,256]{3,2,1,0:T(8,128)(2,1)S(1)}, u32[]{:S(2)}) copy-start(bf16[3,5,192,256]{3,2,1,0:T(8,128)(2,1)S(1)} %get-tuple-element.108.refs_5_) | copy-start | bytes 4423684
  16.7 82.3 %collective-permute-start.2 = (bf16[3,5,192,256]{3,2,1,0:T(8,128)(2,1)S(1)}, bf16[3,5,192,256]{3,2,1,0:T(8,128)(2,1)}, u32[]{:S(2)}, u32[]{:S(2)}) collective-permute-start(bf16[3,5,192,256]{3,2,1,0:T(8,128)(2,1)S(1)} %get-tuple-element.107.refs_4_), channel_id=1, source_target_pairs={{0,8},{4,12},{8,0},{12,4},{16,24},{20,28},{24,16},{28,20},{1,9},{5... | collective-permute-start | bytes 4423688 | tf_op jit(solution)/shard_map/ppermute | solution.py:63
  22.1 76.9 %collective-permute-start.3 = (bf16[3,5,192,256]{3,2,1,0:T(8,128)(2,1)S(1)}, bf16[3,5,192,256]{3,2,1,0:T(8,128)(2,1)}, u32[]{:S(2)}, u32[]{:S(2)}) collective-permute-start(bf16[3,5,192,256]{3,2,1,0:T(8,128)(2,1)S(1)} %get-tuple-element.108.refs_5_), channel_id=1, source_target_pairs={{0,16},{4,20},{8,24},{12,28},{16,0},{20,4},{24,8},{28,12},{1,17},{... | collective-permute-start | bytes 4423688 | tf_op jit(solution)/shard_map/ppermute | solution.py:66
  96.3 84.9 %collective-permute-start.8 = (bf16[512,1664]{1,0:T(8,128)(2,1)}, bf16[512,1664]{1,0:T(8,128)(2,1)}, u32[]{:S(2)}, u32[]{:S(2)}) collective-permute-start(bf16[512,1664]{1,0:T(8,128)(2,1)} %bitcast.71), channel_id=1, source_target_pairs={{0,4},{4,0},{8,12},{12,8},{16,20},{20,16},{24,28},{28,24},{1,5},{5... | collective-permute-start | bytes 5111816 | tf_op jit(solution)/shard_map/ppermute | solution.py:60
  97.8 83.4 %collective-permute-start.4 = (bf16[3,5,192,256]{3,2,1,0:T(8,128)(2,1)S(1)}, bf16[3,5,192,256]{3,2,1,0:T(8,128)(2,1)}, u32[]{:S(2)}, u32[]{:S(2)}) collective-permute-start(bf16[3,5,192,256]{3,2,1,0:T(8,128)(2,1)S(1)} %get-tuple-element.107.refs_4_), channel_id=1, source_target_pairs={{0,16},{4,20},{8,24},{12,28},{16,0},{20,4},{24,8},{28,12},{1,17},{... | collective-permute-start | bytes 4423688 | tf_op jit(solution)/shard_map/ppermute | solution.py:66
  97.9 83.3 %collective-permute-start.6 = (bf16[3,5,192,256]{3,2,1,0:T(8,128)(2,1)S(1)}, bf16[3,5,192,256]{3,2,1,0:T(8,128)(2,1)}, u32[]{:S(2)}, u32[]{:S(2)}) collective-permute-start(bf16[3,5,192,256]{3,2,1,0:T(8,128)(2,1)S(1)} %get-tuple-element.108.refs_5_), channel_id=1, source_target_pairs={{0,8},{4,12},{8,0},{12,4},{16,24},{20,28},{24,16},{28,20},{1,9},{5... | collective-permute-start | bytes 4423688 | tf_op jit(solution)/shard_map/ppermute | solution.py:63
  99.0 82.3 %collective-permute-start.5 = (bf16[3,5,192,256]{3,2,1,0:T(8,128)(2,1)}, bf16[3,5,192,256]{3,2,1,0:T(8,128)(2,1)}, u32[]{:S(2)}, u32[]{:S(2)}) collective-permute-start(bf16[3,5,192,256]{3,2,1,0:T(8,128)(2,1)} %collective-permute-done.2.refs_6_), channel_id=1, source_target_pairs={{0,16},{4,20},{8,24},{12,28},{16,0},{20,4},{24,8},{28,12},{1,17},{... | collective-permute-start | bytes 4423688 | tf_op jit(solution)/shard_map/ppermute | solution.py:66
  99.4 81.8 %collective-permute-start.7 = (bf16[3,5,192,256]{3,2,1,0:T(8,128)(2,1)}, bf16[3,5,192,256]{3,2,1,0:T(8,128)(2,1)}, u32[]{:S(2)}, u32[]{:S(2)}) collective-permute-start(bf16[3,5,192,256]{3,2,1,0:T(8,128)(2,1)} %collective-permute-done.3.refs_7_), channel_id=1, source_target_pairs={{0,8},{4,12},{8,0},{12,4},{16,24},{20,28},{24,16},{28,20},{1,9},{5... | collective-permute-start | bytes 4423688 | tf_op jit(solution)/shard_map/ppermute | solution.py:63
  207.4 27.6 %collective-permute-start.9 = (bf16[512,1664]{1,0:T(8,128)(2,1)}, bf16[512,1664]{1,0:T(8,128)(2,1)S(1)}, u32[]{:S(2)}, u32[]{:S(2)}) collective-permute-start(bf16[512,1664]{1,0:T(8,128)(2,1)} %get-tuple-element.121), channel_id=1, source_target_pairs={{0,4},{4,0},{8,12},{12,8},{16,20},{20,16},{24,28},{28,24},{1,5},{5... | collective-permute-start | bytes 5111816 | tf_op jit(solution)/shard_map/ppermute | solution.py:60
  240.1 27.2 %collective-permute-start.10 = (bf16[128,1664]{1,0:T(8,128)(2,1)}, bf16[128,1664]{1,0:T(8,128)(2,1)S(1)}, u32[]{:S(2)}, u32[]{:S(2)}) collective-permute-start(bf16[128,1664]{1,0:T(8,128)(2,1)} %get-tuple-element.236), channel_id=1, source_target_pairs={{0,3},{1,0},{2,1},{3,2},{4,7},{5,4},{6,5},{7,6},{8,11},{9,8},{10,9... | collective-permute-start | bytes 1277960 | tf_op jit(solution)/shard_map/ppermute | solution.py:73
  240.1 30.5 %collective-permute-start.11 = (bf16[128,1664]{1,0:T(8,128)(2,1)}, bf16[128,1664]{1,0:T(8,128)(2,1)S(1)}, u32[]{:S(2)}, u32[]{:S(2)}) collective-permute-start(bf16[128,1664]{1,0:T(8,128)(2,1)} %get-tuple-element.235), channel_id=1, source_target_pairs={{0,2},{1,3},{2,0},{3,1},{4,6},{5,7},{6,4},{7,5},{8,10},{9,11},{10,... | collective-permute-start | bytes 1277960 | tf_op jit(solution)/shard_map/ppermute | solution.py:73
  242.5 28.1 %collective-permute-start.12 = (bf16[128,1664]{1,0:T(8,128)(2,1)S(1)}, bf16[128,1664]{1,0:T(8,128)(2,1)S(1)}, u32[]{:S(2)}, u32[]{:S(2)}) collective-permute-start(bf16[128,1664]{1,0:T(8,128)(2,1)S(1)} %get-tuple-element.234), channel_id=1, source_target_pairs={{0,1},{1,2},{2,3},{3,0},{4,5},{5,6},{6,7},{7,4},{8,9},{9,10},{10,1... | collective-permute-start | bytes 1277960 | tf_op jit(solution)/shard_map/ppermute | solution.py:73
  243.3 69.1 %collective-permute-start.13 = (bf16[512,1536]{1,0:T(8,128)(2,1)}, bf16[512,1536]{1,0:T(8,128)(2,1)}, u32[]{:S(2)}, u32[]{:S(2)}) collective-permute-start(bf16[512,1536]{1,0:T(8,128)(2,1)} %get-tuple-element.138), channel_id=1, source_target_pairs={{0,4},{4,0},{8,12},{12,8},{16,20},{20,16},{24,28},{28,24},{1,5},{5... | collective-permute-start | bytes 4718600 | tf_op jit(solution)/shard_map/ppermute | solution.py:60
  270.6 73.7 %collective-permute-start.14 = (bf16[2,3,5,192,256]{4,3,2,1,0:T(8,128)(2,1)}, bf16[2,3,5,192,256]{4,3,2,1,0:T(8,128)(2,1)}, u32[]{:S(2)}, u32[]{:S(2)}) collective-permute-start(bf16[2,3,5,192,256]{4,3,2,1,0:T(8,128)(2,1)} %get-tuple-element.144), channel_id=1, source_target_pairs={{0,16},{4,20},{8,24},{12,28},{16,0},{20,4},{24,8},{28,12},{1,17},{... | collective-permute-start | bytes 8847368 | tf_op jit(solution)/shard_map/ppermute | solution.py:66
  271.3 73.0 %collective-permute-start.15 = (bf16[2,3,5,192,256]{4,3,2,1,0:T(8,128)(2,1)}, bf16[2,3,5,192,256]{4,3,2,1,0:T(8,128)(2,1)}, u32[]{:S(2)}, u32[]{:S(2)}) collective-permute-start(bf16[2,3,5,192,256]{4,3,2,1,0:T(8,128)(2,1)} %get-tuple-element.145), channel_id=1, source_target_pairs={{0,8},{4,12},{8,0},{12,4},{16,24},{20,28},{24,16},{28,20},{1,9},{5... | collective-permute-start | bytes 8847368 | tf_op jit(solution)/shard_map/ppermute | solution.py:63
  314.6 18.9 %collective-permute-start.16 = (bf16[128,1536]{1,0:T(8,128)(2,1)S(1)}, bf16[128,1536]{1,0:T(8,128)(2,1)S(1)}, u32[]{:S(2)}, u32[]{:S(2)}) collective-permute-start(bf16[128,1536]{1,0:T(8,128)(2,1)S(1)} %get-tuple-element.155), channel_id=1, source_target_pairs={{0,3},{1,0},{2,1},{3,2},{4,7},{5,4},{6,5},{7,6},{8,11},{9,8},{10,9... | collective-permute-start | bytes 1179656 | tf_op jit(solution)/shard_map/ppermute | solution.py:73
  314.6 29.6 %collective-permute-start.17 = (bf16[128,1536]{1,0:T(8,128)(2,1)S(1)}, bf16[128,1536]{1,0:T(8,128)(2,1)S(1)}, u32[]{:S(2)}, u32[]{:S(2)}) collective-permute-start(bf16[128,1536]{1,0:T(8,128)(2,1)S(1)} %get-tuple-element.156), channel_id=1, source_target_pairs={{0,2},{1,3},{2,0},{3,1},{4,6},{5,7},{6,4},{7,5},{8,10},{9,11},{10,... | collective-permute-start | bytes 1179656 | tf_op jit(solution)/shard_map/ppermute | solution.py:73
  317.8 26.4 %collective-permute-start.18 = (bf16[128,1536]{1,0:T(8,128)(2,1)S(1)}, bf16[128,1536]{1,0:T(8,128)(2,1)S(1)}, u32[]{:S(2)}, u32[]{:S(2)}) collective-permute-start(bf16[128,1536]{1,0:T(8,128)(2,1)S(1)} %get-tuple-element.157), channel_id=1, source_target_pairs={{0,1},{1,2},{2,3},{3,0},{4,5},{5,6},{6,7},{7,4},{8,9},{9,10},{10,1... | collective-permute-start | bytes 1179656 | tf_op jit(solution)/shard_map/ppermute | solution.py:73
  354.9 67.9 %collective-permute-start.19 = (bf16[3,5,192,256]{3,2,1,0:T(8,128)(2,1)}, bf16[3,5,192,256]{3,2,1,0:T(8,128)(2,1)}, u32[]{:S(2)}, u32[]{:S(2)}) collective-permute-start(bf16[3,5,192,256]{3,2,1,0:T(8,128)(2,1)} %get-tuple-element.175), channel_id=1, source_target_pairs={{0,8},{4,12},{8,0},{12,4},{16,24},{20,28},{24,16},{28,20},{1,9},{5... | collective-permute-start | bytes 4423688 | tf_op jit(solution)/shard_map/ppermute | solution.py:63
  355.8 67.0 %collective-permute-start.20 = (bf16[3,5,192,256]{3,2,1,0:T(8,128)(2,1)}, bf16[3,5,192,256]{3,2,1,0:T(8,128)(2,1)}, u32[]{:S(2)}, u32[]{:S(2)}) collective-permute-start(bf16[3,5,192,256]{3,2,1,0:T(8,128)(2,1)} %get-tuple-element.176), channel_id=1, source_target_pairs={{0,16},{4,20},{8,24},{12,28},{16,0},{20,4},{24,8},{28,12},{1,17},{... | collective-permute-start | bytes 4423688 | tf_op jit(solution)/shard_map/ppermute | solution.py:66
  426.0 15.1 %collective-permute-start.22 = (bf16[2,5,192,256]{3,2,1,0:T(8,128)(2,1)}, bf16[2,5,192,256]{3,2,1,0:T(8,128)(2,1)S(1)}, u32[]{:S(2)}, u32[]{:S(2)}) collective-permute-start(bf16[2,5,192,256]{3,2,1,0:T(8,128)(2,1)} %select_convert_fusion), channel_id=1, source_target_pairs={{0,4},{4,0},{8,12},{12,8},{16,20},{20,16},{24,28},{28,24},{1,5},{5... | collective-permute-start | bytes 2949128 | tf_op jit(solution)/shard_map/ppermute | solution.py:60
  429.2 11.1 %collective-permute-start.21 = (bf16[48,1536]{1,0:T(8,128)(2,1)S(1)}, bf16[48,1536]{1,0:T(8,128)(2,1)S(1)}, u32[]{:S(2)}, u32[]{:S(2)}) collective-permute-start(bf16[48,1536]{1,0:T(8,128)(2,1)S(1)} %convert_element_type.153), channel_id=1, source_target_pairs={{0,0},{4,1},{8,2},{12,3},{16,4},{20,5},{24,6},{28,7},{1,8},{5,9},{... | collective-permute-start | bytes 442376 | tf_op jit(solution)/shard_map/ppermute | solution.py:1227
  (30 other events, 546.9 us)

commit v5 on v4

--- a/solution.py
+++ b/solution.py
@@ -42,6 +42,10 @@
     return jax.ShapeDtypeStruct(tuple(dims), dtype)
 
 
+def lasting(us):
+    return pl.CostEstimate(flops=us * 10**9, bytes_accessed=us * 10**6, transcendentals=0)
+
+
 def params(**kw):
     return pltpu.CompilerParams(vmem_limit_bytes=60 * 1024 * 1024, **kw)
 
@@ -84,38 +88,6 @@
     column = lax.broadcasted_iota(jnp.int32, (width // 2, width), 1)
     want = (2 * (line // n) + part) * n + line % n
     return jnp.where(column == want, 1.0, 0.0).astype(dtype)
-
-
-def pack_kernel(blocks, core, gate, up, down, keep, send, halves):
-    width = gate.shape[2]
-    mine = chooser(width, blocks, core[0])
-    theirs = chooser(width, blocks, 1 - core[0])
-    for place, ref in ((0, gate), (1, up)):
-        value = ref[0].astype(BF16)
-        keep[place, 0] = dot_nt(value, mine).astype(BF16)
-        send[place, 0] = dot_nt(value, theirs).astype(BF16)
-    value = down[0].astype(BF16)
-    rows, wide = value.shape[0] // 2, width // 2
-    for part in range(2):
-        for j in range(value.shape[1] // wide):
-            halves[part, 0, j * rows : (j + 1) * rows] = value[
-                part * rows : (part + 1) * rows, j * wide : (j + 1) * wide
-            ]
-
-
-def pack_experts(core, w_gate, w_up, w_down, blocks):
-    local, depth, width = w_gate.shape
-    out = shape_of((2, local, depth, width // 2), BF16)
-    block = pl.BlockSpec((2, 1, depth, width // 2), lambda e: (0, e, 0, 0))
-    return pl.pallas_call(
-        functools.partial(pack_kernel, blocks),
-        grid=(local,),
-        in_specs=[SMEM]
-        + [pl.BlockSpec((1,) + w.shape[1:], lambda e: (e, 0, 0)) for w in (w_gate, w_up, w_down)],
-        out_specs=[block] * 3,
-        out_shape=[out] * 3,
-        name="pack_experts",
-    )(core, w_gate, w_up, w_down)
 
 
 def swap_halves(x):
@@ -331,50 +303,70 @@
         out_shape=[shape_of((n, 3, local, depth, width), BF16) for n in counts],
         scratch_shapes=[pltpu.VMEM((width, model), BF16)],
         compiler_params=params(),
+        cost_estimate=lasting(18),
         name="expert_grads",
     )(where, *operands)
 
 
-def finish_kernel(blocks, core, kept_a, got_a, kept_b, got_b, other, gate, up, down):
-    width, wide = gate.shape[2], kept_a.shape[3]
-    mine = chooser(width, blocks, core[0])
-    theirs = chooser(width, blocks, 1 - core[0])
+def finish_kernel(blocks, count_a, count_b, core, *refs):
+    parts_a, parts_b = refs[:count_a], refs[count_a : count_a + count_b]
+    other, gate, up, down, choose = refs[count_a + count_b :]
+    width, wide = gate.shape[2], other.shape[3]
+
+    @pl.when(pl.program_id(0) == 0)
+    def _():
+        choose[0] = chooser(width, blocks, core[0])
+        choose[1] = chooser(width, blocks, 1 - core[0])
+
+    mine, theirs = choose[0], choose[1]
     first = core[0] == 0
+
+    def total(parts, place):
+        value = parts[0][place, 0].astype(F32)
+        for part in parts[1:]:
+            value = value + part[place, 0].astype(F32)
+        return value
+
     for place, out in ((0, gate), (1, up)):
-        kept = jnp.where(first, kept_a[place, 0].astype(F32), kept_b[place, 0].astype(F32))
-        got = jnp.where(first, got_a[place, 0].astype(F32), got_b[place, 0].astype(F32))
+        kept = jnp.where(first, total(parts_a[:-1], place), total(parts_b[:-1], place))
+        got = jnp.where(
+            first, parts_a[-1][place, 0].astype(F32), parts_b[-1][place, 0].astype(F32)
+        )
         out[0] = (
             dot(kept.astype(BF16), mine)
             + dot(got.astype(BF16), mine)
             + dot(other[place, 0], theirs)
         )
     rows = down.shape[1] // 2
-    for part, kept, got in ((0, kept_a, got_a), (1, kept_b, got_b)):
-        value = kept[2, 0].astype(F32) + got[2, 0].astype(F32)
+    for part, parts in ((0, parts_a), (1, parts_b)):
+        value = total(parts, 2)
         for j in range(value.shape[0] // rows):
             down[0, part * rows : (part + 1) * rows, j * wide : (j + 1) * wide] = value[
                 j * rows : (j + 1) * rows
             ]
 
 
-def finish(core, kept_a, got_a, kept_b, got_b, other, down_rows, model, blocks):
-    local, depth, wide = kept_a.shape[1:]
+def finish(core, parts_a, parts_b, other, down_rows, model, blocks):
+    local, depth, wide = other.shape[1:]
     block = pl.BlockSpec((3, 1, depth, wide), lambda e: (0, e, 0, 0))
+    front = pl.BlockSpec((None, 3, 1, depth, wide), lambda e: (0, 0, e, 0, 0))
     outs = [
         shape_of((local, depth, 2 * wide), F32),
         shape_of((local, depth, 2 * wide), F32),
         shape_of((local, down_rows, model), F32),
     ]
+    parts = list(parts_a) + list(parts_b)
     return pl.pallas_call(
-        functools.partial(finish_kernel, blocks),
+        functools.partial(finish_kernel, blocks, len(parts_a), len(parts_b)),
         grid=(local,),
         in_specs=[SMEM]
-        + [block] * 4
+        + [front if v.ndim == 5 else block for v in parts]
         + [pl.BlockSpec((2, 1, depth, wide), lambda e: (0, e, 0, 0))],
         out_specs=[pl.BlockSpec((1,) + o.shape[1:], lambda e: (e, 0, 0)) for o in outs],
         out_shape=outs,
+        scratch_shapes=[pltpu.VMEM((2, wide, 2 * wide), BF16)],
         name="finish",
-    )(core, kept_a, got_a, kept_b, got_b, other)
+    )(core, *parts, other)
 
 
 def attend_back_kernel(blocks, kv_heads, gain_row, *refs):
@@ -456,6 +448,7 @@
             pltpu.VMEM((seq, rope_width + value_width), BF16),
         ],
         compiler_params=params(),
+        cost_estimate=lasting(16),
         name="attend_back",
     )(dh_stack, x_all, weights, out_weights, *kept, bias, cosine, sine, extra)
     return out[0], out[1], out[2:]
@@ -520,19 +513,56 @@
     return params(collective_id=collective_id, has_side_effects=True)
 
 
-def gather_weights_kernel(
-    ranks, plane_size, by_rank, rows_in, x_in, grads_in, weights, out_rows, x_all, grads_all, *sems
-):
-    z_send, z_recv, p_send, p_recv, c_send, c_recv, local = sems[:7]
+def pack_experts(spot, w_gate, w_up, w_down, held, outgoing):
+    local, width = w_gate.shape[0], w_gate.shape[2]
+    mine = chooser(width, 2 * spot.chips, spot.core)
+    theirs = chooser(width, 2 * spot.chips, 1 - spot.core)
+    rows, wide = w_down.shape[1] // 2, width // 2
+
+    def one(e, carry):
+        for place, ref in ((0, w_gate), (1, w_up)):
+            value = ref[e].astype(BF16)
+            kept = dot_nt(value, mine).astype(BF16)
+            for part in range(2):
+
+                @pl.when(spot.core == part)
+                def _():
+                    held[part][place, e] = kept
+
+            outgoing[place, e] = dot_nt(value, theirs).astype(BF16)
+        value = w_down[e].astype(BF16)
+        for part in range(2):
+            for j in range(value.shape[1] // wide):
+                held[part][2, e, j * rows : (j + 1) * rows] = value[
+                    part * rows : (part + 1) * rows, j * wide : (j + 1) * wide
+                ]
+        return carry
+
+    lax.fori_loop(0, local, one, 0)
+
+
+def gather_weights_kernel(ranks, plane_size, *refs):
+    by_rank, rows_in, x_in, grads_in, w_gate, w_up, w_down = refs[:7]
+    weights, out_rows, x_all, grads_all, parts_a, parts_b, got_a, got_b = refs[7:15]
+    held_a, held_b, outgoing = refs[15:18]
+    z_send, z_recv, p_send, p_recv, c_send, c_recv, local, e_send, e_recv = refs[18:27]
+    x_send, x_recv, grads_send, grads_recv = refs[27:]
     spot = Spot(ranks, plane_size)
-    f, me, chips = spot.index, spot.rank, spot.chips
+    f, me, chips, core = spot.index, spot.rank, spot.chips, spot.core
     others = range(1, ranks)
+    kept = [
+        pltpu.make_async_copy(by_rank.at[me], weights.at[f, me], local.at[0]),
+        pltpu.make_async_copy(rows_in, out_rows.at[f], local.at[1]),
+        pltpu.make_async_copy(x_in, x_all.at[0], local.at[2]),
+        pltpu.make_async_copy(grads_in, grads_all.at[0], local.at[3]),
+    ]
+    for copy in kept:
+        copy.start()
     meet(
         [spot.ahead(s) for s in others]
         + [spot.on_chip(spot.chip_ahead(k)) for k in range(1, chips)]
         + [spot.partner()]
     )
-    waits = []
     z_copies = [
         send(
             by_rank.at[lax.rem(me + s, ranks)],
@@ -543,17 +573,9 @@
         )
         for s in others
     ]
-    kept = [
-        pltpu.make_async_copy(by_rank.at[me], weights.at[f, me], local.at[0]),
-        pltpu.make_async_copy(rows_in, out_rows.at[f], local.at[1]),
-        pltpu.make_async_copy(x_in, x_all.at[0], local.at[2]),
-        pltpu.make_async_copy(grads_in, grads_all.at[0], local.at[3]),
-    ]
-    for copy in kept:
-        copy.start()
     lines = [
-        LineGather(spot, x_all, sems[7], sems[8]),
-        LineGather(spot, grads_all, sems[9], sems[10]),
+        LineGather(spot, x_all, x_send, x_recv),
+        LineGather(spot, grads_all, grads_send, grads_recv),
     ]
 
     def spread(which, src, buf):
@@ -571,18 +593,67 @@
     row_copies = spread(1, rows_in, out_rows)
     for copy in kept:
         copy.wait()
-    lines[0].start(0)
+    for line in lines:
+        line.start(0)
+
+    pack_experts(spot, w_gate, w_up, w_down, (held_a, held_b), outgoing)
+
+    def swap(part, held):
+        return pltpu.make_async_remote_copy(
+            src_ref=outgoing,
+            dst_ref=held.at[pl.ds(0, 2)],
+            send_sem=e_send.at[0],
+            recv_sem=e_recv.at[0],
+            device_id=spot.partner(),
+            device_id_type=MESH,
+        )
+
+    for part, held in ((0, held_a), (1, held_b)):
+
+        @pl.when(core == part)
+        def _():
+            swap(part, held).start()
+
     for copy in z_copies:
         copy.wait()
     weight_copies = spread(0, weights.at[f], weights)
+    for part, held in ((0, held_a), (1, held_b)):
+
+        @pl.when(core == part)
+        def _():
+            swap(part, held).wait_send()
+
+        @pl.when(core == 1 - part)
+        def _():
+            swap(part, held).wait_recv()
+
+    row, mid = spot.chip // 2, lax.rem(spot.chip, 2)
+    expert_copies = [
+        send(held_a, got_a, e_send.at[1], e_recv.at[1], spot.on_chip(row * 2 + (1 - mid)))
+    ] + [
+        send(
+            held_b,
+            got_b.at[s - 1],
+            e_send.at[1 + s],
+            e_recv.at[1 + s],
+            spot.on_chip(lax.rem(row + s, chips // 2) * 2 + mid),
+        )
+        for s in range(1, chips // 2)
+    ]
+    stores = [
+        pltpu.make_async_copy(held_a, parts_a, local.at[4]),
+        pltpu.make_async_copy(held_b, parts_b, local.at[5]),
+    ]
+    for copy in stores:
+        copy.start()
+    waits = []
     for hop in range(ranks - 1):
-        lines[0].arrive(hop)
-        if hop + 1 < ranks - 1:
-            lines[0].start(hop + 1)
-        else:
-            lines[1].start(0)
+        for line in lines:
+            line.arrive(hop)
+            if hop + 1 < line.hops:
+                line.start(hop + 1)
     for k in range(1, chips):
-        source = spot.chip_behind(k) * 2 + spot.core
+        source = spot.chip_behind(k) * 2 + core
         for which, copies, buf in ((1, row_copies, out_rows), (0, weight_copies, weights)):
             copies[k - 1].wait()
             waits.append(
@@ -594,45 +665,52 @@
                     spot.partner(),
                 )
             )
-    for hop in range(ranks - 1):
-        lines[1].arrive(hop)
-        if hop + 1 < ranks - 1:
-            lines[1].start(hop + 1)
     row_copies[-1].wait()
     weight_copies[-1].wait()
-    for copy in waits:
+    for copy in waits + stores + expert_copies:
         copy.wait()
     for line in lines:
         line.drain()
 
 
-def gather_weights(by_rank, rows_in, x_in, grads_in, plane_size):
+def gather_weights(by_rank, rows_in, x_in, grads_in, w_gate, w_up, w_down, plane_size):
     ranks, rows, columns = by_rank.shape
     chips = plane_size // 2
+    local, depth, width = w_gate.shape
     dma = pltpu.SemaphoreType.DMA
+    half = (local, depth, width // 2)
     return pl.pallas_call(
         functools.partial(gather_weights_kernel, ranks, plane_size),
-        in_specs=[VMEM] * 4,
-        out_specs=[VMEM] * 4,
+        in_specs=[VMEM] * 7,
+        out_specs=[VMEM] * 4 + [ANY] * 4,
         out_shape=[
             shape_of((plane_size, ranks, rows, columns), BF16),
             shape_of((plane_size,) + rows_in.shape, BF16),
             shape_of((ranks,) + x_in.shape, BF16),
             shape_of((ranks,) + grads_in.shape, BF16),
+            shape_of((3,) + half, BF16),
+            shape_of((3,) + half, BF16),
+            shape_of((3,) + half, BF16),
+            shape_of((chips // 2 - 1, 3) + half, BF16),
         ],
         scratch_shapes=[
+            pltpu.VMEM((3,) + half, BF16),
+            pltpu.VMEM((3,) + half, BF16),
+            pltpu.VMEM((2,) + half, BF16),
             dma((ranks - 1,)),
             dma((ranks - 1,)),
             dma((2, chips - 1)),
             dma((2, chips - 1)),
             dma((2, chips)),
             dma((2, chips)),
-            dma((4,)),
+            dma((6,)),
+            dma((1 + chips // 2,)),
+            dma((1 + chips // 2,)),
         ]
         + [dma((2, ranks - 1))] * 4,
         compiler_params=remote(0),
         name="gather_weights",
-    )(by_rank, rows_in, x_in, grads_in)
+    )(by_rank, rows_in, x_in, grads_in, w_gate, w_up, w_down)
 
 
 def scatter_start(spot, refs, buf, send_sem, recv_sem):
@@ -643,8 +721,10 @@
 
 
 class LineGather:
-    def __init__(self, spot, buf, send_sem, recv_sem):
+    def __init__(self, spot, buf, send_sem, recv_sem, part=0, parts=1):
         self.spot, self.buf, self.sems = spot, buf, (send_sem, recv_sem)
+        count = buf.shape[1] // parts
+        self.rows = pl.ds(part * count, count)
         me, n = spot.rank, spot.ranks
         self.hops = n - 1
         self.sends = [(me - h >= 0) & (me + 1 < n) for h in range(n - 1)], [
@@ -661,8 +741,8 @@
     def copy(self, way, h):
         source, target = self.slots(way, h)
         return pltpu.make_async_remote_copy(
-            src_ref=self.buf.at[source],
-            dst_ref=self.buf.at[target],
+            src_ref=self.buf.at[source, self.rows],
+            dst_ref=self.buf.at[target, self.rows],
             send_sem=self.sems[0].at[way, h],
             recv_sem=self.sems[1].at[way, h],
             device_id=self.spot.ahead(1) if way == 0 else self.spot.behind(1),
@@ -699,10 +779,17 @@
                     self.copy(way, h).wait_send()
 
 
-def attend_kernel(ranks, plane_size, kv_heads, *refs):
-    x_all, gain, weights, out_weights, bias, cosine, sine, x, gain_two = refs[:9]
-    (a1, qk, val, mixed, maxes, inverse, h_out, a2, gathered, other) = refs[9:19]
-    mixed_t, sums, got, r_send, r_recv, g_send, g_recv, c_send, c_recv = refs[19:]
+def half_lines(spot, buf, send_sem, recv_sem):
+    return [LineGather(spot, buf, send_sem.at[k], recv_sem.at[k], k, 2) for k in range(2)]
+
+
+def attend_kernel(ranks, plane_size, kv_heads, gain_row, *refs):
+    x_all, weights, out_weights, bias, cosine, sine, x = refs[:7]
+    (extra_t, a1, qk, val, mixed, maxes, inverse, h_out, a2, gathered, other) = refs[7:18]
+    mixed_t, sums, got, r_send, r_recv, g_send, g_recv, c_send, c_recv = refs[18:]
+    extra_t[...] = weights[:, weights.shape[1] - LANES :].T
+    gain = extra_t[gain_row : gain_row + 1, :].astype(F32)
+    gain_two = extra_t[gain_row + 1 : gain_row + 2, :].astype(F32)
     spot = Spot(ranks, plane_size)
     peers = [spot.ahead(s) for s in range(1, ranks)] + [spot.partner()]
     greet(peers)
@@ -710,7 +797,7 @@
     rope_width = qk.shape[1]
     q_width = kv_heads * GROUP * HEAD_WIDTH
     for b in range(ranks):
-        a1[b * rows : (b + 1) * rows, :] = (x_all[b].astype(F32) * gain[...]).astype(BF16)
+        a1[b * rows : (b + 1) * rows, :] = (x_all[b].astype(F32) * gain).astype(BF16)
     linear = dot(a1[...], weights[:, : rope_width + val.shape[1]])
     for c in range(rope_width // LANES):
         part = linear[:, c * LANES : (c + 1) * LANES]
@@ -745,37 +832,40 @@
         copies[s - 1].wait()
         total = total + got[s - 1].astype(F32)
     scale = lax.rsqrt(jnp.mean(total * total, axis=-1, keepdims=True) + EPSILON)
-    low = (total * scale * gain_two[...]).astype(BF16)
+    low = (total * scale * gain_two).astype(BF16)
     gathered[0] = low
-    line = LineGather(spot, gathered, g_send, g_recv)
-    line.start(0)
-
-    def across(s):
+    lines = half_lines(spot, gathered, g_send, g_recv)
+    for line in lines:
+        line.start(0)
+
+    def across(s, part):
         return pltpu.make_async_remote_copy(
-            src_ref=gathered.at[s],
-            dst_ref=other.at[s],
-            send_sem=c_send.at[s],
-            recv_sem=c_recv.at[s],
+            src_ref=gathered.at[s, lines[part].rows],
+            dst_ref=other.at[s, lines[part].rows],
+            send_sem=c_send.at[part, s],
+            recv_sem=c_recv.at[part, s],
             device_id=spot.partner(),
             device_id_type=MESH,
         )
 
-    across(0).start()
+    for part in range(2):
+        across(0, part).start()
     a2[...] = low
     h_out[...] = total
-    for hop in range(line.hops):
-        line.arrive(hop)
-        if hop + 1 < line.hops:
-            line.start(hop + 1)
-        line.passed(hop, lambda s: across(s).start())
-    line.drain()
-    for s in range(ranks):
-        across(s).wait()
+    for hop in range(ranks - 1):
+        for part, line in enumerate(lines):
+            line.arrive(hop)
+            if hop + 1 < line.hops:
+                line.start(hop + 1)
+            line.passed(hop, lambda s: across(s, part).start())
+    for part, line in enumerate(lines):
+        line.drain()
+        for s in range(ranks):
+            across(s, part).wait()
 
 
 def attend(
-    x_all, gain, weights, out_weights, bias, cosine, sine, x, gain_two, kv_heads, rope_width,
-    plane_size,
+    x_all, weights, out_weights, bias, cosine, sine, x, gain_row, kv_heads, rope_width, plane_size
 ):
     ranks, rows, model = x_all.shape
     seq = rows * ranks
@@ -784,6 +874,7 @@
     heads = kv_heads * GROUP
     stack = shape_of((ranks, rows, model), BF16)
     outs = [
+        shape_of((LANES, model), BF16),
         shape_of((seq, model), BF16),
         shape_of((seq, rope_width), BF16),
         shape_of((seq, value_width), BF16),
@@ -797,8 +888,8 @@
     ]
     dma = pltpu.SemaphoreType.DMA
     out = pl.pallas_call(
-        functools.partial(attend_kernel, ranks, plane_size, kv_heads),
-        in_specs=[VMEM] * 9,
+        functools.partial(attend_kernel, ranks, plane_size, kv_heads, gain_row),
+        in_specs=[VMEM] * 7,
         out_specs=[VMEM] * len(outs),
         out_shape=outs,
         scratch_shapes=[
@@ -807,15 +898,15 @@
             pltpu.VMEM((ranks - 1, rows, model), BF16),
             dma((ranks - 1,)),
             dma((ranks - 1,)),
-            dma((2, ranks - 1)),
-            dma((2, ranks - 1)),
-            dma((ranks,)),
-            dma((ranks,)),
+            dma((2, 2, ranks - 1)),
+            dma((2, 2, ranks - 1)),
+            dma((2, ranks)),
+            dma((2, ranks)),
         ],
         compiler_params=remote(1),
         name="attend",
-    )(x_all, gain, weights, out_weights, bias, cosine, sine, x, gain_two)
-    return out[:6], out[6:]
+    )(x_all, weights, out_weights, bias, cosine, sine, x)
+    return out[0], out[1:7], out[7:]
 
 
 def rejoin_kernel(ranks, plane_size, gain_row, gates, h, dz, router_t, a2, *refs):
@@ -843,16 +934,19 @@
     )
     gathered[0] = grad.astype(BF16)
     dh[...] = grad
-    line_out = LineGather(spot, gathered, g_send, g_recv)
-    line_out.start(0)
+    lines = half_lines(spot, gathered, g_send, g_recv)
+    for line_out in lines:
+        line_out.start(0)
     gain_grad = jnp.sum(da2 * normed, axis=0, keepdims=True)
     line = lax.broadcasted_iota(jnp.int32, (LANES, model), 0)
     extra[...] = jnp.where(line == gain_row, gain_grad, dot_tn(d_logits, a2[...]))
-    for hop in range(line_out.hops):
-        line_out.arrive(hop)
-        if hop + 1 < line_out.hops:
-            line_out.start(hop + 1)
-    line_out.drain()
+    for hop in range(ranks - 1):
+        for line_out in lines:
+            line_out.arrive(hop)
+            if hop + 1 < line_out.hops:
+                line_out.start(hop + 1)
+    for line_out in lines:
+        line_out.drain()
 
 
 def rejoin(parts, gates, h, dz, router_t, a2, gain_row, plane_size):
@@ -867,13 +961,14 @@
             shape_of((ranks,) + h.shape, BF16),
             shape_of((LANES, h.shape[1]), F32),
         ],
-        scratch_shapes=[dma((2, ranks - 1)), dma((2, ranks - 1))],
+        scratch_shapes=[dma((2, 2, ranks - 1)), dma((2, 2, ranks - 1))],
         compiler_params=remote(2),
+        cost_estimate=lasting(35),
         name="rejoin",
     )(gates, h, dz, router_t, a2, *parts)
 
 
-def last_kernel(ranks, plane_size, x, dh, gain, d_weights, d_rows, *refs):
+def last_kernel(ranks, plane_size, gain_row, x, dh, extra_t, d_weights, d_rows, *refs):
     sums = refs[:ranks]
     out, columns_out, rows_out = refs[ranks : ranks + 3]
     (got, core_w, core_r, sum_w, sum_r, chip_w, chip_r, final) = refs[ranks + 3 : ranks + 11]
@@ -920,7 +1015,7 @@
     for s in range(1, ranks):
         z_copies[s - 1].wait()
         total = total + got[s - 1].astype(F32)
-    weighted = total * gain[...]
+    weighted = total * extra_t[gain_row : gain_row + 1, :].astype(F32)
     grad = scale * (weighted - normed * jnp.mean(weighted * normed, axis=-1, keepdims=True))
     for k in range(1, chips):
         for which in range(2):
@@ -951,13 +1046,13 @@
     kept.wait()
 
 
-def last(x, dh, gain, d_weights, d_rows, sums):
+def last(x, dh, extra_t, d_weights, d_rows, sums, gain_row):
     ranks = len(sums)
     chips, _, _, rows, columns = d_weights.shape
     dma = pltpu.SemaphoreType.DMA
     w_shape, r_shape = d_weights.shape[2:], d_rows.shape[2:]
     return pl.pallas_call(
-        functools.partial(last_kernel, ranks, 2 * chips),
+        functools.partial(last_kernel, ranks, 2 * chips, gain_row),
         in_specs=[VMEM] * (5 + ranks),
         out_specs=[VMEM] * 3,
         out_shape=[shape_of(x.shape, F32), shape_of(w_shape, BF16), shape_of(r_shape, F32)],
@@ -981,8 +1076,9 @@
             dma((1,)),
         ],
         compiler_params=remote(3),
+        cost_estimate=lasting(60),
         name="last",
-    )(x, dh, gain, d_weights, d_rows, *sums)
+    )(x, dh, extra_t, d_weights, d_rows, *sums)
 
 
 def piece_ids(position_index, starts):
@@ -1062,26 +1158,13 @@
     grads_own = jnp.concatenate([cotangent, routed], axis=1).astype(BF16)
 
     core = plane.core.astype(jnp.int32)[None]
-    keep, send, halves = pack_experts(core, w_gate, w_up, w_down, plane.size)
-    got = plane.other_core(send)
-    parts = [
-        jnp.concatenate([jnp.where(plane.core == part, keep, got), halves[part][None]], axis=0)
-        for part in range(2)
-    ]
-    by_rank, parts, out_shard, x_own, grads_own = lax.optimization_barrier(
-        (by_rank, parts, out_shard, x_own, grads_own)
-    )
-    first = [plane.other_mid(parts[0])] + [
-        plane.next_row(parts[1], s) for s in range(1, plane.rows)
-    ]
-    weights, out_weights, x_all, grads = gather_weights(
-        by_rank, out_shard, x_own, grads_own, plane.size
-    )
-    first, weights = lax.optimization_barrier((first, weights))
+    weights, out_weights, x_all, grads, part_a, part_b, got_a, got_b = gather_weights(
+        by_rank, out_shard, x_own, grads_own, w_gate, w_up, w_down, plane.size
+    )
     grads = grads.reshape(seq, grads.shape[2])
-    found = {(0, 0, 0): parts[0], (0, 0, 1): parts[1], (0, 1, 0): first[0]}
+    found = {(0, 0, 0): part_a, (0, 0, 1): part_b, (0, 1, 0): got_a}
     for s in range(1, plane.rows):
-        found[s, 0, 1] = first[s]
+        found[s, 0, 1] = got_b[s - 1]
         for mid in range(2):
             found[s, mid, 0] = plane.next_row(found[0, mid, 0], s)
     for s in range(plane.rows):
@@ -1111,19 +1194,15 @@
     sine = jnp.tile(jnp.sin(angles), (1, LANES // half)) * jnp.where(
         lane_ids % HEAD_WIDTH < half, -1.0, 1.0
     )
-    extra_t = weights[:, columns - LANES :].T
-    gain_one = extra_t[gain_one_row : gain_one_row + 1].astype(F32)
-    gain_two = extra_t[gain_two_row : gain_two_row + 1].astype(F32)
-    kept, (mid_rows, a2, own_a2, other_a2) = attend(
+    extra_t, kept, (mid_rows, a2, own_a2, other_a2) = attend(
         x_all,
-        gain_one,
         weights,
         out_weights,
         bias,
         cosine,
         sine,
         inputs,
-        gain_two,
+        gain_one_row,
         kv_heads,
         rope_width,
         plane.size,
@@ -1146,12 +1225,11 @@
         for s in range(plane.rows)
         for mid in range(2)
     ]
-    own_kept.insert(2, grads[:, :model])
-    other_kept.insert(2, other_grads[:, :model])
+    own_kept.insert(2, grads)
+    other_kept.insert(2, other_grads)
     flat = expert_grads(
         jnp.stack(chips).astype(jnp.int32), own_kept, other_kept, plane.size, plane.rows
     )
-    dx_got, flat = lax.optimization_barrier((dx_got, flat))
     by_row, by_mid = flat[: plane.rows], flat[plane.rows :]
 
     def add(first, *others):
@@ -1188,37 +1266,39 @@
         kv_heads,
         gain_one_row,
     )
-    a_first, b_first, d_weights, out_got = lax.optimization_barrier(
-        (a_first, b_first, d_weights, out_got)
-    )
-    a_sums = [add(by_row[0][mid], *[v[mid] for v in a_first]) for mid in range(2)]
-    b_sums = [add(by_mid[0][s], b_first[s]) for s in range(plane.rows)]
-    a_sums, b_sums, d_weights = lax.optimization_barrier((a_sums, b_sums, d_weights))
-    a_got = plane.other_mid(a_sums[1])
-    b_got = [plane.next_row(b_sums[s], s) for s in steps]
+    a_first, b_first, d_weights = lax.optimization_barrier((a_first, b_first, d_weights))
+    a_next = add(by_row[0][1], *[v[1] for v in a_first])
+    b_next = [add(by_mid[0][s], b_first[s]) for s in steps]
+    a_got = plane.other_mid(a_next)
+    b_got = [plane.next_row(v, s) for s, v in zip(steps, b_next)]
+    a_next, b_next, d_weights, out_got = lax.optimization_barrier(
+        (a_next, b_next, d_weights, out_got)
+    )
     chip_count = plane.size // 2
     input_grad, by_rank, out_part = last(
         inputs,
         dh,
-        gain_one,
+        extra_t,
         d_weights.reshape(chip_count, 2, ranks, weight_rows, columns),
         d_out_weights.reshape(chip_count, 2, weight_rows, model),
         da1,
+        gain_one_row,
     )
     a_got, b_got, out_part = lax.optimization_barrier((a_got, b_got, out_part))
-    b_kept = b_sums[0]
-    if len(b_got) > 1:
-        b_kept = add(b_kept, *b_got[:-1])
-    b_got = b_got[-1]
+    parts_a = [by_row[0], *a_first, a_got]
+    parts_b = [by_mid[0], b_first, *b_got]
+
+    def total(parts):
+        value = 0.0
+        for v in parts:
+            value = value + (v[0] if v.ndim == 5 else v)[:2].astype(F32)
+        return value
+
     other = plane.other_core(
-        jnp.where(
-            plane.core == 0,
-            b_kept[:2].astype(F32) + b_got[:2].astype(F32),
-            a_sums[0][:2].astype(F32) + a_got[:2].astype(F32),
-        ).astype(BF16)
+        jnp.where(plane.core == 0, total(parts_b), total(parts_a)).astype(BF16)
     )
     gate_grad, up_grad, down_grad = finish(
-        core, a_sums[0], a_got, b_kept, b_got, other, w_down.shape[1], model, plane.size
+        core, parts_a, parts_b, other, w_down.shape[1], model, plane.size
     )
     output = mid_rows + outs[0]
     for v in out_got:

time: 457 us -> 423 us (0.926)
  Pallas kernels: 353 us -> 331 us
  starting transfers between devices: 29 us -> 22.7 us
    pallas_call x3 -> x2, Pallas kernels: 79.9 us -> 65.7 us  [the longest x1 57.2 us: last(): pl.pallas_call(functools.partial(last_kernel, ranks, 2 * chips, gain_row)...]
    slice x4 -> x0, local copies, waits for them, and re-layouts: 5.71 us -> none  [the longest x1 2.63 us: on_device(): other_kept.insert(2, other_grads[:, :model])]
    ppermute x5 -> x4, starting transfers between devices: 9.15 us -> 4.09 us  [other_mid(): return lax.ppermute(x, 'fsdp', [(i, i ^ 2) for i in range(self.size)])]
  transfers between devices with their start and end apart: 23 -> 20, of which waited for: 3 -> 2; matrix products, arithmetic and copies ran while one was open for 6% -> 9% of each run, Pallas kernels for 69% -> 53%
where the time goes in v5:
time: 423 us; the launch traced here: 421 us
  Pallas kernels  331 us (78%)
  other arithmetic  29.9 us (7%)
  starting transfers between devices  22.7 us (5%)
  local copies, waits for them, and re-layouts  18.1 us (4%)
  waiting for transfers between devices  17.6 us (4%)
    pallas_call x1, Pallas kernels, gather_weights(): pl.pallas_call(functools.partial(gather_weights_kernel, ranks, plane_size...  72.7 us
    pallas_call x1, Pallas kernels, attend(): pl.pallas_call(functools.partial(attend_kernel, ranks, plane_size, kv_hea...  71.8 us
    pallas_call x1, Pallas kernels, last(): pl.pallas_call(functools.partial(last_kernel, ranks, 2 * chips, gain_row)...  57.2 us
    pallas_call x2, Pallas kernels, experts(): pl.pallas_call(functools.partial(experts_kernel, blocks, len(pieces), pla...  53.3 us
    pallas_call x1, Pallas kernels, rejoin(): pl.pallas_call(functools.partial(rejoin_kernel, ranks, plane_size, gain_r...  34.1 us
    pallas_call x1, Pallas kernels, expert_grads(): pl.pallas_call(functools.partial(expert_grads_kernel, plane_rows, depth,...  18.4 us
    pallas_call x1, Pallas kernels, attend_back(): pl.pallas_call(functools.partial(attend_back_kernel, blocks, kv_heads, ga...  15.3 us
    ppermute x6, waiting for transfers between devices, expert_shift(): lax.ppermute(x, 'expert', [(i, (i + step) % count) for i in range(count)])  12.4 us
  transfers between devices with their start and end apart: 20, of which 2 were waited for; matrix products, arithmetic and copies ran while one was open for 9% of the time, Pallas kernels for 53%

profile of v5, /device:TPU:27, one launch (start us, length us, event | category | flops | bytes accessed | tf_op | source)
XLA Modules:
  0.0 420.8 jit_solution(7835107462579192348)
XLA Ops:
  1.8 2.9 collective-permute-start
  12.8 72.7 %gather_weights.1 = (bf16[8,4,48,768]{3,2,1,0:T(8,128)(2,1)}, bf16[8,48,1536]{2,1,0:T(8,128)(2,1)}, bf16[4,128,1536]{2,1,0:T(8,128)(2,1)}, bf16[4,128,1664]{2,1,...) custom-call(bf16[4,48,768]{2,1,0:T(8,128)(2,1)} %maximum_bitcast_fus, ...), custom_call_target="tpu_custom_call" | custom-call | tf_op jit(solution)/shard_map/gather_weights/pallas_call | solution.py:682
  85.7 2.0 collective-permute-start.4
  93.5 71.8 %attend.1 = (bf16[128,1536]{1,0:T(8,128)(2,1)}, bf16[512,1536]{1,0:T(8,128)(2,1)}, bf16[512,512]{1,0:T(8,128)(2,1)}, bf16[512,128]{1,0:T(8,128)(2,1)}, bf16[512,...) custom-call(bf16[4,128,1536]{2,1,0:T(8,128)(2,1)} %get-tuple-element, ...), custom_call_target="tpu_custom_call" | custom-call | tf_op jit(solution)/shard_map/attend/pallas_call | solution.py:890
  166.9 26.1 %experts.3 = (bf16[512,1536]{1,0:T(8,128)(2,1)}, bf16[512,1664]{1,0:T(8,128)(2,1)}, f32[128,128]{1,0:T(8,128)}, bf16[1536,512]{1,0:T(8,128)(2,1)}, bf16[5,256,51...) custom-call(bf16[512,1536]{1,0:T(8,128)(2,1)} %bitcast.79, ...), custom_call_target="tpu_custom_call" | custom-call | tf_op jit(solution)/shard_map/experts/pallas_call | solution.py:233
  193.8 27.2 %experts.2 = (f32[512,1536]{1,0:T(8,128)}, f32[512,1664]{1,0:T(8,128)}, f32[128,128]{1,0:T(8,128)}, bf16[1536,512]{1,0:T(8,128)(2,1)}, bf16[5,256,512]{2,1,0:T(8...) custom-call(bf16[512,1536]{1,0:T(8,128)(2,1)} %bitcast.78, bf16[512,1664]{1,0:T(8,128)(2,1)} %bitcast.76, ...), custom_call_target="tpu_custom_call" | custom-call | tf_op jit(solution)/shard_map/experts/pallas_call | solution.py:233
  221.4 4.0 fusion.18
  227.9 18.4 %expert_grads.1 = (bf16[2,3,5,192,256]{4,3,2,1,0:T(8,128)(2,1)}, bf16[2,3,5,192,256]{4,3,2,1,0:T(8,128)(2,1)}, bf16[2,3,5,192,256]{4,3,2,1,0:T(8,128)(2,1)}, bf16[2,3,5,192,256]{4,3,2,1,0:T(8,128)(2,1)}) custom-call(s32[4]{0:T(128)} %pad_add_fusion.where_ref, bf16[1536,512]{1,0:T(8,128)(2,1)} %get-tuple-element.104.refs_0_, ...), custom_call_target="tpu_custom_call" | custom-call | flops 17999998976 | bytes 18000000 | tf_op jit(solution)/shard_map/expert_grads/pallas_call | solution.py:296
  247.4 2.1 slice.118.refs_0_
  250.2 12.4 %collective-permute-done.8.refs_2_ = bf16[128,1664]{1,0:T(8,128)(2,1)} collective-permute-done((bf16[128,1664]{1,0:T(8,128)(2,1)S(1)}, bf16[128,1664]{1,0:T(8,128)(2,1)}, u32[]{:S(2)}, u32[]{:S(2)}) %collective-permute-start.8) | collective-permute-done | bytes 426016 | tf_op jit(solution)/shard_map/ppermute | solution.py:77
  262.6 34.1 %rejoin.1 = (f32[128,1536]{1,0:T(8,128)}, bf16[4,128,1536]{2,1,0:T(8,128)(2,1)}, f32[128,1536]{1,0:T(8,128)}) custom-call(f32[128,128]{1,0:T(8,128)} %get-tuple-element.92.gates, f32[128,1536]{1,0:T(8,128)} %get-tuple-element.84.h, f32[128,1536]{1,0:T(8,128)} %dz.1, bf16[128,1536]{1,0:T(8,128)(2,1)} %get-tuple-element.87.refs_2_.router_t.extra_t, ...), custom_call_target="tpu_custom_call" | custom-call | flops 35000000512 | bytes 35000000 | tf_op jit(solution)/shard_map/rejoin/pallas_call | solution.py:955
  296.7 2.9 fusion.17
  302.2 1.8 collective-permute-start.15
  304.0 15.3 %attend_back.1 = (bf16[1536,768]{1,0:T(8,128)(2,1)}, bf16[384,1536]{1,0:T(8,128)(2,1)}, f32[128,1536]{1,0:T(8,128)}, bf16[128,1536]{1,0:T(8,128)(2,1)}, bf16[128...) custom-call(bf16[4,128,1536]{2,1,0:T(8,128)(2,1)} %get-tuple-element.115.refs_0_, ...), custom_call_target="tpu_custom_call" | custom-call | flops 16000000000 | bytes 16000000 | tf_op jit(solution)/shard_map/attend_back/pallas_call | solution.py:438
  319.4 1.7 copy-done.1
  321.0 3.5 fusion.3
  325.6 2.9 fusion.2
  329.2 57.2 %last.1 = (f32[128,1536]{1,0:T(8,128)}, bf16[4,48,768]{2,1,0:T(8,128)(2,1)}, f32[48,1536]{1,0:T(8,128)}) custom-call(f32[128,1536]{1,0:T(8,128)} %x.1, f32[128,1536]{1,0:T(8,128)} %get-tuple-element.134.dh, bf16[128,1536]{1,0:T(8,128)(2,1)} %get-tuple-element.87.refs_2_.router_t.extra_t, bf16[4,2,4,48,768]{4,3,2,1,0:T(8,128)(2,1)} %bitcast.93, ...), custom_call_target="tpu_custom_call" | custom-call | flops 60000002048 | bytes 60000000 | tf_op jit(solution)/shard_map/last/pallas_call | solution.py:1054
  387.4 4.3 %fusion.1 = bf16[2,5,192,256]{3,2,1,0:T(8,128)(2,1)} fusion(bf16[3,5,192,256]{3,2,1,0:T(8,128)(2,1)} %collective-permute-done.16.refs_2_, bf16[2,3,5,192,256]{4,3,2,1,0:T(8,128)(2,1)} %copy-done.1, bf16[2,3,5,192,256]{4,3,2,1,0:T(8,128)(2,1)S(1)} %copy-done, bf16[3,5,192,256]{3,2,1,0:T(8,128)(2,1)} %collective-permute-done.17.refs_5_, ...), kind=kLoop, calls=%fused_computation.6 | loop fusion | flops 5898240 | bytes 6881281 | tf_op jit(solution)/shard_map/convert_element_type | solution.py:1298
  391.7 4.3 %collective-permute-start.19 = (bf16[2,5,192,256]{3,2,1,0:T(8,128)(2,1)}, bf16[2,5,192,256]{3,2,1,0:T(8,128)(2,1)S(1)}, u32[]{:S(2)}, u32[]{:S(2)}) collective-permute-start(bf16[2,5,192,256]{3,2,1,0:T(8,128)(2,1)} %fusion.1), channel_id=1, source_target_pairs={{0,4},{4,0},{8,12},{12,8},{16,20},{20,16},{24,28},{28,24},{1,5},{5... | collective-permute-start | bytes 2949128 | tf_op jit(solution)/shard_map/ppermute | solution.py:64
  396.1 2.2 convert_add_fusion.2
  398.3 2.9 collective-permute-start.18
  404.6 5.1 %collective-permute-done.18 = bf16[48,1536]{1,0:T(8,128)(2,1)S(1)} collective-permute-done((bf16[48,1536]{1,0:T(8,128)(2,1)S(1)}, bf16[48,1536]{1,0:T(8,128)(2,1)S(1)}, u32[]{:S(2)}, u32[]{:S(2)}) %collective-permute-start.18) | collective-permute-done | bytes 147488 | tf_op jit(solution)/shard_map/ppermute | solution.py:1307
  411.5 8.5 %finish.1 = (f32[5,192,512]{2,1,0:T(8,128)}, f32[5,192,512]{2,1,0:T(8,128)}, f32[5,64,1536]{2,1,0:T(8,128)}) custom-call(s32[1]{0:T(128)} %bitcast.27.core, bf16[2,3,5,192,256]{4,3,2,1,0:T(8,128)(2,1)} %get-tuple-element.112.refs_0_, bf16[2,3,5,192,256]{4,3,2,1,0:T(8,128)(2,1)} %copy-done.1, bf16[3,5,192,256]{3,2,1,0:T(8,128)(2,1)} %collective-permute-done.16.refs_2_, ...), custom_call_target="tpu_custom_call" | custom-call | tf_op jit(solution)/shard_map/finish/pallas_call | solution.py:359
  (112 shorter events, 33.3 us)
Async XLA Ops:
  0.6 8.7 %copy-start.2 = (f32[128,1536]{1,0:T(8,128)S(1)}, f32[128,1536]{1,0:T(8,128)}, u32[]{:S(2)}) copy-start(f32[128,1536]{1,0:T(8,128)} %x.1) | copy-start | bytes 2359300
  0.7 9.6 %copy-start.7 = (f32[128,1536]{1,0:T(8,128)S(1)}, f32[128,1536]{1,0:T(8,128)}, u32[]{:S(2)}) copy-start(f32[128,1536]{1,0:T(8,128)} %dz.1) | copy-start | bytes 2359300
  0.7 9.7 %copy-start.13 = (f32[48,512]{1,0:T(8,128)S(1)}, f32[48,512]{1,0:T(8,128)}, u32[]{:S(2)}) copy-start(f32[48,512]{1,0:T(8,128)} %param.19) | copy-start | bytes 294916
  0.7 9.7 %copy-start.12 = (f32[48,512]{1,0:T(8,128)S(1)}, f32[48,512]{1,0:T(8,128)}, u32[]{:S(2)}) copy-start(f32[48,512]{1,0:T(8,128)} %param.18) | copy-start | bytes 294916
  1.8 10.3 %collective-permute-start = (bf16[48,1536]{1,0:T(8,128)(2,1)S(1)}, bf16[48,1536]{1,0:T(8,128)(2,1)S(1)}, u32[]{:S(2)}, u32[]{:S(2)}) collective-permute-start(bf16[48,1536]{1,0:T(8,128)(2,1)S(1)} %convert_element_type.101), channel_id=1, source_target_pairs={{0,0},{1,4},{2,8},{3,12},{4,16},{5,20},{6,24},{7,28},{8,1},{9,5},{... | collective-permute-start | bytes 442376 | tf_op jit(solution)/shard_map/ppermute | solution.py:1154
  85.5 79.8 %collective-permute-start.5 = (bf16[512,1664]{1,0:T(8,128)(2,1)}, bf16[512,1664]{1,0:T(8,128)(2,1)}, u32[]{:S(2)}, u32[]{:S(2)}) collective-permute-start(bf16[512,1664]{1,0:T(8,128)(2,1)} %bitcast.75), channel_id=1, source_target_pairs={{0,4},{4,0},{8,12},{12,8},{16,20},{20,16},{24,28},{28,24},{1,5},{5... | collective-permute-start | bytes 5111816 | tf_op jit(solution)/shard_map/ppermute | solution.py:64
  85.7 79.5 %collective-permute-start.4 = (bf16[3,5,192,256]{3,2,1,0:T(8,128)(2,1)}, bf16[3,5,192,256]{3,2,1,0:T(8,128)(2,1)S(1)}, u32[]{:S(2)}, u32[]{:S(2)}) collective-permute-start(bf16[3,5,192,256]{3,2,1,0:T(8,128)(2,1)} %bitcast.70), channel_id=1, source_target_pairs={{0,8},{4,12},{8,0},{12,4},{16,24},{20,28},{24,16},{28,20},{1,9},{5... | collective-permute-start | bytes 4423688 | tf_op jit(solution)/shard_map/ppermute | solution.py:67
  87.7 77.6 %collective-permute-start.1 = (bf16[3,5,192,256]{3,2,1,0:T(8,128)(2,1)}, bf16[3,5,192,256]{3,2,1,0:T(8,128)(2,1)S(1)}, u32[]{:S(2)}, u32[]{:S(2)}) collective-permute-start(bf16[3,5,192,256]{3,2,1,0:T(8,128)(2,1)} %get-tuple-element.88.refs_4_), channel_id=1, source_target_pairs={{0,16},{4,20},{8,24},{12,28},{16,0},{20,4},{24,8},{28,12},{1,17},{... | collective-permute-start | bytes 4423688 | tf_op jit(solution)/shard_map/ppermute | solution.py:70
  88.0 77.3 %collective-permute-start.3 = (bf16[3,5,192,256]{3,2,1,0:T(8,128)(2,1)}, bf16[3,5,192,256]{3,2,1,0:T(8,128)(2,1)}, u32[]{:S(2)}, u32[]{:S(2)}) collective-permute-start(bf16[3,5,192,256]{3,2,1,0:T(8,128)(2,1)} %get-tuple-element.89.refs_5_), channel_id=1, source_target_pairs={{0,8},{4,12},{8,0},{12,4},{16,24},{20,28},{24,16},{28,20},{1,9},{5... | collective-permute-start | bytes 4423688 | tf_op jit(solution)/shard_map/ppermute | solution.py:67
  88.8 76.5 %collective-permute-start.2 = (bf16[3,5,192,256]{3,2,1,0:T(8,128)(2,1)}, bf16[3,5,192,256]{3,2,1,0:T(8,128)(2,1)}, u32[]{:S(2)}, u32[]{:S(2)}) collective-permute-start(bf16[3,5,192,256]{3,2,1,0:T(8,128)(2,1)} %get-tuple-element.90.refs_6_), channel_id=1, source_target_pairs={{0,16},{4,20},{8,24},{12,28},{16,0},{20,4},{24,8},{28,12},{1,17},{... | collective-permute-start | bytes 4423688 | tf_op jit(solution)/shard_map/ppermute | solution.py:70
  193.0 28.4 %collective-permute-start.6 = (bf16[512,1664]{1,0:T(8,128)(2,1)}, bf16[512,1664]{1,0:T(8,128)(2,1)S(1)}, u32[]{:S(2)}, u32[]{:S(2)}) collective-permute-start(bf16[512,1664]{1,0:T(8,128)(2,1)} %get-tuple-element.96), channel_id=1, source_target_pairs={{0,4},{4,0},{8,12},{12,8},{16,20},{20,16},{24,28},{28,24},{1,5},{5... | collective-permute-start | bytes 5111816 | tf_op jit(solution)/shard_map/ppermute | solution.py:64
  221.0 75.7 %collective-permute-start.10 = (bf16[512,1536]{1,0:T(8,128)(2,1)}, bf16[512,1536]{1,0:T(8,128)(2,1)}, u32[]{:S(2)}, u32[]{:S(2)}) collective-permute-start(bf16[512,1536]{1,0:T(8,128)(2,1)} %get-tuple-element.98), channel_id=1, source_target_pairs={{0,4},{4,0},{8,12},{12,8},{16,20},{20,16},{24,28},{28,24},{1,5},{5... | collective-permute-start | bytes 4718600 | tf_op jit(solution)/shard_map/ppermute | solution.py:64
  226.3 23.2 %collective-permute-start.9 = (bf16[128,1664]{1,0:T(8,128)(2,1)}, bf16[128,1664]{1,0:T(8,128)(2,1)}, u32[]{:S(2)}, u32[]{:S(2)}) collective-permute-start(bf16[128,1664]{1,0:T(8,128)(2,1)} %get-tuple-element.192), channel_id=1, source_target_pairs={{0,1},{1,2},{2,3},{3,0},{4,5},{5,6},{6,7},{7,4},{8,9},{9,10},{10,1... | collective-permute-start | bytes 1277960 | tf_op jit(solution)/shard_map/ppermute | solution.py:77
  227.6 35.0 %collective-permute-start.8 = (bf16[128,1664]{1,0:T(8,128)(2,1)S(1)}, bf16[128,1664]{1,0:T(8,128)(2,1)}, u32[]{:S(2)}, u32[]{:S(2)}) collective-permute-start(bf16[128,1664]{1,0:T(8,128)(2,1)S(1)} %get-tuple-element.193), channel_id=1, source_target_pairs={{0,2},{1,3},{2,0},{3,1},{4,6},{5,7},{6,4},{7,5},{8,10},{9,11},{10,... | collective-permute-start | bytes 1277960 | tf_op jit(solution)/shard_map/ppermute | solution.py:77
  227.6 35.0 %collective-permute-start.7 = (bf16[128,1664]{1,0:T(8,128)(2,1)S(1)}, bf16[128,1664]{1,0:T(8,128)(2,1)}, u32[]{:S(2)}, u32[]{:S(2)}) collective-permute-start(bf16[128,1664]{1,0:T(8,128)(2,1)S(1)} %get-tuple-element.194), channel_id=1, source_target_pairs={{0,3},{1,0},{2,1},{3,2},{4,7},{5,4},{6,5},{7,6},{8,11},{9,8},{10,9... | collective-permute-start | bytes 1277960 | tf_op jit(solution)/shard_map/ppermute | solution.py:77
  246.3 73.0 %collective-permute-start.11 = (bf16[2,3,5,192,256]{4,3,2,1,0:T(8,128)(2,1)}, bf16[2,3,5,192,256]{4,3,2,1,0:T(8,128)(2,1)S(1)}, u32[]{:S(2)}, u32[]{:S(2)}) collective-permute-start(bf16[2,3,5,192,256]{4,3,2,1,0:T(8,128)(2,1)} %get-tuple-element.113), channel_id=1, source_target_pairs={{0,16},{4,20},{8,24},{12,28},{16,0},{20,4},{24,8},{28,12},{1,17},{... | collective-permute-start | bytes 8847368 | tf_op jit(solution)/shard_map/ppermute | solution.py:70
  249.6 69.8 %collective-permute-start.12 = (bf16[2,3,5,192,256]{4,3,2,1,0:T(8,128)(2,1)}, bf16[2,3,5,192,256]{4,3,2,1,0:T(8,128)(2,1)}, u32[]{:S(2)}, u32[]{:S(2)}) collective-permute-start(bf16[2,3,5,192,256]{4,3,2,1,0:T(8,128)(2,1)} %get-tuple-element.114), channel_id=1, source_target_pairs={{0,8},{4,12},{8,0},{12,4},{16,24},{20,28},{24,16},{28,20},{1,9},{5... | collective-permute-start | bytes 8847368 | tf_op jit(solution)/shard_map/ppermute | solution.py:67
  300.8 28.4 %collective-permute-start.13 = (bf16[128,1536]{1,0:T(8,128)(2,1)}, bf16[128,1536]{1,0:T(8,128)(2,1)S(1)}, u32[]{:S(2)}, u32[]{:S(2)}) collective-permute-start(bf16[128,1536]{1,0:T(8,128)(2,1)} %get-tuple-element.128), channel_id=1, source_target_pairs={{0,3},{1,0},{2,1},{3,2},{4,7},{5,4},{6,5},{7,6},{8,11},{9,8},{10,9... | collective-permute-start | bytes 1179656 | tf_op jit(solution)/shard_map/ppermute | solution.py:77
  300.8 28.4 %collective-permute-start.14 = (bf16[128,1536]{1,0:T(8,128)(2,1)}, bf16[128,1536]{1,0:T(8,128)(2,1)}, u32[]{:S(2)}, u32[]{:S(2)}) collective-permute-start(bf16[128,1536]{1,0:T(8,128)(2,1)} %get-tuple-element.129), channel_id=1, source_target_pairs={{0,2},{1,3},{2,0},{3,1},{4,6},{5,7},{6,4},{7,5},{8,10},{9,11},{10,... | collective-permute-start | bytes 1179656 | tf_op jit(solution)/shard_map/ppermute | solution.py:77
  302.2 26.9 %collective-permute-start.15 = (bf16[128,1536]{1,0:T(8,128)(2,1)}, bf16[128,1536]{1,0:T(8,128)(2,1)}, u32[]{:S(2)}, u32[]{:S(2)}) collective-permute-start(bf16[128,1536]{1,0:T(8,128)(2,1)} %get-tuple-element.130), channel_id=1, source_target_pairs={{0,1},{1,2},{2,3},{3,0},{4,5},{5,6},{6,7},{7,4},{8,9},{9,10},{10,1... | collective-permute-start | bytes 1179656 | tf_op jit(solution)/shard_map/ppermute | solution.py:77
  324.5 62.9 %collective-permute-start.17 = (bf16[3,5,192,256]{3,2,1,0:T(8,128)(2,1)}, bf16[3,5,192,256]{3,2,1,0:T(8,128)(2,1)}, u32[]{:S(2)}, u32[]{:S(2)}) collective-permute-start(bf16[3,5,192,256]{3,2,1,0:T(8,128)(2,1)} %fusion.3), channel_id=1, source_target_pairs={{0,16},{4,20},{8,24},{12,28},{16,0},{20,4},{24,8},{28,12},{1,17},{... | collective-permute-start | bytes 4423688 | tf_op jit(solution)/shard_map/ppermute | solution.py:70
  328.5 58.9 %collective-permute-start.16 = (bf16[3,5,192,256]{3,2,1,0:T(8,128)(2,1)}, bf16[3,5,192,256]{3,2,1,0:T(8,128)(2,1)}, u32[]{:S(2)}, u32[]{:S(2)}) collective-permute-start(bf16[3,5,192,256]{3,2,1,0:T(8,128)(2,1)} %fusion.2), channel_id=1, source_target_pairs={{0,8},{4,12},{8,0},{12,4},{16,24},{20,28},{24,16},{28,20},{1,9},{5... | collective-permute-start | bytes 4423688 | tf_op jit(solution)/shard_map/ppermute | solution.py:67
  391.7 18.8 %collective-permute-start.19 = (bf16[2,5,192,256]{3,2,1,0:T(8,128)(2,1)}, bf16[2,5,192,256]{3,2,1,0:T(8,128)(2,1)S(1)}, u32[]{:S(2)}, u32[]{:S(2)}) collective-permute-start(bf16[2,5,192,256]{3,2,1,0:T(8,128)(2,1)} %fusion.1), channel_id=1, source_target_pairs={{0,4},{4,0},{8,12},{12,8},{16,20},{20,16},{24,28},{28,24},{1,5},{5... | collective-permute-start | bytes 2949128 | tf_op jit(solution)/shard_map/ppermute | solution.py:64
  398.3 11.5 %collective-permute-start.18 = (bf16[48,1536]{1,0:T(8,128)(2,1)S(1)}, bf16[48,1536]{1,0:T(8,128)(2,1)S(1)}, u32[]{:S(2)}, u32[]{:S(2)}) collective-permute-start(bf16[48,1536]{1,0:T(8,128)(2,1)S(1)} %convert_element_type.119), channel_id=1, source_target_pairs={{0,0},{4,1},{8,2},{12,3},{16,4},{20,5},{24,6},{28,7},{1,8},{5,9},{... | collective-permute-start | bytes 442376 | tf_op jit(solution)/shard_map/ppermute | solution.py:1307
  (11 other events, 45.4 us)

commit v6 on v5

--- a/solution.py
+++ b/solution.py
@@ -779,6 +779,64 @@
                     self.copy(way, h).wait_send()
 
 
+class LineScatter:
+    def __init__(self, spot, coming, going, send_sem, recv_sem):
+        self.spot, self.coming, self.going, self.sems = spot, coming, going, (send_sem, recv_sem)
+        me, n = spot.rank, spot.ranks
+        self.more = me >= 1, me + 1 < n
+        self.goes = [(me + t < n, me - t >= 0) for t in range(n)]
+
+    def copy(self, way, t):
+        return pltpu.make_async_remote_copy(
+            src_ref=self.going.at[way, t - 1],
+            dst_ref=self.coming.at[way, t - 1],
+            send_sem=self.sems[0].at[way, t - 1],
+            recv_sem=self.sems[1].at[way, t - 1],
+            device_id=self.spot.ahead(1) if way == 0 else self.spot.behind(1),
+            device_id_type=MESH,
+        )
+
+    def run(self, own, total):
+        n = self.spot.ranks
+        for t in range(n - 1, 0, -1):
+            for way in range(2):
+                slot = n - t if way == 0 else t
+
+                @pl.when(self.goes[t][way])
+                def _():
+                    if t == n - 1:
+                        self.going[way, t - 1] = own[slot].astype(BF16)
+                    else:
+
+                        @pl.when(self.more[way])
+                        def _():
+                            self.copy(way, t + 1).wait_recv()
+                            self.going[way, t - 1] = (
+                                own[slot] + self.coming[way, t].astype(F32)
+                            ).astype(BF16)
+
+                        @pl.when(jnp.logical_not(self.more[way]))
+                        def _():
+                            self.going[way, t - 1] = own[slot].astype(BF16)
+
+                    self.copy(way, t).start()
+
+        for way in range(2):
+
+            @pl.when(self.more[way])
+            def _():
+                self.copy(way, 1).wait_recv()
+                total[...] += self.coming[way, 0].astype(F32)
+
+    def drain(self):
+        for t in range(self.spot.ranks - 1, 0, -1):
+            for way in range(2):
+
+                @pl.when(self.goes[t][way])
+                def _():
+                    self.copy(way, t).wait_send()
+
+
 def half_lines(spot, buf, send_sem, recv_sem):
     return [LineGather(spot, buf, send_sem.at[k], recv_sem.at[k], k, 2) for k in range(2)]
 
@@ -786,7 +844,7 @@
 def attend_kernel(ranks, plane_size, kv_heads, gain_row, *refs):
     x_all, weights, out_weights, bias, cosine, sine, x = refs[:7]
     (extra_t, a1, qk, val, mixed, maxes, inverse, h_out, a2, gathered, other) = refs[7:18]
-    mixed_t, sums, got, r_send, r_recv, g_send, g_recv, c_send, c_recv = refs[18:]
+    mixed_t, sums, got, going, r_send, r_recv, g_send, g_recv, c_send, c_recv = refs[18:]
     extra_t[...] = weights[:, weights.shape[1] - LANES :].T
     gain = extra_t[gain_row : gain_row + 1, :].astype(F32)
     gain_two = extra_t[gain_row + 1 : gain_row + 2, :].astype(F32)
@@ -822,15 +880,12 @@
     mixed[...] = mixed_t[...].T.astype(BF16)
     await_peers(peers)
     total = dot(mixed[...], out_weights[...])
-    for b in range(1, ranks):
-        sums[b - 1] = total[b * rows : (b + 1) * rows, :].astype(BF16)
-    copies = scatter_start(
-        spot, [None] + [sums.at[s - 1] for s in range(1, ranks)], got, r_send, r_recv
-    )
-    total = x[...] + total[:rows, :]
-    for s in range(1, ranks):
-        copies[s - 1].wait()
-        total = total + got[s - 1].astype(F32)
+    for b in range(ranks):
+        sums[b] = total[b * rows : (b + 1) * rows, :]
+    h_out[...] = x[...] + sums[0]
+    scatter = LineScatter(spot, got, going, r_send, r_recv)
+    scatter.run(sums, h_out)
+    total = h_out[...]
     scale = lax.rsqrt(jnp.mean(total * total, axis=-1, keepdims=True) + EPSILON)
     low = (total * scale * gain_two).astype(BF16)
     gathered[0] = low
@@ -851,13 +906,13 @@
     for part in range(2):
         across(0, part).start()
     a2[...] = low
-    h_out[...] = total
     for hop in range(ranks - 1):
         for part, line in enumerate(lines):
             line.arrive(hop)
             if hop + 1 < line.hops:
                 line.start(hop + 1)
             line.passed(hop, lambda s: across(s, part).start())
+    scatter.drain()
     for part, line in enumerate(lines):
         line.drain()
         for s in range(ranks):
@@ -894,10 +949,11 @@
         out_shape=outs,
         scratch_shapes=[
             pltpu.VMEM((q_width, seq), F32),
-            pltpu.VMEM((ranks - 1, rows, model), BF16),
-            pltpu.VMEM((ranks - 1, rows, model), BF16),
-            dma((ranks - 1,)),
-            dma((ranks - 1,)),
+            pltpu.VMEM((ranks, rows, model), F32),
+            pltpu.VMEM((2, ranks - 1, rows, model), BF16),
+            pltpu.VMEM((2, ranks - 1, rows, model), BF16),
+            dma((2, ranks - 1)),
+            dma((2, ranks - 1)),
             dma((2, 2, ranks - 1)),
             dma((2, 2, ranks - 1)),
             dma((2, ranks)),
@@ -1212,13 +1268,15 @@
     other_out, other_dx, _, *other_kept = experts(
         [other_a2.reshape(seq, model)], other_grads, extra_t, where, pieces, place, BF16
     )
+    own_a2, other_out, other_dx = lax.optimization_barrier((own_a2, other_out, other_dx))
     out_all, dx_all, gates, *own_kept = experts(
-        [own_a2.reshape(seq, model)], grads, extra_t, where, pieces, place, F32
-    )
-    dx_all = dx_all + plane.other_core(other_dx).astype(F32)
+        [own_a2.reshape(seq, model)], grads, extra_t, where, pieces, place, BF16
+    )
+    dx_all = dx_all.astype(F32) + plane.other_core(other_dx).astype(F32)
     dxs = [
         dx_all[b * rows : (b + 1) * rows].astype(F32 if b == 0 else BF16) for b in range(ranks)
     ]
+    dxs, own_kept = lax.optimization_barrier((dxs, own_kept))
     dx_got = expert_scatter(dxs)
     chips = [
         ((plane.row + s) % plane.rows) * 2 + (plane.mid + mid) % 2
@@ -1242,14 +1300,14 @@
     a_first = [plane.next_row(by_row[s], s) for s in steps]
     b_first = plane.other_mid(by_mid[1])
 
-    dh, dh_stack, extra = rejoin(
-        [dxs[0]] + dx_got, gates, mid_rows, cotangent, extra_t, a2, gain_two_row, plane.size
-    )
     other_out = plane.other_core(other_out)
-    dh_stack, other_out, out_all = lax.optimization_barrier((dh_stack, other_out, out_all))
-    out_all = out_all + other_out.astype(F32)
+    out_all = out_all.astype(F32) + other_out.astype(F32)
     outs = [out_all[b * rows : (b + 1) * rows] for b in range(ranks)]
     outs = [outs[0]] + [v.astype(BF16) for v in outs[1:]]
+    outs, dx_own = lax.optimization_barrier((outs, dxs[0]))
+    dh, dh_stack, extra = rejoin(
+        [dx_own] + dx_got, gates, mid_rows, cotangent, extra_t, a2, gain_two_row, plane.size
+    )
     dh_stack, outs = lax.optimization_barrier((dh_stack, outs))
     out_got = expert_scatter(outs)
 

time: 423 us -> 415 us (0.981)
  waiting for transfers between devices: 17.6 us -> 13.2 us
  other arithmetic: 29.9 us -> 25.5 us
    pallas_call x1, Pallas kernels: 34.1 us -> 39.7 us  [rejoin(): pl.pallas_call(functools.partial(rejoin_kernel, ranks, plane_size, gain_r...]
    ppermute x6, waiting for transfers between devices: 12.4 us -> 7.78 us  [expert_shift(): lax.ppermute(x, 'expert', [(i, (i + step) % count) for i in range(count)])]
    another operation x5, other arithmetic: 7.09 us -> 2.49 us
    unnamed x35 -> x37, local copies, waits for them, and re-layouts: 8.05 us -> 8.77 us
  transfers between devices with their start and end apart: 20 -> 20, of which waited for: 2 -> 3; matrix products, arithmetic and copies ran while one was open for 9% -> 7% of each run, Pallas kernels for 53% -> 54%
where the time goes in v6:
time: 415 us; the launch traced here: 413 us
  Pallas kernels  332 us (80%)
  other arithmetic  25.5 us (6%)
  starting transfers between devices  23.5 us (6%)
  local copies, waits for them, and re-layouts  17.8 us (4%)
  waiting for transfers between devices  13.2 us (3%)
    pallas_call x1, Pallas kernels, gather_weights(): pl.pallas_call(functools.partial(gather_weights_kernel, ranks, plane_size...  72.5 us
    pallas_call x1, Pallas kernels, attend(): pl.pallas_call(functools.partial(attend_kernel, ranks, plane_size, kv_hea...  68 us
    pallas_call x1, Pallas kernels, last(): pl.pallas_call(functools.partial(last_kernel, ranks, 2 * chips, gain_row)...  57.5 us
    pallas_call x2, Pallas kernels, experts(): pl.pallas_call(functools.partial(experts_kernel, blocks, len(pieces), pla...  52.1 us
    pallas_call x1, Pallas kernels, rejoin(): pl.pallas_call(functools.partial(rejoin_kernel, ranks, plane_size, gain_r...  39.7 us
    pallas_call x1, Pallas kernels, expert_grads(): pl.pallas_call(functools.partial(expert_grads_kernel, plane_rows, depth,...  18.4 us
    pallas_call x1, Pallas kernels, attend_back(): pl.pallas_call(functools.partial(attend_back_kernel, blocks, kv_heads, ga...  15.4 us
    unnamed x37, local copies, waits for them, and re-layouts  8.77 us
  transfers between devices with their start and end apart: 20, of which 3 were waited for; matrix products, arithmetic and copies ran while one was open for 7% of the time, Pallas kernels for 54%

profile of v6, /device:TPU:27, one launch (start us, length us, event | category | flops | bytes accessed | tf_op | source)
XLA Modules:
  0.0 413.2 jit_solution(13879662543713212879)
XLA Ops:
  1.8 3.1 collective-permute-start
  12.9 72.5 %gather_weights.1 = (bf16[8,4,48,768]{3,2,1,0:T(8,128)(2,1)}, bf16[8,48,1536]{2,1,0:T(8,128)(2,1)}, bf16[4,128,1536]{2,1,0:T(8,128)(2,1)}, bf16[4,128,1664]{2,1,...) custom-call(bf16[4,48,768]{2,1,0:T(8,128)(2,1)} %maximum_bitcast_fus, ...), custom_call_target="tpu_custom_call" | custom-call | tf_op jit(solution)/shard_map/gather_weights/pallas_call | solution.py:682
  85.6 2.0 collective-permute-start.5
  93.3 68.0 %attend.1 = (bf16[128,1536]{1,0:T(8,128)(2,1)}, bf16[512,1536]{1,0:T(8,128)(2,1)}, bf16[512,512]{1,0:T(8,128)(2,1)}, bf16[512,128]{1,0:T(8,128)(2,1)}, bf16[512,...) custom-call(bf16[4,128,1536]{2,1,0:T(8,128)(2,1)} %get-tuple-element, ...), custom_call_target="tpu_custom_call" | custom-call | tf_op jit(solution)/shard_map/attend/pallas_call | solution.py:945
  162.9 26.1 %experts.2 = (bf16[512,1536]{1,0:T(8,128)(2,1)}, bf16[512,1664]{1,0:T(8,128)(2,1)}, f32[128,128]{1,0:T(8,128)}, bf16[1536,512]{1,0:T(8,128)(2,1)}, bf16[5,256,51...) custom-call(bf16[512,1536]{1,0:T(8,128)(2,1)} %bitcast.79, ...), custom_call_target="tpu_custom_call" | custom-call | tf_op jit(solution)/shard_map/experts/pallas_call | solution.py:233
  190.2 26.1 %experts.3 = (bf16[512,1536]{1,0:T(8,128)(2,1)}, bf16[512,1664]{1,0:T(8,128)(2,1)}, f32[128,128]{1,0:T(8,128)}, bf16[1536,512]{1,0:T(8,128)(2,1)}, bf16[5,256,51...) custom-call(bf16[512,1536]{1,0:T(8,128)(2,1)} %bitcast.78, bf16[512,1664]{1,0:T(8,128)(2,1)} %bitcast.76, ...), custom_call_target="tpu_custom_call" | custom-call | tf_op jit(solution)/shard_map/experts/pallas_call | solution.py:233
  216.3 2.0 fusion.17
  222.4 1.4 collective-permute-start.9
  223.8 1.8 collective-permute-start.10
  225.6 18.4 %expert_grads.1 = (bf16[2,3,5,192,256]{4,3,2,1,0:T(8,128)(2,1)}, bf16[2,3,5,192,256]{4,3,2,1,0:T(8,128)(2,1)}, bf16[2,3,5,192,256]{4,3,2,1,0:T(8,128)(2,1)}, bf16[2,3,5,192,256]{4,3,2,1,0:T(8,128)(2,1)}) custom-call(s32[4]{0:T(128)} %pad_add_fusion.where_ref, bf16[1536,512]{1,0:T(8,128)(2,1)} %get-tuple-element.130.refs_0_, ...), custom_call_target="tpu_custom_call" | custom-call | flops 17999998976 | bytes 18000000 | tf_op jit(solution)/shard_map/expert_grads/pallas_call | solution.py:296
  245.6 7.6 %collective-permute-done.9.refs_2_ = bf16[128,1664]{1,0:T(8,128)(2,1)} collective-permute-done((bf16[128,1664]{1,0:T(8,128)(2,1)}, bf16[128,1664]{1,0:T(8,128)(2,1)}, u32[]{:S(2)}, u32[]{:S(2)}) %collective-permute-start.9) | collective-permute-done | bytes 426016 | tf_op jit(solution)/shard_map/ppermute | solution.py:77
  253.1 39.7 %rejoin.1 = (f32[128,1536]{1,0:T(8,128)}, bf16[4,128,1536]{2,1,0:T(8,128)(2,1)}, f32[128,1536]{1,0:T(8,128)}) custom-call(f32[128,128]{1,0:T(8,128)} %get-tuple-element.109.gates, f32[128,1536]{1,0:T(8,128)} %get-tuple-element.97.h, f32[128,1536]{1,0:T(8,128)} %dz.1, bf16[128,1536]{1,0:T(8,128)(2,1)} %get-tuple-element.101.refs_2_.router_t.extra_t, ...), custom_call_target="tpu_custom_call" | custom-call | flops 35000000512 | bytes 35000000 | tf_op jit(solution)/shard_map/rejoin/pallas_call | solution.py:1011
  292.9 2.3 collective-permute-start.14
  296.2 15.4 %attend_back.1 = (bf16[1536,768]{1,0:T(8,128)(2,1)}, bf16[384,1536]{1,0:T(8,128)(2,1)}, f32[128,1536]{1,0:T(8,128)}, bf16[128,1536]{1,0:T(8,128)(2,1)}, bf16[128...) custom-call(bf16[4,128,1536]{2,1,0:T(8,128)(2,1)} %get-tuple-element.141.refs_0_, ...), custom_call_target="tpu_custom_call" | custom-call | flops 16000000000 | bytes 16000000 | tf_op jit(solution)/shard_map/attend_back/pallas_call | solution.py:438
  311.6 1.7 copy-done.1
  313.3 3.5 fusion.3
  317.5 2.9 fusion.2
  321.3 57.5 %last.1 = (f32[128,1536]{1,0:T(8,128)}, bf16[4,48,768]{2,1,0:T(8,128)(2,1)}, f32[48,1536]{1,0:T(8,128)}) custom-call(f32[128,1536]{1,0:T(8,128)} %x.1, f32[128,1536]{1,0:T(8,128)} %get-tuple-element.160.dh, bf16[128,1536]{1,0:T(8,128)(2,1)} %get-tuple-element.101.refs_2_.router_t.extra_t, bf16[4,2,4,48,768]{4,3,2,1,0:T(8,128)(2,1)} %bitcast.93, ...), custom_call_target="tpu_custom_call" | custom-call | flops 60000002048 | bytes 60000000 | tf_op jit(solution)/shard_map/last/pallas_call | solution.py:1110
  379.8 4.3 %fusion.1 = bf16[2,5,192,256]{3,2,1,0:T(8,128)(2,1)} fusion(bf16[3,5,192,256]{3,2,1,0:T(8,128)(2,1)} %collective-permute-done.16.refs_2_, bf16[2,3,5,192,256]{4,3,2,1,0:T(8,128)(2,1)} %copy-done.1, bf16[2,3,5,192,256]{4,3,2,1,0:T(8,128)(2,1)S(1)} %copy-done, bf16[3,5,192,256]{3,2,1,0:T(8,128)(2,1)} %collective-permute-done.17.refs_5_, ...), kind=kLoop, calls=%fused_computation.6 | loop fusion | flops 5898240 | bytes 6881281 | tf_op jit(solution)/shard_map/convert_element_type | solution.py:1356
  384.1 4.2 %collective-permute-start.19 = (bf16[2,5,192,256]{3,2,1,0:T(8,128)(2,1)}, bf16[2,5,192,256]{3,2,1,0:T(8,128)(2,1)S(1)}, u32[]{:S(2)}, u32[]{:S(2)}) collective-permute-start(bf16[2,5,192,256]{3,2,1,0:T(8,128)(2,1)} %fusion.1), channel_id=1, source_target_pairs={{0,4},{4,0},{8,12},{12,8},{16,20},{20,16},{24,28},{28,24},{1,5},{5... | collective-permute-start | bytes 2949128 | tf_op jit(solution)/shard_map/ppermute | solution.py:64
  388.4 2.4 convert_add_fusion.2
  390.8 2.5 collective-permute-start.18
  396.8 5.4 %collective-permute-done.18 = bf16[48,1536]{1,0:T(8,128)(2,1)S(1)} collective-permute-done((bf16[48,1536]{1,0:T(8,128)(2,1)S(1)}, bf16[48,1536]{1,0:T(8,128)(2,1)S(1)}, u32[]{:S(2)}, u32[]{:S(2)}) %collective-permute-start.18) | collective-permute-done | bytes 147488 | tf_op jit(solution)/shard_map/ppermute | solution.py:1365
  403.9 8.5 %finish.1 = (f32[5,192,512]{2,1,0:T(8,128)}, f32[5,192,512]{2,1,0:T(8,128)}, f32[5,64,1536]{2,1,0:T(8,128)}) custom-call(s32[1]{0:T(128)} %bitcast.27.core, bf16[2,3,5,192,256]{4,3,2,1,0:T(8,128)(2,1)} %get-tuple-element.138.refs_0_, bf16[2,3,5,192,256]{4,3,2,1,0:T(8,128)(2,1)} %copy-done.1, bf16[3,5,192,256]{3,2,1,0:T(8,128)(2,1)} %collective-permute-done.16.refs_2_, ...), custom_call_target="tpu_custom_call" | custom-call | tf_op jit(solution)/shard_map/finish/pallas_call | solution.py:359
  (114 shorter events, 32.9 us)
Async XLA Ops:
  0.6 8.8 %copy-start.2 = (f32[128,1536]{1,0:T(8,128)S(1)}, f32[128,1536]{1,0:T(8,128)}, u32[]{:S(2)}) copy-start(f32[128,1536]{1,0:T(8,128)} %x.1) | copy-start | bytes 2359300
  0.7 9.7 %copy-start.8 = (f32[128,1536]{1,0:T(8,128)S(1)}, f32[128,1536]{1,0:T(8,128)}, u32[]{:S(2)}) copy-start(f32[128,1536]{1,0:T(8,128)} %dz.1) | copy-start | bytes 2359300
  1.8 8.7 %copy-start.13 = (f32[48,512]{1,0:T(8,128)S(1)}, f32[48,512]{1,0:T(8,128)}, u32[]{:S(2)}) copy-start(f32[48,512]{1,0:T(8,128)} %param.18) | copy-start | bytes 294916
  1.8 8.7 %copy-start.14 = (f32[48,512]{1,0:T(8,128)S(1)}, f32[48,512]{1,0:T(8,128)}, u32[]{:S(2)}) copy-start(f32[48,512]{1,0:T(8,128)} %param.19) | copy-start | bytes 294916
  1.8 10.4 %collective-permute-start = (bf16[48,1536]{1,0:T(8,128)(2,1)S(1)}, bf16[48,1536]{1,0:T(8,128)(2,1)S(1)}, u32[]{:S(2)}, u32[]{:S(2)}) collective-permute-start(bf16[48,1536]{1,0:T(8,128)(2,1)S(1)} %convert_element_type.107), channel_id=1, source_target_pairs={{0,0},{1,4},{2,8},{3,12},{4,16},{5,20},{6,24},{7,28},{8,1},{9,5},{... | collective-permute-start | bytes 442376 | tf_op jit(solution)/shard_map/ppermute | solution.py:1210
  85.4 75.9 %collective-permute-start.1 = (bf16[512,1664]{1,0:T(8,128)(2,1)}, bf16[512,1664]{1,0:T(8,128)(2,1)}, u32[]{:S(2)}, u32[]{:S(2)}) collective-permute-start(bf16[512,1664]{1,0:T(8,128)(2,1)} %bitcast.75), channel_id=1, source_target_pairs={{0,4},{4,0},{8,12},{12,8},{16,20},{20,16},{24,28},{28,24},{1,5},{5... | collective-permute-start | bytes 5111816 | tf_op jit(solution)/shard_map/ppermute | solution.py:64
  85.6 75.7 %collective-permute-start.5 = (bf16[3,5,192,256]{3,2,1,0:T(8,128)(2,1)}, bf16[3,5,192,256]{3,2,1,0:T(8,128)(2,1)S(1)}, u32[]{:S(2)}, u32[]{:S(2)}) collective-permute-start(bf16[3,5,192,256]{3,2,1,0:T(8,128)(2,1)} %bitcast.70), channel_id=1, source_target_pairs={{0,8},{4,12},{8,0},{12,4},{16,24},{20,28},{24,16},{28,20},{1,9},{5... | collective-permute-start | bytes 4423688 | tf_op jit(solution)/shard_map/ppermute | solution.py:67
  87.6 73.7 %collective-permute-start.2 = (bf16[3,5,192,256]{3,2,1,0:T(8,128)(2,1)}, bf16[3,5,192,256]{3,2,1,0:T(8,128)(2,1)S(1)}, u32[]{:S(2)}, u32[]{:S(2)}) collective-permute-start(bf16[3,5,192,256]{3,2,1,0:T(8,128)(2,1)} %get-tuple-element.102.refs_4_), channel_id=1, source_target_pairs={{0,16},{4,20},{8,24},{12,28},{16,0},{20,4},{24,8},{28,12},{1,17},{... | collective-permute-start | bytes 4423688 | tf_op jit(solution)/shard_map/ppermute | solution.py:70
  87.9 73.4 %collective-permute-start.4 = (bf16[3,5,192,256]{3,2,1,0:T(8,128)(2,1)}, bf16[3,5,192,256]{3,2,1,0:T(8,128)(2,1)}, u32[]{:S(2)}, u32[]{:S(2)}) collective-permute-start(bf16[3,5,192,256]{3,2,1,0:T(8,128)(2,1)} %get-tuple-element.103.refs_5_), channel_id=1, source_target_pairs={{0,8},{4,12},{8,0},{12,4},{16,24},{20,28},{24,16},{28,20},{1,9},{5... | collective-permute-start | bytes 4423688 | tf_op jit(solution)/shard_map/ppermute | solution.py:67
  88.7 72.6 %collective-permute-start.3 = (bf16[3,5,192,256]{3,2,1,0:T(8,128)(2,1)}, bf16[3,5,192,256]{3,2,1,0:T(8,128)(2,1)}, u32[]{:S(2)}, u32[]{:S(2)}) collective-permute-start(bf16[3,5,192,256]{3,2,1,0:T(8,128)(2,1)} %get-tuple-element.104.refs_6_), channel_id=1, source_target_pairs={{0,16},{4,20},{8,24},{12,28},{16,0},{20,4},{24,8},{28,12},{1,17},{... | collective-permute-start | bytes 4423688 | tf_op jit(solution)/shard_map/ppermute | solution.py:70
  189.0 27.3 %collective-permute-start.6 = (bf16[512,1536]{1,0:T(8,128)(2,1)}, bf16[512,1536]{1,0:T(8,128)(2,1)S(1)}, u32[]{:S(2)}, u32[]{:S(2)}) collective-permute-start(bf16[512,1536]{1,0:T(8,128)(2,1)} %get-tuple-element.112), channel_id=1, source_target_pairs={{0,4},{4,0},{8,12},{12,8},{16,20},{20,16},{24,28},{28,24},{1,5},{5... | collective-permute-start | bytes 4718600 | tf_op jit(solution)/shard_map/ppermute | solution.py:64
  189.2 30.1 %collective-permute-start.7 = (bf16[512,1664]{1,0:T(8,128)(2,1)}, bf16[512,1664]{1,0:T(8,128)(2,1)S(1)}, u32[]{:S(2)}, u32[]{:S(2)}) collective-permute-start(bf16[512,1664]{1,0:T(8,128)(2,1)} %get-tuple-element.114), channel_id=1, source_target_pairs={{0,4},{4,0},{8,12},{12,8},{16,20},{20,16},{24,28},{28,24},{1,5},{5... | collective-permute-start | bytes 5111816 | tf_op jit(solution)/shard_map/ppermute | solution.py:64
  222.4 23.2 %collective-permute-start.8 = (bf16[128,1664]{1,0:T(8,128)(2,1)}, bf16[128,1664]{1,0:T(8,128)(2,1)}, u32[]{:S(2)}, u32[]{:S(2)}) collective-permute-start(bf16[128,1664]{1,0:T(8,128)(2,1)} %get-tuple-element.121), channel_id=1, source_target_pairs={{0,3},{1,0},{2,1},{3,2},{4,7},{5,4},{6,5},{7,6},{8,11},{9,8},{10,9... | collective-permute-start | bytes 1277960 | tf_op jit(solution)/shard_map/ppermute | solution.py:77
  222.4 30.7 %collective-permute-start.9 = (bf16[128,1664]{1,0:T(8,128)(2,1)}, bf16[128,1664]{1,0:T(8,128)(2,1)}, u32[]{:S(2)}, u32[]{:S(2)}) collective-permute-start(bf16[128,1664]{1,0:T(8,128)(2,1)} %get-tuple-element.122), channel_id=1, source_target_pairs={{0,2},{1,3},{2,0},{3,1},{4,6},{5,7},{6,4},{7,5},{8,10},{9,11},{10,... | collective-permute-start | bytes 1277960 | tf_op jit(solution)/shard_map/ppermute | solution.py:77
  223.8 29.3 %collective-permute-start.10 = (bf16[128,1664]{1,0:T(8,128)(2,1)}, bf16[128,1664]{1,0:T(8,128)(2,1)}, u32[]{:S(2)}, u32[]{:S(2)}) collective-permute-start(bf16[128,1664]{1,0:T(8,128)(2,1)} %get-tuple-element.123), channel_id=1, source_target_pairs={{0,1},{1,2},{2,3},{3,0},{4,5},{5,6},{6,7},{7,4},{8,9},{9,10},{10,1... | collective-permute-start | bytes 1277960 | tf_op jit(solution)/shard_map/ppermute | solution.py:77
  244.1 67.5 %collective-permute-start.11 = (bf16[2,3,5,192,256]{4,3,2,1,0:T(8,128)(2,1)}, bf16[2,3,5,192,256]{4,3,2,1,0:T(8,128)(2,1)S(1)}, u32[]{:S(2)}, u32[]{:S(2)}) collective-permute-start(bf16[2,3,5,192,256]{4,3,2,1,0:T(8,128)(2,1)} %get-tuple-element.139), channel_id=1, source_target_pairs={{0,16},{4,20},{8,24},{12,28},{16,0},{20,4},{24,8},{28,12},{1,17},{... | collective-permute-start | bytes 8847368 | tf_op jit(solution)/shard_map/ppermute | solution.py:70
  244.9 66.7 %collective-permute-start.12 = (bf16[2,3,5,192,256]{4,3,2,1,0:T(8,128)(2,1)}, bf16[2,3,5,192,256]{4,3,2,1,0:T(8,128)(2,1)}, u32[]{:S(2)}, u32[]{:S(2)}) collective-permute-start(bf16[2,3,5,192,256]{4,3,2,1,0:T(8,128)(2,1)} %get-tuple-element.140), channel_id=1, source_target_pairs={{0,8},{4,12},{8,0},{12,4},{16,24},{20,28},{24,16},{28,20},{1,9},{5... | collective-permute-start | bytes 8847368 | tf_op jit(solution)/shard_map/ppermute | solution.py:67
  292.8 28.3 %collective-permute-start.13 = (bf16[128,1536]{1,0:T(8,128)(2,1)}, bf16[128,1536]{1,0:T(8,128)(2,1)}, u32[]{:S(2)}, u32[]{:S(2)}) collective-permute-start(bf16[128,1536]{1,0:T(8,128)(2,1)} %get-tuple-element.154), channel_id=1, source_target_pairs={{0,3},{1,0},{2,1},{3,2},{4,7},{5,4},{6,5},{7,6},{8,11},{9,8},{10,9... | collective-permute-start | bytes 1179656 | tf_op jit(solution)/shard_map/ppermute | solution.py:77
  292.9 28.4 %collective-permute-start.14 = (bf16[128,1536]{1,0:T(8,128)(2,1)}, bf16[128,1536]{1,0:T(8,128)(2,1)}, u32[]{:S(2)}, u32[]{:S(2)}) collective-permute-start(bf16[128,1536]{1,0:T(8,128)(2,1)} %get-tuple-element.155), channel_id=1, source_target_pairs={{0,2},{1,3},{2,0},{3,1},{4,6},{5,7},{6,4},{7,5},{8,10},{9,11},{10,... | collective-permute-start | bytes 1179656 | tf_op jit(solution)/shard_map/ppermute | solution.py:77
  295.3 26.1 %collective-permute-start.15 = (bf16[128,1536]{1,0:T(8,128)(2,1)S(1)}, bf16[128,1536]{1,0:T(8,128)(2,1)}, u32[]{:S(2)}, u32[]{:S(2)}) collective-permute-start(bf16[128,1536]{1,0:T(8,128)(2,1)S(1)} %get-tuple-element.156), channel_id=1, source_target_pairs={{0,1},{1,2},{2,3},{3,0},{4,5},{5,6},{6,7},{7,4},{8,9},{9,10},{10,1... | collective-permute-start | bytes 1179656 | tf_op jit(solution)/shard_map/ppermute | solution.py:77
  316.8 63.0 %collective-permute-start.17 = (bf16[3,5,192,256]{3,2,1,0:T(8,128)(2,1)}, bf16[3,5,192,256]{3,2,1,0:T(8,128)(2,1)}, u32[]{:S(2)}, u32[]{:S(2)}) collective-permute-start(bf16[3,5,192,256]{3,2,1,0:T(8,128)(2,1)} %fusion.3), channel_id=1, source_target_pairs={{0,16},{4,20},{8,24},{12,28},{16,0},{20,4},{24,8},{28,12},{1,17},{... | collective-permute-start | bytes 4423688 | tf_op jit(solution)/shard_map/ppermute | solution.py:70
  320.4 59.3 %collective-permute-start.16 = (bf16[3,5,192,256]{3,2,1,0:T(8,128)(2,1)}, bf16[3,5,192,256]{3,2,1,0:T(8,128)(2,1)}, u32[]{:S(2)}, u32[]{:S(2)}) collective-permute-start(bf16[3,5,192,256]{3,2,1,0:T(8,128)(2,1)} %fusion.2), channel_id=1, source_target_pairs={{0,8},{4,12},{8,0},{12,4},{16,24},{20,28},{24,16},{28,20},{1,9},{5... | collective-permute-start | bytes 4423688 | tf_op jit(solution)/shard_map/ppermute | solution.py:67
  384.1 18.8 %collective-permute-start.19 = (bf16[2,5,192,256]{3,2,1,0:T(8,128)(2,1)}, bf16[2,5,192,256]{3,2,1,0:T(8,128)(2,1)S(1)}, u32[]{:S(2)}, u32[]{:S(2)}) collective-permute-start(bf16[2,5,192,256]{3,2,1,0:T(8,128)(2,1)} %fusion.1), channel_id=1, source_target_pairs={{0,4},{4,0},{8,12},{12,8},{16,20},{20,16},{24,28},{28,24},{1,5},{5... | collective-permute-start | bytes 2949128 | tf_op jit(solution)/shard_map/ppermute | solution.py:64
  390.8 11.4 %collective-permute-start.18 = (bf16[48,1536]{1,0:T(8,128)(2,1)S(1)}, bf16[48,1536]{1,0:T(8,128)(2,1)S(1)}, u32[]{:S(2)}, u32[]{:S(2)}) collective-permute-start(bf16[48,1536]{1,0:T(8,128)(2,1)S(1)} %convert_element_type.127), channel_id=1, source_target_pairs={{0,0},{4,1},{8,2},{12,3},{16,4},{20,5},{24,6},{28,7},{1,8},{5,9},{... | collective-permute-start | bytes 442376 | tf_op jit(solution)/shard_map/ppermute | solution.py:1365
  (12 other events, 39.2 us)

commit v7 on v6

--- a/solution.py
+++ b/solution.py
@@ -1084,7 +1084,7 @@
     value = sum_r[0].astype(F32)
     for k in range(1, chips):
         value = value + chip_r[k - 1].astype(F32)
-    rows_out[...] = value
+    rows_out[...] = value.astype(BF16)
     kept = pltpu.make_async_copy(final.at[me], columns_out.at[me], local.at[0])
     kept.start()
     copies = [
@@ -1111,7 +1111,7 @@
         functools.partial(last_kernel, ranks, 2 * chips, gain_row),
         in_specs=[VMEM] * (5 + ranks),
         out_specs=[VMEM] * 3,
-        out_shape=[shape_of(x.shape, F32), shape_of(w_shape, BF16), shape_of(r_shape, F32)],
+        out_shape=[shape_of(x.shape, F32), shape_of(w_shape, BF16), shape_of(r_shape, BF16)],
         scratch_shapes=[
             pltpu.VMEM((ranks - 1,) + x.shape, BF16),
             pltpu.VMEM((chips,) + w_shape, BF16),
@@ -1362,9 +1362,7 @@
     for v in out_got:
         output = output + v.astype(F32)
 
-    w_output_grad = lax.ppermute(
-        out_part.astype(BF16), axes, [(b, a) for a, b in move]
-    ).astype(F32)
+    w_output_grad = lax.ppermute(out_part, axes, [(b, a) for a, b in move]).astype(F32)
     by_rank = by_rank.astype(F32)
 
     def columns_of(start, width):

time: 415 us -> 415 us (level)
  no operation moved by 1% of the time
where the time goes in v7:
time: 415 us; the launch traced here: 413 us
  Pallas kernels  332 us (80%)
  other arithmetic  25.4 us (6%)
  starting transfers between devices  23.5 us (6%)
  local copies, waits for them, and re-layouts  17.8 us (4%)
  waiting for transfers between devices  13.2 us (3%)
    pallas_call x1, Pallas kernels, gather_weights(): pl.pallas_call(functools.partial(gather_weights_kernel, ranks, plane_size...  72.5 us
    pallas_call x1, Pallas kernels, attend(): pl.pallas_call(functools.partial(attend_kernel, ranks, plane_size, kv_hea...  68 us
    pallas_call x1, Pallas kernels, last(): pl.pallas_call(functools.partial(last_kernel, ranks, 2 * chips, gain_row)...  57.4 us
    pallas_call x2, Pallas kernels, experts(): pl.pallas_call(functools.partial(experts_kernel, blocks, len(pieces), pla...  52.1 us
    pallas_call x1, Pallas kernels, rejoin(): pl.pallas_call(functools.partial(rejoin_kernel, ranks, plane_size, gain_r...  39.7 us
    pallas_call x1, Pallas kernels, expert_grads(): pl.pallas_call(functools.partial(expert_grads_kernel, plane_rows, depth,...  18.4 us
    pallas_call x1, Pallas kernels, attend_back(): pl.pallas_call(functools.partial(attend_back_kernel, blocks, kv_heads, ga...  15.4 us
    unnamed x37, local copies, waits for them, and re-layouts  8.77 us
  transfers between devices with their start and end apart: 20, of which 3 were waited for; matrix products, arithmetic and copies ran while one was open for 7% of the time, Pallas kernels for 54%

profile of v7, /device:TPU:27, one launch (start us, length us, event | category | flops | bytes accessed | tf_op | source)
XLA Modules:
  0.0 413.2 jit_solution(17074335062676665297)
XLA Ops:
  1.8 3.1 collective-permute-start
  12.9 72.5 %gather_weights.1 = (bf16[8,4,48,768]{3,2,1,0:T(8,128)(2,1)}, bf16[8,48,1536]{2,1,0:T(8,128)(2,1)}, bf16[4,128,1536]{2,1,0:T(8,128)(2,1)}, bf16[4,128,1664]{2,1,...) custom-call(bf16[4,48,768]{2,1,0:T(8,128)(2,1)} %maximum_bitcast_fus, ...), custom_call_target="tpu_custom_call" | custom-call | tf_op jit(solution)/shard_map/gather_weights/pallas_call | solution.py:682
  85.6 2.0 collective-permute-start.5
  93.3 68.0 %attend.1 = (bf16[128,1536]{1,0:T(8,128)(2,1)}, bf16[512,1536]{1,0:T(8,128)(2,1)}, bf16[512,512]{1,0:T(8,128)(2,1)}, bf16[512,128]{1,0:T(8,128)(2,1)}, bf16[512,...) custom-call(bf16[4,128,1536]{2,1,0:T(8,128)(2,1)} %get-tuple-element, ...), custom_call_target="tpu_custom_call" | custom-call | tf_op jit(solution)/shard_map/attend/pallas_call | solution.py:945
  162.9 26.1 %experts.2 = (bf16[512,1536]{1,0:T(8,128)(2,1)}, bf16[512,1664]{1,0:T(8,128)(2,1)}, f32[128,128]{1,0:T(8,128)}, bf16[1536,512]{1,0:T(8,128)(2,1)}, bf16[5,256,51...) custom-call(bf16[512,1536]{1,0:T(8,128)(2,1)} %bitcast.79, ...), custom_call_target="tpu_custom_call" | custom-call | tf_op jit(solution)/shard_map/experts/pallas_call | solution.py:233
  190.2 26.1 %experts.3 = (bf16[512,1536]{1,0:T(8,128)(2,1)}, bf16[512,1664]{1,0:T(8,128)(2,1)}, f32[128,128]{1,0:T(8,128)}, bf16[1536,512]{1,0:T(8,128)(2,1)}, bf16[5,256,51...) custom-call(bf16[512,1536]{1,0:T(8,128)(2,1)} %bitcast.78, bf16[512,1664]{1,0:T(8,128)(2,1)} %bitcast.76, ...), custom_call_target="tpu_custom_call" | custom-call | tf_op jit(solution)/shard_map/experts/pallas_call | solution.py:233
  216.3 2.0 fusion.17
  222.4 1.4 collective-permute-start.9
  223.8 1.8 collective-permute-start.10
  225.6 18.4 %expert_grads.1 = (bf16[2,3,5,192,256]{4,3,2,1,0:T(8,128)(2,1)}, bf16[2,3,5,192,256]{4,3,2,1,0:T(8,128)(2,1)}, bf16[2,3,5,192,256]{4,3,2,1,0:T(8,128)(2,1)}, bf16[2,3,5,192,256]{4,3,2,1,0:T(8,128)(2,1)}) custom-call(s32[4]{0:T(128)} %pad_add_fusion.where_ref, bf16[1536,512]{1,0:T(8,128)(2,1)} %get-tuple-element.130.refs_0_, ...), custom_call_target="tpu_custom_call" | custom-call | flops 17999998976 | bytes 18000000 | tf_op jit(solution)/shard_map/expert_grads/pallas_call | solution.py:296
  245.6 7.6 %collective-permute-done.9.refs_2_ = bf16[128,1664]{1,0:T(8,128)(2,1)} collective-permute-done((bf16[128,1664]{1,0:T(8,128)(2,1)}, bf16[128,1664]{1,0:T(8,128)(2,1)}, u32[]{:S(2)}, u32[]{:S(2)}) %collective-permute-start.9) | collective-permute-done | bytes 426016 | tf_op jit(solution)/shard_map/ppermute | solution.py:77
  253.1 39.7 %rejoin.1 = (f32[128,1536]{1,0:T(8,128)}, bf16[4,128,1536]{2,1,0:T(8,128)(2,1)}, f32[128,1536]{1,0:T(8,128)}) custom-call(f32[128,128]{1,0:T(8,128)} %get-tuple-element.109.gates, f32[128,1536]{1,0:T(8,128)} %get-tuple-element.97.h, f32[128,1536]{1,0:T(8,128)} %dz.1, bf16[128,1536]{1,0:T(8,128)(2,1)} %get-tuple-element.101.refs_2_.router_t.extra_t, ...), custom_call_target="tpu_custom_call" | custom-call | flops 35000000512 | bytes 35000000 | tf_op jit(solution)/shard_map/rejoin/pallas_call | solution.py:1011
  292.9 2.3 collective-permute-start.14
  296.2 15.4 %attend_back.1 = (bf16[1536,768]{1,0:T(8,128)(2,1)}, bf16[384,1536]{1,0:T(8,128)(2,1)}, f32[128,1536]{1,0:T(8,128)}, bf16[128,1536]{1,0:T(8,128)(2,1)}, bf16[128...) custom-call(bf16[4,128,1536]{2,1,0:T(8,128)(2,1)} %get-tuple-element.141.refs_0_, ...), custom_call_target="tpu_custom_call" | custom-call | flops 16000000000 | bytes 16000000 | tf_op jit(solution)/shard_map/attend_back/pallas_call | solution.py:438
  311.6 1.7 copy-done.1
  313.3 3.5 fusion.3
  317.5 2.9 fusion.2
  321.3 57.4 %last.1 = (f32[128,1536]{1,0:T(8,128)}, bf16[4,48,768]{2,1,0:T(8,128)(2,1)}, bf16[48,1536]{1,0:T(8,128)(2,1)}) custom-call(f32[128,1536]{1,0:T(8,128)} %x.1, f32[128,1536]{1,0:T(8,128)} %get-tuple-element.160.dh, bf16[128,1536]{1,0:T(8,128)(2,1)} %get-tuple-element.101.refs_2_.router_t.extra_t, bf16[4,2,4,48,768]{4,3,2,1,0:T(8,128)(2,1)} %bitcast.93, ...), custom_call_target="tpu_custom_call" | custom-call | flops 60000002048 | bytes 60000000 | tf_op jit(solution)/shard_map/last/pallas_call | solution.py:1110
  379.8 4.3 %fusion.1 = bf16[2,5,192,256]{3,2,1,0:T(8,128)(2,1)} fusion(bf16[3,5,192,256]{3,2,1,0:T(8,128)(2,1)} %collective-permute-done.16.refs_2_, bf16[2,3,5,192,256]{4,3,2,1,0:T(8,128)(2,1)} %copy-done.1, bf16[2,3,5,192,256]{4,3,2,1,0:T(8,128)(2,1)S(1)} %copy-done, bf16[3,5,192,256]{3,2,1,0:T(8,128)(2,1)} %collective-permute-done.17.refs_5_, ...), kind=kLoop, calls=%fused_computation.6 | loop fusion | flops 5898240 | bytes 6881281 | tf_op jit(solution)/shard_map/convert_element_type | solution.py:1356
  384.1 4.2 %collective-permute-start.19 = (bf16[2,5,192,256]{3,2,1,0:T(8,128)(2,1)}, bf16[2,5,192,256]{3,2,1,0:T(8,128)(2,1)S(1)}, u32[]{:S(2)}, u32[]{:S(2)}) collective-permute-start(bf16[2,5,192,256]{3,2,1,0:T(8,128)(2,1)} %fusion.1), channel_id=1, source_target_pairs={{0,4},{4,0},{8,12},{12,8},{16,20},{20,16},{24,28},{28,24},{1,5},{5... | collective-permute-start | bytes 2949128 | tf_op jit(solution)/shard_map/ppermute | solution.py:64
  388.3 2.4 convert_add_fusion.2
  390.7 2.5 collective-permute-start.18
  396.7 5.4 %collective-permute-done.18 = bf16[48,1536]{1,0:T(8,128)(2,1)S(1)} collective-permute-done((bf16[48,1536]{1,0:T(8,128)(2,1)S(1)}, bf16[48,1536]{1,0:T(8,128)(2,1)S(1)}, u32[]{:S(2)}, u32[]{:S(2)}) %collective-permute-start.18) | collective-permute-done | bytes 147488 | tf_op jit(solution)/shard_map/ppermute | solution.py:1365
  403.8 8.5 %finish.1 = (f32[5,192,512]{2,1,0:T(8,128)}, f32[5,192,512]{2,1,0:T(8,128)}, f32[5,64,1536]{2,1,0:T(8,128)}) custom-call(s32[1]{0:T(128)} %bitcast.27.core, bf16[2,3,5,192,256]{4,3,2,1,0:T(8,128)(2,1)} %get-tuple-element.138.refs_0_, bf16[2,3,5,192,256]{4,3,2,1,0:T(8,128)(2,1)} %copy-done.1, bf16[3,5,192,256]{3,2,1,0:T(8,128)(2,1)} %collective-permute-done.16.refs_2_, ...), custom_call_target="tpu_custom_call" | custom-call | tf_op jit(solution)/shard_map/finish/pallas_call | solution.py:359
  (113 shorter events, 32.9 us)
Async XLA Ops:
  0.6 8.8 %copy-start.2 = (f32[128,1536]{1,0:T(8,128)S(1)}, f32[128,1536]{1,0:T(8,128)}, u32[]{:S(2)}) copy-start(f32[128,1536]{1,0:T(8,128)} %x.1) | copy-start | bytes 2359300
  0.7 9.7 %copy-start.8 = (f32[128,1536]{1,0:T(8,128)S(1)}, f32[128,1536]{1,0:T(8,128)}, u32[]{:S(2)}) copy-start(f32[128,1536]{1,0:T(8,128)} %dz.1) | copy-start | bytes 2359300
  1.8 8.7 %copy-start.12 = (f32[48,512]{1,0:T(8,128)S(1)}, f32[48,512]{1,0:T(8,128)}, u32[]{:S(2)}) copy-start(f32[48,512]{1,0:T(8,128)} %param.18) | copy-start | bytes 294916
  1.8 8.7 %copy-start.13 = (f32[48,512]{1,0:T(8,128)S(1)}, f32[48,512]{1,0:T(8,128)}, u32[]{:S(2)}) copy-start(f32[48,512]{1,0:T(8,128)} %param.19) | copy-start | bytes 294916
  1.8 10.4 %collective-permute-start = (bf16[48,1536]{1,0:T(8,128)(2,1)S(1)}, bf16[48,1536]{1,0:T(8,128)(2,1)S(1)}, u32[]{:S(2)}, u32[]{:S(2)}) collective-permute-start(bf16[48,1536]{1,0:T(8,128)(2,1)S(1)} %convert_element_type.104), channel_id=1, source_target_pairs={{0,0},{1,4},{2,8},{3,12},{4,16},{5,20},{6,24},{7,28},{8,1},{9,5},{... | collective-permute-start | bytes 442376 | tf_op jit(solution)/shard_map/ppermute | solution.py:1210
  85.4 75.9 %collective-permute-start.1 = (bf16[512,1664]{1,0:T(8,128)(2,1)}, bf16[512,1664]{1,0:T(8,128)(2,1)}, u32[]{:S(2)}, u32[]{:S(2)}) collective-permute-start(bf16[512,1664]{1,0:T(8,128)(2,1)} %bitcast.75), channel_id=1, source_target_pairs={{0,4},{4,0},{8,12},{12,8},{16,20},{20,16},{24,28},{28,24},{1,5},{5... | collective-permute-start | bytes 5111816 | tf_op jit(solution)/shard_map/ppermute | solution.py:64
  85.6 75.7 %collective-permute-start.5 = (bf16[3,5,192,256]{3,2,1,0:T(8,128)(2,1)}, bf16[3,5,192,256]{3,2,1,0:T(8,128)(2,1)S(1)}, u32[]{:S(2)}, u32[]{:S(2)}) collective-permute-start(bf16[3,5,192,256]{3,2,1,0:T(8,128)(2,1)} %bitcast.70), channel_id=1, source_target_pairs={{0,8},{4,12},{8,0},{12,4},{16,24},{20,28},{24,16},{28,20},{1,9},{5... | collective-permute-start | bytes 4423688 | tf_op jit(solution)/shard_map/ppermute | solution.py:67
  87.6 73.7 %collective-permute-start.2 = (bf16[3,5,192,256]{3,2,1,0:T(8,128)(2,1)}, bf16[3,5,192,256]{3,2,1,0:T(8,128)(2,1)S(1)}, u32[]{:S(2)}, u32[]{:S(2)}) collective-permute-start(bf16[3,5,192,256]{3,2,1,0:T(8,128)(2,1)} %get-tuple-element.102.refs_4_), channel_id=1, source_target_pairs={{0,16},{4,20},{8,24},{12,28},{16,0},{20,4},{24,8},{28,12},{1,17},{... | collective-permute-start | bytes 4423688 | tf_op jit(solution)/shard_map/ppermute | solution.py:70
  87.9 73.4 %collective-permute-start.4 = (bf16[3,5,192,256]{3,2,1,0:T(8,128)(2,1)}, bf16[3,5,192,256]{3,2,1,0:T(8,128)(2,1)}, u32[]{:S(2)}, u32[]{:S(2)}) collective-permute-start(bf16[3,5,192,256]{3,2,1,0:T(8,128)(2,1)} %get-tuple-element.103.refs_5_), channel_id=1, source_target_pairs={{0,8},{4,12},{8,0},{12,4},{16,24},{20,28},{24,16},{28,20},{1,9},{5... | collective-permute-start | bytes 4423688 | tf_op jit(solution)/shard_map/ppermute | solution.py:67
  88.7 72.6 %collective-permute-start.3 = (bf16[3,5,192,256]{3,2,1,0:T(8,128)(2,1)}, bf16[3,5,192,256]{3,2,1,0:T(8,128)(2,1)}, u32[]{:S(2)}, u32[]{:S(2)}) collective-permute-start(bf16[3,5,192,256]{3,2,1,0:T(8,128)(2,1)} %get-tuple-element.104.refs_6_), channel_id=1, source_target_pairs={{0,16},{4,20},{8,24},{12,28},{16,0},{20,4},{24,8},{28,12},{1,17},{... | collective-permute-start | bytes 4423688 | tf_op jit(solution)/shard_map/ppermute | solution.py:70
  189.0 27.3 %collective-permute-start.6 = (bf16[512,1536]{1,0:T(8,128)(2,1)}, bf16[512,1536]{1,0:T(8,128)(2,1)S(1)}, u32[]{:S(2)}, u32[]{:S(2)}) collective-permute-start(bf16[512,1536]{1,0:T(8,128)(2,1)} %get-tuple-element.112), channel_id=1, source_target_pairs={{0,4},{4,0},{8,12},{12,8},{16,20},{20,16},{24,28},{28,24},{1,5},{5... | collective-permute-start | bytes 4718600 | tf_op jit(solution)/shard_map/ppermute | solution.py:64
  189.2 30.1 %collective-permute-start.7 = (bf16[512,1664]{1,0:T(8,128)(2,1)}, bf16[512,1664]{1,0:T(8,128)(2,1)S(1)}, u32[]{:S(2)}, u32[]{:S(2)}) collective-permute-start(bf16[512,1664]{1,0:T(8,128)(2,1)} %get-tuple-element.114), channel_id=1, source_target_pairs={{0,4},{4,0},{8,12},{12,8},{16,20},{20,16},{24,28},{28,24},{1,5},{5... | collective-permute-start | bytes 5111816 | tf_op jit(solution)/shard_map/ppermute | solution.py:64
  222.4 23.2 %collective-permute-start.8 = (bf16[128,1664]{1,0:T(8,128)(2,1)}, bf16[128,1664]{1,0:T(8,128)(2,1)}, u32[]{:S(2)}, u32[]{:S(2)}) collective-permute-start(bf16[128,1664]{1,0:T(8,128)(2,1)} %get-tuple-element.121), channel_id=1, source_target_pairs={{0,3},{1,0},{2,1},{3,2},{4,7},{5,4},{6,5},{7,6},{8,11},{9,8},{10,9... | collective-permute-start | bytes 1277960 | tf_op jit(solution)/shard_map/ppermute | solution.py:77
  222.4 30.7 %collective-permute-start.9 = (bf16[128,1664]{1,0:T(8,128)(2,1)}, bf16[128,1664]{1,0:T(8,128)(2,1)}, u32[]{:S(2)}, u32[]{:S(2)}) collective-permute-start(bf16[128,1664]{1,0:T(8,128)(2,1)} %get-tuple-element.122), channel_id=1, source_target_pairs={{0,2},{1,3},{2,0},{3,1},{4,6},{5,7},{6,4},{7,5},{8,10},{9,11},{10,... | collective-permute-start | bytes 1277960 | tf_op jit(solution)/shard_map/ppermute | solution.py:77
  223.8 29.3 %collective-permute-start.10 = (bf16[128,1664]{1,0:T(8,128)(2,1)}, bf16[128,1664]{1,0:T(8,128)(2,1)}, u32[]{:S(2)}, u32[]{:S(2)}) collective-permute-start(bf16[128,1664]{1,0:T(8,128)(2,1)} %get-tuple-element.123), channel_id=1, source_target_pairs={{0,1},{1,2},{2,3},{3,0},{4,5},{5,6},{6,7},{7,4},{8,9},{9,10},{10,1... | collective-permute-start | bytes 1277960 | tf_op jit(solution)/shard_map/ppermute | solution.py:77
  244.1 67.5 %collective-permute-start.11 = (bf16[2,3,5,192,256]{4,3,2,1,0:T(8,128)(2,1)}, bf16[2,3,5,192,256]{4,3,2,1,0:T(8,128)(2,1)S(1)}, u32[]{:S(2)}, u32[]{:S(2)}) collective-permute-start(bf16[2,3,5,192,256]{4,3,2,1,0:T(8,128)(2,1)} %get-tuple-element.139), channel_id=1, source_target_pairs={{0,16},{4,20},{8,24},{12,28},{16,0},{20,4},{24,8},{28,12},{1,17},{... | collective-permute-start | bytes 8847368 | tf_op jit(solution)/shard_map/ppermute | solution.py:70
  244.9 66.7 %collective-permute-start.12 = (bf16[2,3,5,192,256]{4,3,2,1,0:T(8,128)(2,1)}, bf16[2,3,5,192,256]{4,3,2,1,0:T(8,128)(2,1)}, u32[]{:S(2)}, u32[]{:S(2)}) collective-permute-start(bf16[2,3,5,192,256]{4,3,2,1,0:T(8,128)(2,1)} %get-tuple-element.140), channel_id=1, source_target_pairs={{0,8},{4,12},{8,0},{12,4},{16,24},{20,28},{24,16},{28,20},{1,9},{5... | collective-permute-start | bytes 8847368 | tf_op jit(solution)/shard_map/ppermute | solution.py:67
  292.8 28.3 %collective-permute-start.13 = (bf16[128,1536]{1,0:T(8,128)(2,1)}, bf16[128,1536]{1,0:T(8,128)(2,1)}, u32[]{:S(2)}, u32[]{:S(2)}) collective-permute-start(bf16[128,1536]{1,0:T(8,128)(2,1)} %get-tuple-element.154), channel_id=1, source_target_pairs={{0,3},{1,0},{2,1},{3,2},{4,7},{5,4},{6,5},{7,6},{8,11},{9,8},{10,9... | collective-permute-start | bytes 1179656 | tf_op jit(solution)/shard_map/ppermute | solution.py:77
  292.9 28.4 %collective-permute-start.14 = (bf16[128,1536]{1,0:T(8,128)(2,1)}, bf16[128,1536]{1,0:T(8,128)(2,1)}, u32[]{:S(2)}, u32[]{:S(2)}) collective-permute-start(bf16[128,1536]{1,0:T(8,128)(2,1)} %get-tuple-element.155), channel_id=1, source_target_pairs={{0,2},{1,3},{2,0},{3,1},{4,6},{5,7},{6,4},{7,5},{8,10},{9,11},{10,... | collective-permute-start | bytes 1179656 | tf_op jit(solution)/shard_map/ppermute | solution.py:77
  295.3 26.1 %collective-permute-start.15 = (bf16[128,1536]{1,0:T(8,128)(2,1)S(1)}, bf16[128,1536]{1,0:T(8,128)(2,1)}, u32[]{:S(2)}, u32[]{:S(2)}) collective-permute-start(bf16[128,1536]{1,0:T(8,128)(2,1)S(1)} %get-tuple-element.156), channel_id=1, source_target_pairs={{0,1},{1,2},{2,3},{3,0},{4,5},{5,6},{6,7},{7,4},{8,9},{9,10},{10,1... | collective-permute-start | bytes 1179656 | tf_op jit(solution)/shard_map/ppermute | solution.py:77
  316.8 63.0 %collective-permute-start.17 = (bf16[3,5,192,256]{3,2,1,0:T(8,128)(2,1)}, bf16[3,5,192,256]{3,2,1,0:T(8,128)(2,1)}, u32[]{:S(2)}, u32[]{:S(2)}) collective-permute-start(bf16[3,5,192,256]{3,2,1,0:T(8,128)(2,1)} %fusion.3), channel_id=1, source_target_pairs={{0,16},{4,20},{8,24},{12,28},{16,0},{20,4},{24,8},{28,12},{1,17},{... | collective-permute-start | bytes 4423688 | tf_op jit(solution)/shard_map/ppermute | solution.py:70
  320.4 59.3 %collective-permute-start.16 = (bf16[3,5,192,256]{3,2,1,0:T(8,128)(2,1)}, bf16[3,5,192,256]{3,2,1,0:T(8,128)(2,1)}, u32[]{:S(2)}, u32[]{:S(2)}) collective-permute-start(bf16[3,5,192,256]{3,2,1,0:T(8,128)(2,1)} %fusion.2), channel_id=1, source_target_pairs={{0,8},{4,12},{8,0},{12,4},{16,24},{20,28},{24,16},{28,20},{1,9},{5... | collective-permute-start | bytes 4423688 | tf_op jit(solution)/shard_map/ppermute | solution.py:67
  384.1 18.7 %collective-permute-start.19 = (bf16[2,5,192,256]{3,2,1,0:T(8,128)(2,1)}, bf16[2,5,192,256]{3,2,1,0:T(8,128)(2,1)S(1)}, u32[]{:S(2)}, u32[]{:S(2)}) collective-permute-start(bf16[2,5,192,256]{3,2,1,0:T(8,128)(2,1)} %fusion.1), channel_id=1, source_target_pairs={{0,4},{4,0},{8,12},{12,8},{16,20},{20,16},{24,28},{28,24},{1,5},{5... | collective-permute-start | bytes 2949128 | tf_op jit(solution)/shard_map/ppermute | solution.py:64
  390.7 11.4 %collective-permute-start.18 = (bf16[48,1536]{1,0:T(8,128)(2,1)S(1)}, bf16[48,1536]{1,0:T(8,128)(2,1)S(1)}, u32[]{:S(2)}, u32[]{:S(2)}) collective-permute-start(bf16[48,1536]{1,0:T(8,128)(2,1)S(1)} %copy-done.15), channel_id=1, source_target_pairs={{0,0},{4,1},{8,2},{12,3},{16,4},{20,5},{24,6},{28,7},{1,8},{5,9},{... | collective-permute-start | bytes 442376 | tf_op jit(solution)/shard_map/ppermute | solution.py:1365
  (12 other events, 39.2 us)
